TPU v7x, 32 devices: a whole 2x2x4 slice. The times are simulated.
32 devices in a mesh: rep: 4 (over y, x), dom: 8 (over z, core).
Axes of the slice: x: 2, y: 2, z: 4, core: 2. Of those that a mesh axis runs over, the one named last changes fastest.
Arguments:
- positions: float32 [4, 3, 8192], P('rep', None, 'dom'), may hold values from -6 to 6
- velocities: float32 [4, 3, 8192], P('rep', None, 'dom'), may hold values from -6 to 6
- charge: float32 [8192], P('dom'), may hold values from 0.5 to 2
- inverse_mass: float32 [8192], P('dom'), may hold values from 0.5 to 2
- pair_tiles: int32 [64, 6], P('dom'), may hold values from -1 to 11, as said below
- halo_tiles: int32 [8, 2, 2], P('dom'), may hold values from 0 to 7, as said below
- owners: int32 [64, 4], P('dom'), may hold values from 0 to 7, all different within a row; in each aligned block of 8 rows (0 to 7, 8 to 15, ...) at most 5 rows name the same one
- centres: float32 [3, 8192], P(None, 'dom'), may hold values from -6 to 6
- widths: float32 [8192], P('dom'), may hold values from 1 to 4
- map_density: float32 [8192], P('dom'), may hold values from 0.1 to 0.6
- map_error: float32 [8192], P('dom'), may hold values from 0.1 to 0.3
- partner: int32 [4], replicated, may hold values from 0 to 3, as said below
- decision: int32 [4], replicated, may hold values from 0 to 1, as said below
Outputs:
- new_positions: float32 [4, 3, 8192], P('rep', None, 'dom')
- new_velocities: float32 [4, 3, 8192], P('rep', None, 'dom')
- model_map: float32 [8192], P('dom')
Inputs may be any that keep to these rules, and one draw needn't show every extreme that they name: `pair_tiles`: entry j of a tile's row names tile j of the same domain if j < 8; tile j - 8 of the upper list (row [d - 1, 1]) of the domain below if j < 10; else tile j - 10 of the lower list (row [d + 1, 0]) of the domain above; domains wrap around. -1 marks an empty entry; live entries of a row are distinct and come first. `halo_tiles`: row [d, 0] lists distinct tiles of domain d for domain d - 1, row [d, 1] distinct tiles for domain d + 1. `owners`: each row names 4 distinct domains; within the 8 rows of one domain no domain is named more than 5 times, a bound that some block reaches. `partner`: a permutation of the replicas; some replica r has partner r + 4 / 2 (counted round) and decision 1. `decision`: the same on all replicas of one cycle of partner; at least one replica is accepted and one is not.
All inputs are finite; a program needn't handle non-finite values.
Results may differ from a plain program's by a relative error of at most 0.0001.
Values sent between devices are 32-bit elements; how exact they have to be, the bound alone decides.
No kernel may reach another device: no remote copies, remote signals or barrier semaphores. Data moves between devices by JAX's collectives and lax.ppermute only.
A program may use at most 64 MiB of HBM per device.

v0:
```python
import jax
import jax.numpy as jnp
from jax import lax
from jax.sharding import PartitionSpec as P

STEPS = 2


highest = lax.Precision.HIGHEST
time_step = 0.5
pair_width = 1.0
map_scale = 2.0


def with_halo(block, sides, width):
    for axis, dim in sides:
        count = lax.axis_size(axis)
        forward = [(i, i + 1) for i in range(count - 1)]
        forward.append((count - 1, 0))
        backward = [(target, source) for source, target in forward]
        low = lax.ppermute(
            lax.slice_in_dim(block, block.shape[dim] - width, None, axis=dim), axis, forward
        )
        high = lax.ppermute(lax.slice_in_dim(block, 0, width, axis=dim), axis, backward)
        block = jnp.concatenate([low, block, high], axis=dim)
    return block


def block_size(count, wanted):
    size = max(1, min(count, wanted))
    while count % size:
        size = size - 1
    return size


def pair_force(own_tiles, neighbours, pair_gain):
    squared = jnp.zeros(
        neighbours.shape[:2] + (own_tiles.shape[2], neighbours.shape[3]), jnp.float32
    )
    for dim_index in range(3):
        apart = own_tiles[:, None, dim_index, :, None] - neighbours[:, :, dim_index, None, :]
        squared = squared + apart * apart
    weights = jnp.exp(-squared / (2.0 * pair_width)) * neighbours[:, :, 3, None, :]
    weight_sum = jnp.sum(weights, (1, 3))
    pulled = jnp.einsum("bjat,bjct->bca", weights, neighbours[:, :, :3, :], precision=highest)
    return (
        pair_gain
        / pair_width
        * own_tiles[:, 3, None, :]
        * (own_tiles[:, :3, :] * weight_sum[:, None, :] - pulled)
    )


def slot_gaussians(coords, centre, extent):
    squared = jnp.zeros((coords.shape[0], coords.shape[2], centre.shape[1]), jnp.float32)
    for dim_index in range(3):
        apart = coords[:, dim_index, :, None] - centre[dim_index][None, None, :]
        squared = squared + apart * apart
    return jnp.exp(-squared / (2.0 * extent[None, None, :]))


def owner_matrix(owners, domains, capacity):
    tile_count, owned = owners.shape
    flat_owners = owners.reshape(-1)
    matches = (flat_owners[:, None] == jnp.arange(domains, dtype=jnp.int32)[None, :]).astype(
        jnp.int32
    )
    earlier = jnp.cumsum(matches, 0) - matches
    slot_ids = jnp.sum(earlier * matches, 1)
    targets = (flat_owners * capacity + slot_ids).reshape(tile_count, owned)
    row_ids = jnp.arange(domains * capacity, dtype=jnp.int32)
    return jnp.sum((row_ids[:, None, None] == targets[None, :, :]).astype(jnp.float32), 2)


def nonbonded(position, charges, halo_tiles, pair_tiles):
    tile_count = position.shape[0]
    tile_len = position.shape[2]
    stacked = jnp.concatenate([position, charges[:, None, :]], 1)
    halo_sides = halo_tiles[0]
    side_select = (
        halo_sides[:, :, None] == jnp.arange(tile_count, dtype=jnp.int32)[None, None, :]
    ).astype(jnp.float32)
    rim_out = jnp.einsum("shn,nck->shck", side_select, stacked, precision=highest)
    padded = with_halo(rim_out, (("dom", 0),), 1)
    tile_table = jnp.concatenate([stacked, padded[0], padded[3]], 0)
    extent = tile_table.shape[0]
    selection = (
        pair_tiles[:, :, None] == jnp.arange(extent, dtype=jnp.int32)[None, None, :]
    ).astype(jnp.float32)
    near_tiles = jnp.einsum("njw,wck->njck", selection, tile_table, precision=highest)
    group_size = block_size(tile_count, max(1, 512 // tile_len))
    pair_gain = (pair_tiles.shape[1] * tile_len) ** (-0.5)

    def one_block(pieces):
        return pair_force(pieces[0], pieces[1], pair_gain)

    shaped = (
        stacked.reshape((-1, group_size) + stacked.shape[1:]),
        near_tiles.reshape((-1, group_size) + near_tiles.shape[1:]),
    )
    return lax.map(one_block, shaped).reshape(tile_count, 3, tile_len)


def map_send(position, owners, centre, extent, density, error, intersection_scale):
    domains = lax.axis_size("dom")
    tile_count, owned = owners.shape
    tile_len = position.shape[2]
    map_gain = map_scale / (owned * centre.shape[1])
    capacity = max(2, tile_count * owned // domains + 1)
    matrix = owner_matrix(owners, domains, capacity)
    outgoing = jnp.einsum("sn,nck->sck", matrix, position, precision=highest).reshape(
        domains, capacity, 3, tile_len
    )
    live_slots = jnp.sum(matrix, 1).reshape(domains, capacity)
    arrived, alive_flags = (
        lax.all_to_all(outgoing, "dom", split_axis=0, concat_axis=0, tiled=True),
        lax.all_to_all(live_slots, "dom", split_axis=0, concat_axis=0, tiled=True),
    )
    slot_total = domains * capacity
    group_size = block_size(slot_total, max(1, 512 // tile_len))
    coords_block = arrived.reshape(-1, group_size, 3, tile_len)
    alive_blocks = alive_flags.reshape(-1, group_size)

    def intersection_pass(pieces):
        return jnp.sum(slot_gaussians(pieces[0], centre, extent) * pieces[1][:, None, None], (0, 1))

    partial_value = (
        jnp.sum(lax.map(intersection_pass, (coords_block, alive_blocks)), 0) * intersection_scale
    )
    totals = lax.psum(partial_value, "rep")
    model_map = totals / lax.axis_size("rep")
    coefficient = map_gain * (model_map - density) / (error * error) / extent

    def force_pass(pieces):
        weighted = (
            slot_gaussians(pieces[0], centre, extent)
            * coefficient[None, None, :]
            * pieces[1][:, None, None]
        )
        pulled = jnp.einsum("gak,ck->gca", weighted, centre, precision=highest)
        return pieces[0] * jnp.sum(weighted, 2)[:, None, :] - pulled

    pushes = lax.map(force_pass, (coords_block, alive_blocks)).reshape(
        domains, capacity, 3, tile_len
    )
    returned = lax.all_to_all(pushes, "dom", split_axis=0, concat_axis=0, tiled=True)
    forces = jnp.einsum(
        "sn,sck->nck", matrix, returned.reshape(slot_total, 3, tile_len), precision=highest
    )
    return (forces, model_map)


def local(
    positions,
    velocities,
    charge,
    inverse_mass,
    pair_tiles,
    halo_tiles,
    owners,
    centres,
    widths,
    map_density,
    map_error,
    partner,
    decision,
):
    tile_count = pair_tiles.shape[0]
    tile_len = positions.shape[2] // tile_count
    position = positions[0].reshape(3, tile_count, tile_len).transpose(1, 0, 2)
    velocity = velocities[0].reshape(3, tile_count, tile_len).transpose(1, 0, 2)
    charges = charge.reshape(tile_count, tile_len)
    inverse = inverse_mass.reshape(tile_count, tile_len)
    intersection_scale = 1.0 / (owners.shape[1] * tile_count * tile_len)
    model_map = jnp.zeros_like(widths)
    for step_index in range(STEPS):
        pushed = nonbonded(position, charges, halo_tiles, pair_tiles)
        pulled, model_map = map_send(
            position, owners, centres, widths, map_density, map_error, intersection_scale
        )
        velocity = velocity + time_step * inverse[:, None, :] * (pushed + pulled)
        position = position + time_step * velocity
    replicas = lax.axis_size("rep")
    replica_ids = jnp.arange(replicas, dtype=jnp.int32)
    source = jnp.where(decision == 1, partner, replica_ids)
    states = jnp.stack([position, velocity]).reshape(-1, tile_len)
    spread = lax.all_to_all(states, "rep", split_axis=0, concat_axis=0, tiled=True)
    selector = (source[:, None] == replica_ids[None, :]).astype(jnp.float32)
    permuted = jnp.dot(selector, spread.reshape(replicas, -1), precision=highest).reshape(
        -1, tile_len
    )
    returned = lax.all_to_all(permuted, "rep", split_axis=0, concat_axis=0, tiled=True).reshape(
        2, tile_count, 3, tile_len
    )
    position = returned[0]
    velocity = returned[1]
    new_positions = position.transpose(1, 0, 2).reshape(1, 3, tile_count * tile_len)
    new_velocities = velocity.transpose(1, 0, 2).reshape(1, 3, tile_count * tile_len)
    return (new_positions, new_velocities, model_map)


def solution(mesh):
    placed = (
        P("rep", None, "dom"),
        P("rep", None, "dom"),
        P("dom"),
        P("dom"),
        P("dom", None),
        P("dom", None, None),
        P("dom", None),
        P(None, "dom"),
        P("dom"),
        P("dom"),
        P("dom"),
        P(),
        P(),
    )
    return jax.shard_map(
        local,
        mesh=mesh,
        in_specs=placed,
        out_specs=(P("rep", None, "dom"), P("rep", None, "dom"), P("dom")),
        check_vma=False,
    )
```

profile of v0, /device:TPU:0, one launch (start us, length us, event | category | flops | bytes accessed | tf_op | source)
XLA Modules:
  0.0 214.3 jit_solution(2627661170757417328)
XLA Ops:
  2.8 6.4 %all-to-all-start.1 = ((f32[8,1,5]{2,1,0:T(1,128)}), f32[8,1,5]{2,1,0:T(1,128)S(1)}, u32[]{:S(2)}, u32[]{:S(2)}) async-start(f32[8,1,5]{2,1,0:T(1,128)} %bitcast.91), calls=%async_computation.1 | async-start | bytes 8192 | tf_op jit(solution)/shard_map/all_to_all | solution.py:117
  19.5 4.5 %all-to-all-done = f32[8,5,3,128]{3,2,1,0:T(4,128)S(1)} async-done(((f32[8,5,3,128]{3,2,1,0:T(4,128)}), f32[8,5,3,128]{3,2,1,0:T(4,128)S(1)}, u32[]{:S(2)}, u32[]{:S(2)}) %all-to-all-start) | async-done | bytes 61472 | tf_op jit(solution)/shard_map/all_to_all | solution.py:116
  24.8 12.5 %while.61 = (s32[]{:T(128)}, f32[10,1024]{1,0:T(8,128)S(1)}, f32[10,4,3,128]{3,1,2,0:T(4,128)S(1)}, f32[3,1024]{1,0:T(4,128)S(1)}, f32[1024]{0:T(1024)S(1)}, /*index=5*/f32[10,4]{1,0:T(8,128)S(1)}, s32[]{:T(128)}, s32[]{:T(128)}) while((s32[]{:T(128)}, f32[10,1024]{1,0:T(8,128)S(1)}, f32[10,4,3,128]{3,1,2,0:T(4,128)S(1)}, ...), condition=%wide.region_9.10_spmd, body=%wide.region_7.9_spmd.sunk | while | flops 6291458 | bytes 92305 | solution.py:128
  37.3 9.9 %psum.14 = f32[1024]{0:T(1024)S(1)} all-reduce(f32[1024]{0:T(1024)S(1)} %broadcast_multiply_fusion.6), channel_id=1, replica_groups=mesh['rep'=4,'dom'=8] {'rep'}, use_global_device_ids=true, to_apply=%region_11.12 | all-reduce | flops 1024 | bytes 8192 | tf_op jit(solution)/shard_map/psum | solution.py:130
  47.9 47.8 %while.62 = (s32[]{:T(128)}, f32[10,4,3,128]{3,2,1,0:T(4,128)}, f32[10,4,3,128]{3,2,1,0:T(4,128)S(1)}, f32[3,1024]{1,0:T(4,128)S(1)}, f32[1024]{0:T(1024)S(1)}, ...) while((s32[]{:T(128)}, f32[10,4,3,128]{3,2,1,0:T(4,128)}, f32[10,4,3,128]{3,2,1,0:T(4,128)S(1)}, ...), condition=%wide.region_14.15_spmd, body=%wide.region_12.14_spmd.sunk | while | flops 31985152 | bytes 141981 | solution.py:143
  49.2 3.5 %fusion.144 = f32[10,4,3,128]{3,2,1,0:T(4,128)} fusion(f32[10,4,3,128]{3,2,1,0:T(4,128)} %get-tuple-element.826, s32[]{:T(128)} %get-tuple-element.825, f32[4]{0:T(128)S(1)} %fusion.140, f32[1024]{0:T(1024)S(1)} %get-tuple-element.838, f32[1024]{0:T(1024)S(1)} %broadcast_multiply_fusion.13, f32[1024]{0:T(1024)S(1)} %bitcast.373, ...), kind=kOutput, calls=%fused_computation.38.clone.1 | convolution fusion | flops 25168896 | bytes 55824 | tf_op jit(solution)/shard_map/while/body/eval_jaxpr/gak,ck->gca/dot_general | solution.py:140
  54.0 3.5 %fusion.144 = f32[10,4,3,128]{3,2,1,0:T(4,128)} fusion(f32[10,4,3,128]{3,2,1,0:T(4,128)} %get-tuple-element.826, s32[]{:T(128)} %get-tuple-element.825, f32[4]{0:T(128)S(1)} %fusion.140, f32[1024]{0:T(1024)S(1)} %get-tuple-element.838, f32[1024]{0:T(1024)S(1)} %broadcast_multiply_fusion.13, f32[1024]{0:T(1024)S(1)} %bitcast.373, ...), kind=kOutput, calls=%fused_computation.38.clone.1 | convolution fusion | flops 25168896 | bytes 55824 | tf_op jit(solution)/shard_map/while/body/eval_jaxpr/gak,ck->gca/dot_general | solution.py:140
  58.7 3.5 %fusion.144 = f32[10,4,3,128]{3,2,1,0:T(4,128)} fusion(f32[10,4,3,128]{3,2,1,0:T(4,128)} %get-tuple-element.826, s32[]{:T(128)} %get-tuple-element.825, f32[4]{0:T(128)S(1)} %fusion.140, f32[1024]{0:T(1024)S(1)} %get-tuple-element.838, f32[1024]{0:T(1024)S(1)} %broadcast_multiply_fusion.13, f32[1024]{0:T(1024)S(1)} %bitcast.373, ...), kind=kOutput, calls=%fused_computation.38.clone.1 | convolution fusion | flops 25168896 | bytes 55824 | tf_op jit(solution)/shard_map/while/body/eval_jaxpr/gak,ck->gca/dot_general | solution.py:140
  63.5 3.5 %fusion.144 = f32[10,4,3,128]{3,2,1,0:T(4,128)} fusion(f32[10,4,3,128]{3,2,1,0:T(4,128)} %get-tuple-element.826, s32[]{:T(128)} %get-tuple-element.825, f32[4]{0:T(128)S(1)} %fusion.140, f32[1024]{0:T(1024)S(1)} %get-tuple-element.838, f32[1024]{0:T(1024)S(1)} %broadcast_multiply_fusion.13, f32[1024]{0:T(1024)S(1)} %bitcast.373, ...), kind=kOutput, calls=%fused_computation.38.clone.1 | convolution fusion | flops 25168896 | bytes 55824 | tf_op jit(solution)/shard_map/while/body/eval_jaxpr/gak,ck->gca/dot_general | solution.py:140
  68.3 3.5 %fusion.144 = f32[10,4,3,128]{3,2,1,0:T(4,128)} fusion(f32[10,4,3,128]{3,2,1,0:T(4,128)} %get-tuple-element.826, s32[]{:T(128)} %get-tuple-element.825, f32[4]{0:T(128)S(1)} %fusion.140, f32[1024]{0:T(1024)S(1)} %get-tuple-element.838, f32[1024]{0:T(1024)S(1)} %broadcast_multiply_fusion.13, f32[1024]{0:T(1024)S(1)} %bitcast.373, ...), kind=kOutput, calls=%fused_computation.38.clone.1 | convolution fusion | flops 25168896 | bytes 55824 | tf_op jit(solution)/shard_map/while/body/eval_jaxpr/gak,ck->gca/dot_general | solution.py:140
  73.1 3.5 %fusion.144 = f32[10,4,3,128]{3,2,1,0:T(4,128)} fusion(f32[10,4,3,128]{3,2,1,0:T(4,128)} %get-tuple-element.826, s32[]{:T(128)} %get-tuple-element.825, f32[4]{0:T(128)S(1)} %fusion.140, f32[1024]{0:T(1024)S(1)} %get-tuple-element.838, f32[1024]{0:T(1024)S(1)} %broadcast_multiply_fusion.13, f32[1024]{0:T(1024)S(1)} %bitcast.373, ...), kind=kOutput, calls=%fused_computation.38.clone.1 | convolution fusion | flops 25168896 | bytes 55824 | tf_op jit(solution)/shard_map/while/body/eval_jaxpr/gak,ck->gca/dot_general | solution.py:140
  77.9 3.5 %fusion.144 = f32[10,4,3,128]{3,2,1,0:T(4,128)} fusion(f32[10,4,3,128]{3,2,1,0:T(4,128)} %get-tuple-element.826, s32[]{:T(128)} %get-tuple-element.825, f32[4]{0:T(128)S(1)} %fusion.140, f32[1024]{0:T(1024)S(1)} %get-tuple-element.838, f32[1024]{0:T(1024)S(1)} %broadcast_multiply_fusion.13, f32[1024]{0:T(1024)S(1)} %bitcast.373, ...), kind=kOutput, calls=%fused_computation.38.clone.1 | convolution fusion | flops 25168896 | bytes 55824 | tf_op jit(solution)/shard_map/while/body/eval_jaxpr/gak,ck->gca/dot_general | solution.py:140
  82.7 3.5 %fusion.144 = f32[10,4,3,128]{3,2,1,0:T(4,128)} fusion(f32[10,4,3,128]{3,2,1,0:T(4,128)} %get-tuple-element.826, s32[]{:T(128)} %get-tuple-element.825, f32[4]{0:T(128)S(1)} %fusion.140, f32[1024]{0:T(1024)S(1)} %get-tuple-element.838, f32[1024]{0:T(1024)S(1)} %broadcast_multiply_fusion.13, f32[1024]{0:T(1024)S(1)} %bitcast.373, ...), kind=kOutput, calls=%fused_computation.38.clone.1 | convolution fusion | flops 25168896 | bytes 55824 | tf_op jit(solution)/shard_map/while/body/eval_jaxpr/gak,ck->gca/dot_general | solution.py:140
  92.2 3.5 %fusion.144 = f32[10,4,3,128]{3,2,1,0:T(4,128)} fusion(f32[10,4,3,128]{3,2,1,0:T(4,128)} %get-tuple-element.826, s32[]{:T(128)} %get-tuple-element.825, f32[4]{0:T(128)S(1)} %fusion.140, f32[1024]{0:T(1024)S(1)} %get-tuple-element.838, f32[1024]{0:T(1024)S(1)} %broadcast_multiply_fusion.13, f32[1024]{0:T(1024)S(1)} %bitcast.373, ...), kind=kOutput, calls=%fused_computation.38.clone.1 | convolution fusion | flops 25168896 | bytes 55824 | tf_op jit(solution)/shard_map/while/body/eval_jaxpr/gak,ck->gca/dot_general | solution.py:140
  99.1 6.1 %while.60 = (s32[]{:T(128)}, f32[2,4,3,128]{3,1,0,2:T(4,128)S(1)}, f32[2,4,4,128]{3,2,1,0:T(4,128)S(1)}, f32[2,4,6,4,128]{4,1,0,3,2:T(4,128)S(1)}, s32[]{:T(128)}) while((s32[]{:T(128)}, f32[2,4,3,128]{3,1,0,2:T(4,128)S(1)}, f32[2,4,4,128]{3,2,1,0:T(4,128)S(1)}, f32[2,4,6,4,128]{4,1,0,3,2:T(4,128)S(1)}, s32[]{:T(128)}) %tuple.213), condition=%wide.region_2.3_spmd, body=%wide.region_0.2_spmd.sunk | while | flops 23204352 | bytes 716873 | solution.py:101
  106.5 5.0 %all-to-all-start.3 = ((f32[8,5,3,128]{3,2,1,0:T(4,128)}), f32[8,5,3,128]{3,2,1,0:T(4,128)S(1)}, u32[]{:S(2)}, u32[]{:S(2)}) async-start(f32[8,5,3,128]{3,2,1,0:T(4,128)} %copy.183), calls=%async_computation.3 | async-start | bytes 163840 | tf_op jit(solution)/shard_map/all_to_all | solution.py:116
  117.7 12.5 %while.64 = (s32[]{:T(128)}, f32[10,1024]{1,0:T(8,128)S(1)}, f32[10,4,3,128]{3,1,2,0:T(4,128)S(1)}, f32[3,1024]{1,0:T(4,128)S(1)}, f32[1024]{0:T(1024)S(1)}, /*index=5*/f32[10,4]{1,0:T(8,128)S(1)}, s32[]{:T(128)}, s32[]{:T(128)}) while((s32[]{:T(128)}, f32[10,1024]{1,0:T(8,128)S(1)}, f32[10,4,3,128]{3,1,2,0:T(4,128)S(1)}, ...), condition=%wide.region_20.21_spmd, body=%wide.region_18.20_spmd.sunk | while | flops 6291458 | bytes 92305 | solution.py:128
  130.2 8.0 %psum.15 = f32[1024]{0:T(1024)S(1)} all-reduce(f32[1024]{0:T(1024)S(1)} %broadcast_multiply_fusion.5), channel_id=1, replica_groups=mesh['rep'=4,'dom'=8] {'rep'}, use_global_device_ids=true, to_apply=%region_22.23 | all-reduce | flops 1024 | bytes 8192 | tf_op jit(solution)/shard_map/psum | solution.py:130
  139.4 47.9 %while.65 = (s32[]{:T(128)}, f32[10,4,3,128]{3,2,1,0:T(4,128)}, f32[10,4,3,128]{3,2,1,0:T(4,128)S(1)}, f32[3,1024]{1,0:T(4,128)S(1)}, f32[1024]{0:T(1024)S(1)}, ...) while((s32[]{:T(128)}, f32[10,4,3,128]{3,2,1,0:T(4,128)}, f32[10,4,3,128]{3,2,1,0:T(4,128)S(1)}, ...), condition=%wide.region_25.26_spmd, body=%wide.region_23.25_spmd.sunk | while | flops 31985152 | bytes 141981 | solution.py:143
  140.7 3.5 %fusion.155 = f32[10,4,3,128]{3,2,1,0:T(4,128)} fusion(f32[10,4,3,128]{3,2,1,0:T(4,128)} %get-tuple-element.889, s32[]{:T(128)} %get-tuple-element.888, f32[4]{0:T(128)S(1)} %fusion.151, f32[1024]{0:T(1024)S(1)} %get-tuple-element.901, f32[1024]{0:T(1024)S(1)} %broadcast_multiply_fusion.15, f32[1024]{0:T(1024)S(1)} %bitcast.379, ...), kind=kOutput, calls=%fused_computation.83.clone.1 | convolution fusion | flops 25168896 | bytes 55824 | tf_op jit(solution)/shard_map/while/body/eval_jaxpr/gak,ck->gca/dot_general | solution.py:140
  145.5 3.5 %fusion.155 = f32[10,4,3,128]{3,2,1,0:T(4,128)} fusion(f32[10,4,3,128]{3,2,1,0:T(4,128)} %get-tuple-element.889, s32[]{:T(128)} %get-tuple-element.888, f32[4]{0:T(128)S(1)} %fusion.151, f32[1024]{0:T(1024)S(1)} %get-tuple-element.901, f32[1024]{0:T(1024)S(1)} %broadcast_multiply_fusion.15, f32[1024]{0:T(1024)S(1)} %bitcast.379, ...), kind=kOutput, calls=%fused_computation.83.clone.1 | convolution fusion | flops 25168896 | bytes 55824 | tf_op jit(solution)/shard_map/while/body/eval_jaxpr/gak,ck->gca/dot_general | solution.py:140
  150.3 3.5 %fusion.155 = f32[10,4,3,128]{3,2,1,0:T(4,128)} fusion(f32[10,4,3,128]{3,2,1,0:T(4,128)} %get-tuple-element.889, s32[]{:T(128)} %get-tuple-element.888, f32[4]{0:T(128)S(1)} %fusion.151, f32[1024]{0:T(1024)S(1)} %get-tuple-element.901, f32[1024]{0:T(1024)S(1)} %broadcast_multiply_fusion.15, f32[1024]{0:T(1024)S(1)} %bitcast.379, ...), kind=kOutput, calls=%fused_computation.83.clone.1 | convolution fusion | flops 25168896 | bytes 55824 | tf_op jit(solution)/shard_map/while/body/eval_jaxpr/gak,ck->gca/dot_general | solution.py:140
  155.1 3.5 %fusion.155 = f32[10,4,3,128]{3,2,1,0:T(4,128)} fusion(f32[10,4,3,128]{3,2,1,0:T(4,128)} %get-tuple-element.889, s32[]{:T(128)} %get-tuple-element.888, f32[4]{0:T(128)S(1)} %fusion.151, f32[1024]{0:T(1024)S(1)} %get-tuple-element.901, f32[1024]{0:T(1024)S(1)} %broadcast_multiply_fusion.15, f32[1024]{0:T(1024)S(1)} %bitcast.379, ...), kind=kOutput, calls=%fused_computation.83.clone.1 | convolution fusion | flops 25168896 | bytes 55824 | tf_op jit(solution)/shard_map/while/body/eval_jaxpr/gak,ck->gca/dot_general | solution.py:140
  159.9 3.5 %fusion.155 = f32[10,4,3,128]{3,2,1,0:T(4,128)} fusion(f32[10,4,3,128]{3,2,1,0:T(4,128)} %get-tuple-element.889, s32[]{:T(128)} %get-tuple-element.888, f32[4]{0:T(128)S(1)} %fusion.151, f32[1024]{0:T(1024)S(1)} %get-tuple-element.901, f32[1024]{0:T(1024)S(1)} %broadcast_multiply_fusion.15, f32[1024]{0:T(1024)S(1)} %bitcast.379, ...), kind=kOutput, calls=%fused_computation.83.clone.1 | convolution fusion | flops 25168896 | bytes 55824 | tf_op jit(solution)/shard_map/while/body/eval_jaxpr/gak,ck->gca/dot_general | solution.py:140
  164.7 3.5 %fusion.155 = f32[10,4,3,128]{3,2,1,0:T(4,128)} fusion(f32[10,4,3,128]{3,2,1,0:T(4,128)} %get-tuple-element.889, s32[]{:T(128)} %get-tuple-element.888, f32[4]{0:T(128)S(1)} %fusion.151, f32[1024]{0:T(1024)S(1)} %get-tuple-element.901, f32[1024]{0:T(1024)S(1)} %broadcast_multiply_fusion.15, f32[1024]{0:T(1024)S(1)} %bitcast.379, ...), kind=kOutput, calls=%fused_computation.83.clone.1 | convolution fusion | flops 25168896 | bytes 55824 | tf_op jit(solution)/shard_map/while/body/eval_jaxpr/gak,ck->gca/dot_general | solution.py:140
  169.5 3.5 %fusion.155 = f32[10,4,3,128]{3,2,1,0:T(4,128)} fusion(f32[10,4,3,128]{3,2,1,0:T(4,128)} %get-tuple-element.889, s32[]{:T(128)} %get-tuple-element.888, f32[4]{0:T(128)S(1)} %fusion.151, f32[1024]{0:T(1024)S(1)} %get-tuple-element.901, f32[1024]{0:T(1024)S(1)} %broadcast_multiply_fusion.15, f32[1024]{0:T(1024)S(1)} %bitcast.379, ...), kind=kOutput, calls=%fused_computation.83.clone.1 | convolution fusion | flops 25168896 | bytes 55824 | tf_op jit(solution)/shard_map/while/body/eval_jaxpr/gak,ck->gca/dot_general | solution.py:140
  174.3 3.5 %fusion.155 = f32[10,4,3,128]{3,2,1,0:T(4,128)} fusion(f32[10,4,3,128]{3,2,1,0:T(4,128)} %get-tuple-element.889, s32[]{:T(128)} %get-tuple-element.888, f32[4]{0:T(128)S(1)} %fusion.151, f32[1024]{0:T(1024)S(1)} %get-tuple-element.901, f32[1024]{0:T(1024)S(1)} %broadcast_multiply_fusion.15, f32[1024]{0:T(1024)S(1)} %bitcast.379, ...), kind=kOutput, calls=%fused_computation.83.clone.1 | convolution fusion | flops 25168896 | bytes 55824 | tf_op jit(solution)/shard_map/while/body/eval_jaxpr/gak,ck->gca/dot_general | solution.py:140
  179.1 3.5 %fusion.155 = f32[10,4,3,128]{3,2,1,0:T(4,128)} fusion(f32[10,4,3,128]{3,2,1,0:T(4,128)} %get-tuple-element.889, s32[]{:T(128)} %get-tuple-element.888, f32[4]{0:T(128)S(1)} %fusion.151, f32[1024]{0:T(1024)S(1)} %get-tuple-element.901, f32[1024]{0:T(1024)S(1)} %broadcast_multiply_fusion.15, f32[1024]{0:T(1024)S(1)} %bitcast.379, ...), kind=kOutput, calls=%fused_computation.83.clone.1 | convolution fusion | flops 25168896 | bytes 55824 | tf_op jit(solution)/shard_map/while/body/eval_jaxpr/gak,ck->gca/dot_general | solution.py:140
  183.8 3.5 %fusion.155 = f32[10,4,3,128]{3,2,1,0:T(4,128)} fusion(f32[10,4,3,128]{3,2,1,0:T(4,128)} %get-tuple-element.889, s32[]{:T(128)} %get-tuple-element.888, f32[4]{0:T(128)S(1)} %fusion.151, f32[1024]{0:T(1024)S(1)} %get-tuple-element.901, f32[1024]{0:T(1024)S(1)} %broadcast_multiply_fusion.15, f32[1024]{0:T(1024)S(1)} %bitcast.379, ...), kind=kOutput, calls=%fused_computation.83.clone.1 | convolution fusion | flops 25168896 | bytes 55824 | tf_op jit(solution)/shard_map/while/body/eval_jaxpr/gak,ck->gca/dot_general | solution.py:140
  190.7 6.1 %while.63 = (s32[]{:T(128)}, f32[2,4,3,128]{3,1,0,2:T(4,128)S(1)}, f32[2,4,4,128]{3,2,1,0:T(4,128)S(1)}, f32[2,4,6,4,128]{4,1,0,3,2:T(4,128)S(1)}, s32[]{:T(128)}) while((s32[]{:T(128)}, f32[2,4,3,128]{3,1,0,2:T(4,128)S(1)}, f32[2,4,4,128]{3,2,1,0:T(4,128)S(1)}, f32[2,4,6,4,128]{4,1,0,3,2:T(4,128)S(1)}, s32[]{:T(128)}) %tuple.212), condition=%wide.region_17.18_spmd, body=%wide.region_15.17_spmd.sunk | while | flops 23204352 | bytes 716873 | solution.py:101
  201.0 4.7 %all-to-all-done.5 = f32[4,12,128]{2,1,0:T(8,128)S(1)} async-done(((f32[4,12,128]{2,1,0:T(8,128)}), f32[4,12,128]{2,1,0:T(8,128)S(1)}, u32[]{:S(2)}, u32[]{:S(2)}) %all-to-all-start.5) | async-done | bytes 24608 | tf_op jit(solution)/shard_map/all_to_all | solution.py:187
  205.9 7.1 %all_to_all.45 = f32[4,12,128]{2,1,0:T(8,128)S(1)} all-to-all(f32[4,12,128]{2,1,0:T(8,128)S(1)} %copy.189), channel_id=1, replica_groups=mesh['rep'=4,'dom'=8] {'rep'}, dimensions={0} | all-to-all | bytes 49152 | tf_op jit(solution)/shard_map/all_to_all | solution.py:192
  (416 shorter events, 99.1 us)
Async XLA Ops:
  0.6 8.5 %copy-start.3 = (f32[1024]{0:T(1024)S(1)}, f32[1024]{0:T(1024)}, u32[]{:S(2)}) copy-start(f32[1024]{0:T(1024)} %param.27) | copy-start | bytes 12292
  0.6 8.5 %copy-start.2 = (f32[1,3,1024]{2,0,1:T(1,128)S(1)}, f32[1,3,1024]{2,0,1:T(1,128)}, u32[]{:S(2)}) copy-start(f32[1,3,1024]{2,0,1:T(1,128)} %param.25) | copy-start | bytes 36868
  0.7 8.5 %copy-start.9 = (s32[1,2,2]{2,1,0:T(2,128)S(1)}, s32[1,2,2]{2,1,0:T(2,128)}, u32[]{:S(2)}) copy-start(s32[1,2,2]{2,1,0:T(2,128)} %param.30) | copy-start | bytes 52
  2.8 11.9 %all-to-all-start.1 = ((f32[8,1,5]{2,1,0:T(1,128)}), f32[8,1,5]{2,1,0:T(1,128)S(1)}, u32[]{:S(2)}, u32[]{:S(2)}) async-start(f32[8,1,5]{2,1,0:T(1,128)} %bitcast.91), calls=%async_computation.1 | async-start | bytes 8192 | tf_op jit(solution)/shard_map/all_to_all | solution.py:117
  9.2 4.1 %copy-start.7 = (f32[1024]{0:T(1024)S(1)}, f32[1024]{0:T(1024)}, u32[]{:S(2)}) copy-start(f32[1024]{0:T(1024)} %param.28) | copy-start | bytes 12292
  9.4 9.9 %collective-permute-start = (f32[1,2,4,128]{3,1,2,0:T(2,128)S(1)}, f32[1,2,4,128]{3,1,2,0:T(2,128)S(1)}, u32[]{:S(2)}, u32[]{:S(2)}) collective-permute-start(f32[1,2,4,128]{3,1,2,0:T(2,128)S(1)} %get-tuple-element.468), channel_id=1, source_target_pairs={{0,1},{1,2},{2,3},{3,4},{4,5},{5,6},{6,7},{7,0},{8,9},{9,10},{10,1... | collective-permute-start | bytes 12296 | tf_op jit(solution)/shard_map/ppermute | solution.py:21
  10.0 9.3 %collective-permute-start.1 = (f32[1,2,4,128]{3,1,2,0:T(2,128)S(1)}, f32[1,2,4,128]{3,1,2,0:T(2,128)S(1)}, u32[]{:S(2)}, u32[]{:S(2)}) collective-permute-start(f32[1,2,4,128]{3,1,2,0:T(2,128)S(1)} %get-tuple-element.469), channel_id=1, source_target_pairs={{1,0},{2,1},{3,2},{4,3},{5,4},{6,5},{7,6},{0,7},{9,8},{10,9},{11,1... | collective-permute-start | bytes 12296 | tf_op jit(solution)/shard_map/ppermute | solution.py:24
  13.5 0.7 copy-start.8
  14.7 9.4 %all-to-all-start = ((f32[8,5,3,128]{3,2,1,0:T(4,128)}), f32[8,5,3,128]{3,2,1,0:T(4,128)S(1)}, u32[]{:S(2)}, u32[]{:S(2)}) async-start(f32[8,5,3,128]{3,2,1,0:T(4,128)} %copy.173), calls=%async_computation | async-start | bytes 163840 | tf_op jit(solution)/shard_map/all_to_all | solution.py:116
  24.0 0.7 copy-start
  24.0 0.7 copy-start.1
  24.8 22.5 %copy-start.4 = (f32[1024]{0:T(1024)S(1)}, f32[1024]{0:T(1024)}, u32[]{:S(2)}) copy-start(f32[1024]{0:T(1024)} %param.34) | copy-start | bytes 12292
  24.8 22.5 %copy-start.5 = (f32[1024]{0:T(1024)S(1)}, f32[1024]{0:T(1024)}, u32[]{:S(2)}) copy-start(f32[1024]{0:T(1024)} %param.35) | copy-start | bytes 12292
  95.7 9.5 %all-to-all-start.2 = ((f32[8,5,3,128]{3,2,1,0:T(4,128)}), f32[8,5,3,128]{3,2,1,0:T(4,128)S(1)}, u32[]{:S(2)}, u32[]{:S(2)}) async-start(f32[8,5,3,128]{3,2,1,0:T(4,128)} %bitcast.92), calls=%async_computation.2 | async-start | bytes 163840 | tf_op jit(solution)/shard_map/all_to_all | solution.py:146
  99.1 6.2 %copy-start.6 = (f32[1,3,1024]{2,0,1:T(1,128)S(1)}, f32[1,3,1024]{2,0,1:T(1,128)}, u32[]{:S(2)}) copy-start(f32[1,3,1024]{2,0,1:T(1,128)} %param.26) | copy-start | bytes 36868
  106.5 11.2 %all-to-all-start.3 = ((f32[8,5,3,128]{3,2,1,0:T(4,128)}), f32[8,5,3,128]{3,2,1,0:T(4,128)S(1)}, u32[]{:S(2)}, u32[]{:S(2)}) async-start(f32[8,5,3,128]{3,2,1,0:T(4,128)} %copy.183), calls=%async_computation.3 | async-start | bytes 163840 | tf_op jit(solution)/shard_map/all_to_all | solution.py:116
  111.5 5.8 %collective-permute-start.2 = (f32[1,2,4,128]{3,1,2,0:T(2,128)S(1)}, f32[1,2,4,128]{3,1,2,0:T(2,128)S(1)}, u32[]{:S(2)}, u32[]{:S(2)}) collective-permute-start(f32[1,2,4,128]{3,1,2,0:T(2,128)S(1)} %get-tuple-element.466), channel_id=1, source_target_pairs={{0,1},{1,2},{2,3},{3,4},{4,5},{5,6},{6,7},{7,0},{8,9},{9,10},{10,1... | collective-permute-start | bytes 12296 | tf_op jit(solution)/shard_map/ppermute | solution.py:21
  112.0 5.3 %collective-permute-start.3 = (f32[1,2,4,128]{3,1,2,0:T(2,128)S(1)}, f32[1,2,4,128]{3,1,2,0:T(2,128)S(1)}, u32[]{:S(2)}, u32[]{:S(2)}) collective-permute-start(f32[1,2,4,128]{3,1,2,0:T(2,128)S(1)} %get-tuple-element.467), channel_id=1, source_target_pairs={{1,0},{2,1},{3,2},{4,3},{5,4},{6,5},{7,6},{0,7},{9,8},{10,9},{11,1... | collective-permute-start | bytes 12296 | tf_op jit(solution)/shard_map/ppermute | solution.py:24
  187.3 9.5 %all-to-all-start.4 = ((f32[8,5,3,128]{3,2,1,0:T(4,128)}), f32[8,5,3,128]{3,2,1,0:T(4,128)S(1)}, u32[]{:S(2)}, u32[]{:S(2)}) async-start(f32[8,5,3,128]{3,2,1,0:T(4,128)} %bitcast.106), calls=%async_computation.4 | async-start | bytes 163840 | tf_op jit(solution)/shard_map/all_to_all | solution.py:146
  197.1 3.9 %copy-start.10 = (s32[4]{0:T(128)S(1)}, s32[4]{0:T(128)}, u32[]{:S(2)}) copy-start(s32[4]{0:T(128)} %param.36) | copy-start | bytes 52
  197.1 3.9 %copy-start.11 = (s32[4]{0:T(128)S(1)}, s32[4]{0:T(128)}, u32[]{:S(2)}) copy-start(s32[4]{0:T(128)} %param.37) | copy-start | bytes 52
  197.7 8.0 %all-to-all-start.5 = ((f32[4,12,128]{2,1,0:T(8,128)}), f32[4,12,128]{2,1,0:T(8,128)S(1)}, u32[]{:S(2)}, u32[]{:S(2)}) async-start(f32[4,12,128]{2,1,0:T(8,128)} %all_to_all.35), calls=%async_computation.5 | async-start | bytes 65536 | tf_op jit(solution)/shard_map/all_to_all | solution.py:187
where the time goes:
time: 215 us; the launch traced here: 214 us
  matrix products  79.5 us (37%)
  other arithmetic  50.7 us (24%)
  starting transfers between devices  31.9 us (15%)
  blocking collectives  25 us (12%)
  local copies, waits for them, and re-layouts  11.9 us (6%)
  waiting for transfers between devices  11.9 us (6%)
  loops' own time  2.31 us (1%)
    dot_general x20, matrix products, force_pass(): pulled = jnp.einsum('gak,ck->gca', weighted, centre, precision=highest)  69.8 us
    reduce_sum x20, other arithmetic, force_pass(): return pieces[0] * jnp.sum(weighted, 2)[:, None, :] - pulled  24.7 us
    reduce_sum x20, other arithmetic, intersection_pass(): jnp.sum(slot_gaussians(pieces[0], centre, extent) * pieces[1][:, None, No...  20.7 us
    psum x2, blocking collectives, map_send(): totals = lax.psum(partial_value, 'rep')  17.9 us
    all_to_all x2, starting transfers between devices, map_send(): lax.all_to_all(outgoing, 'dom', split_axis=0, concat_axis=0, tiled=True)  8.37 us
    dot_general x4, matrix products, pair_force(): jnp.einsum('bjat,bjct->bca', weights, neighbours[:, :, :3, :], precision=...  7.89 us
    all_to_all x1, blocking collectives, local(): lax.all_to_all(permuted, 'rep', split_axis=0, concat_axis=0, tiled=True)  7.11 us
    all_to_all x2, starting transfers between devices, map_send(): lax.all_to_all(pushes, 'dom', split_axis=0, concat_axis=0, tiled=True)  6.71 us
  transfers between devices with their start and end apart: 10, of which 5 were waited for; matrix products, arithmetic and copies ran while one was open for 7% of the time, Pallas kernels for 0%

commit v1 on v0

v1 whole, which is shorter than its diff:
```python
import functools
import math

import jax
import jax.numpy as jnp
from jax import lax
from jax.experimental import pallas as pl
from jax.experimental.pallas import tpu as pltpu
from jax.sharding import Mesh, PartitionSpec as P

STEPS = 2
CORES = 2
DEPTH = 32
ROWS = 16
ONE_PHASE_BYTES = 1 << 20

time_step = 0.5
pair_width = 1.0
map_scale = 2.0
log2e = math.log2(math.e)
f32 = jnp.float32
bf16 = jnp.bfloat16

LEFT_PARTS = (0, 0, 1, 1, 0, 2)
RIGHT_PARTS = (0, 1, 0, 1, 2, 0)


def split3(value):
    high = value.astype(bf16).astype(f32)
    rest = value - high
    middle = rest.astype(bf16).astype(f32)
    return high, middle, rest - middle


def point_rows(coords):
    rows = []
    for coord in coords:
        parts = split3(coord)
        rows += [parts[i] for i in LEFT_PARTS]
    parts = split3(coords[0] * coords[0] + coords[1] * coords[1] + coords[2] * coords[2])
    rows += [parts[i] for i in LEFT_PARTS]
    one = jnp.ones_like(coords[0])
    return rows + [one, one, one]


def centre_rows(coords, extent):
    scale = log2e / extent
    rows = []
    for coord in coords:
        parts = split3(coord * scale)
        rows += [parts[i] for i in RIGHT_PARTS]
    parts = split3(-0.5 * scale)
    rows += [parts[i] for i in RIGHT_PARTS]
    square = coords[0] * coords[0] + coords[1] * coords[1] + coords[2] * coords[2]
    return rows + list(split3(-0.5 * scale * square))


def pull_rows(coords, weight):
    rows = list(split3(weight))
    for coord in coords:
        rows += list(split3(coord * weight))
    return rows


def gaussians(left, right):
    return jnp.exp2(jnp.dot(left, right, preferred_element_type=f32))


def pulled_by(rows, weights):
    dims = (((1,), (1,)), ((), ()))
    high = weights.astype(bf16)
    low = (weights - high.astype(f32)).astype(bf16)
    return lax.dot_general(rows, high, dims, preferred_element_type=f32) + lax.dot_general(
        rows, low, dims, preferred_element_type=f32
    )


def pushes(coords, sums):
    def total(first):
        return sums[first : first + 1] + sums[first + 1 : first + 2] + sums[first + 2 : first + 3]

    strength = total(0)
    return [coords[i] * strength - total(3 + 3 * i) for i in range(3)]


def store_rows(ref, rows):
    for index, row in enumerate(rows):
        ref[:, index, :] = row
    depth = ref.shape[1]
    if len(rows) < depth:
        ref[:, len(rows) : depth, :] = jnp.zeros(
            (ref.shape[0], depth - len(rows), ref.shape[2]), f32
        )


def chunks(total, wanted):
    size = wanted if total % wanted == 0 else total
    return [(start, size) for start in range(0, total, size)]


def intersect_kernel(scale, owners_ref, x_ref, comp_ref, out_ref, left_ref, right_ref, xs, cs, acc):
    domains, _, width = comp_ref.shape
    tiles = x_ref.shape[1]
    owned = owners_ref.shape[0] // tiles
    store_rows(xs, point_rows([x_ref[i] for i in range(3)]))
    store_rows(cs, centre_rows([comp_ref[:, i, :] for i in range(3)], comp_ref[:, 3, :]))
    right_ref[...] = cs[...].astype(bf16)
    acc[...] = jnp.zeros_like(acc)

    def one_tile(tile, carry):
        left = xs[tile].T.astype(bf16)
        left_ref[tile] = left
        for j in range(owned):
            owner = owners_ref[tile * owned + j]
            for start, size in chunks(width, 256):
                g = gaussians(left, right_ref[owner, :, start : start + size])
                acc[owner, :, start : start + size] += jnp.sum(
                    g.reshape(g.shape[0] // 8, 8, size), 0
                )
        return carry

    lax.fori_loop(0, tiles, one_tile, 0)
    total = jnp.sum(acc[...], 1) * scale
    for row in range(out_ref.shape[0]):
        out_ref[row] = total


def push_kernel(
    gain, replicas, owners_ref, core_ref, x_ref, comp_ref, sums_ref, left_ref, right_ref, pair_ref,
    out_ref, mean_ref, rs
):
    domains, _, width = comp_ref.shape
    tiles = x_ref.shape[1]
    owned = owners_ref.shape[0] // tiles
    mean = jnp.sum(sums_ref[...], 0) / replicas
    mean_ref[...] = mean
    error = comp_ref[:, 5, :]
    coefficient = gain * (mean - comp_ref[:, 4, :]) / (error * error) / comp_ref[:, 3, :]
    store_rows(rs, pull_rows([comp_ref[:, i, :] for i in range(3)], coefficient))

    def one_tile(tile, carry):
        left = left_ref[tile]
        sums = jnp.zeros((ROWS, x_ref.shape[2]), f32)
        for j in range(owned):
            owner = owners_ref[tile * owned + j]
            for start, size in chunks(width, 256):
                g = gaussians(left, right_ref[owner, :, start : start + size])
                sums += pulled_by(rs[owner, :, start : start + size].astype(bf16), g)
        coords = [x_ref[i, pl.ds(tile, 1), :] for i in range(3)]
        for i, push in enumerate(pushes(coords, sums)):
            out_ref[i, pl.ds(tile, 1), :] = push
        return carry

    lax.fori_loop(0, tiles, one_tile, 0)
    own = tiles // CORES
    for core in range(CORES):

        @pl.when(core_ref[0] == core)
        def _():
            out_ref[:, core * own : (core + 1) * own, :] += pair_ref[...]


def pair_kernel(
    gain, pairs_ref, lists_ref, core_ref, x_ref, charge_ref, far_ref, left_ref, out_ref, table, cs, rs
):
    own = out_ref.shape[1]
    near = pairs_ref.shape[0] // own
    listed = far_ref.shape[1]
    core = core_ref[0]
    base = core * own
    other = (1 - core) * own
    extent = own + 2 * listed
    table[...] = jnp.zeros_like(table)
    for i in range(4):
        source = charge_ref if i == 3 else x_ref.at[i]
        table[i, 0:own, :] = source[pl.ds(pl.multiple_of(base, own), own), :]
        for k in range(listed):
            local = source[pl.ds(other + lists_ref[k], 1), :]
            distant = far_ref[i, k : k + 1, :]
            low = jnp.where(core == 0, distant, local)
            high = jnp.where(core == 0, local, distant)
            table[i, own + k : own + k + 1, :] = low
            table[i, own + listed + k : own + listed + k + 1, :] = high
    coords = [table[i] for i in range(3)]
    store_rows(cs, centre_rows(coords, jnp.full_like(coords[0], pair_width)))
    store_rows(rs, pull_rows(coords, table[3]))

    def one_tile(tile, carry):
        left = left_ref[base + tile]
        sums = jnp.zeros((ROWS, x_ref.shape[2]), f32)
        for j in range(near):
            entry = pairs_ref[tile * near + j]
            entry = jnp.where(entry < 0, extent, entry)
            g = gaussians(left, cs[entry].astype(bf16))
            sums += pulled_by(rs[entry].astype(bf16), g)
        coords = [x_ref[i, pl.ds(base + tile, 1), :] for i in range(3)]
        strength = gain / pair_width * charge_ref[pl.ds(base + tile, 1), :]
        for i, push in enumerate(pushes(coords, sums)):
            out_ref[i, pl.ds(tile, 1), :] = strength * push
        return carry

    lax.fori_loop(0, own, one_tile, 0)


def vmem(count):
    return [pl.BlockSpec(memory_space=pltpu.VMEM)] * count


def smem(count):
    return [pl.BlockSpec(memory_space=pltpu.SMEM)] * count


def shape(*dims, dtype=f32):
    return jax.ShapeDtypeStruct(dims, dtype)


def intersect(owners, x, comps, copies, scale):
    domains, _, width = comps.shape
    tiles, lanes = x.shape[1:]
    return pl.pallas_call(
        functools.partial(intersect_kernel, scale),
        out_shape=(
            shape(copies, domains, width),
            shape(tiles, lanes, DEPTH, dtype=bf16),
            shape(domains, DEPTH, width, dtype=bf16),
        ),
        in_specs=smem(1) + vmem(2),
        out_specs=tuple(vmem(3)),
        scratch_shapes=[
            pltpu.VMEM((tiles, DEPTH, lanes), f32),
            pltpu.VMEM((domains, DEPTH, width), f32),
            pltpu.VMEM((domains, 8, width), f32),
        ],
        name="intersect",
    )(owners, x, comps)


def push(owners, core, x, comps, sums, left, right, pair, gain, replicas):
    domains, _, width = comps.shape
    tiles, lanes = x.shape[1:]
    return pl.pallas_call(
        functools.partial(push_kernel, gain, replicas),
        out_shape=(shape(3, tiles, lanes), shape(domains, width)),
        in_specs=smem(2) + vmem(6),
        out_specs=tuple(vmem(2)),
        scratch_shapes=[pltpu.VMEM((domains, ROWS, width), f32)],
        name="push",
    )(owners, core, x, comps, sums, left, right, pair)


def pair_push(pairs, lists, core, x, charge, far, left, gain):
    tiles, lanes = x.shape[1:]
    own = tiles // CORES
    listed = far.shape[1]
    padded = -(-(own + 2 * listed + 1) // 8) * 8
    return pl.pallas_call(
        functools.partial(pair_kernel, gain),
        out_shape=shape(3, own, lanes),
        in_specs=smem(3) + vmem(4),
        out_specs=vmem(1)[0],
        scratch_shapes=[
            pltpu.VMEM((4, padded, lanes), f32),
            pltpu.VMEM((padded, DEPTH, lanes), f32),
            pltpu.VMEM((padded, ROWS, lanes), f32),
        ],
        name="pair",
    )(pairs, lists, core, x, charge, far, left)


def swap_cores(value):
    return lax.ppermute(value, "core", [(0, 1), (1, 0)])


def both_cores(mine, theirs, core):
    first = jnp.where(core == 0, mine, theirs)
    second = jnp.where(core == 0, theirs, mine)
    return jnp.concatenate([first, second], 1)


def local(
    positions,
    velocities,
    charge,
    inverse_mass,
    pair_tiles,
    halo_tiles,
    owners,
    centres,
    widths,
    map_density,
    map_error,
    partner,
    decision,
):
    replicas = lax.axis_size("rep")
    heights = lax.axis_size("z")
    domains = heights * CORES
    tile_count, owned = owners.shape
    lanes = positions.shape[2] // tile_count
    components = widths.shape[0]
    half = components // CORES
    core = lax.axis_index("core")
    core_id = core.astype(jnp.int32).reshape(1)
    ids = jnp.arange(replicas, dtype=jnp.int32)
    source = jnp.where(decision == 1, partner, ids)
    mine = source[lax.axis_index("rep")]

    packed = jnp.concatenate(
        [positions[0], velocities[0], charge[None, :], inverse_mass[None, :]], 0
    )
    spread = lax.all_to_all(
        jnp.broadcast_to(packed[None], (replicas,) + packed.shape), "rep", 0, 0, tiled=True
    )
    comp_rows = jnp.stack(
        [centres[0], centres[1], centres[2], widths, map_density, map_error], 0
    )
    comp_send = comp_rows.reshape(6, CORES, half).transpose(1, 0, 2)
    comp_send = jnp.broadcast_to(comp_send[None], (heights, CORES, 6, half)).reshape(
        domains, 6, half
    )
    comps = lax.all_to_all(comp_send, ("z", "core"), 0, 0, tiled=True)
    ints = jnp.concatenate([owners.reshape(-1), halo_tiles.reshape(-1)])
    other_ints = swap_cores(ints)
    count = tile_count * owned
    other_lists = lax.dynamic_index_in_dim(
        other_ints[count:].reshape(halo_tiles.shape[1:]), core, 0, False
    )
    own_list = lax.dynamic_index_in_dim(halo_tiles[0], core, 0, False)
    owners_all = both_cores(ints[None, :count], other_ints[None, :count], core)[0]
    pairs = pair_tiles.reshape(-1)

    state = lax.dynamic_index_in_dim(spread, mine, 0, False)
    other_state = swap_cores(state)
    state = state.reshape(8, tile_count, lanes)
    other_state = other_state.reshape(8, tile_count, lanes)
    full = both_cores(state, other_state, core)
    x, v = full[:3], full[3:6]
    charges, inverse = full[6], full[7]

    map_gain = map_scale / (owned * components)
    scale = 1.0 / (owned * tile_count * lanes)
    pair_gain = (pair_tiles.shape[1] * lanes) ** (-0.5)
    group = replicas * heights
    one_phase = group * domains * half * 4 <= ONE_PHASE_BYTES
    across = [(2 * i + 1, (2 * i + 2) % domains) for i in range(heights)]
    across += [(b, a) for a, b in across]
    base = core * tile_count
    mean = None
    for _ in range(STEPS):
        partial, left, right = intersect(owners_all, x, comps, group if one_phase else 1, scale)
        if one_phase:
            sums = lax.all_to_all(partial, ("rep", "z"), 0, 0, tiled=True)
        else:
            pieces = lax.all_to_all(
                partial.reshape(group, -1), ("rep", "z"), 0, 0, tiled=True
            )
            piece = jnp.sum(pieces, 0)
            sums = lax.all_to_all(
                jnp.broadcast_to(piece[None], (group,) + piece.shape), ("rep", "z"), 0, 0, tiled=True
            ).reshape(1, domains, half)
        own_x = lax.dynamic_slice_in_dim(x, base, tile_count, 1)
        own_q = lax.dynamic_slice_in_dim(charges, base, tile_count, 0)
        rim = jnp.concatenate([own_x, own_q[None]], 0)
        rim = jnp.concatenate(
            [
                lax.dynamic_index_in_dim(rim, own_list[k], 1, True)
                for k in range(own_list.shape[0])
            ],
            1,
        )
        far = lax.ppermute(rim, ("z", "core"), across)
        pair = pair_push(pairs, other_lists, core_id, x, charges, far, left, pair_gain)
        force, mean = push(
            owners_all, core_id, x, comps, sums, left, right, pair, map_gain, float(replicas)
        )
        force = force + swap_cores(force)
        v = v + time_step * inverse[None] * force
        x = x + time_step * v

    new_x = lax.dynamic_slice_in_dim(x, base, tile_count, 1).reshape(1, 3, tile_count * lanes)
    new_v = lax.dynamic_slice_in_dim(v, base, tile_count, 1).reshape(1, 3, tile_count * lanes)
    here = lax.axis_index("z") * CORES
    pair_means = lax.dynamic_slice_in_dim(mean, here, CORES, 0)
    keep = lax.dynamic_index_in_dim(pair_means, core, 0, False)
    give = lax.dynamic_index_in_dim(pair_means, 1 - core, 0, False)
    got = swap_cores(give)
    model_map = jnp.where(
        core == 0, jnp.concatenate([keep, got]), jnp.concatenate([got, keep])
    )
    return (new_x, new_v, model_map)


def solution(mesh):
    replicas, domains = mesh.devices.shape
    split = Mesh(
        mesh.devices.reshape(replicas, domains // CORES, CORES), ("rep", "z", "core")
    )
    dom = ("z", "core")
    placed = (
        P("rep", None, dom),
        P("rep", None, dom),
        P(dom),
        P(dom),
        P(dom, None),
        P(dom, None, None),
        P(dom, None),
        P(None, dom),
        P(dom),
        P(dom),
        P(dom),
        P(),
        P(),
    )
    return jax.shard_map(
        local,
        mesh=split,
        in_specs=placed,
        out_specs=(P("rep", None, dom), P("rep", None, dom), P(dom)),
        check_vma=False,
    )
```

time: 215 us -> 149 us (0.69)
  Pallas kernels: 0 us -> 82.1 us
  matrix products: 79.5 us -> 0 us
  other arithmetic: 50.7 us -> 3.81 us
  blocking collectives: 25 us -> 0 us
  between operations: 1.05 us -> 6.81 us
  starting transfers between devices: 31.9 us -> 28 us
  waiting for transfers between devices: 11.9 us -> 14.4 us
  loops' own time: 2.31 us -> 0 us
    pallas_call x0 -> x6, Pallas kernels: none -> 82.1 us  [the longest x2 46.5 us: push(): pl.pallas_call(functools.partial(push_kernel, gain, replicas), out_shape=...]
    dot_general x33 -> x0, matrix products: 79.5 us -> none  [the longest x20 69.8 us: force_pass(): pulled = jnp.einsum('gak,ck->gca', weighted, centre, precision=highest)]
    reduce_sum x48 -> x0, other arithmetic: 49.1 us -> none  [the longest x20 24.7 us: force_pass(): return pieces[0] * jnp.sum(weighted, 2)[:, None, :] - pulled]
    psum x2 -> x0, blocking collectives: 17.9 us -> none  [map_send(): totals = lax.psum(partial_value, 'rep')]
    ppermute x4 -> x7, waiting for transfers between devices: 2.21 us -> 10.3 us  [the longest x2 8.12 us: local(): far = lax.ppermute(rim, ('z', 'core'), across)]
    all_to_all x1 -> x0, blocking collectives: 7.11 us -> none  [local(): lax.all_to_all(permuted, 'rep', split_axis=0, concat_axis=0, tiled=True)]
    all_to_all x6 -> x4, waiting for transfers between devices: 9.67 us -> 4.1 us  [the longest x1 4.09 us: local(): comps = lax.all_to_all(comp_send, ('z', 'core'), 0, 0, tiled=True)]
    unnamed x28 -> x47, local copies, waits for them, and re-layouts: 2.82 us -> 8.1 us
  transfers between devices with their start and end apart: 10 -> 11, of which waited for: 5 -> 6; matrix products, arithmetic and copies ran while one was open for 7% -> 4% of each run, Pallas kernels for 0% -> 14%
where the time goes in v1:
time: 149 us; the launch traced here: 148 us
  Pallas kernels  82.1 us (55%)
  starting transfers between devices  28 us (19%)
  waiting for transfers between devices  14.4 us (10%)
  local copies, waits for them, and re-layouts  12.9 us (9%)
  between operations  6.81 us (5%)
  other arithmetic  3.81 us (3%)
    pallas_call x2, Pallas kernels, push(): pl.pallas_call(functools.partial(push_kernel, gain, replicas), out_shape=...  46.5 us
    pallas_call x2, Pallas kernels, pair_push(): pl.pallas_call(functools.partial(pair_kernel, gain), out_shape=shape(3, o...  20.1 us
    pallas_call x2, Pallas kernels, intersect(): pl.pallas_call(functools.partial(intersect_kernel, scale), out_shape=(sha...  15.5 us
    all_to_all x2, starting transfers between devices, local(): sums = lax.all_to_all(partial, ('rep', 'z'), 0, 0, tiled=True)  10.9 us
    ppermute x2, waiting for transfers between devices, local(): far = lax.ppermute(rim, ('z', 'core'), across)  8.12 us
    unnamed x47, local copies, waits for them, and re-layouts  8.1 us
    ppermute x2, starting transfers between devices, local(): far = lax.ppermute(rim, ('z', 'core'), across)  5.61 us
    all_to_all x1, starting transfers between devices, local(): lax.all_to_all(jnp.broadcast_to(packed[None], (replicas,) + packed.shape)...  5.32 us
  transfers between devices with their start and end apart: 11, of which 6 were waited for; matrix products, arithmetic and copies ran while one was open for 4% of the time, Pallas kernels for 14%

profile of v1, /device:TPU:0, one launch (start us, length us, event | category | flops | bytes accessed | tf_op | source)
XLA Modules:
  0.0 148.0 jit_solution(67558899464068646)
XLA Ops:
  0.6 0.7 copy_bitcast_fusion
  1.4 0.7 copy-done.12
  2.1 0.7 broadcast_in_dim.10
  2.8 5.3 %all-to-all-start = ((f32[4,8,1024]{2,1,0:T(8,128)}), f32[4,8,1024]{2,1,0:T(8,128)S(1)}, u32[]{:S(2)}, u32[]{:S(2)}) async-start(f32[4,8,1024]{2,1,0:T(8,128)} %broadcast_in_dim.10), calls=%async_computation | async-start | bytes 262144 | tf_op jit(solution)/shard_map/all_to_all | solution.py:311
  9.0 0.6 copy-done.20
  14.9 0.7 copy-done.17
  15.6 0.7 copy-done.14
  18.8 0.7 broadcast_in_dim.11
  19.5 5.0 %all-to-all-start.1 = ((f32[8,6,512]{2,1,0:T(8,128)}), f32[8,6,512]{2,1,0:T(8,128)S(1)}, u32[]{:S(2)}, u32[]{:S(2)}) async-start(f32[8,6,512]{2,1,0:T(8,128)} %bitcast.10), calls=%async_computation.1 | async-start | bytes 262144 | tf_op jit(solution)/shard_map/all_to_all | solution.py:321
  25.9 0.6 maximum_bitcast_fusion.1
  27.1 4.1 %all-to-all-done.1.comp_ref = f32[8,6,512]{2,1,0:T(8,128)S(1)} async-done(((f32[8,6,512]{2,1,0:T(8,128)}), f32[8,6,512]{2,1,0:T(8,128)S(1)}, u32[]{:S(2)}, u32[]{:S(2)}) %all-to-all-start.1) | async-done | bytes 98336 | tf_op jit(solution)/shard_map/all_to_all | solution.py:321
  31.2 0.6 copy-done
  31.9 7.7 %intersect.2 = (f32[16,8,512]{2,1,0:T(8,128)}, bf16[16,128,32]{2,1,0:T(8,128)(2,1)}, bf16[8,32,512]{2,1,0:T(8,128)(2,1)}) custom-call(s32[64]{0:T(128)} %add_bitcast_fusion.owners_ref, f32[3,16,128]{2,1,0:T(8,128)} %fusion.x_ref, f32[8,6,512]{2,1,0:T(8,128)} %copy-done), custom_call_target="tpu_custom_call" | custom-call | tf_op jit(solution)/shard_map/intersect/pallas_call | solution.py:220
  39.6 5.3 %all-to-all-start.2 = ((f32[16,8,512]{2,1,0:T(8,128)}), f32[16,8,512]{2,1,0:T(8,128)S(1)}, u32[]{:S(2)}, u32[]{:S(2)}) async-start(f32[16,8,512]{2,1,0:T(8,128)} %get-tuple-element.12), calls=%async_computation.2 | async-start | bytes 524288 | tf_op jit(solution)/shard_map/all_to_all | solution.py:352
  45.1 2.4 %collective-permute-start.2 = (f32[4,2,128]{2,1,0:T(2,128)S(1)}, f32[4,2,128]{2,1,0:T(2,128)S(1)}, u32[]{:S(2)}, u32[]{:S(2)}) collective-permute-start(f32[4,2,128]{2,1,0:T(2,128)S(1)} %pad_maximum_fusion.1), channel_id=1, source_target_pairs={{1,2},{3,4},{5,6},{7,0},{2,1},{4,3},{6,5},{0,7},{9,10},{11,12},{13... | collective-permute-start | bytes 12296 | tf_op jit(solution)/shard_map/ppermute | solution.py:371
  48.1 3.4 %collective-permute-done.2.far_ref = f32[4,2,128]{2,1,0:T(2,128)S(1)} collective-permute-done((f32[4,2,128]{2,1,0:T(2,128)S(1)}, f32[4,2,128]{2,1,0:T(2,128)S(1)}, u32[]{:S(2)}, u32[]{:S(2)}) %collective-permute-start.2) | collective-permute-done | bytes 4128 | tf_op jit(solution)/shard_map/ppermute | solution.py:371
  52.1 10.0 %pair.2.pair_ref = f32[3,8,128]{2,1,0:T(8,128)} custom-call(s32[48]{0:T(128)} %reshape.70.pairs_ref, s32[2]{0:T(128)} %fusion.12.lists_ref, s32[1]{0:T(128)} %bitcast.8.core_ref, f32[3,16,128]{2,1,0:T(8,128)} %fusion.x_ref, f32[16,128]{1,0:T(8,128)} %get-tuple-element.25.charge_ref, f32[4,2,128]{2,1,0:T(2,128)} %copy-done.11, ...), custom_call_target="tpu_custom_call" | custom-call | tf_op jit(solution)/shard_map/pair/pallas_call | solution.py:256
  62.1 0.7 copy-done.2
  62.8 23.3 %push.2 = (f32[3,16,128]{2,1,0:T(8,128)}, f32[8,512]{1,0:T(8,128)}) custom-call(s32[64]{0:T(128)} %add_bitcast_fusion.owners_ref, s32[1]{0:T(128)} %bitcast.8.core_ref, f32[3,16,128]{2,1,0:T(8,128)} %fusion.x_ref, f32[8,6,512]{2,1,0:T(8,128)} %copy-done, f32[16,8,512]{2,1,0:T(8,128)} %copy-done.2, bf16[16,128,32]{2,1,0:T(8,128)(2,1)} %get-tuple-element.13.left_ref, ...), custom_call_target="tpu_custom_call" | custom-call | tf_op jit(solution)/shard_map/push/pallas_call | solution.py:241
  86.2 1.4 collective-permute-done.3
  87.6 0.6 multiply_add_fusion.1
  88.2 7.8 %intersect.3 = (f32[16,8,512]{2,1,0:T(8,128)}, bf16[16,128,32]{2,1,0:T(8,128)(2,1)}, bf16[8,32,512]{2,1,0:T(8,128)(2,1)}) custom-call(s32[64]{0:T(128)} %add_bitcast_fusion.owners_ref, f32[3,16,128]{2,1,0:T(8,128)} %get-tuple-element.23.x_ref, f32[8,6,512]{2,1,0:T(8,128)} %copy-done), custom_call_target="tpu_custom_call" | custom-call | tf_op jit(solution)/shard_map/intersect/pallas_call | solution.py:220
  95.9 5.6 %all-to-all-start.3 = ((f32[16,8,512]{2,1,0:T(8,128)}), f32[16,8,512]{2,1,0:T(8,128)S(1)}, u32[]{:S(2)}, u32[]{:S(2)}) async-start(f32[16,8,512]{2,1,0:T(8,128)} %get-tuple-element.16), calls=%async_computation.3 | async-start | bytes 524288 | tf_op jit(solution)/shard_map/all_to_all | solution.py:352
  101.6 3.2 %collective-permute-start.4 = (f32[4,2,128]{2,1,0:T(2,128)S(1)}, f32[4,2,128]{2,1,0:T(2,128)S(1)}, u32[]{:S(2)}, u32[]{:S(2)}) collective-permute-start(f32[4,2,128]{2,1,0:T(2,128)S(1)} %pad_maximum_fusion.2), channel_id=1, source_target_pairs={{1,2},{3,4},{5,6},{7,0},{2,1},{4,3},{6,5},{0,7},{9,10},{11,12},{13... | collective-permute-start | bytes 12296 | tf_op jit(solution)/shard_map/ppermute | solution.py:371
  104.7 4.7 %collective-permute-done.4.far_ref = f32[4,2,128]{2,1,0:T(2,128)S(1)} collective-permute-done((f32[4,2,128]{2,1,0:T(2,128)S(1)}, f32[4,2,128]{2,1,0:T(2,128)S(1)}, u32[]{:S(2)}, u32[]{:S(2)}) %collective-permute-start.4) | collective-permute-done | bytes 4128 | tf_op jit(solution)/shard_map/ppermute | solution.py:371
  110.0 10.0 %pair.3.pair_ref = f32[3,8,128]{2,1,0:T(8,128)} custom-call(s32[48]{0:T(128)} %reshape.70.pairs_ref, s32[2]{0:T(128)} %fusion.12.lists_ref, s32[1]{0:T(128)} %bitcast.8.core_ref, f32[3,16,128]{2,1,0:T(8,128)} %get-tuple-element.23.x_ref, f32[16,128]{1,0:T(8,128)} %get-tuple-element.25.charge_ref, f32[4,2,128]{2,1,0:T(2,128)} %copy-done.10, ...), custom_call_target="tpu_custom_call" | custom-call | tf_op jit(solution)/shard_map/pair/pallas_call | solution.py:256
  120.1 0.7 copy-done.1
  120.8 23.3 %push.3 = (f32[3,16,128]{2,1,0:T(8,128)}, f32[8,512]{1,0:T(8,128)}) custom-call(s32[64]{0:T(128)} %add_bitcast_fusion.owners_ref, s32[1]{0:T(128)} %bitcast.8.core_ref, f32[3,16,128]{2,1,0:T(8,128)} %get-tuple-element.23.x_ref, f32[8,6,512]{2,1,0:T(8,128)} %copy-done, f32[16,8,512]{2,1,0:T(8,128)} %copy-done.1, ...), custom_call_target="tpu_custom_call" | custom-call | tf_op jit(solution)/shard_map/push/pallas_call | solution.py:241
  144.1 0.8 constant_dynamic-slice_fusion.1
  145.4 0.7 collective-permute-done.6
  146.7 0.7 copy-done.6
  147.4 0.6 multiply_add_fusion.2
  (81 shorter events, 7.9 us)
Async XLA Ops:
  0.6 0.8 copy-start.13
  1.4 0.7 copy-start.12
  2.8 5.3 %copy-start.18 = (s32[8,4]{0,1:T(4,128)S(1)}, s32[8,4]{0,1:T(4,128)}, u32[]{:S(2)}) copy-start(s32[8,4]{0,1:T(4,128)} %param.19) | copy-start | bytes 388
  2.8 16.1 %all-to-all-start = ((f32[4,8,1024]{2,1,0:T(8,128)}), f32[4,8,1024]{2,1,0:T(8,128)S(1)}, u32[]{:S(2)}, u32[]{:S(2)}) async-start(f32[4,8,1024]{2,1,0:T(8,128)} %broadcast_in_dim.10), calls=%async_computation | async-start | bytes 262144 | tf_op jit(solution)/shard_map/all_to_all | solution.py:311
  8.2 0.7 copy-start.19
  9.0 9.8 %collective-permute-start.1 = (s32[36]{0:T(128)S(1)}, s32[36]{0:T(128)S(1)}, u32[]{:S(2)}, u32[]{:S(2)}) collective-permute-start(s32[36]{0:T(128)S(1)} %pad_add_fusion), channel_id=1, source_target_pairs={{0,1},{1,0},{2,3},{3,2},{4,5},{5,4},{6,7},{7,6},{8,9},{9,8},{10,11... | collective-permute-start | bytes 440 | tf_op jit(solution)/shard_map/ppermute | solution.py:271
  9.0 0.7 copy-start.20
  9.0 0.7 copy-start.21
  12.2 2.7 %copy-start.16 = (f32[1024]{0:T(1024)S(1)}, f32[1024]{0:T(1024)}, u32[]{:S(2)}) copy-start(f32[1024]{0:T(1024)} %param.22) | copy-start | bytes 12292
  13.5 1.3 copy-start.15
  13.5 2.1 %copy-start.9 = (f32[3,1024]{1,0:T(4,128)S(1)}, f32[3,1024]{1,0:T(4,128)}, u32[]{:S(2)}) copy-start(f32[3,1024]{1,0:T(4,128)} %param.20) | copy-start | bytes 36868
  14.9 0.7 copy-start.17
  15.6 0.7 copy-start.14
  19.5 11.7 %all-to-all-start.1 = ((f32[8,6,512]{2,1,0:T(8,128)}), f32[8,6,512]{2,1,0:T(8,128)S(1)}, u32[]{:S(2)}, u32[]{:S(2)}) async-start(f32[8,6,512]{2,1,0:T(8,128)} %bitcast.10), calls=%async_computation.1 | async-start | bytes 262144 | tf_op jit(solution)/shard_map/all_to_all | solution.py:321
  24.5 1.4 collective-permute-start
  31.2 0.7 copy-start
  39.6 5.4 %copy-start.3 = (f32[3,16,128]{2,1,0:T(8,128)S(1)}, f32[3,16,128]{2,1,0:T(8,128)}, u32[]{:S(2)}) copy-start(f32[3,16,128]{2,1,0:T(8,128)} %fusion.x_ref) | copy-start | bytes 73732
  39.6 22.5 %all-to-all-start.2 = ((f32[16,8,512]{2,1,0:T(8,128)}), f32[16,8,512]{2,1,0:T(8,128)S(1)}, u32[]{:S(2)}, u32[]{:S(2)}) async-start(f32[16,8,512]{2,1,0:T(8,128)} %get-tuple-element.12), calls=%async_computation.2 | async-start | bytes 524288 | tf_op jit(solution)/shard_map/all_to_all | solution.py:352
  45.1 6.4 %collective-permute-start.2 = (f32[4,2,128]{2,1,0:T(2,128)S(1)}, f32[4,2,128]{2,1,0:T(2,128)S(1)}, u32[]{:S(2)}, u32[]{:S(2)}) collective-permute-start(f32[4,2,128]{2,1,0:T(2,128)S(1)} %pad_maximum_fusion.1), channel_id=1, source_target_pairs={{1,2},{3,4},{5,6},{7,0},{2,1},{4,3},{6,5},{0,7},{9,10},{11,12},{13... | collective-permute-start | bytes 12296 | tf_op jit(solution)/shard_map/ppermute | solution.py:371
  51.5 0.6 copy-start.11
  62.1 0.7 copy-start.2
  86.1 1.5 copy-start.4
  86.1 1.5 copy-start.7
  86.1 1.5 collective-permute-start.3
  95.9 5.6 %copy-start.5 = (f32[3,16,128]{2,1,0:T(8,128)S(1)}, f32[3,16,128]{2,1,0:T(8,128)}, u32[]{:S(2)}) copy-start(f32[3,16,128]{2,1,0:T(8,128)} %get-tuple-element.23.x_ref) | copy-start | bytes 73732
  95.9 24.2 %all-to-all-start.3 = ((f32[16,8,512]{2,1,0:T(8,128)}), f32[16,8,512]{2,1,0:T(8,128)S(1)}, u32[]{:S(2)}, u32[]{:S(2)}) async-start(f32[16,8,512]{2,1,0:T(8,128)} %get-tuple-element.16), calls=%async_computation.3 | async-start | bytes 524288 | tf_op jit(solution)/shard_map/all_to_all | solution.py:352
  101.6 7.9 %collective-permute-start.4 = (f32[4,2,128]{2,1,0:T(2,128)S(1)}, f32[4,2,128]{2,1,0:T(2,128)S(1)}, u32[]{:S(2)}, u32[]{:S(2)}) collective-permute-start(f32[4,2,128]{2,1,0:T(2,128)S(1)} %pad_maximum_fusion.2), channel_id=1, source_target_pairs={{1,2},{3,4},{5,6},{7,0},{2,1},{4,3},{6,5},{0,7},{9,10},{11,12},{13... | collective-permute-start | bytes 12296 | tf_op jit(solution)/shard_map/ppermute | solution.py:371
  120.1 0.7 copy-start.1
  144.1 2.6 %copy-start.8 = (f32[3,16,128]{2,1,0:T(8,128)S(1)}, f32[3,16,128]{2,1,0:T(8,128)}, u32[]{:S(2)}) copy-start(f32[3,16,128]{2,1,0:T(8,128)} %get-tuple-element.19) | copy-start | bytes 73732
  144.9 1.2 collective-permute-start.6
  144.9 1.8 %collective-permute-start.5 = (f32[3,16,128]{2,1,0:T(8,128)}, f32[3,16,128]{2,1,0:T(8,128)S(1)}, u32[]{:S(2)}, u32[]{:S(2)}) collective-permute-start(f32[3,16,128]{2,1,0:T(8,128)} %get-tuple-element.19), channel_id=1, source_target_pairs={{0,1},{1,0},{2,3},{3,2},{4,5},{5,4},{6,7},{7,6},{8,9},{9,8},{10,11... | collective-permute-start | bytes 73736 | tf_op jit(solution)/shard_map/ppermute | solution.py:271
  146.6 0.7 copy-start.6
  (1 other events, 0.6 us)

commit v2 on v1

v2 whole, which is shorter than its diff:
```python
import functools
import math

import jax
import jax.numpy as jnp
from jax import lax
from jax.experimental import pallas as pl
from jax.experimental.pallas import tpu as pltpu
from jax.sharding import Mesh, PartitionSpec as P

STEPS = 2
CORES = 2
DEPTH = 32
ROWS = 16
ONE_PHASE_BYTES = 1 << 20

time_step = 0.5
pair_width = 1.0
map_scale = 2.0
log2e = math.log2(math.e)
f32 = jnp.float32
bf16 = jnp.bfloat16

LEFT_PARTS = (0, 0, 1, 1, 0, 2)
RIGHT_PARTS = (0, 1, 0, 1, 2, 0)


def split3(value):
    high = value.astype(bf16).astype(f32)
    rest = value - high
    middle = rest.astype(bf16).astype(f32)
    return high, middle, rest - middle


def point_rows(coords):
    rows = []
    for coord in coords:
        parts = split3(coord)
        rows += [parts[i] for i in LEFT_PARTS]
    parts = split3(coords[0] * coords[0] + coords[1] * coords[1] + coords[2] * coords[2])
    rows += [parts[i] for i in LEFT_PARTS]
    one = jnp.ones_like(coords[0])
    return rows + [one, one, one]


def centre_rows(coords, extent):
    scale = log2e / extent
    rows = []
    for coord in coords:
        parts = split3(coord * scale)
        rows += [parts[i] for i in RIGHT_PARTS]
    parts = split3(-0.5 * scale)
    rows += [parts[i] for i in RIGHT_PARTS]
    square = coords[0] * coords[0] + coords[1] * coords[1] + coords[2] * coords[2]
    return rows + list(split3(-0.5 * scale * square))


def pull_rows(coords, weight):
    rows = list(split3(weight))
    for coord in coords:
        rows += list(split3(coord * weight))
    return rows


def squeeze_sums(coords, sums):
    def total(first):
        return sums[first : first + 1] + sums[first + 1 : first + 2] + sums[first + 2 : first + 3]

    strength = total(0)
    return [coords[i] * strength - total(3 + 3 * i) for i in range(3)]


def dot(left, right):
    return jnp.dot(left, right, preferred_element_type=f32)


def high_low(value):
    high = value.astype(bf16)
    return high, (value - high.astype(f32)).astype(bf16)


def store_rows(ref, rows):
    for index, row in enumerate(rows):
        ref[:, index, :] = row
    depth = ref.shape[1]
    if len(rows) < depth:
        ref[:, len(rows) : depth, :] = jnp.zeros(
            (ref.shape[0], depth - len(rows), ref.shape[2]), f32
        )


def chunks(total, wanted):
    size = wanted if total % wanted == 0 else total
    return [(start, size) for start in range(0, total, size)]


def pack_kernel(pos_hbm, vel_hbm, charge_hbm, mass_hbm, centre_hbm, width_hbm, density_hbm,
                error_hbm, state_ref, comp_ref, pos_ref, vel_ref, charge_ref, mass_ref, centre_ref,
                width_ref, density_ref, error_ref, sems):
    sources = (pos_hbm, vel_hbm, charge_hbm, mass_hbm, centre_hbm, width_hbm, density_hbm, error_hbm)
    targets = (pos_ref, vel_ref, charge_ref, mass_ref, centre_ref, width_ref, density_ref, error_ref)
    copies = [
        pltpu.make_async_copy(source, target, sems.at[n])
        for n, (source, target) in enumerate(zip(sources, targets))
    ]
    for copy in copies:
        copy.start()
    for copy in copies:
        copy.wait()
    half = comp_ref.shape[2]
    for row in range(state_ref.shape[0]):
        for i in range(3):
            state_ref[row, i : i + 1, :] = pos_ref[i]
            state_ref[row, 3 + i : 4 + i, :] = vel_ref[i]
        state_ref[row, 6:7, :] = charge_ref[...]
        state_ref[row, 7:8, :] = mass_ref[...]
    for row in range(comp_ref.shape[0]):
        part = pl.ds((row % CORES) * half, half)
        comp_ref[row, 0:3, :] = centre_ref[:, part]
        comp_ref[row, 3:4, :] = width_ref[:, part]
        comp_ref[row, 4:5, :] = density_ref[:, part]
        comp_ref[row, 5:6, :] = error_ref[:, part]


def owner_of(plan, mine_ref, theirs_ref, tile, j):
    row = lax.rem(tile, plan.own)
    here = lax.div(tile, plan.own) == lax.axis_index("core")
    return jnp.where(here, mine_ref[row, j], theirs_ref[row, j])


def sum_gaussians(plan, scale, mine_ref, theirs_ref, halo_ref, state_ref, right_ref, points_ref,
                  out_ref, xs, acc, rim):
    tiles, owned, listed = plan.tiles, plan.owned, plan.listed
    store_rows(xs, point_rows([state_ref[i] for i in range(3)]))
    core = lax.axis_index("core")
    for k in range(listed):
        tile = (1 - core) * plan.own + halo_ref[0, 1 - core, k]
        for i, row in enumerate((0, 1, 2, 6)):
            rim[i * listed + k : i * listed + k + 1, :] = state_ref[row, pl.ds(tile, 1), :]
    acc[...] = jnp.zeros_like(acc)

    def one_tile(tile, carry):
        points = xs[tile]
        points_ref[tile] = points.astype(bf16)
        left = points.T.astype(bf16)
        for j in range(owned):
            owner = owner_of(plan, mine_ref, theirs_ref, tile, j)
            for start, size in chunks(right_ref.shape[2], 256):
                g = jnp.exp2(dot(left, right_ref[owner, :, start : start + size]))
                acc[owner, :, start : start + size] += jnp.sum(
                    g.reshape(g.shape[0] // 8, 8, size), 0
                )
        return carry

    lax.fori_loop(0, tiles, one_tile, 0)
    total = jnp.sum(acc[...], 1) * scale
    for row in range(out_ref.shape[0]):
        out_ref[row, 0 : acc.shape[0], 0 : plan.half] = total
        out_ref[row, 0 : rim.shape[0], plan.half :] = rim[...]


def first_kernel(plan, scale, mine_ref, theirs_ref, halo_ref, partner_ref, decision_ref, spread_ref, comp_ref,
                 out_ref, state_ref, points_ref, right_ref, xs, acc, rim, cs):
    store_rows(cs, centre_rows([comp_ref[:, i, :] for i in range(3)], comp_ref[:, 3, :]))
    right_ref[...] = cs[...].astype(bf16)
    row = lax.axis_index("rep")
    source = jnp.where(decision_ref[row] == 1, partner_ref[row], row)
    for core in range(CORES):
        for tile in range(plan.own):
            lanes = slice(tile * plan.lanes, (tile + 1) * plan.lanes)
            state_ref[:, core * plan.own + tile, :] = spread_ref[source * CORES + core, :, lanes]
    sum_gaussians(plan, scale, mine_ref, theirs_ref, halo_ref, state_ref, right_ref, points_ref,
                  out_ref, xs, acc, rim)


def stepped(old_ref, mine_ref, theirs_ref):
    mass = time_step * old_ref[7]
    for i in range(3):
        v = old_ref[3 + i] + mass * (mine_ref[i] + theirs_ref[i])
        yield old_ref[i] + time_step * v, v


def next_kernel(plan, scale, mine_ref, theirs_ref, halo_ref, old_ref, force_ref, swapped_ref, right_ref,
                out_ref, state_ref, points_ref, xs, acc, rim):
    for i, (x, v) in enumerate(stepped(old_ref, force_ref, swapped_ref)):
        state_ref[i] = x
        state_ref[3 + i] = v
    state_ref[6] = old_ref[6]
    state_ref[7] = old_ref[7]
    sum_gaussians(plan, scale, mine_ref, theirs_ref, halo_ref, state_ref, right_ref, points_ref,
                  out_ref, xs, acc, rim)


def finish_kernel(plan, old_ref, mine_ref, theirs_ref, x_ref, v_ref, map_ref, state):
    for i, (x, v) in enumerate(stepped(old_ref, mine_ref, theirs_ref)):
        state[i] = x
        state[3 + i] = v
    core = lax.axis_index("core")
    base = core * plan.own
    for tile in range(plan.own):
        lanes = slice(tile * plan.lanes, (tile + 1) * plan.lanes)
        for i in range(3):
            x_ref[i, :, lanes] = state[i, pl.ds(base + tile, 1), :]
            v_ref[i, :, lanes] = state[3 + i, pl.ds(base + tile, 1), :]
    first = core == 0
    pieces = plan.half // plan.lanes
    for n in range(pieces):
        keep = mine_ref[3, n : n + 1, :]
        got = theirs_ref[3, pieces + n : pieces + n + 1, :]
        low = slice(n * plan.lanes, (n + 1) * plan.lanes)
        high = slice(plan.half + n * plan.lanes, plan.half + (n + 1) * plan.lanes)
        map_ref[:, low] = jnp.where(first, keep, got)
        map_ref[:, high] = jnp.where(first, got, keep)


def fill_kernel(plan, gain, mine_ref, theirs_ref, pairs_ref, halo_ref, state_ref, points_ref, right_ref,
                high_ref, low_ref, pair_ref, turned, table, cs, rs, near_turned, high, low, sems):
    for domain in range(right_ref.shape[0]):
        for start, size in chunks(right_ref.shape[2], 128):
            turned[domain, start : start + size, :] = (
                right_ref[domain, :, start : start + size].astype(f32).T.astype(bf16)
            )

    def leave(tile, part, kept, out):
        blocks = pl.ds(tile * plan.owned, plan.owned)
        return pltpu.make_async_copy(kept.at[blocks], out.at[blocks], sems.at[part, tile])

    def one_tile(tile, carry):
        points = points_ref[tile]
        for j in range(plan.owned):
            block = tile * plan.owned + j
            owner = owner_of(plan, mine_ref, theirs_ref, tile, j)
            for start, size in chunks(turned.shape[1], 256):
                rows = slice(start, start + size)
                g = jnp.exp2(dot(turned[owner, rows, :], points))
                high[block, rows, :], low[block, rows, :] = high_low(g)
        leave(tile, 0, high, high_ref).start()
        leave(tile, 1, low, low_ref).start()
        return carry

    lax.fori_loop(0, plan.tiles, one_tile, 0)
    pair_pushes(plan, gain, pairs_ref, halo_ref, state_ref, points_ref, pair_ref, table, cs, rs, near_turned)

    def settle(tile, carry):
        leave(tile, 0, high, high_ref).wait()
        leave(tile, 1, low, low_ref).wait()
        return carry

    lax.fori_loop(0, plan.tiles, settle, 0)


def pair_pushes(plan, gain, pairs_ref, halo_ref, state_ref, points_ref, out_ref, table, cs, rs, turned):
    own, near, listed = plan.own, plan.near, plan.listed
    core = lax.axis_index("core")
    base = pl.multiple_of(core * own, own)
    extent = own + 2 * listed
    table[...] = jnp.zeros_like(table)
    for i, source in enumerate((0, 1, 2, 6)):
        table[i, 0:own, :] = state_ref[source, pl.ds(base, own), :]
        for k in range(listed):
            listed_tile = (1 - core) * own + halo_ref[0, core, k]
            table[i, pl.ds(own + (1 - core) * listed + k, 1), :] = state_ref[
                source, pl.ds(listed_tile, 1), :
            ]
    coords = [table[i] for i in range(3)]
    store_rows(cs, centre_rows(coords, jnp.full_like(coords[0], pair_width)))
    store_rows(rs, pull_rows(coords, table[3]))
    for entry in range(table.shape[1]):
        turned[entry] = cs[entry].T.astype(bf16)
    for tile in range(own):
        points = points_ref[base + tile]
        sums = jnp.zeros((ROWS, plan.lanes), f32)
        for j in range(near):
            entry = pairs_ref[tile, j]
            entry = jnp.where(entry < 0, extent, entry)
            rows = rs[entry].astype(bf16)
            high, low = high_low(jnp.exp2(dot(turned[entry], points)))
            sums += dot(rows, high) + dot(rows, low)
        coords = [state_ref[i, pl.ds(base + tile, 1), :] for i in range(3)]
        strength = gain / pair_width * state_ref[6, pl.ds(base + tile, 1), :]
        for i, push in enumerate(squeeze_sums(coords, sums)):
            out_ref[i, tile : tile + 1, :] = strength * push


def far_pushes(plan, gain, pairs_ref, state_ref, far, points_ref, out_ref, cs, rs):
    own, near, listed = plan.own, plan.near, plan.listed
    core = lax.axis_index("core")
    base = core * own
    coords = [far[i * listed : (i + 1) * listed] for i in range(3)]
    store_rows(cs, centre_rows(coords, jnp.full_like(coords[0], pair_width)))
    store_rows(rs, pull_rows(coords, far[3 * listed : 4 * listed]))
    turned = [cs[k].T.astype(bf16) for k in range(listed)]
    for tile in range(own):
        points = points_ref[base + tile]
        sums = jnp.zeros((ROWS, plan.lanes), f32)
        for k in range(listed):
            entry = own + core * listed + k
            named = pairs_ref[tile, 0] == entry
            for j in range(1, near):
                named = named | (pairs_ref[tile, j] == entry)
            rows = (rs[k] * jnp.where(named, 1.0, 0.0)).astype(bf16)
            high, low = high_low(jnp.exp2(dot(turned[k], points)))
            sums += dot(rows, high) + dot(rows, low)
        coords = [state_ref[i, pl.ds(base + tile, 1), :] for i in range(3)]
        strength = gain / pair_width * state_ref[6, pl.ds(base + tile, 1), :]
        for i, push in enumerate(squeeze_sums(coords, sums)):
            out_ref[i, pl.ds(base + tile, 1), :] += strength * push


def push_kernel(plan, gain, pair_gain, replicas, mine_ref, theirs_ref, pairs_ref, state_ref, comp_ref,
                sums_ref, far_ref, pair_ref, points_ref, high_ref, low_ref, out_ref, rs, means, far_cs, far_rs,
                high, low, sems):
    def bring(tile, part, source, kept):
        blocks = pl.ds(tile * plan.owned, plan.owned)
        return pltpu.make_async_copy(source.at[blocks], kept.at[blocks], sems.at[part, tile])

    def fetch(tile, carry):
        bring(tile, 0, high_ref, high).start()
        bring(tile, 1, low_ref, low).start()
        return carry

    lax.fori_loop(0, plan.tiles, fetch, 0)
    domains = comp_ref.shape[0]
    mean = jnp.sum(sums_ref[:, 0:domains, 0 : plan.half], 0) / replicas
    for n in range(plan.half // plan.lanes):
        means[n] = mean[:, n * plan.lanes : (n + 1) * plan.lanes]
    error = comp_ref[:, 5, :]
    coefficient = gain * (mean - comp_ref[:, 4, :]) / (error * error) / comp_ref[:, 3, :]
    store_rows(rs, pull_rows([comp_ref[:, i, :] for i in range(3)], coefficient))

    def one_tile(tile, carry):
        bring(tile, 0, high_ref, high).wait()
        bring(tile, 1, low_ref, low).wait()
        sums = jnp.zeros((ROWS, plan.lanes), f32)
        for j in range(plan.owned):
            block = tile * plan.owned + j
            rows = rs[owner_of(plan, mine_ref, theirs_ref, tile, j)].astype(bf16)
            sums += dot(rows, high[block]) + dot(rows, low[block])
        coords = [state_ref[i, pl.ds(tile, 1), :] for i in range(3)]
        for i, push in enumerate(squeeze_sums(coords, sums)):
            out_ref[i, pl.ds(tile, 1), :] = push
        return carry

    lax.fori_loop(0, plan.tiles, one_tile, 0)
    for core in range(CORES):

        @pl.when(lax.axis_index("core") == core)
        def _():
            out_ref[0:3, core * plan.own : (core + 1) * plan.own, :] += pair_ref[...]

    far_rows = 4 * plan.listed
    if plan.one_phase:
        heights = lax.axis_size("z")
        turn = jnp.where(lax.axis_index("core") == 0, heights - 1, 1)
        row = lax.axis_index("rep") * heights + lax.rem(lax.axis_index("z") + turn, heights)
        far = far_ref[row, 0:far_rows, plan.half :]
    else:
        far = far_ref[0, 0:far_rows, plan.half :]
    far_pushes(plan, pair_gain, pairs_ref, state_ref, far, points_ref, out_ref, far_cs, far_rs)

    pieces = plan.half // plan.lanes
    core = lax.axis_index("core")
    here = lax.axis_index("z") * CORES
    out_ref[3] = jnp.zeros_like(out_ref[3])
    for n in range(pieces):
        keep = means[n, pl.ds(here + core, 1), :]
        give = means[n, pl.ds(here + 1 - core, 1), :]
        out_ref[3, n : n + 1, :] = keep
        out_ref[3, pieces + n : pieces + n + 1, :] = give


VMEM = pl.BlockSpec(memory_space=pltpu.VMEM)
SMEM = pl.BlockSpec(memory_space=pltpu.SMEM)
HBM = pl.BlockSpec(memory_space=pltpu.HBM)


def shape(*dims, dtype=f32):
    return jax.ShapeDtypeStruct(dims, dtype)


def with_types(scratch):
    for entry in scratch:
        if not isinstance(entry, tuple):
            yield entry
        else:
            dims, dtype = entry if isinstance(entry[0], tuple) else (entry, f32)
            yield pltpu.VMEM(dims, dtype)


def call(name, kernel, lists, args, outs, scratch=(), limit=12, spaces=None, out_spaces=None):
    many = isinstance(outs, (list, tuple))
    return pl.pallas_call(
        kernel,
        out_shape=tuple(outs) if many else outs,
        in_specs=[SMEM] * len(lists) + (spaces or [VMEM] * len(args)),
        out_specs=tuple(out_spaces or [VMEM] * len(outs)) if many else VMEM,
        scratch_shapes=list(with_types(scratch)),
        compiler_params=pltpu.CompilerParams(vmem_limit_bytes=limit and limit << 20),
        name=name,
    )(*lists, *args)


class Plan:
    pass


def swap_cores(value):
    return lax.ppermute(value, "core", [(0, 1), (1, 0)])


def local(
    positions,
    velocities,
    charge,
    inverse_mass,
    pair_tiles,
    halo_tiles,
    owners,
    centres,
    widths,
    map_density,
    map_error,
    partner,
    decision,
):
    replicas = lax.axis_size("rep")
    heights = lax.axis_size("z")
    domains = heights * CORES
    own, owned = owners.shape
    plan = Plan()
    plan.own, plan.owned, plan.tiles = own, owned, own * CORES
    plan.lanes = positions.shape[2] // own
    plan.near, plan.listed = pair_tiles.shape[1], halo_tiles.shape[2]
    components = widths.shape[0]
    half = plan.half = components // CORES
    tiles, lanes, listed = plan.tiles, plan.lanes, plan.listed

    args = [
        positions.transpose(1, 0, 2),
        velocities.transpose(1, 0, 2),
        charge[None],
        inverse_mass[None],
        centres,
        widths[None],
        map_density[None],
        map_error[None],
    ]
    state_send, comp_send = call(
        "pack",
        pack_kernel,
        [],
        args,
        [shape(replicas * CORES, 8, own * lanes), shape(domains, 6, half)],
        [(arg.shape, f32) for arg in args] + [pltpu.SemaphoreType.DMA((len(args),))],
        limit=None,
        spaces=[HBM] * len(args),
    )
    other_owners, other_halo = swap_cores(owners), swap_cores(halo_tiles)
    both = [owners, other_owners]
    spread = lax.all_to_all(state_send, ("rep", "core"), 0, 0, tiled=True)
    comps = lax.all_to_all(comp_send, ("z", "core"), 0, 0, tiled=True)

    map_gain = map_scale / (owned * components)
    scale = 1.0 / (owned * own * lanes)
    pair_gain = (plan.near * lanes) ** (-0.5)
    group = replicas * heights
    plan.one_phase = group * domains * half * 4 <= ONE_PHASE_BYTES
    copies = group if plan.one_phase else 1
    rim_rows = -(-4 * listed // 8) * 8
    onward = [(2 * i, (2 * i + 2) % domains) for i in range(heights)]
    onward += [((2 * i + 3) % domains, 2 * i + 1) for i in range(heights)]
    padded = -(-(own + 2 * listed + 1) // 8) * 8
    outs = [
        shape(copies, max(domains, rim_rows), half + lanes),
        shape(8, tiles, lanes),
        shape(tiles, DEPTH, lanes, dtype=bf16),
    ]
    scratch = [(tiles, DEPTH, lanes), (domains, 8, half), (rim_rows, lanes)]
    kept = [((tiles * owned, half, lanes), bf16)] * 2 + [pltpu.SemaphoreType.DMA((2, tiles))]
    for step in range(STEPS):
        if step == 0:
            partial, state, points, right = call(
                "first",
                functools.partial(first_kernel, plan, scale),
                both + [other_halo, partner, decision],
                [spread, comps],
                outs + [shape(domains, DEPTH, half, dtype=bf16)],
                scratch + [(domains, DEPTH, half)],
            )
        else:
            partial, state, points = call(
                "next",
                functools.partial(next_kernel, plan, scale),
                both + [other_halo],
                [state, force, swapped, right],
                outs,
                scratch,
            )
        if plan.one_phase:
            sums = far = lax.all_to_all(partial, ("rep", "z"), 0, 0, tiled=True)
        else:
            far = lax.ppermute(partial, ("z", "core"), onward)
            pieces = lax.all_to_all(
                partial[0, :domains, :half].reshape(group, -1), ("rep", "z"), 0, 0, tiled=True
            )
            piece = jnp.sum(pieces, 0)
            sums = lax.all_to_all(
                jnp.broadcast_to(piece[None], (group,) + piece.shape), ("rep", "z"), 0, 0, tiled=True
            ).reshape(1, domains, half)
        high, low, pair = call(
            "fill",
            functools.partial(fill_kernel, plan, pair_gain),
            both + [pair_tiles, other_halo],
            [state, points, right],
            [shape(tiles * owned, half, lanes, dtype=bf16)] * 2 + [shape(3, own, lanes)],
            [((domains, half, DEPTH), bf16), (4, padded, lanes), (padded, DEPTH, lanes),
             (padded, ROWS, lanes), ((padded, lanes, DEPTH), bf16)] + kept,
            limit=56,
            out_spaces=[HBM, HBM, VMEM],
        )
        force = call(
            "push",
            functools.partial(push_kernel, plan, map_gain, pair_gain, float(replicas)),
            both + [pair_tiles],
            [state, comps, sums, far, pair, points, high, low],
            shape(4, tiles, lanes),
            [(domains, ROWS, half), (half // lanes, domains, lanes), (listed, DEPTH, lanes),
             (listed, ROWS, lanes)] + kept,
            limit=56,
            spaces=[VMEM] * 6 + [HBM, HBM],
        )
        swapped = swap_cores(force)

    new_x, new_v, model_map = call(
        "finish",
        functools.partial(finish_kernel, plan),
        [],
        [state, force, swapped],
        [shape(3, 1, own * lanes), shape(3, 1, own * lanes), shape(1, components)],
        [(6, tiles, lanes)],
    )
    return (new_x.transpose(1, 0, 2), new_v.transpose(1, 0, 2), model_map.reshape(components))


def solution(mesh):
    replicas, domains = mesh.devices.shape
    split = Mesh(
        mesh.devices.reshape(replicas, domains // CORES, CORES), ("rep", "z", "core")
    )
    dom = ("z", "core")
    placed = (
        P("rep", None, dom),
        P("rep", None, dom),
        P(dom),
        P(dom),
        P(dom, None),
        P(dom, None, None),
        P(dom, None),
        P(None, dom),
        P(dom),
        P(dom),
        P(dom),
        P(),
        P(),
    )
    return jax.shard_map(
        local,
        mesh=split,
        in_specs=placed,
        out_specs=(P("rep", None, dom), P("rep", None, dom), P(dom)),
        check_vma=False,
    )
```

time: 149 us -> 106 us (0.71)
  Pallas kernels: 82.1 us -> 58.3 us
  starting transfers between devices: 28 us -> 14.1 us
  blocking collectives: 0 us -> 13.1 us
  between operations: 6.81 us -> 0.79 us
  local copies, waits for them, and re-layouts: 12.9 us -> 8.34 us
  other arithmetic: 3.81 us -> 0 us
  waiting for transfers between devices: 14.4 us -> 10.6 us
    pallas_call x6 -> x8, Pallas kernels: 82.1 us -> 58.3 us  [call(): pl.pallas_call(kernel, out_shape=tuple(outs) if many else outs, in_specs=...]
    all_to_all x0 -> x1, blocking collectives: none -> 13.1 us  [local(): comps = lax.all_to_all(comp_send, ('z', 'core'), 0, 0, tiled=True)]
    ppermute x2 -> x0, waiting for transfers between devices: 8.12 us -> none  [local(): far = lax.ppermute(rim, ('z', 'core'), across)]
    all_to_all x4 -> x3, starting transfers between devices: 21.2 us -> 13.4 us  [the longest x2 9.68 us: local(): sums = far = lax.all_to_all(partial, ('rep', 'z'), 0, 0, tiled=True)]
    ppermute x2 -> x0, starting transfers between devices: 5.61 us -> none  [local(): far = lax.ppermute(rim, ('z', 'core'), across)]
    all_to_all x4 -> x3, waiting for transfers between devices: 4.1 us -> 6.46 us  [the longest x1 4.26 us: local(): spread = lax.all_to_all(state_send, ('rep', 'core'), 0, 0, tiled=True)]
    ppermute x5 -> x4, waiting for transfers between devices: 2.15 us -> 4.18 us  [swap_cores(): return lax.ppermute(value, 'core', [(0, 1), (1, 0)])]
    unnamed x47 -> x43, local copies, waits for them, and re-layouts: 8.1 us -> 8.34 us
  transfers between devices with their start and end apart: 11 -> 7, of which waited for: 6 -> 6; matrix products, arithmetic and copies ran while one was open for 4% -> 1% of each run, Pallas kernels for 14% -> 21%
where the time goes in v2:
time: 106 us; the launch traced here: 105 us
  Pallas kernels  58.3 us (55%)
  starting transfers between devices  14.1 us (13%)
  blocking collectives  13.1 us (12%)
  waiting for transfers between devices  10.6 us (10%)
  local copies, waits for them, and re-layouts  8.34 us (8%)
    pallas_call x8, Pallas kernels, call(): pl.pallas_call(kernel, out_shape=tuple(outs) if many else outs, in_specs=...  58.3 us
    all_to_all x1, blocking collectives, local(): comps = lax.all_to_all(comp_send, ('z', 'core'), 0, 0, tiled=True)  13.1 us
    all_to_all x2, starting transfers between devices, local(): sums = far = lax.all_to_all(partial, ('rep', 'z'), 0, 0, tiled=True)  9.68 us
    unnamed x43, local copies, waits for them, and re-layouts  8.34 us
    all_to_all x1, waiting for transfers between devices, local(): spread = lax.all_to_all(state_send, ('rep', 'core'), 0, 0, tiled=True)  4.26 us
    ppermute x4, waiting for transfers between devices, swap_cores(): return lax.ppermute(value, 'core', [(0, 1), (1, 0)])  4.18 us
    all_to_all x1, starting transfers between devices, local(): spread = lax.all_to_all(state_send, ('rep', 'core'), 0, 0, tiled=True)  3.72 us
    all_to_all x2, waiting for transfers between devices, local(): sums = far = lax.all_to_all(partial, ('rep', 'z'), 0, 0, tiled=True)  2.2 us
  transfers between devices with their start and end apart: 7, of which 6 were waited for; matrix products, arithmetic and copies ran while one was open for 1% of the time, Pallas kernels for 21%

profile of v2, /device:TPU:0, one launch (start us, length us, event | category | flops | bytes accessed | tf_op | source)
XLA Modules:
  0.0 105.3 jit_solution(17447697545393329803)
XLA Ops:
  0.6 1.7 %pack.1 = (f32[8,8,1024]{2,1,0:T(8,128)}, f32[8,6,512]{2,1,0:T(8,128)}) custom-call(f32[3,1,1024]{2,1,0:T(1,128)} %bitcast.10, f32[3,1,1024]{2,1,0:T(1,128)} %bitcast.11, f32[1,1024]{1,0:T(1,128)} %bitcast.12, f32[1,1024]{1,0:T(1,128)} %bitcast.13, f32[3,1024]{1,0:T(4,128)} %centre_hbm.1, f32[1,1024]{1,0:T(1,128)} %bitcast.14, f32[1,1024]{1,0:T(1,128)} %bitcast.15, ...), custom_call_target="tpu_custom_call" | custom-call | tf_op jit(solution)/shard_map/pack/pallas_call | solution.py:392
  2.3 13.1 %all_to_all.20.comp_ref = f32[8,6,512]{2,1,0:T(8,128)S(1)} all-to-all(f32[8,6,512]{2,1,0:T(8,128)} %get-tuple-element.22), channel_id=1, replica_groups=mesh['rep'=4,'z'=4,'core'=2] {'z','core'}, dimensions={0} | all-to-all | bytes 196608 | tf_op jit(solution)/shard_map/all_to_all | solution.py:461
  15.4 3.7 %all-to-all-start = ((f32[8,8,1024]{2,1,0:T(8,128)}), f32[8,8,1024]{2,1,0:T(8,128)S(1)}, u32[]{:S(2)}, u32[]{:S(2)}) async-start(f32[8,8,1024]{2,1,0:T(8,128)} %get-tuple-element.21), calls=%async_computation | async-start | bytes 524288 | tf_op jit(solution)/shard_map/all_to_all | solution.py:460
  19.1 0.8 copy.20.mine_ref
  19.9 0.5 collective-permute-start
  20.4 1.4 %collective-permute-done.1.halo_ref = s32[1,2,2]{2,1,0:T(2,128)S(1)} collective-permute-done((s32[1,2,2]{2,1,0:T(2,128)}, s32[1,2,2]{2,1,0:T(2,128)S(1)}, u32[]{:S(2)}, u32[]{:S(2)}) %collective-permute-start.1) | collective-permute-done | bytes 48 | tf_op jit(solution)/shard_map/ppermute | solution.py:408
  21.8 4.3 %all-to-all-done.spread_ref = f32[8,8,1024]{2,1,0:T(8,128)S(1)} async-done(((f32[8,8,1024]{2,1,0:T(8,128)}), f32[8,8,1024]{2,1,0:T(8,128)S(1)}, u32[]{:S(2)}, u32[]{:S(2)}) %all-to-all-start) | async-done | bytes 262176 | tf_op jit(solution)/shard_map/all_to_all | solution.py:460
  26.0 0.7 copy-done.17
  26.7 0.7 copy-done.18
  27.3 7.6 %first.1 = (f32[16,8,640]{2,1,0:T(8,128)}, f32[8,16,128]{2,1,0:T(8,128)S(1)}, bf16[16,32,128]{2,1,0:T(8,128)(2,1)S(1)}, bf16[8,32,512]{2,1,0:T(8,128)(2,1)S(1)}) custom-call(s32[8,4]{1,0:T(8,128)S(1)} %copy.20.mine_ref, s32[8,4]{1,0:T(8,128)S(1)} %collective-permute-done.theirs_ref, s32[1,2,2]{2,1,0:T(2,128)S(1)} %collective-permute-done.1.halo_ref, ...), custom_call_target="tpu_custom_call" | custom-call | tf_op jit(solution)/shard_map/first/pallas_call | solution.py:392
  34.9 0.7 copy-done
  35.6 0.6 copy-done.3
  36.3 0.7 copy-done.8
  36.9 3.5 %all-to-all-start.2 = ((f32[16,8,640]{2,1,0:T(8,128)}), f32[16,8,640]{2,1,0:T(8,128)S(1)}, u32[]{:S(2)}, u32[]{:S(2)}) async-start(f32[16,8,640]{2,1,0:T(8,128)} %get-tuple-element.24), calls=%async_computation.2 | async-start | bytes 655360 | tf_op jit(solution)/shard_map/all_to_all | solution.py:500
  40.5 10.8 %fill.2 = (bf16[64,512,128]{2,1,0:T(8,128)(2,1)}, bf16[64,512,128]{2,1,0:T(8,128)(2,1)}, f32[3,8,128]{2,1,0:T(8,128)}) custom-call(s32[8,4]{1,0:T(8,128)} %copy-done.9, s32[8,4]{1,0:T(8,128)} %copy-done.11, s32[8,6]{1,0:T(8,128)} %pairs_ref.7, s32[1,2,2]{2,1,0:T(2,128)} %copy-done.15, f32[8,16,128]{2,1,0:T(8,128)} %copy-done.3, ...), custom_call_target="tpu_custom_call" | custom-call | tf_op jit(solution)/shard_map/fill/pallas_call | solution.py:392
  51.4 0.8 all-to-all-done.2.sums_ref.far_ref
  52.1 0.7 copy-done.20
  52.9 9.8 %push.2.force_ref = f32[4,16,128]{2,1,0:T(8,128)} custom-call(s32[8,4]{1,0:T(8,128)} %copy-done.9, s32[8,4]{1,0:T(8,128)} %copy-done.11, s32[8,6]{1,0:T(8,128)} %pairs_ref.7, f32[8,16,128]{2,1,0:T(8,128)} %copy-done.3, f32[8,6,512]{2,1,0:T(8,128)} %copy-done.2, f32[16,8,640]{2,1,0:T(8,128)} %copy-done.20, f32[16,8,640]{2,1,0:T(8,128)} %copy-done.20, ...), custom_call_target="tpu_custom_call" | custom-call | tf_op jit(solution)/shard_map/push/pallas_call | solution.py:392
  62.7 0.1 collective-permute-start.2
  62.7 1.4 %collective-permute-done.2.swapped_ref = f32[4,16,128]{2,1,0:T(8,128)S(1)} collective-permute-done((f32[4,16,128]{2,1,0:T(8,128)}, f32[4,16,128]{2,1,0:T(8,128)S(1)}, u32[]{:S(2)}, u32[]{:S(2)}) %collective-permute-start.2) | collective-permute-done | bytes 32800 | tf_op jit(solution)/shard_map/ppermute | solution.py:408
  64.2 0.7 copy-done.13
  64.9 7.2 %next.1 = (f32[16,8,640]{2,1,0:T(8,128)}, f32[8,16,128]{2,1,0:T(8,128)S(1)}, bf16[16,32,128]{2,1,0:T(8,128)(2,1)S(1)}) custom-call(s32[8,4]{1,0:T(8,128)S(1)} %copy-done.10, s32[8,4]{1,0:T(8,128)S(1)} %copy-done.12, s32[1,2,2]{2,1,0:T(2,128)S(1)} %copy-done.16, f32[8,16,128]{2,1,0:T(8,128)S(1)} %copy-done.4, f32[4,16,128]{2,1,0:T(8,128)S(1)} %copy-done.13, ...), custom_call_target="tpu_custom_call" | custom-call | tf_op jit(solution)/shard_map/next/pallas_call | solution.py:392
  72.1 0.6 copy-done.5
  72.8 0.7 copy-done.7
  73.4 6.1 %all-to-all-start.3 = ((f32[16,8,640]{2,1,0:T(8,128)}), f32[16,8,640]{2,1,0:T(8,128)S(1)}, u32[]{:S(2)}, u32[]{:S(2)}) async-start(f32[16,8,640]{2,1,0:T(8,128)} %get-tuple-element.31), calls=%async_computation.3 | async-start | bytes 655360 | tf_op jit(solution)/shard_map/all_to_all | solution.py:500
  79.6 10.8 %fill.3 = (bf16[64,512,128]{2,1,0:T(8,128)(2,1)}, bf16[64,512,128]{2,1,0:T(8,128)(2,1)}, f32[3,8,128]{2,1,0:T(8,128)}) custom-call(s32[8,4]{1,0:T(8,128)} %copy-done.9, s32[8,4]{1,0:T(8,128)} %copy-done.11, s32[8,6]{1,0:T(8,128)} %pairs_ref.7, s32[1,2,2]{2,1,0:T(2,128)} %copy-done.15, f32[8,16,128]{2,1,0:T(8,128)} %copy-done.5, ...), custom_call_target="tpu_custom_call" | custom-call | tf_op jit(solution)/shard_map/fill/pallas_call | solution.py:392
  90.4 1.4 %all-to-all-done.3.sums_ref.far_ref = f32[16,8,640]{2,1,0:T(8,128)S(1)} async-done(((f32[16,8,640]{2,1,0:T(8,128)}), f32[16,8,640]{2,1,0:T(8,128)S(1)}, u32[]{:S(2)}, u32[]{:S(2)}) %all-to-all-start.3) | async-done | bytes 327712 | tf_op jit(solution)/shard_map/all_to_all | solution.py:500
  91.9 0.7 copy-done.19
  92.6 9.8 %push.3.mine_ref = f32[4,16,128]{2,1,0:T(8,128)} custom-call(s32[8,4]{1,0:T(8,128)} %copy-done.9, s32[8,4]{1,0:T(8,128)} %copy-done.11, s32[8,6]{1,0:T(8,128)} %pairs_ref.7, f32[8,16,128]{2,1,0:T(8,128)} %copy-done.5, f32[8,6,512]{2,1,0:T(8,128)} %copy-done.2, f32[16,8,640]{2,1,0:T(8,128)} %copy-done.19, f32[16,8,640]{2,1,0:T(8,128)} %copy-done.19, ...), custom_call_target="tpu_custom_call" | custom-call | tf_op jit(solution)/shard_map/push/pallas_call | solution.py:392
  102.5 1.4 %collective-permute-done.3.theirs_ref = f32[4,16,128]{2,1,0:T(8,128)S(1)} collective-permute-done((f32[4,16,128]{2,1,0:T(8,128)}, f32[4,16,128]{2,1,0:T(8,128)S(1)}, u32[]{:S(2)}, u32[]{:S(2)}) %collective-permute-start.3) | collective-permute-done | bytes 32800 | tf_op jit(solution)/shard_map/ppermute | solution.py:408
  103.9 0.8 copy-done.14
  104.6 0.6 finish.1
  (34 shorter events, 0.1 us)
Async XLA Ops:
  15.4 36.7 %copy-start.2 = (f32[8,6,512]{2,1,0:T(8,128)}, f32[8,6,512]{2,1,0:T(8,128)S(1)}, u32[]{:S(2)}) copy-start(f32[8,6,512]{2,1,0:T(8,128)S(1)} %all_to_all.20.comp_ref) | copy-start | bytes 294916
  15.4 10.6 %all-to-all-start = ((f32[8,8,1024]{2,1,0:T(8,128)}), f32[8,8,1024]{2,1,0:T(8,128)S(1)}, u32[]{:S(2)}, u32[]{:S(2)}) async-start(f32[8,8,1024]{2,1,0:T(8,128)} %get-tuple-element.21), calls=%async_computation | async-start | bytes 524288 | tf_op jit(solution)/shard_map/all_to_all | solution.py:460
  19.9 20.6 %copy-start.9 = (s32[8,4]{1,0:T(8,128)}, s32[8,4]{1,0:T(8,128)S(1)}, u32[]{:S(2)}) copy-start(s32[8,4]{1,0:T(8,128)S(1)} %copy.20.mine_ref) | copy-start | bytes 388
  19.9 1.9 %collective-permute-start = (s32[8,4]{1,0:T(8,128)S(1)}, s32[8,4]{1,0:T(8,128)S(1)}, u32[]{:S(2)}, u32[]{:S(2)}) collective-permute-start(s32[8,4]{1,0:T(8,128)S(1)} %copy.20.mine_ref), channel_id=1, source_target_pairs={{0,1},{1,0},{2,3},{3,2},{4,5},{5,4},{6,7},{7,6},{8,9},{9,8},{10,11... | collective-permute-start | bytes 392 | tf_op jit(solution)/shard_map/ppermute | solution.py:408
  20.4 1.4 %collective-permute-start.1 = (s32[1,2,2]{2,1,0:T(2,128)}, s32[1,2,2]{2,1,0:T(2,128)S(1)}, u32[]{:S(2)}, u32[]{:S(2)}) collective-permute-start(s32[1,2,2]{2,1,0:T(2,128)} %param.18), channel_id=1, source_target_pairs={{0,1},{1,0},{2,3},{3,2},{4,5},{5,4},{6,7},{7,6},{8,9},{9,8},{10,11... | collective-permute-start | bytes 56 | tf_op jit(solution)/shard_map/ppermute | solution.py:408
  21.8 18.7 %copy-start.15 = (s32[1,2,2]{2,1,0:T(2,128)}, s32[1,2,2]{2,1,0:T(2,128)S(1)}, u32[]{:S(2)}) copy-start(s32[1,2,2]{2,1,0:T(2,128)S(1)} %collective-permute-done.1.halo_ref) | copy-start | bytes 52
  21.8 18.7 %copy-start.11 = (s32[8,4]{1,0:T(8,128)}, s32[8,4]{1,0:T(8,128)S(1)}, u32[]{:S(2)}) copy-start(s32[8,4]{1,0:T(8,128)S(1)} %collective-permute-done.theirs_ref) | copy-start | bytes 388
  26.0 0.7 copy-start.17
  26.7 0.7 copy-start.18
  34.9 0.7 copy-start
  35.6 0.6 copy-start.3
  36.3 0.7 copy-start.8
  36.9 15.2 %all-to-all-start.2 = ((f32[16,8,640]{2,1,0:T(8,128)}), f32[16,8,640]{2,1,0:T(8,128)S(1)}, u32[]{:S(2)}, u32[]{:S(2)}) async-start(f32[16,8,640]{2,1,0:T(8,128)} %get-tuple-element.24), calls=%async_computation.2 | async-start | bytes 655360 | tf_op jit(solution)/shard_map/all_to_all | solution.py:500
  52.1 0.7 copy-start.20
  52.9 11.3 %copy-start.1 = (bf16[8,32,512]{2,1,0:T(8,128)(2,1)S(1)}, bf16[8,32,512]{2,1,0:T(8,128)(2,1)}, u32[]{:S(2)}) copy-start(bf16[8,32,512]{2,1,0:T(8,128)(2,1)} %copy-done) | copy-start | bytes 786436
  52.9 11.3 %copy-start.4 = (f32[8,16,128]{2,1,0:T(8,128)S(1)}, f32[8,16,128]{2,1,0:T(8,128)}, u32[]{:S(2)}) copy-start(f32[8,16,128]{2,1,0:T(8,128)} %copy-done.3) | copy-start | bytes 196612
  52.9 11.3 %copy-start.10 = (s32[8,4]{1,0:T(8,128)S(1)}, s32[8,4]{1,0:T(8,128)}, u32[]{:S(2)}) copy-start(s32[8,4]{1,0:T(8,128)} %copy-done.9) | copy-start | bytes 388
  52.9 11.3 %copy-start.12 = (s32[8,4]{1,0:T(8,128)S(1)}, s32[8,4]{1,0:T(8,128)}, u32[]{:S(2)}) copy-start(s32[8,4]{1,0:T(8,128)} %copy-done.11) | copy-start | bytes 388
  52.9 11.3 %copy-start.16 = (s32[1,2,2]{2,1,0:T(2,128)S(1)}, s32[1,2,2]{2,1,0:T(2,128)}, u32[]{:S(2)}) copy-start(s32[1,2,2]{2,1,0:T(2,128)} %copy-done.15) | copy-start | bytes 52
  62.7 1.5 %collective-permute-start.2 = (f32[4,16,128]{2,1,0:T(8,128)}, f32[4,16,128]{2,1,0:T(8,128)S(1)}, u32[]{:S(2)}, u32[]{:S(2)}) collective-permute-start(f32[4,16,128]{2,1,0:T(8,128)} %push.2.force_ref), channel_id=1, source_target_pairs={{0,1},{1,0},{2,3},{3,2},{4,5},{5,4},{6,7},{7,6},{8,9},{9,8},{10,11... | collective-permute-start | bytes 98312 | tf_op jit(solution)/shard_map/ppermute | solution.py:408
  64.2 0.8 copy-start.13
  72.1 0.6 copy-start.5
  72.8 0.7 copy-start.7
  73.4 18.4 %all-to-all-start.3 = ((f32[16,8,640]{2,1,0:T(8,128)}), f32[16,8,640]{2,1,0:T(8,128)S(1)}, u32[]{:S(2)}, u32[]{:S(2)}) async-start(f32[16,8,640]{2,1,0:T(8,128)} %get-tuple-element.31), calls=%async_computation.3 | async-start | bytes 655360 | tf_op jit(solution)/shard_map/all_to_all | solution.py:500
  91.9 0.7 copy-start.19
  92.6 11.3 %copy-start.6 = (f32[8,16,128]{2,1,0:T(8,128)S(1)}, f32[8,16,128]{2,1,0:T(8,128)}, u32[]{:S(2)}) copy-start(f32[8,16,128]{2,1,0:T(8,128)} %copy-done.5) | copy-start | bytes 196612
  102.4 1.5 %collective-permute-start.3 = (f32[4,16,128]{2,1,0:T(8,128)}, f32[4,16,128]{2,1,0:T(8,128)S(1)}, u32[]{:S(2)}, u32[]{:S(2)}) collective-permute-start(f32[4,16,128]{2,1,0:T(8,128)} %push.3.mine_ref), channel_id=1, source_target_pairs={{0,1},{1,0},{2,3},{3,2},{4,5},{5,4},{6,7},{7,6},{8,9},{9,8},{10,11... | collective-permute-start | bytes 98312 | tf_op jit(solution)/shard_map/ppermute | solution.py:408
  103.9 0.8 copy-start.14

commit v3 on v2

v3 whole, which is shorter than its diff:
```python
import functools
import math

import jax
import jax.numpy as jnp
from jax import lax
from jax.experimental import pallas as pl
from jax.experimental.pallas import tpu as pltpu
from jax.sharding import Mesh, PartitionSpec as P

STEPS = 2
CORES = 2
DEPTH = 32
ROWS = 16
ONE_PHASE_BYTES = 1 << 20
UNROLL = 2
FAR_SQUARE = 1048576.0

time_step = 0.5
pair_width = 1.0
map_scale = 2.0
log2e = math.log2(math.e)
f32 = jnp.float32
bf16 = jnp.bfloat16

LEFT_PARTS = (0, 0, 1, 1, 0, 2)
RIGHT_PARTS = (0, 1, 0, 1, 2, 0)


def split3(value):
    high = value.astype(bf16).astype(f32)
    rest = value - high
    middle = rest.astype(bf16).astype(f32)
    return high, middle, rest - middle


def point_rows(coords):
    rows = []
    for coord in coords:
        parts = split3(coord)
        rows += [parts[i] for i in LEFT_PARTS]
    parts = split3(coords[0] * coords[0] + coords[1] * coords[1] + coords[2] * coords[2])
    rows += [parts[i] for i in LEFT_PARTS]
    one = jnp.ones_like(coords[0])
    return rows + [one, one, one]


def nowhere(ref, tile):
    shape = ref.shape[1:]
    row = lax.broadcasted_iota(jnp.int32, shape, 0)
    square = len(LEFT_PARTS) * 3
    ref[tile] = jnp.where(row == square, FAR_SQUARE, 0.0)


def centre_rows(coords, extent):
    scale = log2e / extent
    rows = []
    for coord in coords:
        parts = split3(coord * scale)
        rows += [parts[i] for i in RIGHT_PARTS]
    parts = split3(-0.5 * scale)
    rows += [parts[i] for i in RIGHT_PARTS]
    square = coords[0] * coords[0] + coords[1] * coords[1] + coords[2] * coords[2]
    return rows + list(split3(-0.5 * scale * square))


def pull_rows(coords, weight):
    rows = list(split3(weight))
    for coord in coords:
        rows += list(split3(coord * weight))
    return rows


def squeeze_sums(coords, sums):
    def total(first):
        return sums[first : first + 1] + sums[first + 1 : first + 2] + sums[first + 2 : first + 3]

    strength = total(0)
    return [coords[i] * strength - total(3 + 3 * i) for i in range(3)]


def dot(left, right):
    return jnp.dot(left, right, preferred_element_type=f32)


def high_low(value):
    high = value.astype(bf16)
    return high, (value - high.astype(f32)).astype(bf16)


def store_rows(ref, rows):
    count, depth, width = rows[0].shape[0], ref.shape[1], ref.shape[2]
    for index, row in enumerate(rows):
        ref[0:count, index, :] = row
    if len(rows) < depth:
        ref[0:count, len(rows) : depth, :] = jnp.zeros((count, depth - len(rows), width), f32)


def chunks(total, wanted):
    size = wanted if total % wanted == 0 else total
    return [(start, size) for start in range(0, total, size)]


def pack_kernel(pos_hbm, vel_hbm, charge_hbm, mass_hbm, centre_hbm, width_hbm, density_hbm,
                error_hbm, owners_hbm, halo_hbm, state_ref, comp_ref, ints_ref, pos_ref, vel_ref,
                charge_ref, mass_ref, centre_ref, width_ref, density_ref, error_ref, owners_ref,
                halo_ref, sems):
    sources = (pos_hbm, vel_hbm, charge_hbm, mass_hbm, centre_hbm, width_hbm, density_hbm,
               error_hbm, owners_hbm, halo_hbm)
    targets = (pos_ref, vel_ref, charge_ref, mass_ref, centre_ref, width_ref, density_ref,
               error_ref, owners_ref, halo_ref)
    copies = [
        pltpu.make_async_copy(source, target, sems.at[n])
        for n, (source, target) in enumerate(zip(sources, targets))
    ]
    for copy in copies:
        copy.start()
    for copy in copies:
        copy.wait()
    half = comp_ref.shape[2]
    for i in range(3):
        state_ref[i : i + 1, :] = pos_ref[i]
        state_ref[3 + i : 4 + i, :] = vel_ref[i]
    state_ref[6:7, :] = charge_ref[...]
    state_ref[7:8, :] = mass_ref[...]
    own, owned = owners_ref.shape
    _, sides, listed = halo_ref.shape
    ints_ref[...] = jnp.zeros_like(ints_ref)
    ints_ref[0:own, 0:owned] = owners_ref[...]
    ints_ref[own : own + sides, 0:listed] = halo_ref[0]
    for row in range(comp_ref.shape[0]):
        part = pl.ds((row % CORES) * half, half)
        comp_ref[row, 0:3, :] = centre_ref[:, part]
        comp_ref[row, 3:4, :] = width_ref[:, part]
        comp_ref[row, 4:5, :] = density_ref[:, part]
        comp_ref[row, 5:6, :] = error_ref[:, part]


def choose_kernel(partner_ref, decision_ref, mine_ref, *refs):
    others, out_ref = refs[:-1], refs[-1]
    row = lax.axis_index("rep")
    source = jnp.where(decision_ref[row] == 1, partner_ref[row], row)
    if len(others) == 1:
        out_ref[...] = others[0][source]
        return
    out_ref[...] = mine_ref[...]
    for n, other_ref in enumerate(others):

        @pl.when(source == (row ^ (n + 1)))
        def _():
            out_ref[...] = other_ref[...]


def list_kernel(plan, mine_ref, theirs_ref, pairs_ref, out_ref, waiting):
    core = lax.axis_index("core")

    def clear(domain, carry):
        waiting[domain] = -1
        return carry

    lax.fori_loop(0, plan.domains, clear, 0)

    def one_tile(tile, count):
        row = lax.rem(tile, plan.own)
        here = lax.div(tile, plan.own) == core
        for j in range(plan.owned):
            owner = jnp.where(here, mine_ref[row, j], theirs_ref[row, j])
            first = waiting[owner]
            out_ref[0, count] = owner
            out_ref[1, count] = first
            out_ref[2, count] = tile
            count = count + jnp.where(first < 0, 0, 1)
            waiting[owner] = jnp.where(first < 0, tile, -1)
        return count

    count = lax.fori_loop(0, plan.tiles, one_tile, 0)

    def leftover(domain, count):
        first = waiting[domain]
        out_ref[0, count] = domain
        out_ref[1, count] = first
        out_ref[2, count] = plan.tiles
        return count + jnp.where(first < 0, 0, 1)

    count = lax.fori_loop(0, plan.domains, leftover, count)
    for extra in range(UNROLL - 1):
        out_ref[0, count + extra] = 0
        out_ref[1, count + extra] = plan.tiles
        out_ref[2, count + extra] = plan.tiles
    out_ref[3, 0] = lax.div(count + UNROLL - 1, UNROLL)
    for side in range(2):
        for k in range(plan.listed):
            out_ref[3, 1 + side * plan.listed + k] = theirs_ref[plan.own + side, k]
    for tile in range(plan.own):
        for j in range(plan.near):
            out_ref[4 + j, tile] = pairs_ref[tile, j]


def partner_tile(plan, lists_ref, side, k):
    core = lax.axis_index("core")
    return (1 - core) * plan.own + lists_ref[3, 1 + side * plan.listed + k]


def for_pairs(lists_ref, body):
    def step(n, carry):
        for u in range(UNROLL):
            place = n * UNROLL + u
            body(lists_ref[0, place], lists_ref[1, place], lists_ref[2, place])
        return carry

    lax.fori_loop(0, lists_ref[3, 0], step, 0)


def sum_gaussians(plan, scale, lists_ref, state_ref, right_ref, points_ref, out_ref, xs, acc, rim, left):
    tiles, listed = plan.tiles, plan.listed
    store_rows(xs, point_rows([state_ref[i] for i in range(3)]))
    nowhere(xs, tiles)
    for tile in range(tiles + 1):
        points = xs[tile]
        points_ref[tile] = points.astype(bf16)
        left[tile] = points.T.astype(bf16)
    core = lax.axis_index("core")
    for k in range(listed):
        tile = partner_tile(plan, lists_ref, 1 - core, k)
        for i, row in enumerate((0, 1, 2, 6)):
            rim[i * listed + k : i * listed + k + 1, :] = state_ref[row, pl.ds(tile, 1), :]
    acc[...] = jnp.zeros_like(acc)

    def one_pair(owner, first, second):
        both = jnp.concatenate([left[first], left[second]], 0)
        for start, size in chunks(right_ref.shape[2], 256):
            g = jnp.exp2(dot(both, right_ref[owner, :, start : start + size]))
            acc[owner, :, start : start + size] += jnp.sum(g.reshape(g.shape[0] // 8, 8, size), 0)

    for_pairs(lists_ref, one_pair)
    total = jnp.sum(acc[...], 1) * scale
    for row in range(out_ref.shape[0]):
        out_ref[row, 0 : acc.shape[0], 0 : plan.half] = total
        out_ref[row, 0 : rim.shape[0], plan.half :] = rim[...]


def first_kernel(plan, scale, lists_ref, mine_ref, theirs_ref, comp_ref,
                 out_ref, state_ref, points_ref, right_ref, xs, acc, rim, left, cs):
    core = lax.axis_index("core")
    for tile in range(plan.own):
        lanes = slice(tile * plan.lanes, (tile + 1) * plan.lanes)
        mine, theirs = mine_ref[:, lanes], theirs_ref[:, lanes]
        state_ref[:, tile, :] = jnp.where(core == 0, mine, theirs)
        state_ref[:, plan.own + tile, :] = jnp.where(core == 0, theirs, mine)
    store_rows(cs, centre_rows([comp_ref[:, i, :] for i in range(3)], comp_ref[:, 3, :]))
    right_ref[...] = cs[...].astype(bf16)
    sum_gaussians(plan, scale, lists_ref, state_ref, right_ref, points_ref, out_ref, xs, acc, rim, left)


def stepped(old_ref, mine_ref, theirs_ref):
    mass = time_step * old_ref[7]
    for i in range(3):
        v = old_ref[3 + i] + mass * (mine_ref[i] + theirs_ref[i])
        yield old_ref[i] + time_step * v, v


def next_kernel(plan, scale, lists_ref, old_ref, force_ref, swapped_ref, right_ref,
                out_ref, state_ref, points_ref, xs, acc, rim, left):
    for i, (x, v) in enumerate(stepped(old_ref, force_ref, swapped_ref)):
        state_ref[i] = x
        state_ref[3 + i] = v
    state_ref[6] = old_ref[6]
    state_ref[7] = old_ref[7]
    sum_gaussians(plan, scale, lists_ref, state_ref, right_ref, points_ref, out_ref, xs, acc, rim, left)


def finish_kernel(plan, old_ref, mine_ref, theirs_ref, x_ref, v_ref, map_ref, state):
    for i, (x, v) in enumerate(stepped(old_ref, mine_ref, theirs_ref)):
        state[i] = x
        state[3 + i] = v
    core = lax.axis_index("core")
    base = core * plan.own
    for tile in range(plan.own):
        lanes = slice(tile * plan.lanes, (tile + 1) * plan.lanes)
        for i in range(3):
            x_ref[i, :, lanes] = state[i, pl.ds(base + tile, 1), :]
            v_ref[i, :, lanes] = state[3 + i, pl.ds(base + tile, 1), :]
    first = core == 0
    pieces = plan.half // plan.lanes
    for n in range(pieces):
        keep = mine_ref[3, n : n + 1, :]
        got = theirs_ref[3, pieces + n : pieces + n + 1, :]
        low = slice(n * plan.lanes, (n + 1) * plan.lanes)
        high = slice(plan.half + n * plan.lanes, plan.half + (n + 1) * plan.lanes)
        map_ref[:, low] = jnp.where(first, keep, got)
        map_ref[:, high] = jnp.where(first, got, keep)


def turn_kernel(right_ref, turned_ref):
    for domain in range(right_ref.shape[0]):
        for start, size in chunks(right_ref.shape[2], 128):
            turned_ref[domain, start : start + size, :] = (
                right_ref[domain, :, start : start + size].astype(f32).T.astype(bf16)
            )


def near_kernel(plan, gain, lists_ref, state_ref, points_ref, out_ref, table, cs, rs, turned):
    own, near, listed = plan.own, plan.near, plan.listed
    core = lax.axis_index("core")
    base = pl.multiple_of(core * own, own)
    extent = own + 2 * listed
    table[...] = jnp.zeros_like(table)
    for i, source in enumerate((0, 1, 2, 6)):
        table[i, 0:own, :] = state_ref[source, pl.ds(base, own), :]
        for k in range(listed):
            table[i, pl.ds(own + (1 - core) * listed + k, 1), :] = state_ref[
                source, pl.ds(partner_tile(plan, lists_ref, core, k), 1), :
            ]
    coords = [table[i] for i in range(3)]
    store_rows(cs, centre_rows(coords, jnp.full_like(coords[0], pair_width)))
    store_rows(rs, pull_rows(coords, table[3]))
    for entry in range(table.shape[1]):
        turned[entry] = cs[entry].T.astype(bf16)
    for tile in range(own):
        points = points_ref[base + tile]
        sums = jnp.zeros((ROWS, plan.lanes), f32)
        for j in range(near):
            entry = lists_ref[4 + j, tile]
            entry = jnp.where(entry < 0, extent, entry)
            rows = rs[entry].astype(bf16)
            high, low = high_low(jnp.exp2(dot(turned[entry], points)))
            sums += dot(rows, high) + dot(rows, low)
        coords = [state_ref[i, pl.ds(base + tile, 1), :] for i in range(3)]
        strength = gain / pair_width * state_ref[6, pl.ds(base + tile, 1), :]
        for i, push in enumerate(squeeze_sums(coords, sums)):
            out_ref[i, tile : tile + 1, :] = strength * push


def far_pushes(plan, gain, lists_ref, state_ref, far, points_ref, out_ref, cs, rs):
    own, near, listed = plan.own, plan.near, plan.listed
    core = lax.axis_index("core")
    base = core * own
    coords = [far[i * listed : (i + 1) * listed] for i in range(3)]
    store_rows(cs, centre_rows(coords, jnp.full_like(coords[0], pair_width)))
    store_rows(rs, pull_rows(coords, far[3 * listed : 4 * listed]))
    turned = [cs[k].T.astype(bf16) for k in range(listed)]
    for tile in range(own):
        points = points_ref[base + tile]
        sums = jnp.zeros((ROWS, plan.lanes), f32)
        for k in range(listed):
            entry = own + core * listed + k
            named = lists_ref[4, tile] == entry
            for j in range(1, near):
                named = named | (lists_ref[4 + j, tile] == entry)
            rows = (rs[k] * jnp.where(named, 1.0, 0.0)).astype(bf16)
            high, low = high_low(jnp.exp2(dot(turned[k], points)))
            sums += dot(rows, high) + dot(rows, low)
        coords = [state_ref[i, pl.ds(base + tile, 1), :] for i in range(3)]
        strength = gain / pair_width * state_ref[6, pl.ds(base + tile, 1), :]
        for i, push in enumerate(squeeze_sums(coords, sums)):
            out_ref[i, pl.ds(base + tile, 1), :] += strength * push


def push_kernel(plan, gain, pair_gain, replicas, lists_ref, state_ref, comp_ref, sums_ref, far_ref,
                pair_ref, points_ref, turned_ref, out_ref, rs, rows, means, sums, far_cs, far_rs):
    domains, tiles = comp_ref.shape[0], plan.tiles
    mean = jnp.sum(sums_ref[:, 0:domains, 0 : plan.half], 0) / replicas
    for n in range(plan.half // plan.lanes):
        means[n] = mean[:, n * plan.lanes : (n + 1) * plan.lanes]
    error = comp_ref[:, 5, :]
    coefficient = gain * (mean - comp_ref[:, 4, :]) / (error * error) / comp_ref[:, 3, :]
    store_rows(rs, pull_rows([comp_ref[:, i, :] for i in range(3)], coefficient))
    rows[...] = rs[...].astype(bf16)
    sums[...] = jnp.zeros_like(sums)

    def one_pair(owner, first, second):
        points = jnp.concatenate([points_ref[first], points_ref[second]], 1)
        total = None
        for start, size in chunks(plan.half, 256):
            part = slice(start, start + size)
            high, low = high_low(jnp.exp2(dot(turned_ref[owner, part, :], points)))
            weights = rows[owner, :, part]
            term = dot(weights, high) + dot(weights, low)
            total = term if total is None else total + term
        sums[first] += total[:, : plan.lanes]
        sums[second] += total[:, plan.lanes :]

    for_pairs(lists_ref, one_pair)

    def added(row):
        return sums[0:tiles, row, :] + sums[0:tiles, row + 1, :] + sums[0:tiles, row + 2, :]

    strength = added(0)
    for i in range(3):
        out_ref[i] = state_ref[i] * strength - added(3 + 3 * i)
    for core in range(CORES):

        @pl.when(lax.axis_index("core") == core)
        def _():
            out_ref[0:3, core * plan.own : (core + 1) * plan.own, :] += pair_ref[...]

    far_rows = 4 * plan.listed
    if plan.one_phase:
        heights = lax.axis_size("z")
        turn = jnp.where(lax.axis_index("core") == 0, heights - 1, 1)
        row = lax.axis_index("rep") * heights + lax.rem(lax.axis_index("z") + turn, heights)
        far = far_ref[row, 0:far_rows, plan.half :]
    else:
        far = far_ref[0, 0:far_rows, plan.half :]
    far_pushes(plan, pair_gain, lists_ref, state_ref, far, points_ref, out_ref, far_cs, far_rs)

    pieces = plan.half // plan.lanes
    core = lax.axis_index("core")
    here = lax.axis_index("z") * CORES
    out_ref[3] = jnp.zeros_like(out_ref[3])
    for n in range(pieces):
        keep = means[n, pl.ds(here + core, 1), :]
        give = means[n, pl.ds(here + 1 - core, 1), :]
        out_ref[3, n : n + 1, :] = keep
        out_ref[3, pieces + n : pieces + n + 1, :] = give


VMEM = pl.BlockSpec(memory_space=pltpu.VMEM)
SMEM = pl.BlockSpec(memory_space=pltpu.SMEM)
HBM = pl.BlockSpec(memory_space=pltpu.HBM)


def shape(*dims, dtype=f32):
    return jax.ShapeDtypeStruct(dims, dtype)


def with_types(scratch):
    for entry in scratch:
        if not isinstance(entry, tuple):
            yield entry
        else:
            dims, dtype = entry if isinstance(entry[0], tuple) else (entry, f32)
            yield pltpu.VMEM(dims, dtype)


def call(name, kernel, lists, args, outs, scratch=(), limit=12, spaces=None, out_spaces=None):
    many = isinstance(outs, (list, tuple))
    return pl.pallas_call(
        kernel,
        out_shape=tuple(outs) if many else outs,
        in_specs=[SMEM] * len(lists) + (spaces or [VMEM] * len(args)),
        out_specs=tuple(out_spaces or [VMEM] * len(outs)) if many else (out_spaces or VMEM),
        scratch_shapes=list(with_types(scratch)),
        compiler_params=pltpu.CompilerParams(vmem_limit_bytes=limit and limit << 20),
        name=name,
    )(*lists, *args)


class Plan:
    pass


def swap_cores(value):
    return lax.ppermute(value, "core", [(0, 1), (1, 0)])


def local(
    positions,
    velocities,
    charge,
    inverse_mass,
    pair_tiles,
    halo_tiles,
    owners,
    centres,
    widths,
    map_density,
    map_error,
    partner,
    decision,
):
    replicas = lax.axis_size("rep")
    heights = lax.axis_size("z")
    domains = heights * CORES
    own, owned = owners.shape
    plan = Plan()
    plan.own, plan.owned, plan.tiles, plan.domains = own, owned, own * CORES, domains
    plan.lanes = positions.shape[2] // own
    plan.near, plan.listed = pair_tiles.shape[1], halo_tiles.shape[2]
    components = widths.shape[0]
    half = plan.half = components // CORES
    tiles, lanes, listed = plan.tiles, plan.lanes, plan.listed

    args = [
        positions.transpose(1, 0, 2),
        velocities.transpose(1, 0, 2),
        charge[None],
        inverse_mass[None],
        centres,
        widths[None],
        map_density[None],
        map_error[None],
        owners,
        halo_tiles,
    ]
    int_rows = -(-(own + halo_tiles.shape[1]) // 8) * 8
    state_own, comp_send, ints = call(
        "pack",
        pack_kernel,
        [],
        args,
        [shape(8, own * lanes), shape(domains, 6, half), shape(int_rows, lanes, dtype=jnp.int32)],
        [(arg.shape, arg.dtype) for arg in args] + [pltpu.SemaphoreType.DMA((len(args),))],
        limit=None,
        spaces=[HBM] * len(args),
    )
    comps = lax.all_to_all(comp_send, ("z", "core"), 0, 0, tiled=True)
    width = -(-((tiles * owned + domains) // 2 + UNROLL + 1) // lanes) * lanes
    lists = call(
        "lists",
        functools.partial(list_kernel, plan),
        [ints, swap_cores(ints), pair_tiles],
        [],
        shape(4 + plan.near, width, dtype=jnp.int32),
        [pltpu.SMEM((domains,), jnp.int32)],
        out_spaces=SMEM,
    )
    if replicas <= 4:
        others = [
            lax.ppermute(state_own, "rep", [(r, r ^ n) for r in range(replicas)])
            for n in range(1, replicas)
        ]
    else:
        others = [
            lax.all_to_all(
                jnp.broadcast_to(state_own[None], (replicas,) + state_own.shape),
                "rep", 0, 0, tiled=True,
            )
        ]
    chosen = call(
        "choose",
        choose_kernel,
        [partner, decision],
        [state_own] + others,
        shape(8, own * lanes),
    )
    chosen_other = swap_cores(chosen)

    map_gain = map_scale / (owned * components)
    scale = 1.0 / (owned * own * lanes)
    pair_gain = (plan.near * lanes) ** (-0.5)
    group = replicas * heights
    plan.one_phase = group * domains * half * 4 <= ONE_PHASE_BYTES
    copies = group if plan.one_phase else 1
    rim_rows = -(-4 * listed // 8) * 8
    onward = [(2 * i, (2 * i + 2) % domains) for i in range(heights)]
    onward += [((2 * i + 3) % domains, 2 * i + 1) for i in range(heights)]
    padded = -(-(own + 2 * listed + 1) // 8) * 8
    outs = [
        shape(copies, max(domains, rim_rows), half + lanes),
        shape(8, tiles, lanes),
        shape(tiles + 1, DEPTH, lanes, dtype=bf16),
    ]
    scratch = [(tiles + 1, DEPTH, lanes), (domains, 8, half), (rim_rows, lanes),
               ((tiles + 1, lanes, DEPTH), bf16)]
    for step in range(STEPS):
        if step == 0:
            partial, state, points, right = call(
                "first",
                functools.partial(first_kernel, plan, scale),
                [lists],
                [chosen, chosen_other, comps],
                outs + [shape(domains, DEPTH, half, dtype=bf16)],
                scratch + [(domains, DEPTH, half)],
            )
            turned = call("turn", turn_kernel, [], [right], shape(domains, half, DEPTH, dtype=bf16))
        else:
            partial, state, points = call(
                "next",
                functools.partial(next_kernel, plan, scale),
                [lists],
                [state, force, swapped, right],
                outs,
                scratch,
            )
        if plan.one_phase:
            sums = far = lax.all_to_all(partial, ("rep", "z"), 0, 0, tiled=True)
        else:
            far = lax.ppermute(partial, ("z", "core"), onward)
            pieces = lax.all_to_all(
                partial[0, :domains, :half].reshape(group, -1), ("rep", "z"), 0, 0, tiled=True
            )
            piece = jnp.sum(pieces, 0)
            sums = lax.all_to_all(
                jnp.broadcast_to(piece[None], (group,) + piece.shape), ("rep", "z"), 0, 0, tiled=True
            ).reshape(1, domains, half)
        pair = call(
            "near",
            functools.partial(near_kernel, plan, pair_gain),
            [lists],
            [state, points],
            shape(3, own, lanes),
            [(4, padded, lanes), (padded, DEPTH, lanes), (padded, ROWS, lanes),
             ((padded, lanes, DEPTH), bf16)],
        )
        force = call(
            "push",
            functools.partial(push_kernel, plan, map_gain, pair_gain, float(replicas)),
            [lists],
            [state, comps, sums, far, pair, points, turned],
            shape(4, tiles, lanes),
            [(domains, ROWS, half), ((domains, ROWS, half), bf16), (half // lanes, domains, lanes),
             (tiles + 1, ROWS, lanes), (listed, DEPTH, lanes), (listed, ROWS, lanes)],
        )
        swapped = swap_cores(force)

    new_x, new_v, model_map = call(
        "finish",
        functools.partial(finish_kernel, plan),
        [],
        [state, force, swapped],
        [shape(3, 1, own * lanes), shape(3, 1, own * lanes), shape(1, components)],
        [(6, tiles, lanes)],
    )
    return (new_x.transpose(1, 0, 2), new_v.transpose(1, 0, 2), model_map.reshape(components))


def solution(mesh):
    replicas, domains = mesh.devices.shape
    split = Mesh(
        mesh.devices.reshape(replicas, domains // CORES, CORES), ("rep", "z", "core")
    )
    dom = ("z", "core")
    placed = (
        P("rep", None, dom),
        P("rep", None, dom),
        P(dom),
        P(dom),
        P(dom, None),
        P(dom, None, None),
        P(dom, None),
        P(None, dom),
        P(dom),
        P(dom),
        P(dom),
        P(),
        P(),
    )
    return jax.shard_map(
        local,
        mesh=split,
        in_specs=placed,
        out_specs=(P("rep", None, dom), P("rep", None, dom), P(dom)),
        check_vma=False,
    )
```

time: 106 us -> 96.7 us (0.912)
  blocking collectives: 13.1 us -> 0 us
  waiting for transfers between devices: 10.6 us -> 23.2 us
  Pallas kernels: 58.3 us -> 50.7 us
  local copies, waits for them, and re-layouts: 8.34 us -> 1.37 us
  starting transfers between devices: 14.1 us -> 20.3 us
    all_to_all x2, waiting for transfers between devices: 2.2 us -> 16.6 us  [local(): sums = far = lax.all_to_all(partial, ('rep', 'z'), 0, 0, tiled=True)]
    all_to_all x1 -> x0, blocking collectives: 13.1 us -> none  [local(): comps = lax.all_to_all(comp_send, ('z', 'core'), 0, 0, tiled=True)]
    pallas_call x8 -> x11, Pallas kernels: 58.3 us -> 50.7 us  [call(): pl.pallas_call(kernel, out_shape=tuple(outs) if many else outs, in_specs=...]
    unnamed x43 -> x11, local copies, waits for them, and re-layouts: 8.34 us -> 1.37 us
    all_to_all x1, waiting for transfers between devices: 4.26 us -> 0.01 us  [local(): comps = lax.all_to_all(comp_send, ('z', 'core'), 0, 0, tiled=True)]
    ppermute x0 -> x3, starting transfers between devices: none -> 3.55 us  [local(): lax.ppermute(state_own, 'rep', [(r, r ^ n) for r in range(replicas)])]
    ppermute x0 -> x3, waiting for transfers between devices: none -> 3.38 us  [local(): lax.ppermute(state_own, 'rep', [(r, r ^ n) for r in range(replicas)])]
    all_to_all x1, starting transfers between devices: 3.72 us -> 6.37 us  [local(): comps = lax.all_to_all(comp_send, ('z', 'core'), 0, 0, tiled=True)]
  transfers between devices with their start and end apart: 7 -> 10, of which waited for: 6 -> 8; matrix products, arithmetic and copies ran while one was open for 1% -> 0% of each run, Pallas kernels for 21% -> 12%
where the time goes in v3:
time: 96.7 us; the launch traced here: 96.3 us
  Pallas kernels  50.7 us (52%)
  waiting for transfers between devices  23.2 us (24%)
  starting transfers between devices  20.3 us (21%)
  local copies, waits for them, and re-layouts  1.37 us (1%)
    pallas_call x11, Pallas kernels, call(): pl.pallas_call(kernel, out_shape=tuple(outs) if many else outs, in_specs=...  50.7 us
    all_to_all x2, waiting for transfers between devices, local(): sums = far = lax.all_to_all(partial, ('rep', 'z'), 0, 0, tiled=True)  16.6 us
    all_to_all x2, starting transfers between devices, local(): sums = far = lax.all_to_all(partial, ('rep', 'z'), 0, 0, tiled=True)  9.67 us
    all_to_all x1, starting transfers between devices, local(): comps = lax.all_to_all(comp_send, ('z', 'core'), 0, 0, tiled=True)  6.37 us
    ppermute x3, starting transfers between devices, local(): lax.ppermute(state_own, 'rep', [(r, r ^ n) for r in range(replicas)])  3.55 us
    ppermute x3, waiting for transfers between devices, local(): lax.ppermute(state_own, 'rep', [(r, r ^ n) for r in range(replicas)])  3.38 us
    ppermute x4, waiting for transfers between devices, swap_cores(): return lax.ppermute(value, 'core', [(0, 1), (1, 0)])  3.22 us
  transfers between devices with their start and end apart: 10, of which 8 were waited for; matrix products, arithmetic and copies ran while one was open for 0% of the time, Pallas kernels for 12%

profile of v3, /device:TPU:0, one launch (start us, length us, event | category | flops | bytes accessed | tf_op | source)
XLA Modules:
  0.0 96.3 jit_solution(9216121206239711386)
XLA Ops:
  0.6 1.3 %copy.16.owners_hbm = s32[8,4]{1,0:T(8,128)} copy(s32[8,4]{0,1:T(4,128)} %param.19) | data formatting | bytes 256 | tf_op args[6]
  2.0 1.6 %pack.1 = (f32[8,1024]{1,0:T(8,128)}, f32[8,6,512]{2,1,0:T(8,128)}, s32[16,128]{1,0:T(8,128)}) custom-call(f32[3,1,1024]{2,1,0:T(1,128)} %bitcast.10, f32[3,1,1024]{2,1,0:T(1,128)} %bitcast.11, f32[1,1024]{1,0:T(1,128)} %bitcast.12, f32[1,1024]{1,0:T(1,128)} %bitcast.13, f32[3,1024]{1,0:T(4,128)} %centre_hbm.1, f32[1,1024]{1,0:T(1,128)} %bitcast.14, ...), custom_call_target="tpu_custom_call" | custom-call | tf_op jit(solution)/shard_map/pack/pallas_call | solution.py:438
  3.6 6.4 %all-to-all-start = ((f32[8,6,512]{2,1,0:T(8,128)}), f32[8,6,512]{2,1,0:T(8,128)S(1)}, u32[]{:S(2)}, u32[]{:S(2)}) async-start(f32[8,6,512]{2,1,0:T(8,128)} %get-tuple-element.18), calls=%async_computation | async-start | bytes 262144 | tf_op jit(solution)/shard_map/all_to_all | solution.py:507
  10.0 0.0 copy-start.4
  10.0 0.0 copy-start.1
  10.0 2.5 %collective-permute-start.3 = (f32[8,1024]{1,0:T(8,128)S(1)}, f32[8,1024]{1,0:T(8,128)S(1)}, u32[]{:S(2)}, u32[]{:S(2)}) collective-permute-start(f32[8,1024]{1,0:T(8,128)S(1)} %copy-done), channel_id=1, source_target_pairs={{0,24},{8,16},{16,8},{24,0},{1,25},{9,17},{17,9},{25,1},{2,26},{10... | collective-permute-start | bytes 98312 | tf_op jit(solution)/shard_map/ppermute | solution.py:520
  12.5 0.5 collective-permute-start.2
  13.0 0.5 collective-permute-start.1
  13.5 1.3 %collective-permute-done.3.refs_2_ = f32[8,1024]{1,0:T(8,128)S(1)} collective-permute-done((f32[8,1024]{1,0:T(8,128)S(1)}, f32[8,1024]{1,0:T(8,128)S(1)}, u32[]{:S(2)}, u32[]{:S(2)}) %collective-permute-start.3) | collective-permute-done | bytes 32800 | tf_op jit(solution)/shard_map/ppermute | solution.py:520
  14.9 1.5 %collective-permute-done.2.refs_1_ = f32[8,1024]{1,0:T(8,128)S(1)} collective-permute-done((f32[8,1024]{1,0:T(8,128)S(1)}, f32[8,1024]{1,0:T(8,128)S(1)}, u32[]{:S(2)}, u32[]{:S(2)}) %collective-permute-start.2) | collective-permute-done | bytes 32800 | tf_op jit(solution)/shard_map/ppermute | solution.py:520
  16.4 0.5 collective-permute-done.1.refs_0_
  16.9 0.6 choose.1.mine_ref
  17.5 0.1 collective-permute-start.4
  17.6 0.5 collective-permute-start
  18.1 0.8 collective-permute-done.theirs_ref
  18.9 2.3 %lists.1.lists_ref = s32[10,128]{1,0:T(8,128)S(1)} custom-call(s32[16,128]{1,0:T(8,128)S(1)} %copy-done.1, s32[16,128]{1,0:T(8,128)S(1)} %collective-permute-done.theirs_ref, s32[8,6]{1,0:T(8,128)S(1)} %copy-done.2), custom_call_target="tpu_custom_call" | custom-call | tf_op jit(solution)/shard_map/lists/pallas_call | solution.py:438
  21.3 6.9 %first.1 = (f32[16,8,640]{2,1,0:T(8,128)}, f32[8,16,128]{2,1,0:T(8,128)S(1)}, bf16[17,32,128]{2,1,0:T(8,128)(2,1)S(1)}, bf16[8,32,512]{2,1,0:T(8,128)(2,1)S(1)}) custom-call(s32[10,128]{1,0:T(8,128)S(1)} %lists.1.lists_ref, f32[8,1024]{1,0:T(8,128)S(1)} %choose.1.mine_ref, f32[8,1024]{1,0:T(8,128)S(1)} %collective-permute-done.4.theirs_ref, ...), custom_call_target="tpu_custom_call" | custom-call | tf_op jit(solution)/shard_map/first/pallas_call | solution.py:438
  28.2 6.1 %all-to-all-start.1 = ((f32[16,8,640]{2,1,0:T(8,128)}), f32[16,8,640]{2,1,0:T(8,128)S(1)}, u32[]{:S(2)}, u32[]{:S(2)}) async-start(f32[16,8,640]{2,1,0:T(8,128)} %get-tuple-element.20), calls=%async_computation.1 | async-start | bytes 655360 | tf_op jit(solution)/shard_map/all_to_all | solution.py:577
  34.3 0.3 turn.1.turned_ref
  34.6 4.0 %near.2.pair_ref = f32[3,8,128]{2,1,0:T(8,128)S(1)} custom-call(s32[10,128]{1,0:T(8,128)S(1)} %lists.1.lists_ref, f32[8,16,128]{2,1,0:T(8,128)S(1)} %get-tuple-element.19.state_ref.old_ref, bf16[17,32,128]{2,1,0:T(8,128)(2,1)S(1)} %get-tuple-element.21.points_ref), custom_call_target="tpu_custom_call" | custom-call | tf_op jit(solution)/shard_map/near/pallas_call | solution.py:438
  38.7 8.1 %all-to-all-done.1.sums_ref.far_ref = f32[16,8,640]{2,1,0:T(8,128)S(1)} async-done(((f32[16,8,640]{2,1,0:T(8,128)}), f32[16,8,640]{2,1,0:T(8,128)S(1)}, u32[]{:S(2)}, u32[]{:S(2)}) %all-to-all-start.1) | async-done | bytes 327712 | tf_op jit(solution)/shard_map/all_to_all | solution.py:577
  46.8 11.9 %push.2.force_ref = f32[4,16,128]{2,1,0:T(8,128)S(1)} custom-call(s32[10,128]{1,0:T(8,128)S(1)} %lists.1.lists_ref, f32[8,16,128]{2,1,0:T(8,128)S(1)} %get-tuple-element.19.state_ref.old_ref, f32[8,6,512]{2,1,0:T(8,128)S(1)} %all-to-all-done.comp_ref, f32[16,8,640]{2,1,0:T(8,128)S(1)} %all-to-all-done.1.sums_ref.far_ref, ...), custom_call_target="tpu_custom_call" | custom-call | tf_op jit(solution)/shard_map/push/pallas_call | solution.py:438
  58.7 0.1 collective-permute-start.5
  58.7 1.2 %collective-permute-done.5.swapped_ref = f32[4,16,128]{2,1,0:T(8,128)S(1)} collective-permute-done((f32[4,16,128]{2,1,0:T(8,128)S(1)}, f32[4,16,128]{2,1,0:T(8,128)S(1)}, u32[]{:S(2)}, u32[]{:S(2)}) %collective-permute-start.5) | collective-permute-done | bytes 32800 | tf_op jit(solution)/shard_map/ppermute | solution.py:454
  59.9 6.5 %next.1 = (f32[16,8,640]{2,1,0:T(8,128)}, f32[8,16,128]{2,1,0:T(8,128)S(1)}, bf16[17,32,128]{2,1,0:T(8,128)(2,1)S(1)}) custom-call(s32[10,128]{1,0:T(8,128)S(1)} %lists.1.lists_ref, f32[8,16,128]{2,1,0:T(8,128)S(1)} %get-tuple-element.19.state_ref.old_ref, f32[4,16,128]{2,1,0:T(8,128)S(1)} %push.2.force_ref, ...), custom_call_target="tpu_custom_call" | custom-call | tf_op jit(solution)/shard_map/next/pallas_call | solution.py:438
  66.5 3.5 %all-to-all-start.2 = ((f32[16,8,640]{2,1,0:T(8,128)}), f32[16,8,640]{2,1,0:T(8,128)S(1)}, u32[]{:S(2)}, u32[]{:S(2)}) async-start(f32[16,8,640]{2,1,0:T(8,128)} %get-tuple-element.24), calls=%async_computation.2 | async-start | bytes 655360 | tf_op jit(solution)/shard_map/all_to_all | solution.py:577
  70.0 4.0 %near.3.pair_ref = f32[3,8,128]{2,1,0:T(8,128)S(1)} custom-call(s32[10,128]{1,0:T(8,128)S(1)} %lists.1.lists_ref, f32[8,16,128]{2,1,0:T(8,128)S(1)} %get-tuple-element.23.state_ref.old_ref, bf16[17,32,128]{2,1,0:T(8,128)(2,1)S(1)} %get-tuple-element.25.points_ref), custom_call_target="tpu_custom_call" | custom-call | tf_op jit(solution)/shard_map/near/pallas_call | solution.py:438
  74.0 8.5 %all-to-all-done.2.sums_ref.far_ref = f32[16,8,640]{2,1,0:T(8,128)S(1)} async-done(((f32[16,8,640]{2,1,0:T(8,128)}), f32[16,8,640]{2,1,0:T(8,128)S(1)}, u32[]{:S(2)}, u32[]{:S(2)}) %all-to-all-start.2) | async-done | bytes 327712 | tf_op jit(solution)/shard_map/all_to_all | solution.py:577
  82.6 11.9 %push.3.mine_ref = f32[4,16,128]{2,1,0:T(8,128)S(1)} custom-call(s32[10,128]{1,0:T(8,128)S(1)} %lists.1.lists_ref, f32[8,16,128]{2,1,0:T(8,128)S(1)} %get-tuple-element.23.state_ref.old_ref, f32[8,6,512]{2,1,0:T(8,128)S(1)} %all-to-all-done.comp_ref, f32[16,8,640]{2,1,0:T(8,128)S(1)} %all-to-all-done.2.sums_ref.far_ref, ...), custom_call_target="tpu_custom_call" | custom-call | tf_op jit(solution)/shard_map/push/pallas_call | solution.py:438
  94.4 0.1 collective-permute-start.6
  94.5 1.2 %collective-permute-done.6.theirs_ref = f32[4,16,128]{2,1,0:T(8,128)S(1)} collective-permute-done((f32[4,16,128]{2,1,0:T(8,128)S(1)}, f32[4,16,128]{2,1,0:T(8,128)S(1)}, u32[]{:S(2)}, u32[]{:S(2)}) %collective-permute-start.6) | collective-permute-done | bytes 32800 | tf_op jit(solution)/shard_map/ppermute | solution.py:454
  95.7 0.6 finish.1
  (10 shorter events, 0.0 us)
Async XLA Ops:
  3.6 6.4 %copy-start = (f32[8,1024]{1,0:T(8,128)S(1)}, f32[8,1024]{1,0:T(8,128)}, u32[]{:S(2)}) copy-start(f32[8,1024]{1,0:T(8,128)} %get-tuple-element.17.mine_ref) | copy-start | bytes 98308
  3.6 17.7 %all-to-all-start = ((f32[8,6,512]{2,1,0:T(8,128)}), f32[8,6,512]{2,1,0:T(8,128)S(1)}, u32[]{:S(2)}, u32[]{:S(2)}) async-start(f32[8,6,512]{2,1,0:T(8,128)} %get-tuple-element.18), calls=%async_computation | async-start | bytes 262144 | tf_op jit(solution)/shard_map/all_to_all | solution.py:507
  10.0 7.0 %copy-start.3 = (s32[4]{0:T(128)S(1)}, s32[4]{0:T(128)}, u32[]{:S(2)}) copy-start(s32[4]{0:T(128)} %partner_ref.1) | copy-start | bytes 52
  10.0 7.0 %copy-start.4 = (s32[4]{0:T(128)S(1)}, s32[4]{0:T(128)}, u32[]{:S(2)}) copy-start(s32[4]{0:T(128)} %decision_ref.1) | copy-start | bytes 52
  10.0 7.6 %copy-start.1 = (s32[16,128]{1,0:T(8,128)S(1)}, s32[16,128]{1,0:T(8,128)}, u32[]{:S(2)}) copy-start(s32[16,128]{1,0:T(8,128)} %get-tuple-element.16.mine_ref) | copy-start | bytes 24580
  10.0 4.9 %collective-permute-start.3 = (f32[8,1024]{1,0:T(8,128)S(1)}, f32[8,1024]{1,0:T(8,128)S(1)}, u32[]{:S(2)}, u32[]{:S(2)}) collective-permute-start(f32[8,1024]{1,0:T(8,128)S(1)} %copy-done), channel_id=1, source_target_pairs={{0,24},{8,16},{16,8},{24,0},{1,25},{9,17},{17,9},{25,1},{2,26},{10... | collective-permute-start | bytes 98312 | tf_op jit(solution)/shard_map/ppermute | solution.py:520
  12.5 3.9 %collective-permute-start.2 = (f32[8,1024]{1,0:T(8,128)S(1)}, f32[8,1024]{1,0:T(8,128)S(1)}, u32[]{:S(2)}, u32[]{:S(2)}) collective-permute-start(f32[8,1024]{1,0:T(8,128)S(1)} %copy-done), channel_id=1, source_target_pairs={{0,16},{8,24},{16,0},{24,8},{1,17},{9,25},{17,1},{25,9},{2,18},{10... | collective-permute-start | bytes 98312 | tf_op jit(solution)/shard_map/ppermute | solution.py:520
  13.0 3.9 %collective-permute-start.1 = (f32[8,1024]{1,0:T(8,128)S(1)}, f32[8,1024]{1,0:T(8,128)S(1)}, u32[]{:S(2)}, u32[]{:S(2)}) collective-permute-start(f32[8,1024]{1,0:T(8,128)S(1)} %copy-done), channel_id=1, source_target_pairs={{0,8},{8,0},{16,24},{24,16},{1,9},{9,1},{17,25},{25,17},{2,10},{10... | collective-permute-start | bytes 98312 | tf_op jit(solution)/shard_map/ppermute | solution.py:520
  16.9 2.0 %copy-start.2 = (s32[8,6]{1,0:T(8,128)S(1)}, s32[8,6]{1,0:T(8,128)}, u32[]{:S(2)}) copy-start(s32[8,6]{1,0:T(8,128)} %pairs_ref.1) | copy-start | bytes 580
  17.5 3.8 %collective-permute-start.4 = (f32[8,1024]{1,0:T(8,128)S(1)}, f32[8,1024]{1,0:T(8,128)S(1)}, u32[]{:S(2)}, u32[]{:S(2)}) collective-permute-start(f32[8,1024]{1,0:T(8,128)S(1)} %choose.1.mine_ref), channel_id=1, source_target_pairs={{0,1},{1,0},{2,3},{3,2},{4,5},{5,4},{6,7},{7,6},{8,9},{9,8},{10,11... | collective-permute-start | bytes 98312 | tf_op jit(solution)/shard_map/ppermute | solution.py:454
  17.6 1.3 %collective-permute-start = (s32[16,128]{1,0:T(8,128)S(1)}, s32[16,128]{1,0:T(8,128)S(1)}, u32[]{:S(2)}, u32[]{:S(2)}) collective-permute-start(s32[16,128]{1,0:T(8,128)S(1)} %copy-done.1), channel_id=1, source_target_pairs={{0,1},{1,0},{2,3},{3,2},{4,5},{5,4},{6,7},{7,6},{8,9},{9,8},{10,11... | collective-permute-start | bytes 24584 | tf_op jit(solution)/shard_map/ppermute | solution.py:454
  28.2 18.6 %all-to-all-start.1 = ((f32[16,8,640]{2,1,0:T(8,128)}), f32[16,8,640]{2,1,0:T(8,128)S(1)}, u32[]{:S(2)}, u32[]{:S(2)}) async-start(f32[16,8,640]{2,1,0:T(8,128)} %get-tuple-element.20), calls=%async_computation.1 | async-start | bytes 655360 | tf_op jit(solution)/shard_map/all_to_all | solution.py:577
  58.7 1.3 %collective-permute-start.5 = (f32[4,16,128]{2,1,0:T(8,128)S(1)}, f32[4,16,128]{2,1,0:T(8,128)S(1)}, u32[]{:S(2)}, u32[]{:S(2)}) collective-permute-start(f32[4,16,128]{2,1,0:T(8,128)S(1)} %push.2.force_ref), channel_id=1, source_target_pairs={{0,1},{1,0},{2,3},{3,2},{4,5},{5,4},{6,7},{7,6},{8,9},{9,8},{10,11... | collective-permute-start | bytes 98312 | tf_op jit(solution)/shard_map/ppermute | solution.py:454
  66.5 16.1 %all-to-all-start.2 = ((f32[16,8,640]{2,1,0:T(8,128)}), f32[16,8,640]{2,1,0:T(8,128)S(1)}, u32[]{:S(2)}, u32[]{:S(2)}) async-start(f32[16,8,640]{2,1,0:T(8,128)} %get-tuple-element.24), calls=%async_computation.2 | async-start | bytes 655360 | tf_op jit(solution)/shard_map/all_to_all | solution.py:577
  94.4 1.3 %collective-permute-start.6 = (f32[4,16,128]{2,1,0:T(8,128)S(1)}, f32[4,16,128]{2,1,0:T(8,128)S(1)}, u32[]{:S(2)}, u32[]{:S(2)}) collective-permute-start(f32[4,16,128]{2,1,0:T(8,128)S(1)} %push.3.mine_ref), channel_id=1, source_target_pairs={{0,1},{1,0},{2,3},{3,2},{4,5},{5,4},{6,7},{7,6},{8,9},{9,8},{10,11... | collective-permute-start | bytes 98312 | tf_op jit(solution)/shard_map/ppermute | solution.py:454

commit v4 on v3

--- a/solution.py
+++ b/solution.py
@@ -12,7 +12,7 @@
 CORES = 2
 DEPTH = 32
 ROWS = 16
-ONE_PHASE_BYTES = 1 << 20
+CHUNK = 256
 UNROLL = 2
 FAR_SQUARE = 1048576.0
 
@@ -123,11 +123,11 @@
         state_ref[3 + i : 4 + i, :] = vel_ref[i]
     state_ref[6:7, :] = charge_ref[...]
     state_ref[7:8, :] = mass_ref[...]
-    own, owned = owners_ref.shape
+    owned, own = owners_ref.shape
     _, sides, listed = halo_ref.shape
     ints_ref[...] = jnp.zeros_like(ints_ref)
-    ints_ref[0:own, 0:owned] = owners_ref[...]
-    ints_ref[own : own + sides, 0:listed] = halo_ref[0]
+    ints_ref[0:owned, 0:own] = owners_ref[...]
+    ints_ref[owned : owned + sides, 0:listed] = halo_ref[0]
     for row in range(comp_ref.shape[0]):
         part = pl.ds((row % CORES) * half, half)
         comp_ref[row, 0:3, :] = centre_ref[:, part]
@@ -164,7 +164,7 @@
         row = lax.rem(tile, plan.own)
         here = lax.div(tile, plan.own) == core
         for j in range(plan.owned):
-            owner = jnp.where(here, mine_ref[row, j], theirs_ref[row, j])
+            owner = jnp.where(here, mine_ref[j, row], theirs_ref[j, row])
             first = waiting[owner]
             out_ref[0, count] = owner
             out_ref[1, count] = first
@@ -190,7 +190,7 @@
     out_ref[3, 0] = lax.div(count + UNROLL - 1, UNROLL)
     for side in range(2):
         for k in range(plan.listed):
-            out_ref[3, 1 + side * plan.listed + k] = theirs_ref[plan.own + side, k]
+            out_ref[3, 1 + side * plan.listed + k] = theirs_ref[plan.owned + side, k]
     for tile in range(plan.own):
         for j in range(plan.near):
             out_ref[4 + j, tile] = pairs_ref[tile, j]
@@ -205,42 +205,42 @@
     def step(n, carry):
         for u in range(UNROLL):
             place = n * UNROLL + u
-            body(lists_ref[0, place], lists_ref[1, place], lists_ref[2, place])
+            body(place, lists_ref[0, place], lists_ref[1, place], lists_ref[2, place])
         return carry
 
     lax.fori_loop(0, lists_ref[3, 0], step, 0)
 
 
-def sum_gaussians(plan, scale, lists_ref, state_ref, right_ref, points_ref, out_ref, xs, acc, rim, left):
-    tiles, listed = plan.tiles, plan.listed
+def sum_gaussians(plan, scale, lists_ref, state_ref, turned_ref, points_ref, out_ref, rim_ref, high_ref,
+                  low_ref, xs, acc):
+    tiles, listed, lanes = plan.tiles, plan.listed, plan.lanes
     store_rows(xs, point_rows([state_ref[i] for i in range(3)]))
     nowhere(xs, tiles)
-    for tile in range(tiles + 1):
-        points = xs[tile]
-        points_ref[tile] = points.astype(bf16)
-        left[tile] = points.T.astype(bf16)
+    points_ref[...] = xs[...].astype(bf16)
     core = lax.axis_index("core")
     for k in range(listed):
         tile = partner_tile(plan, lists_ref, 1 - core, k)
         for i, row in enumerate((0, 1, 2, 6)):
-            rim[i * listed + k : i * listed + k + 1, :] = state_ref[row, pl.ds(tile, 1), :]
+            rim_ref[i * listed + k : i * listed + k + 1, :] = state_ref[row, pl.ds(tile, 1), :]
     acc[...] = jnp.zeros_like(acc)
 
-    def one_pair(owner, first, second):
-        both = jnp.concatenate([left[first], left[second]], 0)
-        for start, size in chunks(right_ref.shape[2], 256):
-            g = jnp.exp2(dot(both, right_ref[owner, :, start : start + size]))
-            acc[owner, :, start : start + size] += jnp.sum(g.reshape(g.shape[0] // 8, 8, size), 0)
+    def one_pair(place, owner, first, second):
+        points = jnp.concatenate([points_ref[first], points_ref[second]], 1)
+        for start, size in chunks(plan.half, CHUNK):
+            part = slice(start, start + size)
+            g = jnp.exp2(dot(turned_ref[owner, part, :], points))
+            acc[owner, part, :] += g[:, :lanes] + g[:, lanes:]
+            high_ref[place, part, :], low_ref[place, part, :] = high_low(g)
 
     for_pairs(lists_ref, one_pair)
-    total = jnp.sum(acc[...], 1) * scale
-    for row in range(out_ref.shape[0]):
-        out_ref[row, 0 : acc.shape[0], 0 : plan.half] = total
-        out_ref[row, 0 : rim.shape[0], plan.half :] = rim[...]
+    for domain in range(plan.domains):
+        for start, size in chunks(plan.half, lanes):
+            total = jnp.sum(acc[domain, start : start + size, :].T, 0, keepdims=True)
+            out_ref[domain : domain + 1, start : start + size] = total * scale
 
 
 def first_kernel(plan, scale, lists_ref, mine_ref, theirs_ref, comp_ref,
-                 out_ref, state_ref, points_ref, right_ref, xs, acc, rim, left, cs):
+                 out_ref, rim_ref, state_ref, points_ref, high_ref, low_ref, turned_ref, xs, acc, cs):
     core = lax.axis_index("core")
     for tile in range(plan.own):
         lanes = slice(tile * plan.lanes, (tile + 1) * plan.lanes)
@@ -248,8 +248,13 @@
         state_ref[:, tile, :] = jnp.where(core == 0, mine, theirs)
         state_ref[:, plan.own + tile, :] = jnp.where(core == 0, theirs, mine)
     store_rows(cs, centre_rows([comp_ref[:, i, :] for i in range(3)], comp_ref[:, 3, :]))
-    right_ref[...] = cs[...].astype(bf16)
-    sum_gaussians(plan, scale, lists_ref, state_ref, right_ref, points_ref, out_ref, xs, acc, rim, left)
+    for domain in range(plan.domains):
+        for start, size in chunks(plan.half, 128):
+            turned_ref[domain, start : start + size, :] = cs[
+                domain, :, start : start + size
+            ].T.astype(bf16)
+    sum_gaussians(plan, scale, lists_ref, state_ref, turned_ref, points_ref, out_ref, rim_ref, high_ref,
+                  low_ref, xs, acc)
 
 
 def stepped(old_ref, mine_ref, theirs_ref):
@@ -259,14 +264,26 @@
         yield old_ref[i] + time_step * v, v
 
 
-def next_kernel(plan, scale, lists_ref, old_ref, force_ref, swapped_ref, right_ref,
-                out_ref, state_ref, points_ref, xs, acc, rim, left):
+def next_kernel(plan, scale, lists_ref, old_ref, force_ref, swapped_ref, turned_ref,
+                out_ref, rim_ref, state_ref, points_ref, high_ref, low_ref, xs, acc):
     for i, (x, v) in enumerate(stepped(old_ref, force_ref, swapped_ref)):
         state_ref[i] = x
         state_ref[3 + i] = v
     state_ref[6] = old_ref[6]
     state_ref[7] = old_ref[7]
-    sum_gaussians(plan, scale, lists_ref, state_ref, right_ref, points_ref, out_ref, xs, acc, rim, left)
+    sum_gaussians(plan, scale, lists_ref, state_ref, turned_ref, points_ref, out_ref, rim_ref, high_ref,
+                  low_ref, xs, acc)
+
+
+def tree_sum(refs):
+    values = [ref[...] for ref in refs]
+    while len(values) > 1:
+        values = [values[i] + values[i + 1] for i in range(0, len(values), 2)]
+    return values[0]
+
+
+def add_kernel(*refs):
+    refs[-1][...] = tree_sum(refs[:-1])
 
 
 def finish_kernel(plan, old_ref, mine_ref, theirs_ref, x_ref, v_ref, map_ref, state):
@@ -291,15 +308,8 @@
         map_ref[:, high] = jnp.where(first, got, keep)
 
 
-def turn_kernel(right_ref, turned_ref):
-    for domain in range(right_ref.shape[0]):
-        for start, size in chunks(right_ref.shape[2], 128):
-            turned_ref[domain, start : start + size, :] = (
-                right_ref[domain, :, start : start + size].astype(f32).T.astype(bf16)
-            )
-
-
-def near_kernel(plan, gain, lists_ref, state_ref, points_ref, out_ref, table, cs, rs, turned):
+def pair_kernel(plan, gain, lists_ref, state_ref, far_ref, points_ref, out_ref, table, cs, rs, rows,
+                turned):
     own, near, listed = plan.own, plan.near, plan.listed
     core = lax.axis_index("core")
     base = pl.multiple_of(core * own, own)
@@ -311,74 +321,46 @@
             table[i, pl.ds(own + (1 - core) * listed + k, 1), :] = state_ref[
                 source, pl.ds(partner_tile(plan, lists_ref, core, k), 1), :
             ]
+            table[i, pl.ds(own + core * listed + k, 1), :] = far_ref[
+                i * listed + k : i * listed + k + 1, :
+            ]
     coords = [table[i] for i in range(3)]
     store_rows(cs, centre_rows(coords, jnp.full_like(coords[0], pair_width)))
     store_rows(rs, pull_rows(coords, table[3]))
-    for entry in range(table.shape[1]):
+    rows[...] = rs[...].astype(bf16)
+    for entry in range(extent + 1):
         turned[entry] = cs[entry].T.astype(bf16)
     for tile in range(own):
         points = points_ref[base + tile]
-        sums = jnp.zeros((ROWS, plan.lanes), f32)
-        for j in range(near):
-            entry = lists_ref[4 + j, tile]
-            entry = jnp.where(entry < 0, extent, entry)
-            rows = rs[entry].astype(bf16)
-            high, low = high_low(jnp.exp2(dot(turned[entry], points)))
-            sums += dot(rows, high) + dot(rows, low)
+        entries = [lists_ref[4 + j, tile] for j in range(near)]
+        entries = [jnp.where(entry < 0, extent, entry) for entry in entries]
+        left = jnp.concatenate([turned[entry] for entry in entries], 0)
+        weights = jnp.concatenate([rows[entry] for entry in entries], 1)
+        high, low = high_low(jnp.exp2(dot(left, points)))
+        sums = dot(weights, high) + dot(weights, low)
         coords = [state_ref[i, pl.ds(base + tile, 1), :] for i in range(3)]
         strength = gain / pair_width * state_ref[6, pl.ds(base + tile, 1), :]
         for i, push in enumerate(squeeze_sums(coords, sums)):
             out_ref[i, tile : tile + 1, :] = strength * push
 
 
-def far_pushes(plan, gain, lists_ref, state_ref, far, points_ref, out_ref, cs, rs):
-    own, near, listed = plan.own, plan.near, plan.listed
-    core = lax.axis_index("core")
-    base = core * own
-    coords = [far[i * listed : (i + 1) * listed] for i in range(3)]
-    store_rows(cs, centre_rows(coords, jnp.full_like(coords[0], pair_width)))
-    store_rows(rs, pull_rows(coords, far[3 * listed : 4 * listed]))
-    turned = [cs[k].T.astype(bf16) for k in range(listed)]
-    for tile in range(own):
-        points = points_ref[base + tile]
-        sums = jnp.zeros((ROWS, plan.lanes), f32)
-        for k in range(listed):
-            entry = own + core * listed + k
-            named = lists_ref[4, tile] == entry
-            for j in range(1, near):
-                named = named | (lists_ref[4 + j, tile] == entry)
-            rows = (rs[k] * jnp.where(named, 1.0, 0.0)).astype(bf16)
-            high, low = high_low(jnp.exp2(dot(turned[k], points)))
-            sums += dot(rows, high) + dot(rows, low)
-        coords = [state_ref[i, pl.ds(base + tile, 1), :] for i in range(3)]
-        strength = gain / pair_width * state_ref[6, pl.ds(base + tile, 1), :]
-        for i, push in enumerate(squeeze_sums(coords, sums)):
-            out_ref[i, pl.ds(base + tile, 1), :] += strength * push
-
-
-def push_kernel(plan, gain, pair_gain, replicas, lists_ref, state_ref, comp_ref, sums_ref, far_ref,
-                pair_ref, points_ref, turned_ref, out_ref, rs, rows, means, sums, far_cs, far_rs):
-    domains, tiles = comp_ref.shape[0], plan.tiles
-    mean = jnp.sum(sums_ref[:, 0:domains, 0 : plan.half], 0) / replicas
-    for n in range(plan.half // plan.lanes):
-        means[n] = mean[:, n * plan.lanes : (n + 1) * plan.lanes]
+def push_kernel(plan, gain, replicas, lists_ref, state_ref, comp_ref, pair_ref, high_ref, low_ref, *refs):
+    parts, (out_ref, rs, rows, means, sums) = refs[:-5], refs[-5:]
+    tiles, lanes = plan.tiles, plan.lanes
+    mean = tree_sum(parts) / replicas
+    for n in range(plan.half // lanes):
+        means[n] = mean[:, n * lanes : (n + 1) * lanes]
     error = comp_ref[:, 5, :]
     coefficient = gain * (mean - comp_ref[:, 4, :]) / (error * error) / comp_ref[:, 3, :]
     store_rows(rs, pull_rows([comp_ref[:, i, :] for i in range(3)], coefficient))
     rows[...] = rs[...].astype(bf16)
     sums[...] = jnp.zeros_like(sums)
 
-    def one_pair(owner, first, second):
-        points = jnp.concatenate([points_ref[first], points_ref[second]], 1)
-        total = None
-        for start, size in chunks(plan.half, 256):
-            part = slice(start, start + size)
-            high, low = high_low(jnp.exp2(dot(turned_ref[owner, part, :], points)))
-            weights = rows[owner, :, part]
-            term = dot(weights, high) + dot(weights, low)
-            total = term if total is None else total + term
-        sums[first] += total[:, : plan.lanes]
-        sums[second] += total[:, plan.lanes :]
+    def one_pair(place, owner, first, second):
+        weights = rows[owner]
+        total = dot(weights, high_ref[place]) + dot(weights, low_ref[place])
+        sums[first] += total[:, :lanes]
+        sums[second] += total[:, lanes:]
 
     for_pairs(lists_ref, one_pair)
 
@@ -388,24 +370,12 @@
     strength = added(0)
     for i in range(3):
         out_ref[i] = state_ref[i] * strength - added(3 + 3 * i)
-    for core in range(CORES):
-
-        @pl.when(lax.axis_index("core") == core)
-        def _():
-            out_ref[0:3, core * plan.own : (core + 1) * plan.own, :] += pair_ref[...]
-
-    far_rows = 4 * plan.listed
-    if plan.one_phase:
-        heights = lax.axis_size("z")
-        turn = jnp.where(lax.axis_index("core") == 0, heights - 1, 1)
-        row = lax.axis_index("rep") * heights + lax.rem(lax.axis_index("z") + turn, heights)
-        far = far_ref[row, 0:far_rows, plan.half :]
-    else:
-        far = far_ref[0, 0:far_rows, plan.half :]
-    far_pushes(plan, pair_gain, lists_ref, state_ref, far, points_ref, out_ref, far_cs, far_rs)
-
-    pieces = plan.half // plan.lanes
     core = lax.axis_index("core")
+    own = pl.ds(pl.multiple_of(core * plan.own, plan.own), plan.own)
+    for i in range(3):
+        out_ref[i, own, :] += pair_ref[i]
+
+    pieces = plan.half // lanes
     here = lax.axis_index("z") * CORES
     out_ref[3] = jnp.zeros_like(out_ref[3])
     for n in range(pieces):
@@ -433,7 +403,7 @@
             yield pltpu.VMEM(dims, dtype)
 
 
-def call(name, kernel, lists, args, outs, scratch=(), limit=12, spaces=None, out_spaces=None):
+def call(name, kernel, lists, args, outs, scratch=(), limit=16, spaces=None, out_spaces=None):
     many = isinstance(outs, (list, tuple))
     return pl.pallas_call(
         kernel,
@@ -452,6 +422,13 @@
 
 def swap_cores(value):
     return lax.ppermute(value, "core", [(0, 1), (1, 0)])
+
+
+def exchange(value, axis):
+    count = lax.axis_size(axis)
+    return [
+        lax.ppermute(value, axis, [(i, i ^ n) for i in range(count)]) for n in range(1, count)
+    ]
 
 
 def local(
@@ -490,10 +467,10 @@
         widths[None],
         map_density[None],
         map_error[None],
-        owners,
+        owners.T,
         halo_tiles,
     ]
-    int_rows = -(-(own + halo_tiles.shape[1]) // 8) * 8
+    int_rows = -(-(owned + halo_tiles.shape[1]) // 8) * 8
     state_own, comp_send, ints = call(
         "pack",
         pack_kernel,
@@ -515,11 +492,9 @@
         [pltpu.SMEM((domains,), jnp.int32)],
         out_spaces=SMEM,
     )
-    if replicas <= 4:
-        others = [
-            lax.ppermute(state_own, "rep", [(r, r ^ n) for r in range(replicas)])
-            for n in range(1, replicas)
-        ]
+    small = replicas in (1, 2, 4) and heights in (1, 2, 4)
+    if small:
+        others = exchange(state_own, "rep")
     else:
         others = [
             lax.all_to_all(
@@ -540,67 +515,72 @@
     scale = 1.0 / (owned * own * lanes)
     pair_gain = (plan.near * lanes) ** (-0.5)
     group = replicas * heights
-    plan.one_phase = group * domains * half * 4 <= ONE_PHASE_BYTES
-    copies = group if plan.one_phase else 1
     rim_rows = -(-4 * listed // 8) * 8
     onward = [(2 * i, (2 * i + 2) % domains) for i in range(heights)]
     onward += [((2 * i + 3) % domains, 2 * i + 1) for i in range(heights)]
     padded = -(-(own + 2 * listed + 1) // 8) * 8
+    most = (tiles * owned + domains) // 2 + UNROLL
+    kept = shape(most, half, 2 * lanes, dtype=bf16)
     outs = [
-        shape(copies, max(domains, rim_rows), half + lanes),
+        shape(domains, half),
+        shape(rim_rows, lanes),
         shape(8, tiles, lanes),
         shape(tiles + 1, DEPTH, lanes, dtype=bf16),
+        kept,
+        kept,
     ]
-    scratch = [(tiles + 1, DEPTH, lanes), (domains, 8, half), (rim_rows, lanes),
-               ((tiles + 1, lanes, DEPTH), bf16)]
+    scratch = [(tiles + 1, DEPTH, lanes), (domains, half, lanes)]
     for step in range(STEPS):
         if step == 0:
-            partial, state, points, right = call(
+            partial, rim, state, points, high, low, turned = call(
                 "first",
                 functools.partial(first_kernel, plan, scale),
                 [lists],
                 [chosen, chosen_other, comps],
-                outs + [shape(domains, DEPTH, half, dtype=bf16)],
+                outs + [shape(domains, half, DEPTH, dtype=bf16)],
                 scratch + [(domains, DEPTH, half)],
             )
-            turned = call("turn", turn_kernel, [], [right], shape(domains, half, DEPTH, dtype=bf16))
         else:
-            partial, state, points = call(
+            partial, rim, state, points, high, low = call(
                 "next",
                 functools.partial(next_kernel, plan, scale),
                 [lists],
-                [state, force, swapped, right],
+                [state, force, swapped, turned],
                 outs,
                 scratch,
             )
-        if plan.one_phase:
-            sums = far = lax.all_to_all(partial, ("rep", "z"), 0, 0, tiled=True)
+        far = lax.ppermute(rim, ("z", "core"), onward)
+        if small:
+            partial = call(
+                "add", add_kernel, [], [partial] + exchange(partial, "rep"), shape(domains, half)
+            )
+            parts = [partial] + exchange(partial, "z")
         else:
-            far = lax.ppermute(partial, ("z", "core"), onward)
-            pieces = lax.all_to_all(
-                partial[0, :domains, :half].reshape(group, -1), ("rep", "z"), 0, 0, tiled=True
-            )
+            pieces = lax.all_to_all(partial.reshape(group, -1), ("rep", "z"), 0, 0, tiled=True)
             piece = jnp.sum(pieces, 0)
-            sums = lax.all_to_all(
-                jnp.broadcast_to(piece[None], (group,) + piece.shape), ("rep", "z"), 0, 0, tiled=True
-            ).reshape(1, domains, half)
+            parts = [
+                lax.all_to_all(
+                    jnp.broadcast_to(piece[None], (group,) + piece.shape),
+                    ("rep", "z"), 0, 0, tiled=True,
+                ).reshape(domains, half)
+            ]
         pair = call(
-            "near",
-            functools.partial(near_kernel, plan, pair_gain),
+            "pair",
+            functools.partial(pair_kernel, plan, pair_gain),
             [lists],
-            [state, points],
+            [state, far, points],
             shape(3, own, lanes),
             [(4, padded, lanes), (padded, DEPTH, lanes), (padded, ROWS, lanes),
-             ((padded, lanes, DEPTH), bf16)],
+             ((padded, ROWS, lanes), bf16), ((padded, lanes, DEPTH), bf16)],
         )
         force = call(
             "push",
-            functools.partial(push_kernel, plan, map_gain, pair_gain, float(replicas)),
+            functools.partial(push_kernel, plan, map_gain, float(replicas)),
             [lists],
-            [state, comps, sums, far, pair, points, turned],
+            [state, comps, pair, high, low] + parts,
             shape(4, tiles, lanes),
             [(domains, ROWS, half), ((domains, ROWS, half), bf16), (half // lanes, domains, lanes),
-             (tiles + 1, ROWS, lanes), (listed, DEPTH, lanes), (listed, ROWS, lanes)],
+             (tiles + 1, ROWS, lanes)],
         )
         swapped = swap_cores(force)
 

time: 96.7 us -> 90.8 us (0.939)
  Pallas kernels: 50.7 us -> 35.5 us
  starting transfers between devices: 20.3 us -> 28.1 us
  local copies, waits for them, and re-layouts: 1.37 us -> 3.44 us
  waiting for transfers between devices: 23.2 us -> 21.8 us
    ppermute x3 -> x17, starting transfers between devices: 3.55 us -> 21.1 us  [the longest x15 19.5 us: exchange(): lax.ppermute(value, axis, [(i, i ^ n) for i in range(count)])]
    all_to_all x2 -> x0, waiting for transfers between devices: 16.6 us -> none  [local(): sums = far = lax.all_to_all(partial, ('rep', 'z'), 0, 0, tiled=True)]
    pallas_call x11 -> x12, Pallas kernels: 50.7 us -> 35.5 us  [call(): pl.pallas_call(kernel, out_shape=tuple(outs) if many else outs, in_specs=...]
    ppermute x3 -> x17, waiting for transfers between devices: 3.38 us -> 18.4 us  [the longest x2 9.37 us: local(): far = lax.ppermute(rim, ('z', 'core'), onward)]
    all_to_all x2 -> x0, starting transfers between devices: 9.67 us -> none  [local(): sums = far = lax.all_to_all(partial, ('rep', 'z'), 0, 0, tiled=True)]
    unnamed x11 -> x10, local copies, waits for them, and re-layouts: 1.37 us -> 3.44 us
  transfers between devices with their start and end apart: 10 -> 22, of which waited for: 8 -> 14; matrix products, arithmetic and copies ran while one was open for 0% -> 0% of each run, Pallas kernels for 12% -> 8%
where the time goes in v4:
time: 90.8 us; the launch traced here: 89.7 us
  Pallas kernels  35.5 us (39%)
  starting transfers between devices  28.1 us (31%)
  waiting for transfers between devices  21.8 us (24%)
  local copies, waits for them, and re-layouts  3.44 us (4%)
    pallas_call x12, Pallas kernels, call(): pl.pallas_call(kernel, out_shape=tuple(outs) if many else outs, in_specs=...  35.5 us
    ppermute x15, starting transfers between devices, exchange(): lax.ppermute(value, axis, [(i, i ^ n) for i in range(count)])  19.5 us
    ppermute x2, waiting for transfers between devices, local(): far = lax.ppermute(rim, ('z', 'core'), onward)  9.37 us
    ppermute x15, waiting for transfers between devices, exchange(): lax.ppermute(value, axis, [(i, i ^ n) for i in range(count)])  9.04 us
    all_to_all x1, starting transfers between devices, local(): comps = lax.all_to_all(comp_send, ('z', 'core'), 0, 0, tiled=True)  6.37 us
    unnamed x10, local copies, waits for them, and re-layouts  3.44 us
    ppermute x4, waiting for transfers between devices, swap_cores(): return lax.ppermute(value, 'core', [(0, 1), (1, 0)])  3.42 us
  transfers between devices with their start and end apart: 22, of which 14 were waited for; matrix products, arithmetic and copies ran while one was open for 0% of the time, Pallas kernels for 8%

profile of v4, /device:TPU:0, one launch (start us, length us, event | category | flops | bytes accessed | tf_op | source)
XLA Modules:
  0.0 89.7 jit_solution(17498533543618885051)
XLA Ops:
  0.6 1.6 %pack.1 = (f32[8,1024]{1,0:T(8,128)}, f32[8,6,512]{2,1,0:T(8,128)}, s32[8,128]{1,0:T(8,128)}) custom-call(f32[3,1,1024]{2,1,0:T(1,128)} %bitcast.11, f32[3,1,1024]{2,1,0:T(1,128)} %bitcast.12, f32[1,1024]{1,0:T(1,128)} %bitcast.13, f32[1,1024]{1,0:T(1,128)} %bitcast.14, f32[3,1024]{1,0:T(4,128)} %centre_hbm.1, f32[1,1024]{1,0:T(1,128)} %bitcast.15, ...), custom_call_target="tpu_custom_call" | custom-call | tf_op jit(solution)/shard_map/pack/pallas_call | solution.py:408
  2.2 6.4 %all-to-all-start = ((f32[8,6,512]{2,1,0:T(8,128)}), f32[8,6,512]{2,1,0:T(8,128)S(1)}, u32[]{:S(2)}, u32[]{:S(2)}) async-start(f32[8,6,512]{2,1,0:T(8,128)} %get-tuple-element.24), calls=%async_computation | async-start | bytes 262144 | tf_op jit(solution)/shard_map/all_to_all | solution.py:484
  8.6 2.4 %collective-permute-start.3 = (f32[8,1024]{1,0:T(8,128)}, f32[8,1024]{1,0:T(8,128)S(1)}, u32[]{:S(2)}, u32[]{:S(2)}) collective-permute-start(f32[8,1024]{1,0:T(8,128)} %get-tuple-element.23.mine_ref), channel_id=1, source_target_pairs={{0,24},{8,16},{16,8},{24,0},{1,25},{9,17},{17,9},{25,1},{2,26},{10... | collective-permute-start | bytes 98312 | tf_op jit(solution)/shard_map/ppermute | solution.py:430
  12.1 1.5 %collective-permute-done.3.refs_2_ = f32[8,1024]{1,0:T(8,128)S(1)} collective-permute-done((f32[8,1024]{1,0:T(8,128)}, f32[8,1024]{1,0:T(8,128)S(1)}, u32[]{:S(2)}, u32[]{:S(2)}) %collective-permute-start.3) | collective-permute-done | bytes 32800 | tf_op jit(solution)/shard_map/ppermute | solution.py:430
  13.6 1.5 %collective-permute-done.2.refs_1_ = f32[8,1024]{1,0:T(8,128)S(1)} collective-permute-done((f32[8,1024]{1,0:T(8,128)}, f32[8,1024]{1,0:T(8,128)S(1)}, u32[]{:S(2)}, u32[]{:S(2)}) %collective-permute-start.2) | collective-permute-done | bytes 32800 | tf_op jit(solution)/shard_map/ppermute | solution.py:430
  15.7 0.8 copy-done
  16.4 0.7 copy-done.3
  17.1 0.7 copy-done.4
  18.9 1.0 %collective-permute-done.theirs_ref = s32[8,128]{1,0:T(8,128)S(1)} collective-permute-done((s32[8,128]{1,0:T(8,128)}, s32[8,128]{1,0:T(8,128)S(1)}, u32[]{:S(2)}, u32[]{:S(2)}) %collective-permute-start) | collective-permute-done | bytes 4128 | tf_op jit(solution)/shard_map/ppermute | solution.py:424
  19.9 0.7 copy-done.1
  20.6 0.7 copy-done.2
  21.3 2.2 %lists.1.lists_ref = s32[10,128]{1,0:T(8,128)S(1)} custom-call(s32[8,128]{1,0:T(8,128)S(1)} %copy-done.2, s32[8,128]{1,0:T(8,128)S(1)} %collective-permute-done.theirs_ref, s32[8,6]{1,0:T(8,128)S(1)} %copy-done.1), custom_call_target="tpu_custom_call" | custom-call | tf_op jit(solution)/shard_map/lists/pallas_call | solution.py:408
  23.5 8.4 %first.1 = (f32[8,512]{1,0:T(8,128)S(1)}, f32[8,128]{1,0:T(8,128)S(1)}, f32[8,16,128]{2,1,0:T(8,128)S(1)}, bf16[17,32,128]{2,1,0:T(8,128)(2,1)S(1)}, bf16[38,512...) custom-call(s32[10,128]{1,0:T(8,128)S(1)} %lists.1.lists_ref, ...), custom_call_target="tpu_custom_call" | custom-call | tf_op jit(solution)/shard_map/first/pallas_call | solution.py:408
  31.9 1.5 %collective-permute-start.8 = (f32[8,512]{1,0:T(8,128)S(1)}, f32[8,512]{1,0:T(8,128)S(1)}, u32[]{:S(2)}, u32[]{:S(2)}) collective-permute-start(f32[8,512]{1,0:T(8,128)S(1)} %get-tuple-element.30.refs_0_), channel_id=1, source_target_pairs={{0,24},{8,16},{16,8},{24,0},{1,25},{9,17},{17,9},{25,1},{2,26},{10... | collective-permute-start | bytes 49160 | tf_op jit(solution)/shard_map/ppermute | solution.py:430
  34.0 1.5 %collective-permute-start.6 = (f32[8,512]{1,0:T(8,128)S(1)}, f32[8,512]{1,0:T(8,128)S(1)}, u32[]{:S(2)}, u32[]{:S(2)}) collective-permute-start(f32[8,512]{1,0:T(8,128)S(1)} %get-tuple-element.30.refs_0_), channel_id=1, source_target_pairs={{0,8},{8,0},{16,24},{24,16},{1,9},{9,1},{17,25},{25,17},{2,10},{10... | collective-permute-start | bytes 49160 | tf_op jit(solution)/shard_map/ppermute | solution.py:430
  35.5 1.1 %collective-permute-done.8.refs_3_ = f32[8,512]{1,0:T(8,128)S(1)} collective-permute-done((f32[8,512]{1,0:T(8,128)S(1)}, f32[8,512]{1,0:T(8,128)S(1)}, u32[]{:S(2)}, u32[]{:S(2)}) %collective-permute-start.8) | collective-permute-done | bytes 16416 | tf_op jit(solution)/shard_map/ppermute | solution.py:430
  37.7 3.8 %collective-permute-start.11 = (f32[8,512]{1,0:T(8,128)S(1)}, f32[8,512]{1,0:T(8,128)S(1)}, u32[]{:S(2)}, u32[]{:S(2)}) collective-permute-start(f32[8,512]{1,0:T(8,128)S(1)} %add.2.refs_0_), channel_id=1, source_target_pairs={{0,6},{2,4},{4,2},{6,0},{1,7},{3,5},{5,3},{7,1},{8,14},{10,12},{12... | collective-permute-start | bytes 49160 | tf_op jit(solution)/shard_map/ppermute | solution.py:430
  42.2 1.5 %collective-permute-start.5 = (f32[8,128]{1,0:T(8,128)S(1)}, f32[8,128]{1,0:T(8,128)S(1)}, u32[]{:S(2)}, u32[]{:S(2)}) collective-permute-start(f32[8,128]{1,0:T(8,128)S(1)} %get-tuple-element.26), channel_id=1, source_target_pairs={{0,2},{2,4},{4,6},{6,0},{3,1},{5,3},{7,5},{1,7},{8,10},{10,12},{12... | collective-permute-start | bytes 12296 | tf_op jit(solution)/shard_map/ppermute | solution.py:552
  43.7 4.0 %collective-permute-done.5.far_ref = f32[8,128]{1,0:T(8,128)S(1)} collective-permute-done((f32[8,128]{1,0:T(8,128)S(1)}, f32[8,128]{1,0:T(8,128)S(1)}, u32[]{:S(2)}, u32[]{:S(2)}) %collective-permute-start.5) | collective-permute-done | bytes 4128 | tf_op jit(solution)/shard_map/ppermute | solution.py:552
  47.7 2.1 %pair.2.pair_ref = f32[3,8,128]{2,1,0:T(8,128)S(1)} custom-call(s32[10,128]{1,0:T(8,128)S(1)} %lists.1.lists_ref, f32[8,16,128]{2,1,0:T(8,128)S(1)} %get-tuple-element.25.state_ref.old_ref, f32[8,128]{1,0:T(8,128)S(1)} %collective-permute-done.5.far_ref, bf16[17,32,128]{2,1,0:T(8,128)(2,1)S(1)} %get-tuple-element.27.points_ref), custom_call_target="tpu_custom_call" | custom-call | tf_op jit(solution)/shard_map/pair/pallas_call | solution.py:408
  49.9 5.0 %push.2.force_ref = f32[4,16,128]{2,1,0:T(8,128)S(1)} custom-call(s32[10,128]{1,0:T(8,128)S(1)} %lists.1.lists_ref, f32[8,16,128]{2,1,0:T(8,128)S(1)} %get-tuple-element.25.state_ref.old_ref, f32[8,6,512]{2,1,0:T(8,128)S(1)} %all-to-all-done.comp_ref, f32[3,8,128]{2,1,0:T(8,128)S(1)} %pair.2.pair_ref, bf16[38,512,256]{2,1,0:T(8,128)(2,1)S(1)} %get-tuple-element.28.high_ref, ...), custom_call_target="tpu_custom_call" | custom-call | tf_op jit(solution)/shard_map/push/pallas_call | solution.py:408
  54.9 1.2 %collective-permute-done.12.swapped_ref = f32[4,16,128]{2,1,0:T(8,128)S(1)} collective-permute-done((f32[4,16,128]{2,1,0:T(8,128)S(1)}, f32[4,16,128]{2,1,0:T(8,128)S(1)}, u32[]{:S(2)}, u32[]{:S(2)}) %collective-permute-start.12) | collective-permute-done | bytes 32800 | tf_op jit(solution)/shard_map/ppermute | solution.py:424
  56.1 7.9 %next.1 = (f32[8,512]{1,0:T(8,128)S(1)}, f32[8,128]{1,0:T(8,128)S(1)}, f32[8,16,128]{2,1,0:T(8,128)S(1)}, bf16[17,32,128]{2,1,0:T(8,128)(2,1)S(1)}, bf16[38,512,...) custom-call(s32[10,128]{1,0:T(8,128)S(1)} %lists.1.lists_ref, ...), custom_call_target="tpu_custom_call" | custom-call | tf_op jit(solution)/shard_map/next/pallas_call | solution.py:408
  64.0 2.6 %collective-permute-start.16 = (f32[8,512]{1,0:T(8,128)S(1)}, f32[8,512]{1,0:T(8,128)S(1)}, u32[]{:S(2)}, u32[]{:S(2)}) collective-permute-start(f32[8,512]{1,0:T(8,128)S(1)} %get-tuple-element.37.refs_0_), channel_id=1, source_target_pairs={{0,24},{8,16},{16,8},{24,0},{1,25},{9,17},{17,9},{25,1},{2,26},{10... | collective-permute-start | bytes 49160 | tf_op jit(solution)/shard_map/ppermute | solution.py:430
  67.6 1.1 %collective-permute-done.16.refs_3_ = f32[8,512]{1,0:T(8,128)S(1)} collective-permute-done((f32[8,512]{1,0:T(8,128)S(1)}, f32[8,512]{1,0:T(8,128)S(1)}, u32[]{:S(2)}, u32[]{:S(2)}) %collective-permute-start.16) | collective-permute-done | bytes 16416 | tf_op jit(solution)/shard_map/ppermute | solution.py:430
  68.7 1.6 %collective-permute-done.15.refs_2_ = f32[8,512]{1,0:T(8,128)S(1)} collective-permute-done((f32[8,512]{1,0:T(8,128)S(1)}, f32[8,512]{1,0:T(8,128)S(1)}, u32[]{:S(2)}, u32[]{:S(2)}) %collective-permute-start.15) | collective-permute-done | bytes 16416 | tf_op jit(solution)/shard_map/ppermute | solution.py:430
  70.8 1.9 %collective-permute-start.19 = (f32[8,512]{1,0:T(8,128)S(1)}, f32[8,512]{1,0:T(8,128)S(1)}, u32[]{:S(2)}, u32[]{:S(2)}) collective-permute-start(f32[8,512]{1,0:T(8,128)S(1)} %add.3.refs_0_), channel_id=1, source_target_pairs={{0,6},{2,4},{4,2},{6,0},{1,7},{3,5},{5,3},{7,1},{8,14},{10,12},{12... | collective-permute-start | bytes 49160 | tf_op jit(solution)/shard_map/ppermute | solution.py:430
  72.7 2.5 %collective-permute-start.17 = (f32[8,512]{1,0:T(8,128)S(1)}, f32[8,512]{1,0:T(8,128)S(1)}, u32[]{:S(2)}, u32[]{:S(2)}) collective-permute-start(f32[8,512]{1,0:T(8,128)S(1)} %add.3.refs_0_), channel_id=1, source_target_pairs={{0,2},{2,0},{4,6},{6,4},{1,3},{3,1},{5,7},{7,5},{8,10},{10,8},{12,... | collective-permute-start | bytes 49160 | tf_op jit(solution)/shard_map/ppermute | solution.py:430
  75.3 5.4 %collective-permute-done.13.far_ref = f32[8,128]{1,0:T(8,128)S(1)} collective-permute-done((f32[8,128]{1,0:T(8,128)S(1)}, f32[8,128]{1,0:T(8,128)S(1)}, u32[]{:S(2)}, u32[]{:S(2)}) %collective-permute-start.13) | collective-permute-done | bytes 4128 | tf_op jit(solution)/shard_map/ppermute | solution.py:552
  80.6 2.1 %pair.3.pair_ref = f32[3,8,128]{2,1,0:T(8,128)S(1)} custom-call(s32[10,128]{1,0:T(8,128)S(1)} %lists.1.lists_ref, f32[8,16,128]{2,1,0:T(8,128)S(1)} %get-tuple-element.32.state_ref.old_ref, f32[8,128]{1,0:T(8,128)S(1)} %collective-permute-done.13.far_ref, bf16[17,32,128]{2,1,0:T(8,128)(2,1)S(1)} %get-tuple-element.34.points_ref), custom_call_target="tpu_custom_call" | custom-call | tf_op jit(solution)/shard_map/pair/pallas_call | solution.py:408
  82.8 5.0 %push.3.mine_ref = f32[4,16,128]{2,1,0:T(8,128)S(1)} custom-call(s32[10,128]{1,0:T(8,128)S(1)} %lists.1.lists_ref, f32[8,16,128]{2,1,0:T(8,128)S(1)} %get-tuple-element.32.state_ref.old_ref, f32[8,6,512]{2,1,0:T(8,128)S(1)} %all-to-all-done.comp_ref, f32[3,8,128]{2,1,0:T(8,128)S(1)} %pair.3.pair_ref, bf16[38,512,256]{2,1,0:T(8,128)(2,1)S(1)} %get-tuple-element.35.high_ref, ...), custom_call_target="tpu_custom_call" | custom-call | tf_op jit(solution)/shard_map/push/pallas_call | solution.py:408
  87.9 1.2 %collective-permute-done.20.theirs_ref = f32[4,16,128]{2,1,0:T(8,128)S(1)} collective-permute-done((f32[4,16,128]{2,1,0:T(8,128)S(1)}, f32[4,16,128]{2,1,0:T(8,128)S(1)}, u32[]{:S(2)}, u32[]{:S(2)}) %collective-permute-start.20) | collective-permute-done | bytes 32800 | tf_op jit(solution)/shard_map/ppermute | solution.py:424
  (34 shorter events, 7.2 us)
Async XLA Ops:
  2.2 21.3 %all-to-all-start = ((f32[8,6,512]{2,1,0:T(8,128)}), f32[8,6,512]{2,1,0:T(8,128)S(1)}, u32[]{:S(2)}, u32[]{:S(2)}) async-start(f32[8,6,512]{2,1,0:T(8,128)} %get-tuple-element.24), calls=%async_computation | async-start | bytes 262144 | tf_op jit(solution)/shard_map/all_to_all | solution.py:484
  8.6 5.0 %collective-permute-start.3 = (f32[8,1024]{1,0:T(8,128)}, f32[8,1024]{1,0:T(8,128)S(1)}, u32[]{:S(2)}, u32[]{:S(2)}) collective-permute-start(f32[8,1024]{1,0:T(8,128)} %get-tuple-element.23.mine_ref), channel_id=1, source_target_pairs={{0,24},{8,16},{16,8},{24,0},{1,25},{9,17},{17,9},{25,1},{2,26},{10... | collective-permute-start | bytes 98312 | tf_op jit(solution)/shard_map/ppermute | solution.py:430
  11.1 4.1 %collective-permute-start.2 = (f32[8,1024]{1,0:T(8,128)}, f32[8,1024]{1,0:T(8,128)S(1)}, u32[]{:S(2)}, u32[]{:S(2)}) collective-permute-start(f32[8,1024]{1,0:T(8,128)} %get-tuple-element.23.mine_ref), channel_id=1, source_target_pairs={{0,16},{8,24},{16,0},{24,8},{1,17},{9,25},{17,1},{25,9},{2,18},{10... | collective-permute-start | bytes 98312 | tf_op jit(solution)/shard_map/ppermute | solution.py:430
  11.6 4.1 %collective-permute-start.1 = (f32[8,1024]{1,0:T(8,128)}, f32[8,1024]{1,0:T(8,128)S(1)}, u32[]{:S(2)}, u32[]{:S(2)}) collective-permute-start(f32[8,1024]{1,0:T(8,128)} %get-tuple-element.23.mine_ref), channel_id=1, source_target_pairs={{0,8},{8,0},{16,24},{24,16},{1,9},{9,1},{17,25},{25,17},{2,10},{10... | collective-permute-start | bytes 98312 | tf_op jit(solution)/shard_map/ppermute | solution.py:430
  15.7 0.8 copy-start
  16.4 0.7 copy-start.3
  17.1 0.7 copy-start.4
  18.3 5.2 %collective-permute-start.4 = (f32[8,1024]{1,0:T(8,128)S(1)}, f32[8,1024]{1,0:T(8,128)S(1)}, u32[]{:S(2)}, u32[]{:S(2)}) collective-permute-start(f32[8,1024]{1,0:T(8,128)S(1)} %choose.1.mine_ref), channel_id=1, source_target_pairs={{0,1},{1,0},{2,3},{3,2},{4,5},{5,4},{6,7},{7,6},{8,9},{9,8},{10,11... | collective-permute-start | bytes 98312 | tf_op jit(solution)/shard_map/ppermute | solution.py:424
  18.4 1.5 %collective-permute-start = (s32[8,128]{1,0:T(8,128)}, s32[8,128]{1,0:T(8,128)S(1)}, u32[]{:S(2)}, u32[]{:S(2)}) collective-permute-start(s32[8,128]{1,0:T(8,128)} %get-tuple-element.22.mine_ref), channel_id=1, source_target_pairs={{0,1},{1,0},{2,3},{3,2},{4,5},{5,4},{6,7},{7,6},{8,9},{9,8},{10,11... | collective-permute-start | bytes 12296 | tf_op jit(solution)/shard_map/ppermute | solution.py:424
  19.9 0.7 copy-start.1
  20.6 0.7 copy-start.2
  31.9 4.7 %collective-permute-start.8 = (f32[8,512]{1,0:T(8,128)S(1)}, f32[8,512]{1,0:T(8,128)S(1)}, u32[]{:S(2)}, u32[]{:S(2)}) collective-permute-start(f32[8,512]{1,0:T(8,128)S(1)} %get-tuple-element.30.refs_0_), channel_id=1, source_target_pairs={{0,24},{8,16},{16,8},{24,0},{1,25},{9,17},{17,9},{25,1},{2,26},{10... | collective-permute-start | bytes 49160 | tf_op jit(solution)/shard_map/ppermute | solution.py:430
  33.4 3.7 %collective-permute-start.7 = (f32[8,512]{1,0:T(8,128)S(1)}, f32[8,512]{1,0:T(8,128)S(1)}, u32[]{:S(2)}, u32[]{:S(2)}) collective-permute-start(f32[8,512]{1,0:T(8,128)S(1)} %get-tuple-element.30.refs_0_), channel_id=1, source_target_pairs={{0,16},{8,24},{16,0},{24,8},{1,17},{9,25},{17,1},{25,9},{2,18},{10... | collective-permute-start | bytes 49160 | tf_op jit(solution)/shard_map/ppermute | solution.py:430
  34.0 3.7 %collective-permute-start.6 = (f32[8,512]{1,0:T(8,128)S(1)}, f32[8,512]{1,0:T(8,128)S(1)}, u32[]{:S(2)}, u32[]{:S(2)}) collective-permute-start(f32[8,512]{1,0:T(8,128)S(1)} %get-tuple-element.30.refs_0_), channel_id=1, source_target_pairs={{0,8},{8,0},{16,24},{24,16},{1,9},{9,1},{17,25},{25,17},{2,10},{10... | collective-permute-start | bytes 49160 | tf_op jit(solution)/shard_map/ppermute | solution.py:430
  37.7 12.1 %collective-permute-start.11 = (f32[8,512]{1,0:T(8,128)S(1)}, f32[8,512]{1,0:T(8,128)S(1)}, u32[]{:S(2)}, u32[]{:S(2)}) collective-permute-start(f32[8,512]{1,0:T(8,128)S(1)} %add.2.refs_0_), channel_id=1, source_target_pairs={{0,6},{2,4},{4,2},{6,0},{1,7},{3,5},{5,3},{7,1},{8,14},{10,12},{12... | collective-permute-start | bytes 49160 | tf_op jit(solution)/shard_map/ppermute | solution.py:430
  41.5 8.3 %collective-permute-start.10 = (f32[8,512]{1,0:T(8,128)S(1)}, f32[8,512]{1,0:T(8,128)S(1)}, u32[]{:S(2)}, u32[]{:S(2)}) collective-permute-start(f32[8,512]{1,0:T(8,128)S(1)} %add.2.refs_0_), channel_id=1, source_target_pairs={{0,4},{2,6},{4,0},{6,2},{1,5},{3,7},{5,1},{7,3},{8,12},{10,14},{12... | collective-permute-start | bytes 49160 | tf_op jit(solution)/shard_map/ppermute | solution.py:430
  41.7 8.2 %collective-permute-start.9 = (f32[8,512]{1,0:T(8,128)S(1)}, f32[8,512]{1,0:T(8,128)S(1)}, u32[]{:S(2)}, u32[]{:S(2)}) collective-permute-start(f32[8,512]{1,0:T(8,128)S(1)} %add.2.refs_0_), channel_id=1, source_target_pairs={{0,2},{2,0},{4,6},{6,4},{1,3},{3,1},{5,7},{7,5},{8,10},{10,8},{12,... | collective-permute-start | bytes 49160 | tf_op jit(solution)/shard_map/ppermute | solution.py:430
  42.2 5.5 %collective-permute-start.5 = (f32[8,128]{1,0:T(8,128)S(1)}, f32[8,128]{1,0:T(8,128)S(1)}, u32[]{:S(2)}, u32[]{:S(2)}) collective-permute-start(f32[8,128]{1,0:T(8,128)S(1)} %get-tuple-element.26), channel_id=1, source_target_pairs={{0,2},{2,4},{4,6},{6,0},{3,1},{5,3},{7,5},{1,7},{8,10},{10,12},{12... | collective-permute-start | bytes 12296 | tf_op jit(solution)/shard_map/ppermute | solution.py:552
  54.9 1.3 %collective-permute-start.12 = (f32[4,16,128]{2,1,0:T(8,128)S(1)}, f32[4,16,128]{2,1,0:T(8,128)S(1)}, u32[]{:S(2)}, u32[]{:S(2)}) collective-permute-start(f32[4,16,128]{2,1,0:T(8,128)S(1)} %push.2.force_ref), channel_id=1, source_target_pairs={{0,1},{1,0},{2,3},{3,2},{4,5},{5,4},{6,7},{7,6},{8,9},{9,8},{10,11... | collective-permute-start | bytes 98312 | tf_op jit(solution)/shard_map/ppermute | solution.py:424
  64.0 4.7 %collective-permute-start.16 = (f32[8,512]{1,0:T(8,128)S(1)}, f32[8,512]{1,0:T(8,128)S(1)}, u32[]{:S(2)}, u32[]{:S(2)}) collective-permute-start(f32[8,512]{1,0:T(8,128)S(1)} %get-tuple-element.37.refs_0_), channel_id=1, source_target_pairs={{0,24},{8,16},{16,8},{24,0},{1,25},{9,17},{17,9},{25,1},{2,26},{10... | collective-permute-start | bytes 49160 | tf_op jit(solution)/shard_map/ppermute | solution.py:430
  66.6 3.7 %collective-permute-start.15 = (f32[8,512]{1,0:T(8,128)S(1)}, f32[8,512]{1,0:T(8,128)S(1)}, u32[]{:S(2)}, u32[]{:S(2)}) collective-permute-start(f32[8,512]{1,0:T(8,128)S(1)} %get-tuple-element.37.refs_0_), channel_id=1, source_target_pairs={{0,16},{8,24},{16,0},{24,8},{1,17},{9,25},{17,1},{25,9},{2,18},{10... | collective-permute-start | bytes 49160 | tf_op jit(solution)/shard_map/ppermute | solution.py:430
  67.0 3.7 %collective-permute-start.14 = (f32[8,512]{1,0:T(8,128)S(1)}, f32[8,512]{1,0:T(8,128)S(1)}, u32[]{:S(2)}, u32[]{:S(2)}) collective-permute-start(f32[8,512]{1,0:T(8,128)S(1)} %get-tuple-element.37.refs_0_), channel_id=1, source_target_pairs={{0,8},{8,0},{16,24},{24,16},{1,9},{9,1},{17,25},{25,17},{2,10},{10... | collective-permute-start | bytes 49160 | tf_op jit(solution)/shard_map/ppermute | solution.py:430
  70.8 12.0 %collective-permute-start.19 = (f32[8,512]{1,0:T(8,128)S(1)}, f32[8,512]{1,0:T(8,128)S(1)}, u32[]{:S(2)}, u32[]{:S(2)}) collective-permute-start(f32[8,512]{1,0:T(8,128)S(1)} %add.3.refs_0_), channel_id=1, source_target_pairs={{0,6},{2,4},{4,2},{6,0},{1,7},{3,5},{5,3},{7,1},{8,14},{10,12},{12... | collective-permute-start | bytes 49160 | tf_op jit(solution)/shard_map/ppermute | solution.py:430
  72.7 10.1 %collective-permute-start.18 = (f32[8,512]{1,0:T(8,128)S(1)}, f32[8,512]{1,0:T(8,128)S(1)}, u32[]{:S(2)}, u32[]{:S(2)}) collective-permute-start(f32[8,512]{1,0:T(8,128)S(1)} %add.3.refs_0_), channel_id=1, source_target_pairs={{0,4},{2,6},{4,0},{6,2},{1,5},{3,7},{5,1},{7,3},{8,12},{10,14},{12... | collective-permute-start | bytes 49160 | tf_op jit(solution)/shard_map/ppermute | solution.py:430
  72.7 10.1 %collective-permute-start.17 = (f32[8,512]{1,0:T(8,128)S(1)}, f32[8,512]{1,0:T(8,128)S(1)}, u32[]{:S(2)}, u32[]{:S(2)}) collective-permute-start(f32[8,512]{1,0:T(8,128)S(1)} %add.3.refs_0_), channel_id=1, source_target_pairs={{0,2},{2,0},{4,6},{6,4},{1,3},{3,1},{5,7},{7,5},{8,10},{10,8},{12,... | collective-permute-start | bytes 49160 | tf_op jit(solution)/shard_map/ppermute | solution.py:430
  75.2 5.4 %collective-permute-start.13 = (f32[8,128]{1,0:T(8,128)S(1)}, f32[8,128]{1,0:T(8,128)S(1)}, u32[]{:S(2)}, u32[]{:S(2)}) collective-permute-start(f32[8,128]{1,0:T(8,128)S(1)} %get-tuple-element.33), channel_id=1, source_target_pairs={{0,2},{2,4},{4,6},{6,0},{3,1},{5,3},{7,5},{1,7},{8,10},{10,12},{12... | collective-permute-start | bytes 12296 | tf_op jit(solution)/shard_map/ppermute | solution.py:552
  87.8 1.3 %collective-permute-start.20 = (f32[4,16,128]{2,1,0:T(8,128)S(1)}, f32[4,16,128]{2,1,0:T(8,128)S(1)}, u32[]{:S(2)}, u32[]{:S(2)}) collective-permute-start(f32[4,16,128]{2,1,0:T(8,128)S(1)} %push.3.mine_ref), channel_id=1, source_target_pairs={{0,1},{1,0},{2,3},{3,2},{4,5},{5,4},{6,7},{7,6},{8,9},{9,8},{10,11... | collective-permute-start | bytes 98312 | tf_op jit(solution)/shard_map/ppermute | solution.py:424

commit v5 on v4

--- a/solution.py
+++ b/solution.py
@@ -102,13 +102,14 @@
 
 
 def pack_kernel(pos_hbm, vel_hbm, charge_hbm, mass_hbm, centre_hbm, width_hbm, density_hbm,
-                error_hbm, owners_hbm, halo_hbm, state_ref, comp_ref, ints_ref, pos_ref, vel_ref,
-                charge_ref, mass_ref, centre_ref, width_ref, density_ref, error_ref, owners_ref,
-                halo_ref, sems):
+                error_hbm, owners_hbm, halo_hbm, pairs_hbm, partner_hbm, decision_hbm, state_ref,
+                comp_ref, ints_ref, pos_ref, vel_ref, charge_ref, mass_ref, centre_ref, width_ref,
+                density_ref, error_ref, owners_ref, halo_ref, pairs_ref, partner_ref, decision_ref,
+                sems):
     sources = (pos_hbm, vel_hbm, charge_hbm, mass_hbm, centre_hbm, width_hbm, density_hbm,
-               error_hbm, owners_hbm, halo_hbm)
+               error_hbm, owners_hbm, halo_hbm, pairs_hbm, partner_hbm, decision_hbm)
     targets = (pos_ref, vel_ref, charge_ref, mass_ref, centre_ref, width_ref, density_ref,
-               error_ref, owners_ref, halo_ref)
+               error_ref, owners_ref, halo_ref, pairs_ref, partner_ref, decision_ref)
     copies = [
         pltpu.make_async_copy(source, target, sems.at[n])
         for n, (source, target) in enumerate(zip(sources, targets))
@@ -128,6 +129,11 @@
     ints_ref[...] = jnp.zeros_like(ints_ref)
     ints_ref[0:owned, 0:own] = owners_ref[...]
     ints_ref[owned : owned + sides, 0:listed] = halo_ref[0]
+    last = owned + sides
+    ints_ref[last : last + 1, 0 : partner_ref.shape[1]] = partner_ref[...]
+    ints_ref[last + 1 : last + 2, 0 : decision_ref.shape[1]] = decision_ref[...]
+    rows, near = pairs_ref.shape
+    ints_ref[last + 2 : last + 2 + rows, 0:near] = pairs_ref[...]
     for row in range(comp_ref.shape[0]):
         part = pl.ds((row % CORES) * half, half)
         comp_ref[row, 0:3, :] = centre_ref[:, part]
@@ -136,10 +142,11 @@
         comp_ref[row, 5:6, :] = error_ref[:, part]
 
 
-def choose_kernel(partner_ref, decision_ref, mine_ref, *refs):
+def choose_kernel(plan, ints_ref, mine_ref, *refs):
     others, out_ref = refs[:-1], refs[-1]
     row = lax.axis_index("rep")
-    source = jnp.where(decision_ref[row] == 1, partner_ref[row], row)
+    last = plan.owned + 2
+    source = jnp.where(ints_ref[last + 1, row] == 1, ints_ref[last, row], row)
     if len(others) == 1:
         out_ref[...] = others[0][source]
         return
@@ -151,7 +158,7 @@
             out_ref[...] = other_ref[...]
 
 
-def list_kernel(plan, mine_ref, theirs_ref, pairs_ref, out_ref, waiting):
+def list_kernel(plan, mine_ref, theirs_ref, out_ref, waiting):
     core = lax.axis_index("core")
 
     def clear(domain, carry):
@@ -193,7 +200,7 @@
             out_ref[3, 1 + side * plan.listed + k] = theirs_ref[plan.owned + side, k]
     for tile in range(plan.own):
         for j in range(plan.near):
-            out_ref[4 + j, tile] = pairs_ref[tile, j]
+            out_ref[4 + j, tile] = mine_ref[plan.owned + 4 + tile, j]
 
 
 def partner_tile(plan, lists_ref, side, k):
@@ -211,8 +218,8 @@
     lax.fori_loop(0, lists_ref[3, 0], step, 0)
 
 
-def sum_gaussians(plan, scale, lists_ref, state_ref, turned_ref, points_ref, out_ref, rim_ref, high_ref,
-                  low_ref, xs, acc):
+def sum_gaussians(plan, scale, lists_ref, state_ref, turned_ref, points_ref, out_ref, rim_ref, kept_ref,
+                  xs, acc):
     tiles, listed, lanes = plan.tiles, plan.listed, plan.lanes
     store_rows(xs, point_rows([state_ref[i] for i in range(3)]))
     nowhere(xs, tiles)
@@ -230,7 +237,7 @@
             part = slice(start, start + size)
             g = jnp.exp2(dot(turned_ref[owner, part, :], points))
             acc[owner, part, :] += g[:, :lanes] + g[:, lanes:]
-            high_ref[place, part, :], low_ref[place, part, :] = high_low(g)
+            kept_ref[place, part, :] = g
 
     for_pairs(lists_ref, one_pair)
     for domain in range(plan.domains):
@@ -240,7 +247,7 @@
 
 
 def first_kernel(plan, scale, lists_ref, mine_ref, theirs_ref, comp_ref,
-                 out_ref, rim_ref, state_ref, points_ref, high_ref, low_ref, turned_ref, xs, acc, cs):
+                 out_ref, rim_ref, state_ref, points_ref, kept_ref, turned_ref, xs, acc, cs):
     core = lax.axis_index("core")
     for tile in range(plan.own):
         lanes = slice(tile * plan.lanes, (tile + 1) * plan.lanes)
@@ -253,8 +260,8 @@
             turned_ref[domain, start : start + size, :] = cs[
                 domain, :, start : start + size
             ].T.astype(bf16)
-    sum_gaussians(plan, scale, lists_ref, state_ref, turned_ref, points_ref, out_ref, rim_ref, high_ref,
-                  low_ref, xs, acc)
+    sum_gaussians(plan, scale, lists_ref, state_ref, turned_ref, points_ref, out_ref, rim_ref, kept_ref,
+                  xs, acc)
 
 
 def stepped(old_ref, mine_ref, theirs_ref):
@@ -265,14 +272,14 @@
 
 
 def next_kernel(plan, scale, lists_ref, old_ref, force_ref, swapped_ref, turned_ref,
-                out_ref, rim_ref, state_ref, points_ref, high_ref, low_ref, xs, acc):
+                out_ref, rim_ref, state_ref, points_ref, kept_ref, xs, acc):
     for i, (x, v) in enumerate(stepped(old_ref, force_ref, swapped_ref)):
         state_ref[i] = x
         state_ref[3 + i] = v
     state_ref[6] = old_ref[6]
     state_ref[7] = old_ref[7]
-    sum_gaussians(plan, scale, lists_ref, state_ref, turned_ref, points_ref, out_ref, rim_ref, high_ref,
-                  low_ref, xs, acc)
+    sum_gaussians(plan, scale, lists_ref, state_ref, turned_ref, points_ref, out_ref, rim_ref, kept_ref,
+                  xs, acc)
 
 
 def tree_sum(refs):
@@ -344,7 +351,7 @@
             out_ref[i, tile : tile + 1, :] = strength * push
 
 
-def push_kernel(plan, gain, replicas, lists_ref, state_ref, comp_ref, pair_ref, high_ref, low_ref, *refs):
+def push_kernel(plan, gain, replicas, lists_ref, state_ref, comp_ref, pair_ref, kept_ref, *refs):
     parts, (out_ref, rs, rows, means, sums) = refs[:-5], refs[-5:]
     tiles, lanes = plan.tiles, plan.lanes
     mean = tree_sum(parts) / replicas
@@ -357,8 +364,13 @@
     sums[...] = jnp.zeros_like(sums)
 
     def one_pair(place, owner, first, second):
-        weights = rows[owner]
-        total = dot(weights, high_ref[place]) + dot(weights, low_ref[place])
+        total = None
+        for start, size in chunks(plan.half, CHUNK):
+            part = slice(start, start + size)
+            weights = rows[owner, :, part]
+            high, low = high_low(kept_ref[place, part, :])
+            term = dot(weights, high) + dot(weights, low)
+            total = term if total is None else total + term
         sums[first] += total[:, :lanes]
         sums[second] += total[:, lanes:]
 
@@ -403,8 +415,12 @@
             yield pltpu.VMEM(dims, dtype)
 
 
-def call(name, kernel, lists, args, outs, scratch=(), limit=16, spaces=None, out_spaces=None):
+def call(kernel, lists, args, outs, scratch=(), limit=16, spaces=None, out_spaces=None):
     many = isinstance(outs, (list, tuple))
+    return pallas(kernel, lists, args, outs, scratch, limit, spaces, out_spaces, many)
+
+
+def pallas(kernel, lists, args, outs, scratch, limit, spaces, out_spaces, many):
     return pl.pallas_call(
         kernel,
         out_shape=tuple(outs) if many else outs,
@@ -412,7 +428,6 @@
         out_specs=tuple(out_spaces or [VMEM] * len(outs)) if many else (out_spaces or VMEM),
         scratch_shapes=list(with_types(scratch)),
         compiler_params=pltpu.CompilerParams(vmem_limit_bytes=limit and limit << 20),
-        name=name,
     )(*lists, *args)
 
 
@@ -424,14 +439,19 @@
     return lax.ppermute(value, "core", [(0, 1), (1, 0)])
 
 
+def few(replicas, heights):
+    return replicas in (2, 4) and heights in (2, 4)
+
+
 def exchange(value, axis):
     count = lax.axis_size(axis)
-    return [
-        lax.ppermute(value, axis, [(i, i ^ n) for i in range(count)]) for n in range(1, count)
-    ]
-
-
-def local(
+    others = []
+    for n in range(1, count):
+        others.append(lax.ppermute(value, axis, [(i, i ^ n) for i in range(count)]))
+    return others
+
+
+def program(
     positions,
     velocities,
     charge,
@@ -469,30 +489,32 @@
         map_error[None],
         owners.T,
         halo_tiles,
+        pair_tiles,
+        partner[None],
+        decision[None],
     ]
-    int_rows = -(-(owned + halo_tiles.shape[1]) // 8) * 8
+    int_rows = -(-(owned + halo_tiles.shape[1] + 2 + own) // 8) * 8
     state_own, comp_send, ints = call(
-        "pack",
         pack_kernel,
         [],
         args,
         [shape(8, own * lanes), shape(domains, 6, half), shape(int_rows, lanes, dtype=jnp.int32)],
         [(arg.shape, arg.dtype) for arg in args] + [pltpu.SemaphoreType.DMA((len(args),))],
-        limit=None,
+        limit=60,
         spaces=[HBM] * len(args),
     )
     comps = lax.all_to_all(comp_send, ("z", "core"), 0, 0, tiled=True)
+    other_ints = swap_cores(ints)
     width = -(-((tiles * owned + domains) // 2 + UNROLL + 1) // lanes) * lanes
     lists = call(
-        "lists",
         functools.partial(list_kernel, plan),
-        [ints, swap_cores(ints), pair_tiles],
+        [ints, other_ints],
         [],
         shape(4 + plan.near, width, dtype=jnp.int32),
         [pltpu.SMEM((domains,), jnp.int32)],
         out_spaces=SMEM,
     )
-    small = replicas in (1, 2, 4) and heights in (1, 2, 4)
+    small = few(replicas, heights)
     if small:
         others = exchange(state_own, "rep")
     else:
@@ -503,11 +525,7 @@
             )
         ]
     chosen = call(
-        "choose",
-        choose_kernel,
-        [partner, decision],
-        [state_own] + others,
-        shape(8, own * lanes),
+        functools.partial(choose_kernel, plan), [ints], [state_own] + others, shape(8, own * lanes)
     )
     chosen_other = swap_cores(chosen)
 
@@ -520,20 +538,17 @@
     onward += [((2 * i + 3) % domains, 2 * i + 1) for i in range(heights)]
     padded = -(-(own + 2 * listed + 1) // 8) * 8
     most = (tiles * owned + domains) // 2 + UNROLL
-    kept = shape(most, half, 2 * lanes, dtype=bf16)
     outs = [
         shape(domains, half),
         shape(rim_rows, lanes),
         shape(8, tiles, lanes),
         shape(tiles + 1, DEPTH, lanes, dtype=bf16),
-        kept,
-        kept,
+        shape(most, half, 2 * lanes),
     ]
     scratch = [(tiles + 1, DEPTH, lanes), (domains, half, lanes)]
     for step in range(STEPS):
         if step == 0:
-            partial, rim, state, points, high, low, turned = call(
-                "first",
+            partial, rim, state, points, kept, turned = call(
                 functools.partial(first_kernel, plan, scale),
                 [lists],
                 [chosen, chosen_other, comps],
@@ -541,8 +556,7 @@
                 scratch + [(domains, DEPTH, half)],
             )
         else:
-            partial, rim, state, points, high, low = call(
-                "next",
+            partial, rim, state, points, kept = call(
                 functools.partial(next_kernel, plan, scale),
                 [lists],
                 [state, force, swapped, turned],
@@ -552,7 +566,7 @@
         far = lax.ppermute(rim, ("z", "core"), onward)
         if small:
             partial = call(
-                "add", add_kernel, [], [partial] + exchange(partial, "rep"), shape(domains, half)
+                add_kernel, [], [partial] + exchange(partial, "rep"), shape(domains, half)
             )
             parts = [partial] + exchange(partial, "z")
         else:
@@ -565,7 +579,6 @@
                 ).reshape(domains, half)
             ]
         pair = call(
-            "pair",
             functools.partial(pair_kernel, plan, pair_gain),
             [lists],
             [state, far, points],
@@ -574,10 +587,9 @@
              ((padded, ROWS, lanes), bf16), ((padded, lanes, DEPTH), bf16)],
         )
         force = call(
-            "push",
             functools.partial(push_kernel, plan, map_gain, float(replicas)),
             [lists],
-            [state, comps, pair, high, low] + parts,
+            [state, comps, pair, kept] + parts,
             shape(4, tiles, lanes),
             [(domains, ROWS, half), ((domains, ROWS, half), bf16), (half // lanes, domains, lanes),
              (tiles + 1, ROWS, lanes)],
@@ -585,7 +597,6 @@
         swapped = swap_cores(force)
 
     new_x, new_v, model_map = call(
-        "finish",
         functools.partial(finish_kernel, plan),
         [],
         [state, force, swapped],
@@ -617,7 +628,7 @@
         P(),
     )
     return jax.shard_map(
-        local,
+        program,
         mesh=split,
         in_specs=placed,
         out_specs=(P("rep", None, dom), P("rep", None, dom), P(dom)),

time: 90.8 us -> 87.4 us (0.963)
  Pallas kernels: 35.5 us -> 34.2 us
  local copies, waits for them, and re-layouts: 3.44 us -> 2.15 us
    pallas_call x12, Pallas kernels: 35.5 us -> 34.2 us  [pallas(): pl.pallas_call(kernel, out_shape=tuple(outs) if many else outs, in_specs=...]
    unnamed x10 -> x6, local copies, waits for them, and re-layouts: 3.44 us -> 2.15 us
where the time goes in v5:
time: 87.4 us; the launch traced here: 87 us
  Pallas kernels  34.2 us (39%)
  starting transfers between devices  28.1 us (32%)
  waiting for transfers between devices  21.8 us (25%)
  local copies, waits for them, and re-layouts  2.15 us (2%)
    pallas_call x12, Pallas kernels, pallas(): pl.pallas_call(kernel, out_shape=tuple(outs) if many else outs, in_specs=...  34.2 us
    ppermute x15, starting transfers between devices, exchange(): others.append(lax.ppermute(value, axis, [(i, i ^ n) for i in range(count)]))  19.6 us
    ppermute x2, waiting for transfers between devices, program(): far = lax.ppermute(rim, ('z', 'core'), onward)  9.49 us
    ppermute x15, waiting for transfers between devices, exchange(): others.append(lax.ppermute(value, axis, [(i, i ^ n) for i in range(count)]))  9.04 us
    all_to_all x1, starting transfers between devices, program(): comps = lax.all_to_all(comp_send, ('z', 'core'), 0, 0, tiled=True)  6.37 us
    ppermute x4, waiting for transfers between devices, swap_cores(): return lax.ppermute(value, 'core', [(0, 1), (1, 0)])  3.22 us
    unnamed x6, local copies, waits for them, and re-layouts  2.15 us
  transfers between devices with their start and end apart: 22, of which 14 were waited for; matrix products, arithmetic and copies ran while one was open for 0% of the time, Pallas kernels for 8%

profile of v5, /device:TPU:0, one launch (start us, length us, event | category | flops | bytes accessed | tf_op | source)
XLA Modules:
  0.0 87.0 jit_solution(13410266269724121680)
XLA Ops:
  0.6 1.6 %shard_map.148 = (f32[8,1024]{1,0:T(8,128)}, f32[8,6,512]{2,1,0:T(8,128)}, s32[16,128]{1,0:T(8,128)}) custom-call(f32[3,1,1024]{2,1,0:T(1,128)} %bitcast.13, f32[3,1,1024]{2,1,0:T(1,128)} %bitcast.14, f32[1,1024]{1,0:T(1,128)} %bitcast.15, f32[1,1024]{1,0:T(1,128)} %bitcast.16, f32[3,1024]{1,0:T(4,128)} %centre_hbm.1, f32[1,1024]{1,0:T(1,128)} %bitcast.17, ...), custom_call_target="tpu_custom_call" | custom-call | tf_op jit(solution)/shard_map/pallas_call | solution.py:424
  2.3 6.4 %all-to-all-start = ((f32[8,6,512]{2,1,0:T(8,128)}), f32[8,6,512]{2,1,0:T(8,128)S(1)}, u32[]{:S(2)}, u32[]{:S(2)}) async-start(f32[8,6,512]{2,1,0:T(8,128)} %get-tuple-element.22), calls=%async_computation | async-start | bytes 262144 | tf_op jit(solution)/shard_map/all_to_all | solution.py:506
  8.6 2.4 %collective-permute-start.3 = (f32[8,1024]{1,0:T(8,128)}, f32[8,1024]{1,0:T(8,128)S(1)}, u32[]{:S(2)}, u32[]{:S(2)}) collective-permute-start(f32[8,1024]{1,0:T(8,128)} %get-tuple-element.21.mine_ref), channel_id=1, source_target_pairs={{0,24},{8,16},{16,8},{24,0},{1,25},{9,17},{17,9},{25,1},{2,26},{10... | collective-permute-start | bytes 98312 | tf_op jit(solution)/shard_map/ppermute | solution.py:450
  12.1 1.5 %collective-permute-done.3.refs_2_ = f32[8,1024]{1,0:T(8,128)S(1)} collective-permute-done((f32[8,1024]{1,0:T(8,128)}, f32[8,1024]{1,0:T(8,128)S(1)}, u32[]{:S(2)}, u32[]{:S(2)}) %collective-permute-start.3) | collective-permute-done | bytes 32800 | tf_op jit(solution)/shard_map/ppermute | solution.py:450
  13.7 1.5 %collective-permute-done.2.refs_1_ = f32[8,1024]{1,0:T(8,128)S(1)} collective-permute-done((f32[8,1024]{1,0:T(8,128)}, f32[8,1024]{1,0:T(8,128)S(1)}, u32[]{:S(2)}, u32[]{:S(2)}) %collective-permute-start.2) | collective-permute-done | bytes 32800 | tf_op jit(solution)/shard_map/ppermute | solution.py:450
  15.7 0.8 copy-done
  16.5 0.7 copy-done.1
  17.2 0.7 shard_map.150.mine_ref
  18.5 0.8 collective-permute-done.theirs_ref
  19.3 0.7 copy-done.2
  20.0 2.3 %shard_map.149.lists_ref = s32[10,128]{1,0:T(8,128)S(1)} custom-call(s32[16,128]{1,0:T(8,128)S(1)} %copy-done.2, s32[16,128]{1,0:T(8,128)S(1)} %collective-permute-done.theirs_ref), custom_call_target="tpu_custom_call" | custom-call | tf_op jit(solution)/shard_map/pallas_call | solution.py:424
  22.3 6.9 %shard_map.151 = (f32[8,512]{1,0:T(8,128)S(1)}, f32[8,128]{1,0:T(8,128)S(1)}, f32[8,16,128]{2,1,0:T(8,128)S(1)}, bf16[17,32,128]{2,1,0:T(8,128)(2,1)S(1)}, f32[3...) custom-call(s32[10,128]{1,0:T(8,128)S(1)} %shard_map.149.lists_ref, f32[8,1024]{1,0:T(8,128)S(1)} %shard_map.150.mine_ref, ...), custom_call_target="tpu_custom_call" | custom-call | tf_op jit(solution)/shard_map/pallas_call | solution.py:424
  29.1 1.5 %collective-permute-start.8 = (f32[8,512]{1,0:T(8,128)S(1)}, f32[8,512]{1,0:T(8,128)S(1)}, u32[]{:S(2)}, u32[]{:S(2)}) collective-permute-start(f32[8,512]{1,0:T(8,128)S(1)} %get-tuple-element.27.refs_0_), channel_id=1, source_target_pairs={{0,24},{8,16},{16,8},{24,0},{1,25},{9,17},{17,9},{25,1},{2,26},{10... | collective-permute-start | bytes 49160 | tf_op jit(solution)/shard_map/ppermute | solution.py:450
  31.2 1.5 %collective-permute-start.6 = (f32[8,512]{1,0:T(8,128)S(1)}, f32[8,512]{1,0:T(8,128)S(1)}, u32[]{:S(2)}, u32[]{:S(2)}) collective-permute-start(f32[8,512]{1,0:T(8,128)S(1)} %get-tuple-element.27.refs_0_), channel_id=1, source_target_pairs={{0,8},{8,0},{16,24},{24,16},{1,9},{9,1},{17,25},{25,17},{2,10},{10... | collective-permute-start | bytes 49160 | tf_op jit(solution)/shard_map/ppermute | solution.py:450
  32.7 1.1 %collective-permute-done.8.refs_3_ = f32[8,512]{1,0:T(8,128)S(1)} collective-permute-done((f32[8,512]{1,0:T(8,128)S(1)}, f32[8,512]{1,0:T(8,128)S(1)}, u32[]{:S(2)}, u32[]{:S(2)}) %collective-permute-start.8) | collective-permute-done | bytes 16416 | tf_op jit(solution)/shard_map/ppermute | solution.py:450
  34.9 3.9 %collective-permute-start.11 = (f32[8,512]{1,0:T(8,128)S(1)}, f32[8,512]{1,0:T(8,128)S(1)}, u32[]{:S(2)}, u32[]{:S(2)}) collective-permute-start(f32[8,512]{1,0:T(8,128)S(1)} %shard_map.153.refs_0_), channel_id=1, source_target_pairs={{0,6},{2,4},{4,2},{6,0},{1,7},{3,5},{5,3},{7,1},{8,14},{10,12},{12... | collective-permute-start | bytes 49160 | tf_op jit(solution)/shard_map/ppermute | solution.py:450
  38.8 0.6 collective-permute-start.9
  39.5 1.4 %collective-permute-start.5 = (f32[8,128]{1,0:T(8,128)S(1)}, f32[8,128]{1,0:T(8,128)S(1)}, u32[]{:S(2)}, u32[]{:S(2)}) collective-permute-start(f32[8,128]{1,0:T(8,128)S(1)} %get-tuple-element.24), channel_id=1, source_target_pairs={{0,2},{2,4},{4,6},{6,0},{3,1},{5,3},{7,5},{1,7},{8,10},{10,12},{12... | collective-permute-start | bytes 12296 | tf_op jit(solution)/shard_map/ppermute | solution.py:566
  40.9 4.1 %collective-permute-done.5.far_ref = f32[8,128]{1,0:T(8,128)S(1)} collective-permute-done((f32[8,128]{1,0:T(8,128)S(1)}, f32[8,128]{1,0:T(8,128)S(1)}, u32[]{:S(2)}, u32[]{:S(2)}) %collective-permute-start.5) | collective-permute-done | bytes 4128 | tf_op jit(solution)/shard_map/ppermute | solution.py:566
  45.0 2.1 %shard_map.152.pair_ref = f32[3,8,128]{2,1,0:T(8,128)S(1)} custom-call(s32[10,128]{1,0:T(8,128)S(1)} %shard_map.149.lists_ref, f32[8,16,128]{2,1,0:T(8,128)S(1)} %get-tuple-element.23.state_ref.old_ref, f32[8,128]{1,0:T(8,128)S(1)} %collective-permute-done.5.far_ref, bf16[17,32,128]{2,1,0:T(8,128)(2,1)S(1)} %get-tuple-element.25.points_ref), custom_call_target="tpu_custom_call" | custom-call | tf_op jit(solution)/shard_map/pallas_call | solution.py:424
  47.1 5.7 %shard_map.154.force_ref = f32[4,16,128]{2,1,0:T(8,128)S(1)} custom-call(s32[10,128]{1,0:T(8,128)S(1)} %shard_map.149.lists_ref, f32[8,16,128]{2,1,0:T(8,128)S(1)} %get-tuple-element.23.state_ref.old_ref, f32[8,6,512]{2,1,0:T(8,128)S(1)} %all-to-all-done.comp_ref, f32[3,8,128]{2,1,0:T(8,128)S(1)} %shard_map.152.pair_ref, ...), custom_call_target="tpu_custom_call" | custom-call | tf_op jit(solution)/shard_map/pallas_call | solution.py:424
  53.0 1.2 %collective-permute-done.12.swapped_ref = f32[4,16,128]{2,1,0:T(8,128)S(1)} collective-permute-done((f32[4,16,128]{2,1,0:T(8,128)S(1)}, f32[4,16,128]{2,1,0:T(8,128)S(1)}, u32[]{:S(2)}, u32[]{:S(2)}) %collective-permute-start.12) | collective-permute-done | bytes 32800 | tf_op jit(solution)/shard_map/ppermute | solution.py:439
  54.2 6.4 %shard_map.155 = (f32[8,512]{1,0:T(8,128)S(1)}, f32[8,128]{1,0:T(8,128)S(1)}, f32[8,16,128]{2,1,0:T(8,128)S(1)}, bf16[17,32,128]{2,1,0:T(8,128)(2,1)S(1)}, f32[38,512,256]{2,1,0:T(8,128)S(1)}) custom-call(s32[10,128]{1,0:T(8,128)S(1)} %shard_map.149.lists_ref, f32[8,16,128]{2,1,0:T(8,128)S(1)} %get-tuple-element.23.state_ref.old_ref, ...), custom_call_target="tpu_custom_call" | custom-call | tf_op jit(solution)/shard_map/pallas_call | solution.py:424
  60.5 2.5 %collective-permute-start.16 = (f32[8,512]{1,0:T(8,128)S(1)}, f32[8,512]{1,0:T(8,128)S(1)}, u32[]{:S(2)}, u32[]{:S(2)}) collective-permute-start(f32[8,512]{1,0:T(8,128)S(1)} %get-tuple-element.33.refs_0_), channel_id=1, source_target_pairs={{0,24},{8,16},{16,8},{24,0},{1,25},{9,17},{17,9},{25,1},{2,26},{10... | collective-permute-start | bytes 49160 | tf_op jit(solution)/shard_map/ppermute | solution.py:450
  64.1 1.1 %collective-permute-done.16.refs_3_ = f32[8,512]{1,0:T(8,128)S(1)} collective-permute-done((f32[8,512]{1,0:T(8,128)S(1)}, f32[8,512]{1,0:T(8,128)S(1)}, u32[]{:S(2)}, u32[]{:S(2)}) %collective-permute-start.16) | collective-permute-done | bytes 16416 | tf_op jit(solution)/shard_map/ppermute | solution.py:450
  65.2 1.6 %collective-permute-done.15.refs_2_ = f32[8,512]{1,0:T(8,128)S(1)} collective-permute-done((f32[8,512]{1,0:T(8,128)S(1)}, f32[8,512]{1,0:T(8,128)S(1)}, u32[]{:S(2)}, u32[]{:S(2)}) %collective-permute-start.15) | collective-permute-done | bytes 16416 | tf_op jit(solution)/shard_map/ppermute | solution.py:450
  67.3 1.9 %collective-permute-start.19 = (f32[8,512]{1,0:T(8,128)S(1)}, f32[8,512]{1,0:T(8,128)S(1)}, u32[]{:S(2)}, u32[]{:S(2)}) collective-permute-start(f32[8,512]{1,0:T(8,128)S(1)} %shard_map.157.refs_0_), channel_id=1, source_target_pairs={{0,6},{2,4},{4,2},{6,0},{1,7},{3,5},{5,3},{7,1},{8,14},{10,12},{12... | collective-permute-start | bytes 49160 | tf_op jit(solution)/shard_map/ppermute | solution.py:450
  69.2 2.5 %collective-permute-start.17 = (f32[8,512]{1,0:T(8,128)S(1)}, f32[8,512]{1,0:T(8,128)S(1)}, u32[]{:S(2)}, u32[]{:S(2)}) collective-permute-start(f32[8,512]{1,0:T(8,128)S(1)} %shard_map.157.refs_0_), channel_id=1, source_target_pairs={{0,2},{2,0},{4,6},{6,4},{1,3},{3,1},{5,7},{7,5},{8,10},{10,8},{12,... | collective-permute-start | bytes 49160 | tf_op jit(solution)/shard_map/ppermute | solution.py:450
  71.8 5.4 %collective-permute-done.13.far_ref = f32[8,128]{1,0:T(8,128)S(1)} collective-permute-done((f32[8,128]{1,0:T(8,128)S(1)}, f32[8,128]{1,0:T(8,128)S(1)}, u32[]{:S(2)}, u32[]{:S(2)}) %collective-permute-start.13) | collective-permute-done | bytes 4128 | tf_op jit(solution)/shard_map/ppermute | solution.py:566
  77.1 2.1 %shard_map.156.pair_ref = f32[3,8,128]{2,1,0:T(8,128)S(1)} custom-call(s32[10,128]{1,0:T(8,128)S(1)} %shard_map.149.lists_ref, f32[8,16,128]{2,1,0:T(8,128)S(1)} %get-tuple-element.29.state_ref.old_ref, f32[8,128]{1,0:T(8,128)S(1)} %collective-permute-done.13.far_ref, bf16[17,32,128]{2,1,0:T(8,128)(2,1)S(1)} %get-tuple-element.31.points_ref), custom_call_target="tpu_custom_call" | custom-call | tf_op jit(solution)/shard_map/pallas_call | solution.py:424
  79.3 5.7 %shard_map.158.mine_ref = f32[4,16,128]{2,1,0:T(8,128)S(1)} custom-call(s32[10,128]{1,0:T(8,128)S(1)} %shard_map.149.lists_ref, f32[8,16,128]{2,1,0:T(8,128)S(1)} %get-tuple-element.29.state_ref.old_ref, f32[8,6,512]{2,1,0:T(8,128)S(1)} %all-to-all-done.comp_ref, f32[3,8,128]{2,1,0:T(8,128)S(1)} %shard_map.156.pair_ref, ...), custom_call_target="tpu_custom_call" | custom-call | tf_op jit(solution)/shard_map/pallas_call | solution.py:424
  85.1 1.2 %collective-permute-done.20.theirs_ref = f32[4,16,128]{2,1,0:T(8,128)S(1)} collective-permute-done((f32[4,16,128]{2,1,0:T(8,128)S(1)}, f32[4,16,128]{2,1,0:T(8,128)S(1)}, u32[]{:S(2)}, u32[]{:S(2)}) %collective-permute-start.20) | collective-permute-done | bytes 32800 | tf_op jit(solution)/shard_map/ppermute | solution.py:439
  (30 shorter events, 6.1 us)
Async XLA Ops:
  2.3 20.0 %all-to-all-start = ((f32[8,6,512]{2,1,0:T(8,128)}), f32[8,6,512]{2,1,0:T(8,128)S(1)}, u32[]{:S(2)}, u32[]{:S(2)}) async-start(f32[8,6,512]{2,1,0:T(8,128)} %get-tuple-element.22), calls=%async_computation | async-start | bytes 262144 | tf_op jit(solution)/shard_map/all_to_all | solution.py:506
  8.6 5.0 %collective-permute-start.3 = (f32[8,1024]{1,0:T(8,128)}, f32[8,1024]{1,0:T(8,128)S(1)}, u32[]{:S(2)}, u32[]{:S(2)}) collective-permute-start(f32[8,1024]{1,0:T(8,128)} %get-tuple-element.21.mine_ref), channel_id=1, source_target_pairs={{0,24},{8,16},{16,8},{24,0},{1,25},{9,17},{17,9},{25,1},{2,26},{10... | collective-permute-start | bytes 98312 | tf_op jit(solution)/shard_map/ppermute | solution.py:450
  11.1 4.1 %collective-permute-start.2 = (f32[8,1024]{1,0:T(8,128)}, f32[8,1024]{1,0:T(8,128)S(1)}, u32[]{:S(2)}, u32[]{:S(2)}) collective-permute-start(f32[8,1024]{1,0:T(8,128)} %get-tuple-element.21.mine_ref), channel_id=1, source_target_pairs={{0,16},{8,24},{16,0},{24,8},{1,17},{9,25},{17,1},{25,9},{2,18},{10... | collective-permute-start | bytes 98312 | tf_op jit(solution)/shard_map/ppermute | solution.py:450
  11.6 4.1 %collective-permute-start.1 = (f32[8,1024]{1,0:T(8,128)}, f32[8,1024]{1,0:T(8,128)S(1)}, u32[]{:S(2)}, u32[]{:S(2)}) collective-permute-start(f32[8,1024]{1,0:T(8,128)} %get-tuple-element.21.mine_ref), channel_id=1, source_target_pairs={{0,8},{8,0},{16,24},{24,16},{1,9},{9,1},{17,25},{25,17},{2,10},{10... | collective-permute-start | bytes 98312 | tf_op jit(solution)/shard_map/ppermute | solution.py:450
  15.7 0.8 copy-start
  16.5 0.7 copy-start.1
  17.9 4.4 %collective-permute-start.4 = (f32[8,1024]{1,0:T(8,128)S(1)}, f32[8,1024]{1,0:T(8,128)S(1)}, u32[]{:S(2)}, u32[]{:S(2)}) collective-permute-start(f32[8,1024]{1,0:T(8,128)S(1)} %shard_map.150.mine_ref), channel_id=1, source_target_pairs={{0,1},{1,0},{2,3},{3,2},{4,5},{5,4},{6,7},{7,6},{8,9},{9,8},{10,11... | collective-permute-start | bytes 98312 | tf_op jit(solution)/shard_map/ppermute | solution.py:439
  18.0 1.3 %collective-permute-start = (s32[16,128]{1,0:T(8,128)S(1)}, s32[16,128]{1,0:T(8,128)S(1)}, u32[]{:S(2)}, u32[]{:S(2)}) collective-permute-start(s32[16,128]{1,0:T(8,128)S(1)} %copy-done.1), channel_id=1, source_target_pairs={{0,1},{1,0},{2,3},{3,2},{4,5},{5,4},{6,7},{7,6},{8,9},{9,8},{10,11... | collective-permute-start | bytes 24584 | tf_op jit(solution)/shard_map/ppermute | solution.py:439
  19.3 0.7 copy-start.2
  29.1 4.7 %collective-permute-start.8 = (f32[8,512]{1,0:T(8,128)S(1)}, f32[8,512]{1,0:T(8,128)S(1)}, u32[]{:S(2)}, u32[]{:S(2)}) collective-permute-start(f32[8,512]{1,0:T(8,128)S(1)} %get-tuple-element.27.refs_0_), channel_id=1, source_target_pairs={{0,24},{8,16},{16,8},{24,0},{1,25},{9,17},{17,9},{25,1},{2,26},{10... | collective-permute-start | bytes 49160 | tf_op jit(solution)/shard_map/ppermute | solution.py:450
  30.7 3.7 %collective-permute-start.7 = (f32[8,512]{1,0:T(8,128)S(1)}, f32[8,512]{1,0:T(8,128)S(1)}, u32[]{:S(2)}, u32[]{:S(2)}) collective-permute-start(f32[8,512]{1,0:T(8,128)S(1)} %get-tuple-element.27.refs_0_), channel_id=1, source_target_pairs={{0,16},{8,24},{16,0},{24,8},{1,17},{9,25},{17,1},{25,9},{2,18},{10... | collective-permute-start | bytes 49160 | tf_op jit(solution)/shard_map/ppermute | solution.py:450
  31.2 3.7 %collective-permute-start.6 = (f32[8,512]{1,0:T(8,128)S(1)}, f32[8,512]{1,0:T(8,128)S(1)}, u32[]{:S(2)}, u32[]{:S(2)}) collective-permute-start(f32[8,512]{1,0:T(8,128)S(1)} %get-tuple-element.27.refs_0_), channel_id=1, source_target_pairs={{0,8},{8,0},{16,24},{24,16},{1,9},{9,1},{17,25},{25,17},{2,10},{10... | collective-permute-start | bytes 49160 | tf_op jit(solution)/shard_map/ppermute | solution.py:450
  34.9 12.2 %collective-permute-start.11 = (f32[8,512]{1,0:T(8,128)S(1)}, f32[8,512]{1,0:T(8,128)S(1)}, u32[]{:S(2)}, u32[]{:S(2)}) collective-permute-start(f32[8,512]{1,0:T(8,128)S(1)} %shard_map.153.refs_0_), channel_id=1, source_target_pairs={{0,6},{2,4},{4,2},{6,0},{1,7},{3,5},{5,3},{7,1},{8,14},{10,12},{12... | collective-permute-start | bytes 49160 | tf_op jit(solution)/shard_map/ppermute | solution.py:450
  38.8 8.3 %collective-permute-start.10 = (f32[8,512]{1,0:T(8,128)S(1)}, f32[8,512]{1,0:T(8,128)S(1)}, u32[]{:S(2)}, u32[]{:S(2)}) collective-permute-start(f32[8,512]{1,0:T(8,128)S(1)} %shard_map.153.refs_0_), channel_id=1, source_target_pairs={{0,4},{2,6},{4,0},{6,2},{1,5},{3,7},{5,1},{7,3},{8,12},{10,14},{12... | collective-permute-start | bytes 49160 | tf_op jit(solution)/shard_map/ppermute | solution.py:450
  38.8 8.3 %collective-permute-start.9 = (f32[8,512]{1,0:T(8,128)S(1)}, f32[8,512]{1,0:T(8,128)S(1)}, u32[]{:S(2)}, u32[]{:S(2)}) collective-permute-start(f32[8,512]{1,0:T(8,128)S(1)} %shard_map.153.refs_0_), channel_id=1, source_target_pairs={{0,2},{2,0},{4,6},{6,4},{1,3},{3,1},{5,7},{7,5},{8,10},{10,8},{12,... | collective-permute-start | bytes 49160 | tf_op jit(solution)/shard_map/ppermute | solution.py:450
  39.5 5.5 %collective-permute-start.5 = (f32[8,128]{1,0:T(8,128)S(1)}, f32[8,128]{1,0:T(8,128)S(1)}, u32[]{:S(2)}, u32[]{:S(2)}) collective-permute-start(f32[8,128]{1,0:T(8,128)S(1)} %get-tuple-element.24), channel_id=1, source_target_pairs={{0,2},{2,4},{4,6},{6,0},{3,1},{5,3},{7,5},{1,7},{8,10},{10,12},{12... | collective-permute-start | bytes 12296 | tf_op jit(solution)/shard_map/ppermute | solution.py:566
  52.9 1.3 %collective-permute-start.12 = (f32[4,16,128]{2,1,0:T(8,128)S(1)}, f32[4,16,128]{2,1,0:T(8,128)S(1)}, u32[]{:S(2)}, u32[]{:S(2)}) collective-permute-start(f32[4,16,128]{2,1,0:T(8,128)S(1)} %shard_map.154.force_ref), channel_id=1, source_target_pairs={{0,1},{1,0},{2,3},{3,2},{4,5},{5,4},{6,7},{7,6},{8,9},{9,8},{10,11... | collective-permute-start | bytes 98312 | tf_op jit(solution)/shard_map/ppermute | solution.py:439
  60.5 4.7 %collective-permute-start.16 = (f32[8,512]{1,0:T(8,128)S(1)}, f32[8,512]{1,0:T(8,128)S(1)}, u32[]{:S(2)}, u32[]{:S(2)}) collective-permute-start(f32[8,512]{1,0:T(8,128)S(1)} %get-tuple-element.33.refs_0_), channel_id=1, source_target_pairs={{0,24},{8,16},{16,8},{24,0},{1,25},{9,17},{17,9},{25,1},{2,26},{10... | collective-permute-start | bytes 49160 | tf_op jit(solution)/shard_map/ppermute | solution.py:450
  63.0 3.7 %collective-permute-start.15 = (f32[8,512]{1,0:T(8,128)S(1)}, f32[8,512]{1,0:T(8,128)S(1)}, u32[]{:S(2)}, u32[]{:S(2)}) collective-permute-start(f32[8,512]{1,0:T(8,128)S(1)} %get-tuple-element.33.refs_0_), channel_id=1, source_target_pairs={{0,16},{8,24},{16,0},{24,8},{1,17},{9,25},{17,1},{25,9},{2,18},{10... | collective-permute-start | bytes 49160 | tf_op jit(solution)/shard_map/ppermute | solution.py:450
  63.5 3.7 %collective-permute-start.14 = (f32[8,512]{1,0:T(8,128)S(1)}, f32[8,512]{1,0:T(8,128)S(1)}, u32[]{:S(2)}, u32[]{:S(2)}) collective-permute-start(f32[8,512]{1,0:T(8,128)S(1)} %get-tuple-element.33.refs_0_), channel_id=1, source_target_pairs={{0,8},{8,0},{16,24},{24,16},{1,9},{9,1},{17,25},{25,17},{2,10},{10... | collective-permute-start | bytes 49160 | tf_op jit(solution)/shard_map/ppermute | solution.py:450
  67.3 12.0 %collective-permute-start.19 = (f32[8,512]{1,0:T(8,128)S(1)}, f32[8,512]{1,0:T(8,128)S(1)}, u32[]{:S(2)}, u32[]{:S(2)}) collective-permute-start(f32[8,512]{1,0:T(8,128)S(1)} %shard_map.157.refs_0_), channel_id=1, source_target_pairs={{0,6},{2,4},{4,2},{6,0},{1,7},{3,5},{5,3},{7,1},{8,14},{10,12},{12... | collective-permute-start | bytes 49160 | tf_op jit(solution)/shard_map/ppermute | solution.py:450
  69.2 10.1 %collective-permute-start.18 = (f32[8,512]{1,0:T(8,128)S(1)}, f32[8,512]{1,0:T(8,128)S(1)}, u32[]{:S(2)}, u32[]{:S(2)}) collective-permute-start(f32[8,512]{1,0:T(8,128)S(1)} %shard_map.157.refs_0_), channel_id=1, source_target_pairs={{0,4},{2,6},{4,0},{6,2},{1,5},{3,7},{5,1},{7,3},{8,12},{10,14},{12... | collective-permute-start | bytes 49160 | tf_op jit(solution)/shard_map/ppermute | solution.py:450
  69.2 10.1 %collective-permute-start.17 = (f32[8,512]{1,0:T(8,128)S(1)}, f32[8,512]{1,0:T(8,128)S(1)}, u32[]{:S(2)}, u32[]{:S(2)}) collective-permute-start(f32[8,512]{1,0:T(8,128)S(1)} %shard_map.157.refs_0_), channel_id=1, source_target_pairs={{0,2},{2,0},{4,6},{6,4},{1,3},{3,1},{5,7},{7,5},{8,10},{10,8},{12,... | collective-permute-start | bytes 49160 | tf_op jit(solution)/shard_map/ppermute | solution.py:450
  71.7 5.4 %collective-permute-start.13 = (f32[8,128]{1,0:T(8,128)S(1)}, f32[8,128]{1,0:T(8,128)S(1)}, u32[]{:S(2)}, u32[]{:S(2)}) collective-permute-start(f32[8,128]{1,0:T(8,128)S(1)} %get-tuple-element.30), channel_id=1, source_target_pairs={{0,2},{2,4},{4,6},{6,0},{3,1},{5,3},{7,5},{1,7},{8,10},{10,12},{12... | collective-permute-start | bytes 12296 | tf_op jit(solution)/shard_map/ppermute | solution.py:566
  85.0 1.3 %collective-permute-start.20 = (f32[4,16,128]{2,1,0:T(8,128)S(1)}, f32[4,16,128]{2,1,0:T(8,128)S(1)}, u32[]{:S(2)}, u32[]{:S(2)}) collective-permute-start(f32[4,16,128]{2,1,0:T(8,128)S(1)} %shard_map.158.mine_ref), channel_id=1, source_target_pairs={{0,1},{1,0},{2,3},{3,2},{4,5},{5,4},{6,7},{7,6},{8,9},{9,8},{10,11... | collective-permute-start | bytes 98312 | tf_op jit(solution)/shard_map/ppermute | solution.py:439

commit v6 on v5

--- a/solution.py
+++ b/solution.py
@@ -146,19 +146,22 @@
     others, out_ref = refs[:-1], refs[-1]
     row = lax.axis_index("rep")
     last = plan.owned + 2
-    source = jnp.where(ints_ref[last + 1, row] == 1, ints_ref[last, row], row)
+    partner, decision = ints_ref[last : last + 1, :], ints_ref[last + 1 : last + 2, :]
+    lane = lax.broadcasted_iota(jnp.int32, partner.shape, 1)
+    sources = jnp.where(decision == 1, partner, lane)
+    source = jnp.sum(jnp.where(lane == row, sources, 0).astype(f32), 1, keepdims=True)
+    value = mine_ref[...]
     if len(others) == 1:
-        out_ref[...] = others[0][source]
-        return
-    out_ref[...] = mine_ref[...]
-    for n, other_ref in enumerate(others):
-
-        @pl.when(source == (row ^ (n + 1)))
-        def _():
-            out_ref[...] = other_ref[...]
-
-
-def list_kernel(plan, mine_ref, theirs_ref, out_ref, waiting):
+        for n in range(others[0].shape[0]):
+            value = jnp.where(source == float(n), others[0][n], value)
+    else:
+        for n, other_ref in enumerate(others):
+            other = jnp.bitwise_xor(row, n + 1).astype(f32)
+            value = jnp.where(source == other, other_ref[...], value)
+    out_ref[...] = value
+
+
+def make_lists(plan, mine_ref, theirs_ref, out_ref, waiting):
     core = lax.axis_index("core")
 
     def clear(domain, carry):
@@ -218,18 +221,20 @@
     lax.fori_loop(0, lists_ref[3, 0], step, 0)
 
 
-def sum_gaussians(plan, scale, lists_ref, state_ref, turned_ref, points_ref, out_ref, rim_ref, kept_ref,
+def sum_gaussians(plan, scale, lists_ref, copy, state_ref, turned_ref, points_ref, out_ref, rim_ref, kept_ref,
                   xs, acc):
     tiles, listed, lanes = plan.tiles, plan.listed, plan.lanes
     store_rows(xs, point_rows([state_ref[i] for i in range(3)]))
     nowhere(xs, tiles)
     points_ref[...] = xs[...].astype(bf16)
+    acc[...] = jnp.zeros_like(acc)
+    if copy is not None:
+        copy.wait()
     core = lax.axis_index("core")
     for k in range(listed):
         tile = partner_tile(plan, lists_ref, 1 - core, k)
         for i, row in enumerate((0, 1, 2, 6)):
             rim_ref[i * listed + k : i * listed + k + 1, :] = state_ref[row, pl.ds(tile, 1), :]
-    acc[...] = jnp.zeros_like(acc)
 
     def one_pair(place, owner, first, second):
         points = jnp.concatenate([points_ref[first], points_ref[second]], 1)
@@ -246,8 +251,15 @@
             out_ref[domain : domain + 1, start : start + size] = total * scale
 
 
-def first_kernel(plan, scale, lists_ref, mine_ref, theirs_ref, comp_ref,
-                 out_ref, rim_ref, state_ref, points_ref, kept_ref, turned_ref, xs, acc, cs):
+def first_kernel(plan, scale, ints_any, other_any, mine_ref, theirs_ref, comp_ref,
+                 out_ref, rim_ref, state_ref, points_ref, kept_ref, turned_ref, lists_ref, xs, acc, cs,
+                 ints, other_ints, waiting, sems):
+    copies = [
+        pltpu.make_async_copy(ints_any, ints, sems.at[0]),
+        pltpu.make_async_copy(other_any, other_ints, sems.at[1]),
+    ]
+    for copy in copies:
+        copy.start()
     core = lax.axis_index("core")
     for tile in range(plan.own):
         lanes = slice(tile * plan.lanes, (tile + 1) * plan.lanes)
@@ -260,7 +272,10 @@
             turned_ref[domain, start : start + size, :] = cs[
                 domain, :, start : start + size
             ].T.astype(bf16)
-    sum_gaussians(plan, scale, lists_ref, state_ref, turned_ref, points_ref, out_ref, rim_ref, kept_ref,
+    for copy in copies:
+        copy.wait()
+    make_lists(plan, ints, other_ints, lists_ref, waiting)
+    sum_gaussians(plan, scale, lists_ref, None, state_ref, turned_ref, points_ref, out_ref, rim_ref, kept_ref,
                   xs, acc)
 
 
@@ -271,15 +286,17 @@
         yield old_ref[i] + time_step * v, v
 
 
-def next_kernel(plan, scale, lists_ref, old_ref, force_ref, swapped_ref, turned_ref,
-                out_ref, rim_ref, state_ref, points_ref, kept_ref, xs, acc):
+def next_kernel(plan, scale, lists_any, old_ref, force_ref, swapped_ref, turned_ref,
+                out_ref, rim_ref, state_ref, points_ref, kept_ref, xs, acc, lists_ref, sem):
+    copy = pltpu.make_async_copy(lists_any, lists_ref, sem)
+    copy.start()
     for i, (x, v) in enumerate(stepped(old_ref, force_ref, swapped_ref)):
         state_ref[i] = x
         state_ref[3 + i] = v
     state_ref[6] = old_ref[6]
     state_ref[7] = old_ref[7]
-    sum_gaussians(plan, scale, lists_ref, state_ref, turned_ref, points_ref, out_ref, rim_ref, kept_ref,
-                  xs, acc)
+    sum_gaussians(plan, scale, lists_ref, copy, state_ref, turned_ref, points_ref, out_ref, rim_ref,
+                  kept_ref, xs, acc)
 
 
 def tree_sum(refs):
@@ -315,13 +332,16 @@
         map_ref[:, high] = jnp.where(first, got, keep)
 
 
-def pair_kernel(plan, gain, lists_ref, state_ref, far_ref, points_ref, out_ref, table, cs, rs, rows,
-                turned):
+def pair_kernel(plan, gain, lists_any, state_ref, far_ref, points_ref, out_ref, table, cs, rs, rows,
+                turned, lists_ref, sem):
+    copy = pltpu.make_async_copy(lists_any, lists_ref, sem)
+    copy.start()
     own, near, listed = plan.own, plan.near, plan.listed
     core = lax.axis_index("core")
     base = pl.multiple_of(core * own, own)
     extent = own + 2 * listed
     table[...] = jnp.zeros_like(table)
+    copy.wait()
     for i, source in enumerate((0, 1, 2, 6)):
         table[i, 0:own, :] = state_ref[source, pl.ds(base, own), :]
         for k in range(listed):
@@ -351,8 +371,10 @@
             out_ref[i, tile : tile + 1, :] = strength * push
 
 
-def push_kernel(plan, gain, replicas, lists_ref, state_ref, comp_ref, pair_ref, kept_ref, *refs):
-    parts, (out_ref, rs, rows, means, sums) = refs[:-5], refs[-5:]
+def push_kernel(plan, gain, replicas, lists_any, state_ref, comp_ref, pair_ref, kept_ref, *refs):
+    parts, (out_ref, rs, rows, means, sums, lists_ref, sem) = refs[:-7], refs[-7:]
+    copy = pltpu.make_async_copy(lists_any, lists_ref, sem)
+    copy.start()
     tiles, lanes = plan.tiles, plan.lanes
     mean = tree_sum(parts) / replicas
     for n in range(plan.half // lanes):
@@ -362,6 +384,7 @@
     store_rows(rs, pull_rows([comp_ref[:, i, :] for i in range(3)], coefficient))
     rows[...] = rs[...].astype(bf16)
     sums[...] = jnp.zeros_like(sums)
+    copy.wait()
 
     def one_pair(place, owner, first, second):
         total = None
@@ -400,6 +423,7 @@
 VMEM = pl.BlockSpec(memory_space=pltpu.VMEM)
 SMEM = pl.BlockSpec(memory_space=pltpu.SMEM)
 HBM = pl.BlockSpec(memory_space=pltpu.HBM)
+ANY = pl.BlockSpec(memory_space=pl.ANY)
 
 
 def shape(*dims, dtype=f32):
@@ -415,20 +439,16 @@
             yield pltpu.VMEM(dims, dtype)
 
 
-def call(kernel, lists, args, outs, scratch=(), limit=16, spaces=None, out_spaces=None):
+def call(kernel, args, outs, scratch=(), limit=16, spaces=None, out_spaces=None):
     many = isinstance(outs, (list, tuple))
-    return pallas(kernel, lists, args, outs, scratch, limit, spaces, out_spaces, many)
-
-
-def pallas(kernel, lists, args, outs, scratch, limit, spaces, out_spaces, many):
     return pl.pallas_call(
         kernel,
         out_shape=tuple(outs) if many else outs,
-        in_specs=[SMEM] * len(lists) + (spaces or [VMEM] * len(args)),
-        out_specs=tuple(out_spaces or [VMEM] * len(outs)) if many else (out_spaces or VMEM),
+        in_specs=spaces or [VMEM] * len(args),
+        out_specs=tuple(out_spaces or [VMEM] * len(outs)) if many else VMEM,
         scratch_shapes=list(with_types(scratch)),
-        compiler_params=pltpu.CompilerParams(vmem_limit_bytes=limit and limit << 20),
-    )(*lists, *args)
+        compiler_params=pltpu.CompilerParams(vmem_limit_bytes=limit << 20),
+    )(*args)
 
 
 class Plan:
@@ -496,24 +516,17 @@
     int_rows = -(-(owned + halo_tiles.shape[1] + 2 + own) // 8) * 8
     state_own, comp_send, ints = call(
         pack_kernel,
-        [],
-        args,
+        [pltpu.with_memory_space_constraint(arg, pltpu.HBM) for arg in args],
         [shape(8, own * lanes), shape(domains, 6, half), shape(int_rows, lanes, dtype=jnp.int32)],
         [(arg.shape, arg.dtype) for arg in args] + [pltpu.SemaphoreType.DMA((len(args),))],
-        limit=60,
+        limit=8,
         spaces=[HBM] * len(args),
     )
     comps = lax.all_to_all(comp_send, ("z", "core"), 0, 0, tiled=True)
     other_ints = swap_cores(ints)
     width = -(-((tiles * owned + domains) // 2 + UNROLL + 1) // lanes) * lanes
-    lists = call(
-        functools.partial(list_kernel, plan),
-        [ints, other_ints],
-        [],
-        shape(4 + plan.near, width, dtype=jnp.int32),
-        [pltpu.SMEM((domains,), jnp.int32)],
-        out_spaces=SMEM,
-    )
+    lists_shape = shape(4 + plan.near, width, dtype=jnp.int32)
+    scalars = [pltpu.SMEM(lists_shape.shape, jnp.int32), pltpu.SemaphoreType.DMA]
     small = few(replicas, heights)
     if small:
         others = exchange(state_own, "rep")
@@ -525,7 +538,7 @@
             )
         ]
     chosen = call(
-        functools.partial(choose_kernel, plan), [ints], [state_own] + others, shape(8, own * lanes)
+        functools.partial(choose_kernel, plan), [ints, state_own] + others, shape(8, own * lanes)
     )
     chosen_other = swap_cores(chosen)
 
@@ -548,26 +561,28 @@
     scratch = [(tiles + 1, DEPTH, lanes), (domains, half, lanes)]
     for step in range(STEPS):
         if step == 0:
-            partial, rim, state, points, kept, turned = call(
+            partial, rim, state, points, kept, turned, lists = call(
                 functools.partial(first_kernel, plan, scale),
-                [lists],
-                [chosen, chosen_other, comps],
-                outs + [shape(domains, half, DEPTH, dtype=bf16)],
-                scratch + [(domains, DEPTH, half)],
+                [ints, other_ints, chosen, chosen_other, comps],
+                outs + [shape(domains, half, DEPTH, dtype=bf16), lists_shape],
+                scratch
+                + [(domains, DEPTH, half), pltpu.SMEM(ints.shape, jnp.int32),
+                   pltpu.SMEM(ints.shape, jnp.int32), pltpu.SMEM((domains,), jnp.int32),
+                   pltpu.SemaphoreType.DMA((2,))],
+                spaces=[ANY, ANY] + [VMEM] * 3,
+                out_spaces=[VMEM] * 6 + [SMEM],
             )
         else:
             partial, rim, state, points, kept = call(
                 functools.partial(next_kernel, plan, scale),
-                [lists],
-                [state, force, swapped, turned],
+                [lists, state, force, swapped, turned],
                 outs,
-                scratch,
+                scratch + scalars,
+                spaces=[ANY] + [VMEM] * 4,
             )
         far = lax.ppermute(rim, ("z", "core"), onward)
         if small:
-            partial = call(
-                add_kernel, [], [partial] + exchange(partial, "rep"), shape(domains, half)
-            )
+            partial = call(add_kernel, [partial] + exchange(partial, "rep"), shape(domains, half))
             parts = [partial] + exchange(partial, "z")
         else:
             pieces = lax.all_to_all(partial.reshape(group, -1), ("rep", "z"), 0, 0, tiled=True)
@@ -580,25 +595,24 @@
             ]
         pair = call(
             functools.partial(pair_kernel, plan, pair_gain),
-            [lists],
-            [state, far, points],
+            [lists, state, far, points],
             shape(3, own, lanes),
             [(4, padded, lanes), (padded, DEPTH, lanes), (padded, ROWS, lanes),
-             ((padded, ROWS, lanes), bf16), ((padded, lanes, DEPTH), bf16)],
+             ((padded, ROWS, lanes), bf16), ((padded, lanes, DEPTH), bf16)] + scalars,
+            spaces=[ANY] + [VMEM] * 3,
         )
         force = call(
             functools.partial(push_kernel, plan, map_gain, float(replicas)),
-            [lists],
-            [state, comps, pair, kept] + parts,
+            [lists, state, comps, pair, kept] + parts,
             shape(4, tiles, lanes),
             [(domains, ROWS, half), ((domains, ROWS, half), bf16), (half // lanes, domains, lanes),
-             (tiles + 1, ROWS, lanes)],
+             (tiles + 1, ROWS, lanes)] + scalars,
+            spaces=[ANY] + [VMEM] * (4 + len(parts)),
         )
         swapped = swap_cores(force)
 
     new_x, new_v, model_map = call(
         functools.partial(finish_kernel, plan),
-        [],
         [state, force, swapped],
         [shape(3, 1, own * lanes), shape(3, 1, own * lanes), shape(1, components)],
         [(6, tiles, lanes)],

time: 87.4 us -> 82.3 us (0.942)
  Pallas kernels: 34.2 us -> 31.6 us
  local copies, waits for them, and re-layouts: 2.15 us -> 0 us
    pallas_call x12 -> x11, Pallas kernels: 34.2 us -> 31.6 us  [call(): pl.pallas_call(kernel, out_shape=tuple(outs) if many else outs, in_specs=...]
    unnamed x6 -> x0, local copies, waits for them, and re-layouts: 2.15 us -> none
  transfers between devices with their start and end apart: 22 -> 22, of which waited for: 14 -> 14; matrix products, arithmetic and copies ran while one was open for 0% -> 0% of each run, Pallas kernels for 8% -> 5%
where the time goes in v6:
time: 82.3 us; the launch traced here: 82 us
  Pallas kernels  31.6 us (38%)
  starting transfers between devices  28 us (34%)
  waiting for transfers between devices  21.5 us (26%)
    pallas_call x11, Pallas kernels, call(): pl.pallas_call(kernel, out_shape=tuple(outs) if many else outs, in_specs=...  31.6 us
    ppermute x15, starting transfers between devices, exchange(): others.append(lax.ppermute(value, axis, [(i, i ^ n) for i in range(count)]))  19.6 us
    ppermute x2, waiting for transfers between devices, program(): far = lax.ppermute(rim, ('z', 'core'), onward)  9.49 us
    ppermute x15, waiting for transfers between devices, exchange(): others.append(lax.ppermute(value, axis, [(i, i ^ n) for i in range(count)]))  8.81 us
    all_to_all x1, starting transfers between devices, program(): comps = lax.all_to_all(comp_send, ('z', 'core'), 0, 0, tiled=True)  6.37 us
    ppermute x4, waiting for transfers between devices, swap_cores(): return lax.ppermute(value, 'core', [(0, 1), (1, 0)])  3.22 us
  transfers between devices with their start and end apart: 22, of which 14 were waited for; matrix products, arithmetic and copies ran while one was open for 0% of the time, Pallas kernels for 5%

profile of v6, /device:TPU:0, one launch (start us, length us, event | category | flops | bytes accessed | tf_op | source)
XLA Modules:
  0.0 82.0 jit_solution(8265597867899270642)
XLA Ops:
  0.6 1.6 %shard_map.148 = (f32[8,1024]{1,0:T(8,128)S(1)}, f32[8,6,512]{2,1,0:T(8,128)}, s32[16,128]{1,0:T(8,128)S(1)}) custom-call(f32[3,1,1024]{2,1,0:T(1,128)} %bitcast.13, f32[3,1,1024]{2,1,0:T(1,128)} %bitcast.14, f32[1,1024]{1,0:T(1,128)} %bitcast.15, f32[1,1024]{1,0:T(1,128)} %bitcast.16, f32[3,1024]{1,0:T(4,128)} %centre_hbm.1, f32[1,1024]{1,0:T(1,128)} %bitcast.17, ...), custom_call_target="tpu_custom_call" | custom-call | tf_op jit(solution)/shard_map/pallas_call | solution.py:444
  2.3 6.4 %all-to-all-start = ((f32[8,6,512]{2,1,0:T(8,128)}), f32[8,6,512]{2,1,0:T(8,128)S(1)}, u32[]{:S(2)}, u32[]{:S(2)}) async-start(f32[8,6,512]{2,1,0:T(8,128)} %get-tuple-element.23), calls=%async_computation | async-start | bytes 262144 | tf_op jit(solution)/shard_map/all_to_all | solution.py:525
  8.6 2.4 %collective-permute-start.3 = (f32[8,1024]{1,0:T(8,128)S(1)}, f32[8,1024]{1,0:T(8,128)S(1)}, u32[]{:S(2)}, u32[]{:S(2)}) collective-permute-start(f32[8,1024]{1,0:T(8,128)S(1)} %get-tuple-element.22.mine_ref), channel_id=1, source_target_pairs={{0,24},{8,16},{16,8},{24,0},{1,25},{9,17},{17,9},{25,1},{2,26},{10... | collective-permute-start | bytes 98312 | tf_op jit(solution)/shard_map/ppermute | solution.py:470
  11.6 0.5 collective-permute-start.1
  12.1 1.3 %collective-permute-done.3.refs_2_ = f32[8,1024]{1,0:T(8,128)S(1)} collective-permute-done((f32[8,1024]{1,0:T(8,128)S(1)}, f32[8,1024]{1,0:T(8,128)S(1)}, u32[]{:S(2)}, u32[]{:S(2)}) %collective-permute-start.3) | collective-permute-done | bytes 32800 | tf_op jit(solution)/shard_map/ppermute | solution.py:470
  13.4 1.5 %collective-permute-done.2.refs_1_ = f32[8,1024]{1,0:T(8,128)S(1)} collective-permute-done((f32[8,1024]{1,0:T(8,128)S(1)}, f32[8,1024]{1,0:T(8,128)S(1)}, u32[]{:S(2)}, u32[]{:S(2)}) %collective-permute-start.2) | collective-permute-done | bytes 32800 | tf_op jit(solution)/shard_map/ppermute | solution.py:470
  16.1 0.8 %collective-permute-done.other_any = s32[16,128]{1,0:T(8,128)S(1)} collective-permute-done((s32[16,128]{1,0:T(8,128)S(1)}, s32[16,128]{1,0:T(8,128)S(1)}, u32[]{:S(2)}, u32[]{:S(2)}) %collective-permute-start) | collective-permute-done | bytes 8224 | tf_op jit(solution)/shard_map/ppermute | solution.py:459
  16.9 7.7 %shard_map.150 = (f32[8,512]{1,0:T(8,128)S(1)}, f32[8,128]{1,0:T(8,128)S(1)}, f32[8,16,128]{2,1,0:T(8,128)S(1)}, bf16[17,32,128]{2,1,0:T(8,128)(2,1)S(1)}, f32[3...) custom-call(s32[16,128]{1,0:T(8,128)S(1)} %get-tuple-element.21.ints_ref.ints_any, ...), custom_call_target="tpu_custom_call" | custom-call | tf_op jit(solution)/shard_map/pallas_call | solution.py:444
  24.6 1.6 %collective-permute-start.8 = (f32[8,512]{1,0:T(8,128)S(1)}, f32[8,512]{1,0:T(8,128)S(1)}, u32[]{:S(2)}, u32[]{:S(2)}) collective-permute-start(f32[8,512]{1,0:T(8,128)S(1)} %get-tuple-element.29.refs_0_), channel_id=1, source_target_pairs={{0,24},{8,16},{16,8},{24,0},{1,25},{9,17},{17,9},{25,1},{2,26},{10... | collective-permute-start | bytes 49160 | tf_op jit(solution)/shard_map/ppermute | solution.py:470
  26.7 1.5 %collective-permute-start.6 = (f32[8,512]{1,0:T(8,128)S(1)}, f32[8,512]{1,0:T(8,128)S(1)}, u32[]{:S(2)}, u32[]{:S(2)}) collective-permute-start(f32[8,512]{1,0:T(8,128)S(1)} %get-tuple-element.29.refs_0_), channel_id=1, source_target_pairs={{0,8},{8,0},{16,24},{24,16},{1,9},{9,1},{17,25},{25,17},{2,10},{10... | collective-permute-start | bytes 49160 | tf_op jit(solution)/shard_map/ppermute | solution.py:470
  28.2 1.1 %collective-permute-done.8.refs_3_ = f32[8,512]{1,0:T(8,128)S(1)} collective-permute-done((f32[8,512]{1,0:T(8,128)S(1)}, f32[8,512]{1,0:T(8,128)S(1)}, u32[]{:S(2)}, u32[]{:S(2)}) %collective-permute-start.8) | collective-permute-done | bytes 16416 | tf_op jit(solution)/shard_map/ppermute | solution.py:470
  29.3 0.6 collective-permute-done.7.refs_2_
  30.4 3.9 %collective-permute-start.11 = (f32[8,512]{1,0:T(8,128)S(1)}, f32[8,512]{1,0:T(8,128)S(1)}, u32[]{:S(2)}, u32[]{:S(2)}) collective-permute-start(f32[8,512]{1,0:T(8,128)S(1)} %shard_map.152.refs_0_), channel_id=1, source_target_pairs={{0,6},{2,4},{4,2},{6,0},{1,7},{3,5},{5,3},{7,1},{8,14},{10,12},{12... | collective-permute-start | bytes 49160 | tf_op jit(solution)/shard_map/ppermute | solution.py:470
  34.3 0.6 collective-permute-start.9
  35.0 1.4 %collective-permute-start.5 = (f32[8,128]{1,0:T(8,128)S(1)}, f32[8,128]{1,0:T(8,128)S(1)}, u32[]{:S(2)}, u32[]{:S(2)}) collective-permute-start(f32[8,128]{1,0:T(8,128)S(1)} %get-tuple-element.26), channel_id=1, source_target_pairs={{0,2},{2,4},{4,6},{6,0},{3,1},{5,3},{7,5},{1,7},{8,10},{10,12},{12... | collective-permute-start | bytes 12296 | tf_op jit(solution)/shard_map/ppermute | solution.py:583
  36.4 4.1 %collective-permute-done.5.far_ref = f32[8,128]{1,0:T(8,128)S(1)} collective-permute-done((f32[8,128]{1,0:T(8,128)S(1)}, f32[8,128]{1,0:T(8,128)S(1)}, u32[]{:S(2)}, u32[]{:S(2)}) %collective-permute-start.5) | collective-permute-done | bytes 4128 | tf_op jit(solution)/shard_map/ppermute | solution.py:583
  40.5 2.1 %shard_map.151.pair_ref = f32[3,8,128]{2,1,0:T(8,128)S(1)} custom-call(s32[10,128]{1,0:T(8,128)S(1)} %get-tuple-element.24.lists_any, f32[8,16,128]{2,1,0:T(8,128)S(1)} %get-tuple-element.25.state_ref.old_ref, f32[8,128]{1,0:T(8,128)S(1)} %collective-permute-done.5.far_ref, bf16[17,32,128]{2,1,0:T(8,128)(2,1)S(1)} %get-tuple-element.27.points_ref), custom_call_target="tpu_custom_call" | custom-call | tf_op jit(solution)/shard_map/pallas_call | solution.py:444
  42.6 5.7 %shard_map.153.force_ref = f32[4,16,128]{2,1,0:T(8,128)S(1)} custom-call(s32[10,128]{1,0:T(8,128)S(1)} %get-tuple-element.24.lists_any, f32[8,16,128]{2,1,0:T(8,128)S(1)} %get-tuple-element.25.state_ref.old_ref, f32[8,6,512]{2,1,0:T(8,128)S(1)} %all-to-all-done.comp_ref, f32[3,8,128]{2,1,0:T(8,128)S(1)} %shard_map.151.pair_ref, ...), custom_call_target="tpu_custom_call" | custom-call | tf_op jit(solution)/shard_map/pallas_call | solution.py:444
  48.4 1.2 %collective-permute-done.12.swapped_ref = f32[4,16,128]{2,1,0:T(8,128)S(1)} collective-permute-done((f32[4,16,128]{2,1,0:T(8,128)S(1)}, f32[4,16,128]{2,1,0:T(8,128)S(1)}, u32[]{:S(2)}, u32[]{:S(2)}) %collective-permute-start.12) | collective-permute-done | bytes 32800 | tf_op jit(solution)/shard_map/ppermute | solution.py:459
  49.6 6.1 %shard_map.154 = (f32[8,512]{1,0:T(8,128)S(1)}, f32[8,128]{1,0:T(8,128)S(1)}, f32[8,16,128]{2,1,0:T(8,128)S(1)}, bf16[17,32,128]{2,1,0:T(8,128)(2,1)S(1)}, f32[38,512,256]{2,1,0:T(8,128)S(1)}) custom-call(s32[10,128]{1,0:T(8,128)S(1)} %get-tuple-element.24.lists_any, f32[8,16,128]{2,1,0:T(8,128)S(1)} %get-tuple-element.25.state_ref.old_ref, ...), custom_call_target="tpu_custom_call" | custom-call | tf_op jit(solution)/shard_map/pallas_call | solution.py:444
  55.6 2.5 %collective-permute-start.16 = (f32[8,512]{1,0:T(8,128)S(1)}, f32[8,512]{1,0:T(8,128)S(1)}, u32[]{:S(2)}, u32[]{:S(2)}) collective-permute-start(f32[8,512]{1,0:T(8,128)S(1)} %get-tuple-element.35.refs_0_), channel_id=1, source_target_pairs={{0,24},{8,16},{16,8},{24,0},{1,25},{9,17},{17,9},{25,1},{2,26},{10... | collective-permute-start | bytes 49160 | tf_op jit(solution)/shard_map/ppermute | solution.py:470
  58.1 0.5 collective-permute-start.15
  58.6 0.6 collective-permute-start.14
  59.2 1.1 %collective-permute-done.16.refs_3_ = f32[8,512]{1,0:T(8,128)S(1)} collective-permute-done((f32[8,512]{1,0:T(8,128)S(1)}, f32[8,512]{1,0:T(8,128)S(1)}, u32[]{:S(2)}, u32[]{:S(2)}) %collective-permute-start.16) | collective-permute-done | bytes 16416 | tf_op jit(solution)/shard_map/ppermute | solution.py:470
  60.4 1.5 %collective-permute-done.15.refs_2_ = f32[8,512]{1,0:T(8,128)S(1)} collective-permute-done((f32[8,512]{1,0:T(8,128)S(1)}, f32[8,512]{1,0:T(8,128)S(1)}, u32[]{:S(2)}, u32[]{:S(2)}) %collective-permute-start.15) | collective-permute-done | bytes 16416 | tf_op jit(solution)/shard_map/ppermute | solution.py:470
  62.4 1.9 %collective-permute-start.19 = (f32[8,512]{1,0:T(8,128)S(1)}, f32[8,512]{1,0:T(8,128)S(1)}, u32[]{:S(2)}, u32[]{:S(2)}) collective-permute-start(f32[8,512]{1,0:T(8,128)S(1)} %shard_map.156.refs_0_), channel_id=1, source_target_pairs={{0,6},{2,4},{4,2},{6,0},{1,7},{3,5},{5,3},{7,1},{8,14},{10,12},{12... | collective-permute-start | bytes 49160 | tf_op jit(solution)/shard_map/ppermute | solution.py:470
  64.3 2.6 %collective-permute-start.17 = (f32[8,512]{1,0:T(8,128)S(1)}, f32[8,512]{1,0:T(8,128)S(1)}, u32[]{:S(2)}, u32[]{:S(2)}) collective-permute-start(f32[8,512]{1,0:T(8,128)S(1)} %shard_map.156.refs_0_), channel_id=1, source_target_pairs={{0,2},{2,0},{4,6},{6,4},{1,3},{3,1},{5,7},{7,5},{8,10},{10,8},{12,... | collective-permute-start | bytes 49160 | tf_op jit(solution)/shard_map/ppermute | solution.py:470
  66.9 5.4 %collective-permute-done.13.far_ref = f32[8,128]{1,0:T(8,128)S(1)} collective-permute-done((f32[8,128]{1,0:T(8,128)S(1)}, f32[8,128]{1,0:T(8,128)S(1)}, u32[]{:S(2)}, u32[]{:S(2)}) %collective-permute-start.13) | collective-permute-done | bytes 4128 | tf_op jit(solution)/shard_map/ppermute | solution.py:583
  72.2 2.1 %shard_map.155.pair_ref = f32[3,8,128]{2,1,0:T(8,128)S(1)} custom-call(s32[10,128]{1,0:T(8,128)S(1)} %get-tuple-element.24.lists_any, f32[8,16,128]{2,1,0:T(8,128)S(1)} %get-tuple-element.31.state_ref.old_ref, f32[8,128]{1,0:T(8,128)S(1)} %collective-permute-done.13.far_ref, bf16[17,32,128]{2,1,0:T(8,128)(2,1)S(1)} %get-tuple-element.33.points_ref), custom_call_target="tpu_custom_call" | custom-call | tf_op jit(solution)/shard_map/pallas_call | solution.py:444
  74.4 5.7 %shard_map.157.mine_ref = f32[4,16,128]{2,1,0:T(8,128)S(1)} custom-call(s32[10,128]{1,0:T(8,128)S(1)} %get-tuple-element.24.lists_any, f32[8,16,128]{2,1,0:T(8,128)S(1)} %get-tuple-element.31.state_ref.old_ref, f32[8,6,512]{2,1,0:T(8,128)S(1)} %all-to-all-done.comp_ref, f32[3,8,128]{2,1,0:T(8,128)S(1)} %shard_map.155.pair_ref, ...), custom_call_target="tpu_custom_call" | custom-call | tf_op jit(solution)/shard_map/pallas_call | solution.py:444
  80.1 1.2 %collective-permute-done.20.theirs_ref = f32[4,16,128]{2,1,0:T(8,128)S(1)} collective-permute-done((f32[4,16,128]{2,1,0:T(8,128)S(1)}, f32[4,16,128]{2,1,0:T(8,128)S(1)}, u32[]{:S(2)}, u32[]{:S(2)}) %collective-permute-start.20) | collective-permute-done | bytes 32800 | tf_op jit(solution)/shard_map/ppermute | solution.py:459
  81.3 0.6 shard_map.158
  (23 shorter events, 3.3 us)
Async XLA Ops:
  2.3 14.7 %all-to-all-start = ((f32[8,6,512]{2,1,0:T(8,128)}), f32[8,6,512]{2,1,0:T(8,128)S(1)}, u32[]{:S(2)}, u32[]{:S(2)}) async-start(f32[8,6,512]{2,1,0:T(8,128)} %get-tuple-element.23), calls=%async_computation | async-start | bytes 262144 | tf_op jit(solution)/shard_map/all_to_all | solution.py:525
  8.6 4.8 %collective-permute-start.3 = (f32[8,1024]{1,0:T(8,128)S(1)}, f32[8,1024]{1,0:T(8,128)S(1)}, u32[]{:S(2)}, u32[]{:S(2)}) collective-permute-start(f32[8,1024]{1,0:T(8,128)S(1)} %get-tuple-element.22.mine_ref), channel_id=1, source_target_pairs={{0,24},{8,16},{16,8},{24,0},{1,25},{9,17},{17,9},{25,1},{2,26},{10... | collective-permute-start | bytes 98312 | tf_op jit(solution)/shard_map/ppermute | solution.py:470
  11.1 3.9 %collective-permute-start.2 = (f32[8,1024]{1,0:T(8,128)S(1)}, f32[8,1024]{1,0:T(8,128)S(1)}, u32[]{:S(2)}, u32[]{:S(2)}) collective-permute-start(f32[8,1024]{1,0:T(8,128)S(1)} %get-tuple-element.22.mine_ref), channel_id=1, source_target_pairs={{0,16},{8,24},{16,0},{24,8},{1,17},{9,25},{17,1},{25,9},{2,18},{10... | collective-permute-start | bytes 98312 | tf_op jit(solution)/shard_map/ppermute | solution.py:470
  11.6 3.9 %collective-permute-start.1 = (f32[8,1024]{1,0:T(8,128)S(1)}, f32[8,1024]{1,0:T(8,128)S(1)}, u32[]{:S(2)}, u32[]{:S(2)}) collective-permute-start(f32[8,1024]{1,0:T(8,128)S(1)} %get-tuple-element.22.mine_ref), channel_id=1, source_target_pairs={{0,8},{8,0},{16,24},{24,16},{1,9},{9,1},{17,25},{25,17},{2,10},{10... | collective-permute-start | bytes 98312 | tf_op jit(solution)/shard_map/ppermute | solution.py:470
  15.6 1.4 %collective-permute-start.4 = (f32[8,1024]{1,0:T(8,128)S(1)}, f32[8,1024]{1,0:T(8,128)S(1)}, u32[]{:S(2)}, u32[]{:S(2)}) collective-permute-start(f32[8,1024]{1,0:T(8,128)S(1)} %shard_map.149.mine_ref), channel_id=1, source_target_pairs={{0,1},{1,0},{2,3},{3,2},{4,5},{5,4},{6,7},{7,6},{8,9},{9,8},{10,11... | collective-permute-start | bytes 98312 | tf_op jit(solution)/shard_map/ppermute | solution.py:459
  15.6 1.3 %collective-permute-start = (s32[16,128]{1,0:T(8,128)S(1)}, s32[16,128]{1,0:T(8,128)S(1)}, u32[]{:S(2)}, u32[]{:S(2)}) collective-permute-start(s32[16,128]{1,0:T(8,128)S(1)} %get-tuple-element.21.ints_ref.ints_any), channel_id=1, source_target_pairs={{0,1},{1,0},{2,3},{3,2},{4,5},{5,4},{6,7},{7,6},{8,9},{9,8},{10,11... | collective-permute-start | bytes 24584 | tf_op jit(solution)/shard_map/ppermute | solution.py:459
  24.6 4.7 %collective-permute-start.8 = (f32[8,512]{1,0:T(8,128)S(1)}, f32[8,512]{1,0:T(8,128)S(1)}, u32[]{:S(2)}, u32[]{:S(2)}) collective-permute-start(f32[8,512]{1,0:T(8,128)S(1)} %get-tuple-element.29.refs_0_), channel_id=1, source_target_pairs={{0,24},{8,16},{16,8},{24,0},{1,25},{9,17},{17,9},{25,1},{2,26},{10... | collective-permute-start | bytes 49160 | tf_op jit(solution)/shard_map/ppermute | solution.py:470
  26.2 3.7 %collective-permute-start.7 = (f32[8,512]{1,0:T(8,128)S(1)}, f32[8,512]{1,0:T(8,128)S(1)}, u32[]{:S(2)}, u32[]{:S(2)}) collective-permute-start(f32[8,512]{1,0:T(8,128)S(1)} %get-tuple-element.29.refs_0_), channel_id=1, source_target_pairs={{0,16},{8,24},{16,0},{24,8},{1,17},{9,25},{17,1},{25,9},{2,18},{10... | collective-permute-start | bytes 49160 | tf_op jit(solution)/shard_map/ppermute | solution.py:470
  26.7 3.7 %collective-permute-start.6 = (f32[8,512]{1,0:T(8,128)S(1)}, f32[8,512]{1,0:T(8,128)S(1)}, u32[]{:S(2)}, u32[]{:S(2)}) collective-permute-start(f32[8,512]{1,0:T(8,128)S(1)} %get-tuple-element.29.refs_0_), channel_id=1, source_target_pairs={{0,8},{8,0},{16,24},{24,16},{1,9},{9,1},{17,25},{25,17},{2,10},{10... | collective-permute-start | bytes 49160 | tf_op jit(solution)/shard_map/ppermute | solution.py:470
  30.4 12.2 %collective-permute-start.11 = (f32[8,512]{1,0:T(8,128)S(1)}, f32[8,512]{1,0:T(8,128)S(1)}, u32[]{:S(2)}, u32[]{:S(2)}) collective-permute-start(f32[8,512]{1,0:T(8,128)S(1)} %shard_map.152.refs_0_), channel_id=1, source_target_pairs={{0,6},{2,4},{4,2},{6,0},{1,7},{3,5},{5,3},{7,1},{8,14},{10,12},{12... | collective-permute-start | bytes 49160 | tf_op jit(solution)/shard_map/ppermute | solution.py:470
  34.3 8.3 %collective-permute-start.10 = (f32[8,512]{1,0:T(8,128)S(1)}, f32[8,512]{1,0:T(8,128)S(1)}, u32[]{:S(2)}, u32[]{:S(2)}) collective-permute-start(f32[8,512]{1,0:T(8,128)S(1)} %shard_map.152.refs_0_), channel_id=1, source_target_pairs={{0,4},{2,6},{4,0},{6,2},{1,5},{3,7},{5,1},{7,3},{8,12},{10,14},{12... | collective-permute-start | bytes 49160 | tf_op jit(solution)/shard_map/ppermute | solution.py:470
  34.3 8.3 %collective-permute-start.9 = (f32[8,512]{1,0:T(8,128)S(1)}, f32[8,512]{1,0:T(8,128)S(1)}, u32[]{:S(2)}, u32[]{:S(2)}) collective-permute-start(f32[8,512]{1,0:T(8,128)S(1)} %shard_map.152.refs_0_), channel_id=1, source_target_pairs={{0,2},{2,0},{4,6},{6,4},{1,3},{3,1},{5,7},{7,5},{8,10},{10,8},{12,... | collective-permute-start | bytes 49160 | tf_op jit(solution)/shard_map/ppermute | solution.py:470
  35.0 5.5 %collective-permute-start.5 = (f32[8,128]{1,0:T(8,128)S(1)}, f32[8,128]{1,0:T(8,128)S(1)}, u32[]{:S(2)}, u32[]{:S(2)}) collective-permute-start(f32[8,128]{1,0:T(8,128)S(1)} %get-tuple-element.26), channel_id=1, source_target_pairs={{0,2},{2,4},{4,6},{6,0},{3,1},{5,3},{7,5},{1,7},{8,10},{10,12},{12... | collective-permute-start | bytes 12296 | tf_op jit(solution)/shard_map/ppermute | solution.py:583
  48.3 1.3 %collective-permute-start.12 = (f32[4,16,128]{2,1,0:T(8,128)S(1)}, f32[4,16,128]{2,1,0:T(8,128)S(1)}, u32[]{:S(2)}, u32[]{:S(2)}) collective-permute-start(f32[4,16,128]{2,1,0:T(8,128)S(1)} %shard_map.153.force_ref), channel_id=1, source_target_pairs={{0,1},{1,0},{2,3},{3,2},{4,5},{5,4},{6,7},{7,6},{8,9},{9,8},{10,11... | collective-permute-start | bytes 98312 | tf_op jit(solution)/shard_map/ppermute | solution.py:459
  55.6 4.7 %collective-permute-start.16 = (f32[8,512]{1,0:T(8,128)S(1)}, f32[8,512]{1,0:T(8,128)S(1)}, u32[]{:S(2)}, u32[]{:S(2)}) collective-permute-start(f32[8,512]{1,0:T(8,128)S(1)} %get-tuple-element.35.refs_0_), channel_id=1, source_target_pairs={{0,24},{8,16},{16,8},{24,0},{1,25},{9,17},{17,9},{25,1},{2,26},{10... | collective-permute-start | bytes 49160 | tf_op jit(solution)/shard_map/ppermute | solution.py:470
  58.1 3.7 %collective-permute-start.15 = (f32[8,512]{1,0:T(8,128)S(1)}, f32[8,512]{1,0:T(8,128)S(1)}, u32[]{:S(2)}, u32[]{:S(2)}) collective-permute-start(f32[8,512]{1,0:T(8,128)S(1)} %get-tuple-element.35.refs_0_), channel_id=1, source_target_pairs={{0,16},{8,24},{16,0},{24,8},{1,17},{9,25},{17,1},{25,9},{2,18},{10... | collective-permute-start | bytes 49160 | tf_op jit(solution)/shard_map/ppermute | solution.py:470
  58.6 3.7 %collective-permute-start.14 = (f32[8,512]{1,0:T(8,128)S(1)}, f32[8,512]{1,0:T(8,128)S(1)}, u32[]{:S(2)}, u32[]{:S(2)}) collective-permute-start(f32[8,512]{1,0:T(8,128)S(1)} %get-tuple-element.35.refs_0_), channel_id=1, source_target_pairs={{0,8},{8,0},{16,24},{24,16},{1,9},{9,1},{17,25},{25,17},{2,10},{10... | collective-permute-start | bytes 49160 | tf_op jit(solution)/shard_map/ppermute | solution.py:470
  62.4 12.0 %collective-permute-start.19 = (f32[8,512]{1,0:T(8,128)S(1)}, f32[8,512]{1,0:T(8,128)S(1)}, u32[]{:S(2)}, u32[]{:S(2)}) collective-permute-start(f32[8,512]{1,0:T(8,128)S(1)} %shard_map.156.refs_0_), channel_id=1, source_target_pairs={{0,6},{2,4},{4,2},{6,0},{1,7},{3,5},{5,3},{7,1},{8,14},{10,12},{12... | collective-permute-start | bytes 49160 | tf_op jit(solution)/shard_map/ppermute | solution.py:470
  64.3 10.1 %collective-permute-start.18 = (f32[8,512]{1,0:T(8,128)S(1)}, f32[8,512]{1,0:T(8,128)S(1)}, u32[]{:S(2)}, u32[]{:S(2)}) collective-permute-start(f32[8,512]{1,0:T(8,128)S(1)} %shard_map.156.refs_0_), channel_id=1, source_target_pairs={{0,4},{2,6},{4,0},{6,2},{1,5},{3,7},{5,1},{7,3},{8,12},{10,14},{12... | collective-permute-start | bytes 49160 | tf_op jit(solution)/shard_map/ppermute | solution.py:470
  64.3 10.1 %collective-permute-start.17 = (f32[8,512]{1,0:T(8,128)S(1)}, f32[8,512]{1,0:T(8,128)S(1)}, u32[]{:S(2)}, u32[]{:S(2)}) collective-permute-start(f32[8,512]{1,0:T(8,128)S(1)} %shard_map.156.refs_0_), channel_id=1, source_target_pairs={{0,2},{2,0},{4,6},{6,4},{1,3},{3,1},{5,7},{7,5},{8,10},{10,8},{12,... | collective-permute-start | bytes 49160 | tf_op jit(solution)/shard_map/ppermute | solution.py:470
  66.8 5.4 %collective-permute-start.13 = (f32[8,128]{1,0:T(8,128)S(1)}, f32[8,128]{1,0:T(8,128)S(1)}, u32[]{:S(2)}, u32[]{:S(2)}) collective-permute-start(f32[8,128]{1,0:T(8,128)S(1)} %get-tuple-element.32), channel_id=1, source_target_pairs={{0,2},{2,4},{4,6},{6,0},{3,1},{5,3},{7,5},{1,7},{8,10},{10,12},{12... | collective-permute-start | bytes 12296 | tf_op jit(solution)/shard_map/ppermute | solution.py:583
  80.0 1.3 %collective-permute-start.20 = (f32[4,16,128]{2,1,0:T(8,128)S(1)}, f32[4,16,128]{2,1,0:T(8,128)S(1)}, u32[]{:S(2)}, u32[]{:S(2)}) collective-permute-start(f32[4,16,128]{2,1,0:T(8,128)S(1)} %shard_map.157.mine_ref), channel_id=1, source_target_pairs={{0,1},{1,0},{2,3},{3,2},{4,5},{5,4},{6,7},{7,6},{8,9},{9,8},{10,11... | collective-permute-start | bytes 98312 | tf_op jit(solution)/shard_map/ppermute | solution.py:459

commit v7 on v6

--- a/solution.py
+++ b/solution.py
@@ -13,7 +13,7 @@
 DEPTH = 32
 ROWS = 16
 CHUNK = 256
-UNROLL = 2
+UNROLL = 4
 FAR_SQUARE = 1048576.0
 
 time_step = 0.5
@@ -102,8 +102,8 @@
 
 
 def pack_kernel(pos_hbm, vel_hbm, charge_hbm, mass_hbm, centre_hbm, width_hbm, density_hbm,
-                error_hbm, owners_hbm, halo_hbm, pairs_hbm, partner_hbm, decision_hbm, state_ref,
-                comp_ref, ints_ref, pos_ref, vel_ref, charge_ref, mass_ref, centre_ref, width_ref,
+                error_hbm, owners_hbm, halo_hbm, pairs_hbm, partner_hbm, decision_hbm, keep_ref,
+                give_ref, ints_ref, pos_ref, vel_ref, charge_ref, mass_ref, centre_ref, width_ref,
                 density_ref, error_ref, owners_ref, halo_ref, pairs_ref, partner_ref, decision_ref,
                 sems):
     sources = (pos_hbm, vel_hbm, charge_hbm, mass_hbm, centre_hbm, width_hbm, density_hbm,
@@ -118,12 +118,6 @@
         copy.start()
     for copy in copies:
         copy.wait()
-    half = comp_ref.shape[2]
-    for i in range(3):
-        state_ref[i : i + 1, :] = pos_ref[i]
-        state_ref[3 + i : 4 + i, :] = vel_ref[i]
-    state_ref[6:7, :] = charge_ref[...]
-    state_ref[7:8, :] = mass_ref[...]
     owned, own = owners_ref.shape
     _, sides, listed = halo_ref.shape
     ints_ref[...] = jnp.zeros_like(ints_ref)
@@ -134,31 +128,66 @@
     ints_ref[last + 1 : last + 2, 0 : decision_ref.shape[1]] = decision_ref[...]
     rows, near = pairs_ref.shape
     ints_ref[last + 2 : last + 2 + rows, 0:near] = pairs_ref[...]
-    for row in range(comp_ref.shape[0]):
-        part = pl.ds((row % CORES) * half, half)
-        comp_ref[row, 0:3, :] = centre_ref[:, part]
-        comp_ref[row, 3:4, :] = width_ref[:, part]
-        comp_ref[row, 4:5, :] = density_ref[:, part]
-        comp_ref[row, 5:6, :] = error_ref[:, part]
-
-
-def choose_kernel(plan, ints_ref, mine_ref, *refs):
-    others, out_ref = refs[:-1], refs[-1]
+    core = lax.axis_index("core")
+    atoms, half = pos_ref.shape[2], centre_ref.shape[1] // CORES
+    for out_ref, part in ((keep_ref, core), (give_ref, 1 - core)):
+        for i in range(3):
+            out_ref[i : i + 1, 0:atoms] = pos_ref[i]
+            out_ref[3 + i : 4 + i, 0:atoms] = vel_ref[i]
+        out_ref[6:7, 0:atoms] = charge_ref[...]
+        out_ref[7:8, 0:atoms] = mass_ref[...]
+        for core_of_half in range(CORES):
+
+            @pl.when(part == core_of_half)
+            def _():
+                lanes = slice(core_of_half * half, (core_of_half + 1) * half)
+                out_ref[0:3, atoms : atoms + half] = centre_ref[:, lanes]
+                out_ref[3:4, atoms : atoms + half] = width_ref[:, lanes]
+                out_ref[4:5, atoms : atoms + half] = density_ref[:, lanes]
+                out_ref[5:6, atoms : atoms + half] = error_ref[:, lanes]
+                out_ref[6:8, atoms : atoms + half] = jnp.zeros((2, half), f32)
+
+        for block in range(ints_ref.shape[0] // 8):
+            first = atoms + half + block * ints_ref.shape[1]
+            out_ref[:, first : first + ints_ref.shape[1]] = ints_ref[
+                block * 8 : (block + 1) * 8, :
+            ].astype(f32)
+
+
+def join_kernel(keep_ref, got_ref, state_ref, comp_ref, other_ref):
+    core = lax.axis_index("core")
+    atoms, half, lanes = state_ref.shape[2], comp_ref.shape[2], other_ref.shape[1]
+    for place in range(CORES):
+        mine = core == place
+        state_ref[place] = jnp.where(mine, keep_ref[:, 0:atoms], got_ref[:, 0:atoms])
+        part = slice(atoms, atoms + half)
+        comp_ref[place] = jnp.where(mine, keep_ref[:, part], got_ref[:, part])
+    for block in range(other_ref.shape[0] // 8):
+        first = atoms + half + block * lanes
+        other_ref[block * 8 : (block + 1) * 8, :] = got_ref[:, first : first + lanes].astype(jnp.int32)
+
+
+def chosen(plan, ints_ref, refs):
+    mine_ref, others = refs[0], refs[1:]
     row = lax.axis_index("rep")
     last = plan.owned + 2
     partner, decision = ints_ref[last : last + 1, :], ints_ref[last + 1 : last + 2, :]
     lane = lax.broadcasted_iota(jnp.int32, partner.shape, 1)
     sources = jnp.where(decision == 1, partner, lane)
     source = jnp.sum(jnp.where(lane == row, sources, 0).astype(f32), 1, keepdims=True)
-    value = mine_ref[...]
-    if len(others) == 1:
-        for n in range(others[0].shape[0]):
-            value = jnp.where(source == float(n), others[0][n], value)
-    else:
-        for n, other_ref in enumerate(others):
-            other = jnp.bitwise_xor(row, n + 1).astype(f32)
-            value = jnp.where(source == other, other_ref[...], value)
-    out_ref[...] = value
+
+    def read(*place):
+        value = mine_ref[place]
+        if plan.few:
+            for n, other_ref in enumerate(others):
+                other = jnp.bitwise_xor(row, n + 1).astype(f32)
+                value = jnp.where(source == other, other_ref[place], value)
+        else:
+            for n in range(others[0].shape[0]):
+                value = jnp.where(source == float(n), others[0][(n,) + place], value)
+        return value
+
+    return read
 
 
 def make_lists(plan, mine_ref, theirs_ref, out_ref, waiting):
@@ -228,8 +257,7 @@
     nowhere(xs, tiles)
     points_ref[...] = xs[...].astype(bf16)
     acc[...] = jnp.zeros_like(acc)
-    if copy is not None:
-        copy.wait()
+    copy.wait()
     core = lax.axis_index("core")
     for k in range(listed):
         tile = partner_tile(plan, lists_ref, 1 - core, k)
@@ -245,27 +273,31 @@
             kept_ref[place, part, :] = g
 
     for_pairs(lists_ref, one_pair)
+    square = (lanes, lanes)
+    diagonal = lax.broadcasted_iota(jnp.int32, square, 0) == lax.broadcasted_iota(jnp.int32, square, 1)
     for domain in range(plan.domains):
         for start, size in chunks(plan.half, lanes):
-            total = jnp.sum(acc[domain, start : start + size, :].T, 0, keepdims=True)
+            column = jnp.sum(acc[domain, start : start + size, :], 1, keepdims=True)
+            total = jnp.sum(jnp.where(diagonal, column, 0.0), 0, keepdims=True)
             out_ref[domain : domain + 1, start : start + size] = total * scale
 
 
-def first_kernel(plan, scale, ints_any, other_any, mine_ref, theirs_ref, comp_ref,
-                 out_ref, rim_ref, state_ref, points_ref, kept_ref, turned_ref, lists_ref, xs, acc, cs,
-                 ints, other_ints, waiting, sems):
+def prepare_kernel(plan, ints_any, other_any, *refs):
+    parts, (comp_ref, turned_ref, lists_ref, cs, ints, other_ints, waiting, sems) = refs[:-8], refs[-8:]
     copies = [
         pltpu.make_async_copy(ints_any, ints, sems.at[0]),
         pltpu.make_async_copy(other_any, other_ints, sems.at[1]),
     ]
     for copy in copies:
         copy.start()
-    core = lax.axis_index("core")
-    for tile in range(plan.own):
-        lanes = slice(tile * plan.lanes, (tile + 1) * plan.lanes)
-        mine, theirs = mine_ref[:, lanes], theirs_ref[:, lanes]
-        state_ref[:, tile, :] = jnp.where(core == 0, mine, theirs)
-        state_ref[:, plan.own + tile, :] = jnp.where(core == 0, theirs, mine)
+    height = lax.axis_index("z")
+    for core in range(CORES):
+        if plan.few:
+            for n, part_ref in enumerate(parts):
+                comp_ref[jnp.bitwise_xor(height, n) * CORES + core] = part_ref[core]
+        else:
+            for n in range(parts[1].shape[0]):
+                comp_ref[n * CORES + core] = parts[1][n, core]
     store_rows(cs, centre_rows([comp_ref[:, i, :] for i in range(3)], comp_ref[:, 3, :]))
     for domain in range(plan.domains):
         for start, size in chunks(plan.half, 128):
@@ -275,8 +307,20 @@
     for copy in copies:
         copy.wait()
     make_lists(plan, ints, other_ints, lists_ref, waiting)
-    sum_gaussians(plan, scale, lists_ref, None, state_ref, turned_ref, points_ref, out_ref, rim_ref, kept_ref,
-                  xs, acc)
+
+
+def first_kernel(plan, scale, lists_any, ints_ref, turned_ref, *refs):
+    copies_of_state, refs = refs[:-9], refs[-9:]
+    out_ref, rim_ref, state_ref, points_ref, kept_ref, xs, acc, lists_ref, sem = refs
+    copy = pltpu.make_async_copy(lists_any, lists_ref, sem)
+    copy.start()
+    read = chosen(plan, ints_ref, copies_of_state)
+    for core in range(CORES):
+        for tile in range(plan.own):
+            lanes = slice(tile * plan.lanes, (tile + 1) * plan.lanes)
+            state_ref[:, core * plan.own + tile, :] = read(core, slice(None), lanes)
+    sum_gaussians(plan, scale, lists_ref, copy, state_ref, turned_ref, points_ref, out_ref, rim_ref,
+                  kept_ref, xs, acc)
 
 
 def stepped(old_ref, mine_ref, theirs_ref):
@@ -463,12 +507,21 @@
     return replicas in (2, 4) and heights in (2, 4)
 
 
-def exchange(value, axis):
+def stages(replicas, heights):
+    return [("rep", list(range(1, replicas))), ("z", list(range(1, heights)))]
+
+
+def exchange(value, axis, places):
     count = lax.axis_size(axis)
     others = []
-    for n in range(1, count):
+    for n in places:
         others.append(lax.ppermute(value, axis, [(i, i ^ n) for i in range(count)]))
     return others
+
+
+def everywhere(value, axis):
+    copies = jnp.broadcast_to(value[None], (lax.axis_size(axis),) + value.shape)
+    return lax.all_to_all(copies, axis, 0, 0, tiled=True)
 
 
 def program(
@@ -514,33 +567,41 @@
         decision[None],
     ]
     int_rows = -(-(owned + halo_tiles.shape[1] + 2 + own) // 8) * 8
-    state_own, comp_send, ints = call(
+    wide = own * lanes + half + int_rows // 8 * lanes
+    keep, give, ints = call(
         pack_kernel,
         [pltpu.with_memory_space_constraint(arg, pltpu.HBM) for arg in args],
-        [shape(8, own * lanes), shape(domains, 6, half), shape(int_rows, lanes, dtype=jnp.int32)],
+        [shape(8, wide), shape(8, wide), shape(int_rows, lanes, dtype=jnp.int32)],
         [(arg.shape, arg.dtype) for arg in args] + [pltpu.SemaphoreType.DMA((len(args),))],
         limit=8,
         spaces=[HBM] * len(args),
     )
-    comps = lax.all_to_all(comp_send, ("z", "core"), 0, 0, tiled=True)
-    other_ints = swap_cores(ints)
+    both_state, both_comps, other_ints = call(
+        join_kernel,
+        [keep, swap_cores(give)],
+        [shape(CORES, 8, own * lanes), shape(CORES, 8, half),
+         shape(int_rows, lanes, dtype=jnp.int32)],
+    )
+    plan.few = few(replicas, heights)
+    if plan.few:
+        comp_parts = [both_comps] + exchange(both_comps, "z", range(1, heights))
+        states = [both_state] + exchange(both_state, "rep", range(1, replicas))
+    else:
+        comp_parts = [both_comps, everywhere(both_comps, "z")]
+        states = [both_state, everywhere(both_state, "rep")]
     width = -(-((tiles * owned + domains) // 2 + UNROLL + 1) // lanes) * lanes
     lists_shape = shape(4 + plan.near, width, dtype=jnp.int32)
     scalars = [pltpu.SMEM(lists_shape.shape, jnp.int32), pltpu.SemaphoreType.DMA]
-    small = few(replicas, heights)
-    if small:
-        others = exchange(state_own, "rep")
-    else:
-        others = [
-            lax.all_to_all(
-                jnp.broadcast_to(state_own[None], (replicas,) + state_own.shape),
-                "rep", 0, 0, tiled=True,
-            )
-        ]
-    chosen = call(
-        functools.partial(choose_kernel, plan), [ints, state_own] + others, shape(8, own * lanes)
+    comps, turned, lists = call(
+        functools.partial(prepare_kernel, plan),
+        [ints, other_ints] + comp_parts,
+        [shape(domains, 8, half), shape(domains, half, DEPTH, dtype=bf16), lists_shape],
+        [(domains, DEPTH, half), pltpu.SMEM(ints.shape, jnp.int32),
+         pltpu.SMEM(ints.shape, jnp.int32), pltpu.SMEM((domains,), jnp.int32),
+         pltpu.SemaphoreType.DMA((2,))],
+        spaces=[ANY, ANY] + [VMEM] * len(comp_parts),
+        out_spaces=[VMEM, VMEM, SMEM],
     )
-    chosen_other = swap_cores(chosen)
 
     map_gain = map_scale / (owned * components)
     scale = 1.0 / (owned * own * lanes)
@@ -561,16 +622,12 @@
     scratch = [(tiles + 1, DEPTH, lanes), (domains, half, lanes)]
     for step in range(STEPS):
         if step == 0:
-            partial, rim, state, points, kept, turned, lists = call(
+            partial, rim, state, points, kept = call(
                 functools.partial(first_kernel, plan, scale),
-                [ints, other_ints, chosen, chosen_other, comps],
-                outs + [shape(domains, half, DEPTH, dtype=bf16), lists_shape],
-                scratch
-                + [(domains, DEPTH, half), pltpu.SMEM(ints.shape, jnp.int32),
-                   pltpu.SMEM(ints.shape, jnp.int32), pltpu.SMEM((domains,), jnp.int32),
-                   pltpu.SemaphoreType.DMA((2,))],
-                spaces=[ANY, ANY] + [VMEM] * 3,
-                out_spaces=[VMEM] * 6 + [SMEM],
+                [lists, ints, turned] + states,
+                outs,
+                scratch + scalars,
+                spaces=[ANY] + [VMEM] * (2 + len(states)),
             )
         else:
             partial, rim, state, points, kept = call(
@@ -581,9 +638,11 @@
                 spaces=[ANY] + [VMEM] * 4,
             )
         far = lax.ppermute(rim, ("z", "core"), onward)
-        if small:
-            partial = call(add_kernel, [partial] + exchange(partial, "rep"), shape(domains, half))
-            parts = [partial] + exchange(partial, "z")
+        if plan.few:
+            for number, (axis, places) in enumerate(stages(replicas, heights)):
+                if number > 0:
+                    partial = call(add_kernel, parts, shape(domains, half))
+                parts = [partial] + exchange(partial, axis, places)
         else:
             pieces = lax.all_to_all(partial.reshape(group, -1), ("rep", "z"), 0, 0, tiled=True)
             piece = jnp.sum(pieces, 0)

time: 82.3 us -> 78.3 us (0.951)
  Pallas kernels: 31.6 us -> 27.7 us
  waiting for transfers between devices: 21.5 us -> 23.7 us
  starting transfers between devices: 28 us -> 25.9 us
    all_to_all x1 -> x0, starting transfers between devices: 6.37 us -> none  [program(): comps = lax.all_to_all(comp_send, ('z', 'core'), 0, 0, tiled=True)]
    ppermute x15 -> x18, starting transfers between devices: 19.6 us -> 25.1 us  [exchange(): others.append(lax.ppermute(value, axis, [(i, i ^ n) for i in range(count)]))]
    pallas_call x11 -> x12, Pallas kernels: 31.6 us -> 27.7 us  [call(): pl.pallas_call(kernel, out_shape=tuple(outs) if many else outs, in_specs=...]
    ppermute x2, starting transfers between devices: 1.41 us -> 0.05 us  [program(): far = lax.ppermute(rim, ('z', 'core'), onward)]
    ppermute x2, waiting for transfers between devices: 9.49 us -> 10.8 us  [program(): far = lax.ppermute(rim, ('z', 'core'), onward)]
    ppermute x15 -> x18, waiting for transfers between devices: 8.81 us -> 9.66 us  [exchange(): others.append(lax.ppermute(value, axis, [(i, i ^ n) for i in range(count)]))]
    ppermute x4 -> x3, waiting for transfers between devices: 3.22 us -> 3.28 us  [swap_cores(): return lax.ppermute(value, 'core', [(0, 1), (1, 0)])]
  transfers between devices with their start and end apart: 22 -> 23, of which waited for: 14 -> 12; matrix products, arithmetic and copies ran while one was open for 0% -> 0% of each run, Pallas kernels for 5% -> 8%
where the time goes in v7:
time: 78.3 us; the launch traced here: 78.1 us
  Pallas kernels  27.7 us (35%)
  starting transfers between devices  25.9 us (33%)
  waiting for transfers between devices  23.7 us (30%)
  between operations  0.82 us (1%)
    pallas_call x12, Pallas kernels, call(): pl.pallas_call(kernel, out_shape=tuple(outs) if many else outs, in_specs=...  27.7 us
    ppermute x18, starting transfers between devices, exchange(): others.append(lax.ppermute(value, axis, [(i, i ^ n) for i in range(count)]))  25.1 us
    ppermute x2, waiting for transfers between devices, program(): far = lax.ppermute(rim, ('z', 'core'), onward)  10.8 us
    ppermute x18, waiting for transfers between devices, exchange(): others.append(lax.ppermute(value, axis, [(i, i ^ n) for i in range(count)]))  9.66 us
    ppermute x3, waiting for transfers between devices, swap_cores(): return lax.ppermute(value, 'core', [(0, 1), (1, 0)])  3.28 us
  transfers between devices with their start and end apart: 23, of which 12 were waited for; matrix products, arithmetic and copies ran while one was open for 0% of the time, Pallas kernels for 8%

profile of v7, /device:TPU:0, one launch (start us, length us, event | category | flops | bytes accessed | tf_op | source)
XLA Modules:
  0.0 78.1 jit_solution(7483462203215669240)
XLA Ops:
  0.6 1.0 %shard_map.148 = (f32[8,1792]{1,0:T(8,128)S(1)}, f32[8,1792]{1,0:T(8,128)S(1)}, s32[16,128]{1,0:T(8,128)S(1)}) custom-call(f32[3,1,1024]{2,1,0:T(1,128)} %bitcast.13, f32[3,1,1024]{2,1,0:T(1,128)} %bitcast.14, f32[1,1024]{1,0:T(1,128)} %bitcast.15, f32[1,1024]{1,0:T(1,128)} %bitcast.16, f32[3,1024]{1,0:T(4,128)} %centre_hbm.1, f32[1,1024]{1,0:T(1,128)} %bitcast.17, ...), custom_call_target="tpu_custom_call" | custom-call | tf_op jit(solution)/shard_map/pallas_call | solution.py:488
  1.6 0.6 collective-permute-start
  2.2 0.9 %collective-permute-done.got_ref = f32[8,1792]{1,0:T(8,128)S(1)} collective-permute-done((f32[8,1792]{1,0:T(8,128)S(1)}, f32[8,1792]{1,0:T(8,128)S(1)}, u32[]{:S(2)}, u32[]{:S(2)}) %collective-permute-start) | collective-permute-done | bytes 57376 | tf_op jit(solution)/shard_map/ppermute | solution.py:503
  3.1 5.0 %collective-permute-start.3 = (f32[2,8,512]{2,1,0:T(8,128)S(1)}, f32[2,8,512]{2,1,0:T(8,128)S(1)}, u32[]{:S(2)}, u32[]{:S(2)}) collective-permute-start(f32[2,8,512]{2,1,0:T(8,128)S(1)} %get-tuple-element.29.refs_0_), channel_id=1, source_target_pairs={{0,6},{2,4},{4,2},{6,0},{1,7},{3,5},{5,3},{7,1},{8,14},{10,12},{12... | collective-permute-start | bytes 98312 | tf_op jit(solution)/shard_map/ppermute | solution.py:518
  8.1 2.4 %collective-permute-start.6 = (f32[2,8,1024]{2,1,0:T(8,128)S(1)}, f32[2,8,1024]{2,1,0:T(8,128)S(1)}, u32[]{:S(2)}, u32[]{:S(2)}) collective-permute-start(f32[2,8,1024]{2,1,0:T(8,128)S(1)} %get-tuple-element.32.refs_0_), channel_id=1, source_target_pairs={{0,24},{8,16},{16,8},{24,0},{1,25},{9,17},{17,9},{25,1},{2,26},{10... | collective-permute-start | bytes 196616 | tf_op jit(solution)/shard_map/ppermute | solution.py:518
  11.0 0.5 collective-permute-start.4
  11.6 0.6 collective-permute-start.1
  12.2 4.2 %collective-permute-done.2.refs_2_ = f32[2,8,512]{2,1,0:T(8,128)S(1)} collective-permute-done((f32[2,8,512]{2,1,0:T(8,128)S(1)}, f32[2,8,512]{2,1,0:T(8,128)S(1)}, u32[]{:S(2)}, u32[]{:S(2)}) %collective-permute-start.2) | collective-permute-done | bytes 32800 | tf_op jit(solution)/shard_map/ppermute | solution.py:518
  16.4 2.3 %shard_map.150 = (f32[8,8,512]{2,1,0:T(8,128)S(1)}, bf16[8,512,32]{2,1,0:T(8,128)(2,1)S(1)}, s32[10,128]{1,0:T(8,128)S(1)}) custom-call(s32[16,128]{1,0:T(8,128)S(1)} %get-tuple-element.25.ints_any.ints_ref, s32[16,128]{1,0:T(8,128)S(1)} %get-tuple-element.28.other_any, f32[2,8,512]{2,1,0:T(8,128)S(1)} %get-tuple-element.29.refs_0_, ...), custom_call_target="tpu_custom_call" | custom-call | tf_op jit(solution)/shard_map/pallas_call | solution.py:488
  18.7 5.0 %shard_map.151 = (f32[8,512]{1,0:T(8,128)S(1)}, f32[8,128]{1,0:T(8,128)S(1)}, f32[8,16,128]{2,1,0:T(8,128)S(1)}, bf16[17,32,128]{2,1,0:T(8,128)(2,1)S(1)}, f32[40,512,256]{2,1,0:T(8,128)S(1)}) custom-call(s32[10,128]{1,0:T(8,128)S(1)} %get-tuple-element.30.lists_any, s32[16,128]{1,0:T(8,128)S(1)} %get-tuple-element.25.ints_any.ints_ref, ...), custom_call_target="tpu_custom_call" | custom-call | tf_op jit(solution)/shard_map/pallas_call | solution.py:488
  23.8 2.5 %collective-permute-start.10 = (f32[8,512]{1,0:T(8,128)S(1)}, f32[8,512]{1,0:T(8,128)S(1)}, u32[]{:S(2)}, u32[]{:S(2)}) collective-permute-start(f32[8,512]{1,0:T(8,128)S(1)} %get-tuple-element.38.refs_0_), channel_id=1, source_target_pairs={{0,24},{8,16},{16,8},{24,0},{1,25},{9,17},{17,9},{25,1},{2,26},{10... | collective-permute-start | bytes 49160 | tf_op jit(solution)/shard_map/ppermute | solution.py:518
  26.8 0.5 collective-permute-start.8
  27.3 1.1 %collective-permute-done.10.refs_3_ = f32[8,512]{1,0:T(8,128)S(1)} collective-permute-done((f32[8,512]{1,0:T(8,128)S(1)}, f32[8,512]{1,0:T(8,128)S(1)}, u32[]{:S(2)}, u32[]{:S(2)}) %collective-permute-start.10) | collective-permute-done | bytes 16416 | tf_op jit(solution)/shard_map/ppermute | solution.py:518
  28.5 1.5 %collective-permute-done.9.refs_2_ = f32[8,512]{1,0:T(8,128)S(1)} collective-permute-done((f32[8,512]{1,0:T(8,128)S(1)}, f32[8,512]{1,0:T(8,128)S(1)}, u32[]{:S(2)}, u32[]{:S(2)}) %collective-permute-start.9) | collective-permute-done | bytes 16416 | tf_op jit(solution)/shard_map/ppermute | solution.py:518
  30.5 1.5 %collective-permute-start.13 = (f32[8,512]{1,0:T(8,128)S(1)}, f32[8,512]{1,0:T(8,128)S(1)}, u32[]{:S(2)}, u32[]{:S(2)}) collective-permute-start(f32[8,512]{1,0:T(8,128)S(1)} %shard_map.153.refs_0_), channel_id=1, source_target_pairs={{0,6},{2,4},{4,2},{6,0},{1,7},{3,5},{5,3},{7,1},{8,14},{10,12},{12... | collective-permute-start | bytes 49160 | tf_op jit(solution)/shard_map/ppermute | solution.py:518
  32.1 0.7 collective-permute-start.12
  32.7 2.3 %collective-permute-start.11 = (f32[8,512]{1,0:T(8,128)S(1)}, f32[8,512]{1,0:T(8,128)S(1)}, u32[]{:S(2)}, u32[]{:S(2)}) collective-permute-start(f32[8,512]{1,0:T(8,128)S(1)} %shard_map.153.refs_0_), channel_id=1, source_target_pairs={{0,2},{2,0},{4,6},{6,4},{1,3},{3,1},{5,7},{7,5},{8,10},{10,8},{12,... | collective-permute-start | bytes 49160 | tf_op jit(solution)/shard_map/ppermute | solution.py:518
  35.0 5.4 %collective-permute-done.7.far_ref = f32[8,128]{1,0:T(8,128)S(1)} collective-permute-done((f32[8,128]{1,0:T(8,128)S(1)}, f32[8,128]{1,0:T(8,128)S(1)}, u32[]{:S(2)}, u32[]{:S(2)}) %collective-permute-start.7) | collective-permute-done | bytes 4128 | tf_op jit(solution)/shard_map/ppermute | solution.py:640
  40.4 2.1 %shard_map.152.pair_ref = f32[3,8,128]{2,1,0:T(8,128)S(1)} custom-call(s32[10,128]{1,0:T(8,128)S(1)} %get-tuple-element.30.lists_any, f32[8,16,128]{2,1,0:T(8,128)S(1)} %get-tuple-element.33.state_ref.old_ref, f32[8,128]{1,0:T(8,128)S(1)} %collective-permute-done.7.far_ref, bf16[17,32,128]{2,1,0:T(8,128)(2,1)S(1)} %get-tuple-element.36.points_ref), custom_call_target="tpu_custom_call" | custom-call | tf_op jit(solution)/shard_map/pallas_call | solution.py:488
  42.5 4.8 %shard_map.154.force_ref = f32[4,16,128]{2,1,0:T(8,128)S(1)} custom-call(s32[10,128]{1,0:T(8,128)S(1)} %get-tuple-element.30.lists_any, f32[8,16,128]{2,1,0:T(8,128)S(1)} %get-tuple-element.33.state_ref.old_ref, f32[8,8,512]{2,1,0:T(8,128)S(1)} %get-tuple-element.34.comp_ref, f32[3,8,128]{2,1,0:T(8,128)S(1)} %shard_map.152.pair_ref, ...), custom_call_target="tpu_custom_call" | custom-call | tf_op jit(solution)/shard_map/pallas_call | solution.py:488
  47.4 1.2 %collective-permute-done.14.swapped_ref = f32[4,16,128]{2,1,0:T(8,128)S(1)} collective-permute-done((f32[4,16,128]{2,1,0:T(8,128)S(1)}, f32[4,16,128]{2,1,0:T(8,128)S(1)}, u32[]{:S(2)}, u32[]{:S(2)}) %collective-permute-start.14) | collective-permute-done | bytes 32800 | tf_op jit(solution)/shard_map/ppermute | solution.py:503
  48.6 5.0 %shard_map.155 = (f32[8,512]{1,0:T(8,128)S(1)}, f32[8,128]{1,0:T(8,128)S(1)}, f32[8,16,128]{2,1,0:T(8,128)S(1)}, bf16[17,32,128]{2,1,0:T(8,128)(2,1)S(1)}, f32[40,512,256]{2,1,0:T(8,128)S(1)}) custom-call(s32[10,128]{1,0:T(8,128)S(1)} %get-tuple-element.30.lists_any, f32[8,16,128]{2,1,0:T(8,128)S(1)} %get-tuple-element.33.state_ref.old_ref, ...), custom_call_target="tpu_custom_call" | custom-call | tf_op jit(solution)/shard_map/pallas_call | solution.py:488
  53.6 1.6 %collective-permute-start.18 = (f32[8,512]{1,0:T(8,128)S(1)}, f32[8,512]{1,0:T(8,128)S(1)}, u32[]{:S(2)}, u32[]{:S(2)}) collective-permute-start(f32[8,512]{1,0:T(8,128)S(1)} %get-tuple-element.43.refs_0_), channel_id=1, source_target_pairs={{0,24},{8,16},{16,8},{24,0},{1,25},{9,17},{17,9},{25,1},{2,26},{10... | collective-permute-start | bytes 49160 | tf_op jit(solution)/shard_map/ppermute | solution.py:518
  55.6 1.5 %collective-permute-start.16 = (f32[8,512]{1,0:T(8,128)S(1)}, f32[8,512]{1,0:T(8,128)S(1)}, u32[]{:S(2)}, u32[]{:S(2)}) collective-permute-start(f32[8,512]{1,0:T(8,128)S(1)} %get-tuple-element.43.refs_0_), channel_id=1, source_target_pairs={{0,8},{8,0},{16,24},{24,16},{1,9},{9,1},{17,25},{25,17},{2,10},{10... | collective-permute-start | bytes 49160 | tf_op jit(solution)/shard_map/ppermute | solution.py:518
  57.1 1.1 %collective-permute-done.18.refs_3_ = f32[8,512]{1,0:T(8,128)S(1)} collective-permute-done((f32[8,512]{1,0:T(8,128)S(1)}, f32[8,512]{1,0:T(8,128)S(1)}, u32[]{:S(2)}, u32[]{:S(2)}) %collective-permute-start.18) | collective-permute-done | bytes 16416 | tf_op jit(solution)/shard_map/ppermute | solution.py:518
  58.3 0.6 collective-permute-done.17.refs_2_
  59.5 4.3 %collective-permute-start.19 = (f32[8,512]{1,0:T(8,128)S(1)}, f32[8,512]{1,0:T(8,128)S(1)}, u32[]{:S(2)}, u32[]{:S(2)}) collective-permute-start(f32[8,512]{1,0:T(8,128)S(1)} %shard_map.157.refs_0_), channel_id=1, source_target_pairs={{0,2},{2,0},{4,6},{6,4},{1,3},{3,1},{5,7},{7,5},{8,10},{10,8},{12,... | collective-permute-start | bytes 49160 | tf_op jit(solution)/shard_map/ppermute | solution.py:518
  63.9 5.4 %collective-permute-done.15.far_ref = f32[8,128]{1,0:T(8,128)S(1)} collective-permute-done((f32[8,128]{1,0:T(8,128)S(1)}, f32[8,128]{1,0:T(8,128)S(1)}, u32[]{:S(2)}, u32[]{:S(2)}) %collective-permute-start.15) | collective-permute-done | bytes 4128 | tf_op jit(solution)/shard_map/ppermute | solution.py:640
  69.2 2.1 %shard_map.156.pair_ref = f32[3,8,128]{2,1,0:T(8,128)S(1)} custom-call(s32[10,128]{1,0:T(8,128)S(1)} %get-tuple-element.30.lists_any, f32[8,16,128]{2,1,0:T(8,128)S(1)} %get-tuple-element.39.state_ref.old_ref, f32[8,128]{1,0:T(8,128)S(1)} %collective-permute-done.15.far_ref, bf16[17,32,128]{2,1,0:T(8,128)(2,1)S(1)} %get-tuple-element.41.points_ref), custom_call_target="tpu_custom_call" | custom-call | tf_op jit(solution)/shard_map/pallas_call | solution.py:488
  71.4 4.8 %shard_map.158.mine_ref = f32[4,16,128]{2,1,0:T(8,128)S(1)} custom-call(s32[10,128]{1,0:T(8,128)S(1)} %get-tuple-element.30.lists_any, f32[8,16,128]{2,1,0:T(8,128)S(1)} %get-tuple-element.39.state_ref.old_ref, f32[8,8,512]{2,1,0:T(8,128)S(1)} %get-tuple-element.34.comp_ref, f32[3,8,128]{2,1,0:T(8,128)S(1)} %shard_map.156.pair_ref, ...), custom_call_target="tpu_custom_call" | custom-call | tf_op jit(solution)/shard_map/pallas_call | solution.py:488
  76.2 1.2 %collective-permute-done.22.theirs_ref = f32[4,16,128]{2,1,0:T(8,128)S(1)} collective-permute-done((f32[4,16,128]{2,1,0:T(8,128)S(1)}, f32[4,16,128]{2,1,0:T(8,128)S(1)}, u32[]{:S(2)}, u32[]{:S(2)}) %collective-permute-start.22) | collective-permute-done | bytes 32800 | tf_op jit(solution)/shard_map/ppermute | solution.py:503
  77.4 0.6 shard_map.159
  (26 shorter events, 3.0 us)
Async XLA Ops:
  1.6 1.4 %collective-permute-start = (f32[8,1792]{1,0:T(8,128)S(1)}, f32[8,1792]{1,0:T(8,128)S(1)}, u32[]{:S(2)}, u32[]{:S(2)}) collective-permute-start(f32[8,1792]{1,0:T(8,128)S(1)} %get-tuple-element.27), channel_id=1, source_target_pairs={{0,1},{1,0},{2,3},{3,2},{4,5},{5,4},{6,7},{7,6},{8,9},{9,8},{10,11... | collective-permute-start | bytes 172040 | tf_op jit(solution)/shard_map/ppermute | solution.py:503
  3.1 8.5 %collective-permute-start.3 = (f32[2,8,512]{2,1,0:T(8,128)S(1)}, f32[2,8,512]{2,1,0:T(8,128)S(1)}, u32[]{:S(2)}, u32[]{:S(2)}) collective-permute-start(f32[2,8,512]{2,1,0:T(8,128)S(1)} %get-tuple-element.29.refs_0_), channel_id=1, source_target_pairs={{0,6},{2,4},{4,2},{6,0},{1,7},{3,5},{5,3},{7,1},{8,14},{10,12},{12... | collective-permute-start | bytes 98312 | tf_op jit(solution)/shard_map/ppermute | solution.py:518
  8.1 10.6 %collective-permute-start.6 = (f32[2,8,1024]{2,1,0:T(8,128)S(1)}, f32[2,8,1024]{2,1,0:T(8,128)S(1)}, u32[]{:S(2)}, u32[]{:S(2)}) collective-permute-start(f32[2,8,1024]{2,1,0:T(8,128)S(1)} %get-tuple-element.32.refs_0_), channel_id=1, source_target_pairs={{0,24},{8,16},{16,8},{24,0},{1,25},{9,17},{17,9},{25,1},{2,26},{10... | collective-permute-start | bytes 196616 | tf_op jit(solution)/shard_map/ppermute | solution.py:518
  10.5 8.2 %collective-permute-start.5 = (f32[2,8,1024]{2,1,0:T(8,128)S(1)}, f32[2,8,1024]{2,1,0:T(8,128)S(1)}, u32[]{:S(2)}, u32[]{:S(2)}) collective-permute-start(f32[2,8,1024]{2,1,0:T(8,128)S(1)} %get-tuple-element.32.refs_0_), channel_id=1, source_target_pairs={{0,16},{8,24},{16,0},{24,8},{1,17},{9,25},{17,1},{25,9},{2,18},{10... | collective-permute-start | bytes 196616 | tf_op jit(solution)/shard_map/ppermute | solution.py:518
  11.0 7.7 %collective-permute-start.4 = (f32[2,8,1024]{2,1,0:T(8,128)S(1)}, f32[2,8,1024]{2,1,0:T(8,128)S(1)}, u32[]{:S(2)}, u32[]{:S(2)}) collective-permute-start(f32[2,8,1024]{2,1,0:T(8,128)S(1)} %get-tuple-element.32.refs_0_), channel_id=1, source_target_pairs={{0,8},{8,0},{16,24},{24,16},{1,9},{9,1},{17,25},{25,17},{2,10},{10... | collective-permute-start | bytes 196616 | tf_op jit(solution)/shard_map/ppermute | solution.py:518
  11.6 4.8 %collective-permute-start.2 = (f32[2,8,512]{2,1,0:T(8,128)S(1)}, f32[2,8,512]{2,1,0:T(8,128)S(1)}, u32[]{:S(2)}, u32[]{:S(2)}) collective-permute-start(f32[2,8,512]{2,1,0:T(8,128)S(1)} %get-tuple-element.29.refs_0_), channel_id=1, source_target_pairs={{0,4},{2,6},{4,0},{6,2},{1,5},{3,7},{5,1},{7,3},{8,12},{10,14},{12... | collective-permute-start | bytes 98312 | tf_op jit(solution)/shard_map/ppermute | solution.py:518
  11.6 4.8 %collective-permute-start.1 = (f32[2,8,512]{2,1,0:T(8,128)S(1)}, f32[2,8,512]{2,1,0:T(8,128)S(1)}, u32[]{:S(2)}, u32[]{:S(2)}) collective-permute-start(f32[2,8,512]{2,1,0:T(8,128)S(1)} %get-tuple-element.29.refs_0_), channel_id=1, source_target_pairs={{0,2},{2,0},{4,6},{6,4},{1,3},{3,1},{5,7},{7,5},{8,10},{10,8},{12,... | collective-permute-start | bytes 98312 | tf_op jit(solution)/shard_map/ppermute | solution.py:518
  23.8 4.7 %collective-permute-start.10 = (f32[8,512]{1,0:T(8,128)S(1)}, f32[8,512]{1,0:T(8,128)S(1)}, u32[]{:S(2)}, u32[]{:S(2)}) collective-permute-start(f32[8,512]{1,0:T(8,128)S(1)} %get-tuple-element.38.refs_0_), channel_id=1, source_target_pairs={{0,24},{8,16},{16,8},{24,0},{1,25},{9,17},{17,9},{25,1},{2,26},{10... | collective-permute-start | bytes 49160 | tf_op jit(solution)/shard_map/ppermute | solution.py:518
  26.3 3.7 %collective-permute-start.9 = (f32[8,512]{1,0:T(8,128)S(1)}, f32[8,512]{1,0:T(8,128)S(1)}, u32[]{:S(2)}, u32[]{:S(2)}) collective-permute-start(f32[8,512]{1,0:T(8,128)S(1)} %get-tuple-element.38.refs_0_), channel_id=1, source_target_pairs={{0,16},{8,24},{16,0},{24,8},{1,17},{9,25},{17,1},{25,9},{2,18},{10... | collective-permute-start | bytes 49160 | tf_op jit(solution)/shard_map/ppermute | solution.py:518
  26.8 3.7 %collective-permute-start.8 = (f32[8,512]{1,0:T(8,128)S(1)}, f32[8,512]{1,0:T(8,128)S(1)}, u32[]{:S(2)}, u32[]{:S(2)}) collective-permute-start(f32[8,512]{1,0:T(8,128)S(1)} %get-tuple-element.38.refs_0_), channel_id=1, source_target_pairs={{0,8},{8,0},{16,24},{24,16},{1,9},{9,1},{17,25},{25,17},{2,10},{10... | collective-permute-start | bytes 49160 | tf_op jit(solution)/shard_map/ppermute | solution.py:518
  30.5 12.0 %collective-permute-start.13 = (f32[8,512]{1,0:T(8,128)S(1)}, f32[8,512]{1,0:T(8,128)S(1)}, u32[]{:S(2)}, u32[]{:S(2)}) collective-permute-start(f32[8,512]{1,0:T(8,128)S(1)} %shard_map.153.refs_0_), channel_id=1, source_target_pairs={{0,6},{2,4},{4,2},{6,0},{1,7},{3,5},{5,3},{7,1},{8,14},{10,12},{12... | collective-permute-start | bytes 49160 | tf_op jit(solution)/shard_map/ppermute | solution.py:518
  32.1 10.4 %collective-permute-start.12 = (f32[8,512]{1,0:T(8,128)S(1)}, f32[8,512]{1,0:T(8,128)S(1)}, u32[]{:S(2)}, u32[]{:S(2)}) collective-permute-start(f32[8,512]{1,0:T(8,128)S(1)} %shard_map.153.refs_0_), channel_id=1, source_target_pairs={{0,4},{2,6},{4,0},{6,2},{1,5},{3,7},{5,1},{7,3},{8,12},{10,14},{12... | collective-permute-start | bytes 49160 | tf_op jit(solution)/shard_map/ppermute | solution.py:518
  32.7 9.8 %collective-permute-start.11 = (f32[8,512]{1,0:T(8,128)S(1)}, f32[8,512]{1,0:T(8,128)S(1)}, u32[]{:S(2)}, u32[]{:S(2)}) collective-permute-start(f32[8,512]{1,0:T(8,128)S(1)} %shard_map.153.refs_0_), channel_id=1, source_target_pairs={{0,2},{2,0},{4,6},{6,4},{1,3},{3,1},{5,7},{7,5},{8,10},{10,8},{12,... | collective-permute-start | bytes 49160 | tf_op jit(solution)/shard_map/ppermute | solution.py:518
  35.0 5.4 %collective-permute-start.7 = (f32[8,128]{1,0:T(8,128)S(1)}, f32[8,128]{1,0:T(8,128)S(1)}, u32[]{:S(2)}, u32[]{:S(2)}) collective-permute-start(f32[8,128]{1,0:T(8,128)S(1)} %get-tuple-element.35), channel_id=1, source_target_pairs={{0,2},{2,4},{4,6},{6,0},{3,1},{5,3},{7,5},{1,7},{8,10},{10,12},{12... | collective-permute-start | bytes 12296 | tf_op jit(solution)/shard_map/ppermute | solution.py:640
  47.3 1.3 %collective-permute-start.14 = (f32[4,16,128]{2,1,0:T(8,128)S(1)}, f32[4,16,128]{2,1,0:T(8,128)S(1)}, u32[]{:S(2)}, u32[]{:S(2)}) collective-permute-start(f32[4,16,128]{2,1,0:T(8,128)S(1)} %shard_map.154.force_ref), channel_id=1, source_target_pairs={{0,1},{1,0},{2,3},{3,2},{4,5},{5,4},{6,7},{7,6},{8,9},{9,8},{10,11... | collective-permute-start | bytes 98312 | tf_op jit(solution)/shard_map/ppermute | solution.py:503
  53.6 4.7 %collective-permute-start.18 = (f32[8,512]{1,0:T(8,128)S(1)}, f32[8,512]{1,0:T(8,128)S(1)}, u32[]{:S(2)}, u32[]{:S(2)}) collective-permute-start(f32[8,512]{1,0:T(8,128)S(1)} %get-tuple-element.43.refs_0_), channel_id=1, source_target_pairs={{0,24},{8,16},{16,8},{24,0},{1,25},{9,17},{17,9},{25,1},{2,26},{10... | collective-permute-start | bytes 49160 | tf_op jit(solution)/shard_map/ppermute | solution.py:518
  55.1 3.7 %collective-permute-start.17 = (f32[8,512]{1,0:T(8,128)S(1)}, f32[8,512]{1,0:T(8,128)S(1)}, u32[]{:S(2)}, u32[]{:S(2)}) collective-permute-start(f32[8,512]{1,0:T(8,128)S(1)} %get-tuple-element.43.refs_0_), channel_id=1, source_target_pairs={{0,16},{8,24},{16,0},{24,8},{1,17},{9,25},{17,1},{25,9},{2,18},{10... | collective-permute-start | bytes 49160 | tf_op jit(solution)/shard_map/ppermute | solution.py:518
  55.6 3.7 %collective-permute-start.16 = (f32[8,512]{1,0:T(8,128)S(1)}, f32[8,512]{1,0:T(8,128)S(1)}, u32[]{:S(2)}, u32[]{:S(2)}) collective-permute-start(f32[8,512]{1,0:T(8,128)S(1)} %get-tuple-element.43.refs_0_), channel_id=1, source_target_pairs={{0,8},{8,0},{16,24},{24,16},{1,9},{9,1},{17,25},{25,17},{2,10},{10... | collective-permute-start | bytes 49160 | tf_op jit(solution)/shard_map/ppermute | solution.py:518
  59.4 12.0 %collective-permute-start.21 = (f32[8,512]{1,0:T(8,128)S(1)}, f32[8,512]{1,0:T(8,128)S(1)}, u32[]{:S(2)}, u32[]{:S(2)}) collective-permute-start(f32[8,512]{1,0:T(8,128)S(1)} %shard_map.157.refs_0_), channel_id=1, source_target_pairs={{0,6},{2,4},{4,2},{6,0},{1,7},{3,5},{5,3},{7,1},{8,14},{10,12},{12... | collective-permute-start | bytes 49160 | tf_op jit(solution)/shard_map/ppermute | solution.py:518
  59.5 11.9 %collective-permute-start.20 = (f32[8,512]{1,0:T(8,128)S(1)}, f32[8,512]{1,0:T(8,128)S(1)}, u32[]{:S(2)}, u32[]{:S(2)}) collective-permute-start(f32[8,512]{1,0:T(8,128)S(1)} %shard_map.157.refs_0_), channel_id=1, source_target_pairs={{0,4},{2,6},{4,0},{6,2},{1,5},{3,7},{5,1},{7,3},{8,12},{10,14},{12... | collective-permute-start | bytes 49160 | tf_op jit(solution)/shard_map/ppermute | solution.py:518
  59.5 11.8 %collective-permute-start.19 = (f32[8,512]{1,0:T(8,128)S(1)}, f32[8,512]{1,0:T(8,128)S(1)}, u32[]{:S(2)}, u32[]{:S(2)}) collective-permute-start(f32[8,512]{1,0:T(8,128)S(1)} %shard_map.157.refs_0_), channel_id=1, source_target_pairs={{0,2},{2,0},{4,6},{6,4},{1,3},{3,1},{5,7},{7,5},{8,10},{10,8},{12,... | collective-permute-start | bytes 49160 | tf_op jit(solution)/shard_map/ppermute | solution.py:518
  63.8 5.4 %collective-permute-start.15 = (f32[8,128]{1,0:T(8,128)S(1)}, f32[8,128]{1,0:T(8,128)S(1)}, u32[]{:S(2)}, u32[]{:S(2)}) collective-permute-start(f32[8,128]{1,0:T(8,128)S(1)} %get-tuple-element.40), channel_id=1, source_target_pairs={{0,2},{2,4},{4,6},{6,0},{3,1},{5,3},{7,5},{1,7},{8,10},{10,12},{12... | collective-permute-start | bytes 12296 | tf_op jit(solution)/shard_map/ppermute | solution.py:640
  76.2 1.3 %collective-permute-start.22 = (f32[4,16,128]{2,1,0:T(8,128)S(1)}, f32[4,16,128]{2,1,0:T(8,128)S(1)}, u32[]{:S(2)}, u32[]{:S(2)}) collective-permute-start(f32[4,16,128]{2,1,0:T(8,128)S(1)} %shard_map.158.mine_ref), channel_id=1, source_target_pairs={{0,1},{1,0},{2,3},{3,2},{4,5},{5,4},{6,7},{7,6},{8,9},{9,8},{10,11... | collective-permute-start | bytes 98312 | tf_op jit(solution)/shard_map/ppermute | solution.py:503

commit v8 on v7

--- a/solution.py
+++ b/solution.py
@@ -250,14 +250,13 @@
     lax.fori_loop(0, lists_ref[3, 0], step, 0)
 
 
-def sum_gaussians(plan, scale, lists_ref, copy, state_ref, turned_ref, points_ref, out_ref, rim_ref, kept_ref,
+def sum_gaussians(plan, scale, lists_ref, state_ref, turned_ref, points_ref, out_ref, rim_ref, kept_ref,
                   xs, acc):
     tiles, listed, lanes = plan.tiles, plan.listed, plan.lanes
     store_rows(xs, point_rows([state_ref[i] for i in range(3)]))
     nowhere(xs, tiles)
     points_ref[...] = xs[...].astype(bf16)
     acc[...] = jnp.zeros_like(acc)
-    copy.wait()
     core = lax.axis_index("core")
     for k in range(listed):
         tile = partner_tile(plan, lists_ref, 1 - core, k)
@@ -283,7 +282,8 @@
 
 
 def prepare_kernel(plan, ints_any, other_any, *refs):
-    parts, (comp_ref, turned_ref, lists_ref, cs, ints, other_ints, waiting, sems) = refs[:-8], refs[-8:]
+    parts, refs = refs[:-8], refs[-8:]
+    comp_ref, turned_ref, lists_ref, cs, ints, other_ints, waiting, sems = refs
     copies = [
         pltpu.make_async_copy(ints_any, ints, sems.at[0]),
         pltpu.make_async_copy(other_any, other_ints, sems.at[1]),
@@ -299,27 +299,25 @@
             for n in range(parts[1].shape[0]):
                 comp_ref[n * CORES + core] = parts[1][n, core]
     store_rows(cs, centre_rows([comp_ref[:, i, :] for i in range(3)], comp_ref[:, 3, :]))
+    for copy in copies:
+        copy.wait()
+    make_lists(plan, ints, other_ints, lists_ref, waiting)
     for domain in range(plan.domains):
         for start, size in chunks(plan.half, 128):
             turned_ref[domain, start : start + size, :] = cs[
                 domain, :, start : start + size
             ].T.astype(bf16)
-    for copy in copies:
-        copy.wait()
-    make_lists(plan, ints, other_ints, lists_ref, waiting)
-
-
-def first_kernel(plan, scale, lists_any, ints_ref, turned_ref, *refs):
-    copies_of_state, refs = refs[:-9], refs[-9:]
-    out_ref, rim_ref, state_ref, points_ref, kept_ref, xs, acc, lists_ref, sem = refs
-    copy = pltpu.make_async_copy(lists_any, lists_ref, sem)
-    copy.start()
+
+
+def first_kernel(plan, scale, lists_ref, ints_ref, turned_ref, *refs):
+    copies_of_state, refs = refs[:-7], refs[-7:]
+    out_ref, rim_ref, state_ref, points_ref, kept_ref, xs, acc = refs
     read = chosen(plan, ints_ref, copies_of_state)
     for core in range(CORES):
         for tile in range(plan.own):
             lanes = slice(tile * plan.lanes, (tile + 1) * plan.lanes)
             state_ref[:, core * plan.own + tile, :] = read(core, slice(None), lanes)
-    sum_gaussians(plan, scale, lists_ref, copy, state_ref, turned_ref, points_ref, out_ref, rim_ref,
+    sum_gaussians(plan, scale, lists_ref, state_ref, turned_ref, points_ref, out_ref, rim_ref,
                   kept_ref, xs, acc)
 
 
@@ -330,16 +328,14 @@
         yield old_ref[i] + time_step * v, v
 
 
-def next_kernel(plan, scale, lists_any, old_ref, force_ref, swapped_ref, turned_ref,
-                out_ref, rim_ref, state_ref, points_ref, kept_ref, xs, acc, lists_ref, sem):
-    copy = pltpu.make_async_copy(lists_any, lists_ref, sem)
-    copy.start()
+def next_kernel(plan, scale, lists_ref, old_ref, force_ref, swapped_ref, turned_ref,
+                out_ref, rim_ref, state_ref, points_ref, kept_ref, xs, acc):
     for i, (x, v) in enumerate(stepped(old_ref, force_ref, swapped_ref)):
         state_ref[i] = x
         state_ref[3 + i] = v
     state_ref[6] = old_ref[6]
     state_ref[7] = old_ref[7]
-    sum_gaussians(plan, scale, lists_ref, copy, state_ref, turned_ref, points_ref, out_ref, rim_ref,
+    sum_gaussians(plan, scale, lists_ref, state_ref, turned_ref, points_ref, out_ref, rim_ref,
                   kept_ref, xs, acc)
 
 
@@ -376,16 +372,13 @@
         map_ref[:, high] = jnp.where(first, got, keep)
 
 
-def pair_kernel(plan, gain, lists_any, state_ref, far_ref, points_ref, out_ref, table, cs, rs, rows,
-                turned, lists_ref, sem):
-    copy = pltpu.make_async_copy(lists_any, lists_ref, sem)
-    copy.start()
+def pair_kernel(plan, gain, lists_ref, state_ref, far_ref, points_ref, out_ref, table, cs, rs, rows,
+                turned):
     own, near, listed = plan.own, plan.near, plan.listed
     core = lax.axis_index("core")
     base = pl.multiple_of(core * own, own)
     extent = own + 2 * listed
     table[...] = jnp.zeros_like(table)
-    copy.wait()
     for i, source in enumerate((0, 1, 2, 6)):
         table[i, 0:own, :] = state_ref[source, pl.ds(base, own), :]
         for k in range(listed):
@@ -415,10 +408,8 @@
             out_ref[i, tile : tile + 1, :] = strength * push
 
 
-def push_kernel(plan, gain, replicas, lists_any, state_ref, comp_ref, pair_ref, kept_ref, *refs):
-    parts, (out_ref, rs, rows, means, sums, lists_ref, sem) = refs[:-7], refs[-7:]
-    copy = pltpu.make_async_copy(lists_any, lists_ref, sem)
-    copy.start()
+def push_kernel(plan, gain, replicas, lists_ref, state_ref, comp_ref, pair_ref, kept_ref, *refs):
+    parts, (out_ref, rs, rows, means, sums) = refs[:-5], refs[-5:]
     tiles, lanes = plan.tiles, plan.lanes
     mean = tree_sum(parts) / replicas
     for n in range(plan.half // lanes):
@@ -428,7 +419,6 @@
     store_rows(rs, pull_rows([comp_ref[:, i, :] for i in range(3)], coefficient))
     rows[...] = rs[...].astype(bf16)
     sums[...] = jnp.zeros_like(sums)
-    copy.wait()
 
     def one_pair(place, owner, first, second):
         total = None
@@ -590,18 +580,18 @@
         comp_parts = [both_comps, everywhere(both_comps, "z")]
         states = [both_state, everywhere(both_state, "rep")]
     width = -(-((tiles * owned + domains) // 2 + UNROLL + 1) // lanes) * lanes
-    lists_shape = shape(4 + plan.near, width, dtype=jnp.int32)
-    scalars = [pltpu.SMEM(lists_shape.shape, jnp.int32), pltpu.SemaphoreType.DMA]
+    lists_kept = pltpu.SMEM((4 + plan.near, width), jnp.int32)
     comps, turned, lists = call(
         functools.partial(prepare_kernel, plan),
         [ints, other_ints] + comp_parts,
-        [shape(domains, 8, half), shape(domains, half, DEPTH, dtype=bf16), lists_shape],
+        [shape(domains, 8, half), shape(domains, half, DEPTH, dtype=bf16), lists_kept],
         [(domains, DEPTH, half), pltpu.SMEM(ints.shape, jnp.int32),
          pltpu.SMEM(ints.shape, jnp.int32), pltpu.SMEM((domains,), jnp.int32),
          pltpu.SemaphoreType.DMA((2,))],
         spaces=[ANY, ANY] + [VMEM] * len(comp_parts),
         out_spaces=[VMEM, VMEM, SMEM],
     )
+    lists = pltpu.with_memory_space_constraint(lists, pltpu.SMEM)
 
     map_gain = map_scale / (owned * components)
     scale = 1.0 / (owned * own * lanes)
@@ -626,16 +616,16 @@
                 functools.partial(first_kernel, plan, scale),
                 [lists, ints, turned] + states,
                 outs,
-                scratch + scalars,
-                spaces=[ANY] + [VMEM] * (2 + len(states)),
+                scratch,
+                spaces=[SMEM] + [VMEM] * (2 + len(states)),
             )
         else:
             partial, rim, state, points, kept = call(
                 functools.partial(next_kernel, plan, scale),
                 [lists, state, force, swapped, turned],
                 outs,
-                scratch + scalars,
-                spaces=[ANY] + [VMEM] * 4,
+                scratch,
+                spaces=[SMEM] + [VMEM] * 4,
             )
         far = lax.ppermute(rim, ("z", "core"), onward)
         if plan.few:
@@ -657,16 +647,16 @@
             [lists, state, far, points],
             shape(3, own, lanes),
             [(4, padded, lanes), (padded, DEPTH, lanes), (padded, ROWS, lanes),
-             ((padded, ROWS, lanes), bf16), ((padded, lanes, DEPTH), bf16)] + scalars,
-            spaces=[ANY] + [VMEM] * 3,
+             ((padded, ROWS, lanes), bf16), ((padded, lanes, DEPTH), bf16)],
+            spaces=[SMEM] + [VMEM] * 3,
         )
         force = call(
             functools.partial(push_kernel, plan, map_gain, float(replicas)),
             [lists, state, comps, pair, kept] + parts,
             shape(4, tiles, lanes),
             [(domains, ROWS, half), ((domains, ROWS, half), bf16), (half // lanes, domains, lanes),
-             (tiles + 1, ROWS, lanes)] + scalars,
-            spaces=[ANY] + [VMEM] * (4 + len(parts)),
+             (tiles + 1, ROWS, lanes)],
+            spaces=[SMEM] + [VMEM] * (4 + len(parts)),
         )
         swapped = swap_cores(force)
 

time: 78.3 us -> 74.9 us (0.957)
  Pallas kernels: 27.7 us -> 24.3 us
    pallas_call x12, Pallas kernels: 27.7 us -> 24.3 us  [call(): pl.pallas_call(kernel, out_shape=tuple(outs) if many else outs, in_specs=...]
  transfers between devices with their start and end apart: 23 -> 23, of which waited for: 12 -> 12; matrix products, arithmetic and copies ran while one was open for 0% -> 0% of each run, Pallas kernels for 8% -> 6%
where the time goes in v8:
time: 74.9 us; the launch traced here: 74.7 us
  starting transfers between devices  25.9 us (35%)
  Pallas kernels  24.3 us (32%)
  waiting for transfers between devices  23.7 us (32%)
  between operations  0.81 us (1%)
    ppermute x18, starting transfers between devices, exchange(): others.append(lax.ppermute(value, axis, [(i, i ^ n) for i in range(count)]))  25.1 us
    pallas_call x12, Pallas kernels, call(): pl.pallas_call(kernel, out_shape=tuple(outs) if many else outs, in_specs=...  24.3 us
    ppermute x2, waiting for transfers between devices, program(): far = lax.ppermute(rim, ('z', 'core'), onward)  10.8 us
    ppermute x18, waiting for transfers between devices, exchange(): others.append(lax.ppermute(value, axis, [(i, i ^ n) for i in range(count)]))  9.65 us
    ppermute x3, waiting for transfers between devices, swap_cores(): return lax.ppermute(value, 'core', [(0, 1), (1, 0)])  3.28 us
  transfers between devices with their start and end apart: 23, of which 12 were waited for; matrix products, arithmetic and copies ran while one was open for 0% of the time, Pallas kernels for 6%

profile of v8, /device:TPU:0, one launch (start us, length us, event | category | flops | bytes accessed | tf_op | source)
XLA Modules:
  0.0 74.7 jit_solution(14851051860129799776)
XLA Ops:
  0.6 1.0 %shard_map.148 = (f32[8,1792]{1,0:T(8,128)S(1)}, f32[8,1792]{1,0:T(8,128)S(1)}, s32[16,128]{1,0:T(8,128)S(1)}) custom-call(f32[3,1,1024]{2,1,0:T(1,128)} %bitcast.13, f32[3,1,1024]{2,1,0:T(1,128)} %bitcast.14, f32[1,1024]{1,0:T(1,128)} %bitcast.15, f32[1,1024]{1,0:T(1,128)} %bitcast.16, f32[3,1024]{1,0:T(4,128)} %centre_hbm.1, f32[1,1024]{1,0:T(1,128)} %bitcast.17, ...), custom_call_target="tpu_custom_call" | custom-call | tf_op jit(solution)/shard_map/pallas_call | solution.py:478
  1.6 0.6 collective-permute-start
  2.2 0.9 %collective-permute-done.got_ref = f32[8,1792]{1,0:T(8,128)S(1)} collective-permute-done((f32[8,1792]{1,0:T(8,128)S(1)}, f32[8,1792]{1,0:T(8,128)S(1)}, u32[]{:S(2)}, u32[]{:S(2)}) %collective-permute-start) | collective-permute-done | bytes 57376 | tf_op jit(solution)/shard_map/ppermute | solution.py:493
  3.1 5.0 %collective-permute-start.3 = (f32[2,8,512]{2,1,0:T(8,128)S(1)}, f32[2,8,512]{2,1,0:T(8,128)S(1)}, u32[]{:S(2)}, u32[]{:S(2)}) collective-permute-start(f32[2,8,512]{2,1,0:T(8,128)S(1)} %get-tuple-element.29.refs_0_), channel_id=1, source_target_pairs={{0,6},{2,4},{4,2},{6,0},{1,7},{3,5},{5,3},{7,1},{8,14},{10,12},{12... | collective-permute-start | bytes 98312 | tf_op jit(solution)/shard_map/ppermute | solution.py:508
  8.1 2.4 %collective-permute-start.6 = (f32[2,8,1024]{2,1,0:T(8,128)S(1)}, f32[2,8,1024]{2,1,0:T(8,128)S(1)}, u32[]{:S(2)}, u32[]{:S(2)}) collective-permute-start(f32[2,8,1024]{2,1,0:T(8,128)S(1)} %get-tuple-element.32.refs_0_), channel_id=1, source_target_pairs={{0,24},{8,16},{16,8},{24,0},{1,25},{9,17},{17,9},{25,1},{2,26},{10... | collective-permute-start | bytes 196616 | tf_op jit(solution)/shard_map/ppermute | solution.py:508
  11.0 0.5 collective-permute-start.4
  11.6 0.6 collective-permute-start.1
  12.2 4.2 %collective-permute-done.2.refs_2_ = f32[2,8,512]{2,1,0:T(8,128)S(1)} collective-permute-done((f32[2,8,512]{2,1,0:T(8,128)S(1)}, f32[2,8,512]{2,1,0:T(8,128)S(1)}, u32[]{:S(2)}, u32[]{:S(2)}) %collective-permute-start.2) | collective-permute-done | bytes 32800 | tf_op jit(solution)/shard_map/ppermute | solution.py:508
  16.4 1.9 %shard_map.150 = (f32[8,8,512]{2,1,0:T(8,128)S(1)}, bf16[8,512,32]{2,1,0:T(8,128)(2,1)S(1)}, s32[10,128]{1,0:T(8,128)S(4)}) custom-call(s32[16,128]{1,0:T(8,128)S(1)} %get-tuple-element.25.ints_any.ints_ref, s32[16,128]{1,0:T(8,128)S(1)} %get-tuple-element.28.other_any, f32[2,8,512]{2,1,0:T(8,128)S(1)} %get-tuple-element.29.refs_0_, ...), custom_call_target="tpu_custom_call" | custom-call | tf_op jit(solution)/shard_map/pallas_call | solution.py:478
  18.3 4.8 %shard_map.151 = (f32[8,512]{1,0:T(8,128)S(1)}, f32[8,128]{1,0:T(8,128)S(1)}, f32[8,16,128]{2,1,0:T(8,128)S(1)}, bf16[17,32,128]{2,1,0:T(8,128)(2,1)S(1)}, f32[40,512,256]{2,1,0:T(8,128)S(1)}) custom-call(s32[10,128]{1,0:T(8,128)S(4)} %get-tuple-element.30.lists_ref, s32[16,128]{1,0:T(8,128)S(1)} %get-tuple-element.25.ints_any.ints_ref, ...), custom_call_target="tpu_custom_call" | custom-call | tf_op jit(solution)/shard_map/pallas_call | solution.py:478
  23.1 2.6 %collective-permute-start.10 = (f32[8,512]{1,0:T(8,128)S(1)}, f32[8,512]{1,0:T(8,128)S(1)}, u32[]{:S(2)}, u32[]{:S(2)}) collective-permute-start(f32[8,512]{1,0:T(8,128)S(1)} %get-tuple-element.38.refs_0_), channel_id=1, source_target_pairs={{0,24},{8,16},{16,8},{24,0},{1,25},{9,17},{17,9},{25,1},{2,26},{10... | collective-permute-start | bytes 49160 | tf_op jit(solution)/shard_map/ppermute | solution.py:508
  26.1 0.5 collective-permute-start.8
  26.7 1.1 %collective-permute-done.10.refs_3_ = f32[8,512]{1,0:T(8,128)S(1)} collective-permute-done((f32[8,512]{1,0:T(8,128)S(1)}, f32[8,512]{1,0:T(8,128)S(1)}, u32[]{:S(2)}, u32[]{:S(2)}) %collective-permute-start.10) | collective-permute-done | bytes 16416 | tf_op jit(solution)/shard_map/ppermute | solution.py:508
  27.8 1.6 %collective-permute-done.9.refs_2_ = f32[8,512]{1,0:T(8,128)S(1)} collective-permute-done((f32[8,512]{1,0:T(8,128)S(1)}, f32[8,512]{1,0:T(8,128)S(1)}, u32[]{:S(2)}, u32[]{:S(2)}) %collective-permute-start.9) | collective-permute-done | bytes 16416 | tf_op jit(solution)/shard_map/ppermute | solution.py:508
  29.9 1.5 %collective-permute-start.13 = (f32[8,512]{1,0:T(8,128)S(1)}, f32[8,512]{1,0:T(8,128)S(1)}, u32[]{:S(2)}, u32[]{:S(2)}) collective-permute-start(f32[8,512]{1,0:T(8,128)S(1)} %shard_map.153.refs_0_), channel_id=1, source_target_pairs={{0,6},{2,4},{4,2},{6,0},{1,7},{3,5},{5,3},{7,1},{8,14},{10,12},{12... | collective-permute-start | bytes 49160 | tf_op jit(solution)/shard_map/ppermute | solution.py:508
  31.4 0.7 collective-permute-start.12
  32.0 2.3 %collective-permute-start.11 = (f32[8,512]{1,0:T(8,128)S(1)}, f32[8,512]{1,0:T(8,128)S(1)}, u32[]{:S(2)}, u32[]{:S(2)}) collective-permute-start(f32[8,512]{1,0:T(8,128)S(1)} %shard_map.153.refs_0_), channel_id=1, source_target_pairs={{0,2},{2,0},{4,6},{6,4},{1,3},{3,1},{5,7},{7,5},{8,10},{10,8},{12,... | collective-permute-start | bytes 49160 | tf_op jit(solution)/shard_map/ppermute | solution.py:508
  34.3 5.4 %collective-permute-done.7.far_ref = f32[8,128]{1,0:T(8,128)S(1)} collective-permute-done((f32[8,128]{1,0:T(8,128)S(1)}, f32[8,128]{1,0:T(8,128)S(1)}, u32[]{:S(2)}, u32[]{:S(2)}) %collective-permute-start.7) | collective-permute-done | bytes 4128 | tf_op jit(solution)/shard_map/ppermute | solution.py:630
  39.7 1.4 %shard_map.152.pair_ref = f32[3,8,128]{2,1,0:T(8,128)S(1)} custom-call(s32[10,128]{1,0:T(8,128)S(4)} %get-tuple-element.30.lists_ref, f32[8,16,128]{2,1,0:T(8,128)S(1)} %get-tuple-element.33.state_ref.old_ref, f32[8,128]{1,0:T(8,128)S(1)} %collective-permute-done.7.far_ref, bf16[17,32,128]{2,1,0:T(8,128)(2,1)S(1)} %get-tuple-element.36.points_ref), custom_call_target="tpu_custom_call" | custom-call | tf_op jit(solution)/shard_map/pallas_call | solution.py:478
  41.2 4.2 %shard_map.154.force_ref = f32[4,16,128]{2,1,0:T(8,128)S(1)} custom-call(s32[10,128]{1,0:T(8,128)S(4)} %get-tuple-element.30.lists_ref, f32[8,16,128]{2,1,0:T(8,128)S(1)} %get-tuple-element.33.state_ref.old_ref, f32[8,8,512]{2,1,0:T(8,128)S(1)} %get-tuple-element.34.comp_ref, f32[3,8,128]{2,1,0:T(8,128)S(1)} %shard_map.152.pair_ref, ...), custom_call_target="tpu_custom_call" | custom-call | tf_op jit(solution)/shard_map/pallas_call | solution.py:478
  45.5 1.2 %collective-permute-done.14.swapped_ref = f32[4,16,128]{2,1,0:T(8,128)S(1)} collective-permute-done((f32[4,16,128]{2,1,0:T(8,128)S(1)}, f32[4,16,128]{2,1,0:T(8,128)S(1)}, u32[]{:S(2)}, u32[]{:S(2)}) %collective-permute-start.14) | collective-permute-done | bytes 32800 | tf_op jit(solution)/shard_map/ppermute | solution.py:493
  46.7 4.6 %shard_map.155 = (f32[8,512]{1,0:T(8,128)S(1)}, f32[8,128]{1,0:T(8,128)S(1)}, f32[8,16,128]{2,1,0:T(8,128)S(1)}, bf16[17,32,128]{2,1,0:T(8,128)(2,1)S(1)}, f32[40,512,256]{2,1,0:T(8,128)S(1)}) custom-call(s32[10,128]{1,0:T(8,128)S(4)} %get-tuple-element.30.lists_ref, f32[8,16,128]{2,1,0:T(8,128)S(1)} %get-tuple-element.33.state_ref.old_ref, ...), custom_call_target="tpu_custom_call" | custom-call | tf_op jit(solution)/shard_map/pallas_call | solution.py:478
  51.4 1.6 %collective-permute-start.18 = (f32[8,512]{1,0:T(8,128)S(1)}, f32[8,512]{1,0:T(8,128)S(1)}, u32[]{:S(2)}, u32[]{:S(2)}) collective-permute-start(f32[8,512]{1,0:T(8,128)S(1)} %get-tuple-element.43.refs_0_), channel_id=1, source_target_pairs={{0,24},{8,16},{16,8},{24,0},{1,25},{9,17},{17,9},{25,1},{2,26},{10... | collective-permute-start | bytes 49160 | tf_op jit(solution)/shard_map/ppermute | solution.py:508
  53.4 1.5 %collective-permute-start.16 = (f32[8,512]{1,0:T(8,128)S(1)}, f32[8,512]{1,0:T(8,128)S(1)}, u32[]{:S(2)}, u32[]{:S(2)}) collective-permute-start(f32[8,512]{1,0:T(8,128)S(1)} %get-tuple-element.43.refs_0_), channel_id=1, source_target_pairs={{0,8},{8,0},{16,24},{24,16},{1,9},{9,1},{17,25},{25,17},{2,10},{10... | collective-permute-start | bytes 49160 | tf_op jit(solution)/shard_map/ppermute | solution.py:508
  54.9 1.1 %collective-permute-done.18.refs_3_ = f32[8,512]{1,0:T(8,128)S(1)} collective-permute-done((f32[8,512]{1,0:T(8,128)S(1)}, f32[8,512]{1,0:T(8,128)S(1)}, u32[]{:S(2)}, u32[]{:S(2)}) %collective-permute-start.18) | collective-permute-done | bytes 16416 | tf_op jit(solution)/shard_map/ppermute | solution.py:508
  56.1 0.6 collective-permute-done.17.refs_2_
  57.3 4.3 %collective-permute-start.19 = (f32[8,512]{1,0:T(8,128)S(1)}, f32[8,512]{1,0:T(8,128)S(1)}, u32[]{:S(2)}, u32[]{:S(2)}) collective-permute-start(f32[8,512]{1,0:T(8,128)S(1)} %shard_map.157.refs_0_), channel_id=1, source_target_pairs={{0,2},{2,0},{4,6},{6,4},{1,3},{3,1},{5,7},{7,5},{8,10},{10,8},{12,... | collective-permute-start | bytes 49160 | tf_op jit(solution)/shard_map/ppermute | solution.py:508
  61.7 5.4 %collective-permute-done.15.far_ref = f32[8,128]{1,0:T(8,128)S(1)} collective-permute-done((f32[8,128]{1,0:T(8,128)S(1)}, f32[8,128]{1,0:T(8,128)S(1)}, u32[]{:S(2)}, u32[]{:S(2)}) %collective-permute-start.15) | collective-permute-done | bytes 4128 | tf_op jit(solution)/shard_map/ppermute | solution.py:630
  67.0 1.4 %shard_map.156.pair_ref = f32[3,8,128]{2,1,0:T(8,128)S(1)} custom-call(s32[10,128]{1,0:T(8,128)S(4)} %get-tuple-element.30.lists_ref, f32[8,16,128]{2,1,0:T(8,128)S(1)} %get-tuple-element.39.state_ref.old_ref, f32[8,128]{1,0:T(8,128)S(1)} %collective-permute-done.15.far_ref, bf16[17,32,128]{2,1,0:T(8,128)(2,1)S(1)} %get-tuple-element.41.points_ref), custom_call_target="tpu_custom_call" | custom-call | tf_op jit(solution)/shard_map/pallas_call | solution.py:478
  68.5 4.2 %shard_map.158.mine_ref = f32[4,16,128]{2,1,0:T(8,128)S(1)} custom-call(s32[10,128]{1,0:T(8,128)S(4)} %get-tuple-element.30.lists_ref, f32[8,16,128]{2,1,0:T(8,128)S(1)} %get-tuple-element.39.state_ref.old_ref, f32[8,8,512]{2,1,0:T(8,128)S(1)} %get-tuple-element.34.comp_ref, f32[3,8,128]{2,1,0:T(8,128)S(1)} %shard_map.156.pair_ref, ...), custom_call_target="tpu_custom_call" | custom-call | tf_op jit(solution)/shard_map/pallas_call | solution.py:478
  72.8 1.2 %collective-permute-done.22.theirs_ref = f32[4,16,128]{2,1,0:T(8,128)S(1)} collective-permute-done((f32[4,16,128]{2,1,0:T(8,128)S(1)}, f32[4,16,128]{2,1,0:T(8,128)S(1)}, u32[]{:S(2)}, u32[]{:S(2)}) %collective-permute-start.22) | collective-permute-done | bytes 32800 | tf_op jit(solution)/shard_map/ppermute | solution.py:493
  74.0 0.6 shard_map.159
  (26 shorter events, 2.8 us)
Async XLA Ops:
  1.6 1.4 %collective-permute-start = (f32[8,1792]{1,0:T(8,128)S(1)}, f32[8,1792]{1,0:T(8,128)S(1)}, u32[]{:S(2)}, u32[]{:S(2)}) collective-permute-start(f32[8,1792]{1,0:T(8,128)S(1)} %get-tuple-element.27), channel_id=1, source_target_pairs={{0,1},{1,0},{2,3},{3,2},{4,5},{5,4},{6,7},{7,6},{8,9},{9,8},{10,11... | collective-permute-start | bytes 172040 | tf_op jit(solution)/shard_map/ppermute | solution.py:493
  3.1 8.5 %collective-permute-start.3 = (f32[2,8,512]{2,1,0:T(8,128)S(1)}, f32[2,8,512]{2,1,0:T(8,128)S(1)}, u32[]{:S(2)}, u32[]{:S(2)}) collective-permute-start(f32[2,8,512]{2,1,0:T(8,128)S(1)} %get-tuple-element.29.refs_0_), channel_id=1, source_target_pairs={{0,6},{2,4},{4,2},{6,0},{1,7},{3,5},{5,3},{7,1},{8,14},{10,12},{12... | collective-permute-start | bytes 98312 | tf_op jit(solution)/shard_map/ppermute | solution.py:508
  8.1 10.2 %collective-permute-start.6 = (f32[2,8,1024]{2,1,0:T(8,128)S(1)}, f32[2,8,1024]{2,1,0:T(8,128)S(1)}, u32[]{:S(2)}, u32[]{:S(2)}) collective-permute-start(f32[2,8,1024]{2,1,0:T(8,128)S(1)} %get-tuple-element.32.refs_0_), channel_id=1, source_target_pairs={{0,24},{8,16},{16,8},{24,0},{1,25},{9,17},{17,9},{25,1},{2,26},{10... | collective-permute-start | bytes 196616 | tf_op jit(solution)/shard_map/ppermute | solution.py:508
  10.5 7.8 %collective-permute-start.5 = (f32[2,8,1024]{2,1,0:T(8,128)S(1)}, f32[2,8,1024]{2,1,0:T(8,128)S(1)}, u32[]{:S(2)}, u32[]{:S(2)}) collective-permute-start(f32[2,8,1024]{2,1,0:T(8,128)S(1)} %get-tuple-element.32.refs_0_), channel_id=1, source_target_pairs={{0,16},{8,24},{16,0},{24,8},{1,17},{9,25},{17,1},{25,9},{2,18},{10... | collective-permute-start | bytes 196616 | tf_op jit(solution)/shard_map/ppermute | solution.py:508
  11.0 7.3 %collective-permute-start.4 = (f32[2,8,1024]{2,1,0:T(8,128)S(1)}, f32[2,8,1024]{2,1,0:T(8,128)S(1)}, u32[]{:S(2)}, u32[]{:S(2)}) collective-permute-start(f32[2,8,1024]{2,1,0:T(8,128)S(1)} %get-tuple-element.32.refs_0_), channel_id=1, source_target_pairs={{0,8},{8,0},{16,24},{24,16},{1,9},{9,1},{17,25},{25,17},{2,10},{10... | collective-permute-start | bytes 196616 | tf_op jit(solution)/shard_map/ppermute | solution.py:508
  11.6 4.8 %collective-permute-start.2 = (f32[2,8,512]{2,1,0:T(8,128)S(1)}, f32[2,8,512]{2,1,0:T(8,128)S(1)}, u32[]{:S(2)}, u32[]{:S(2)}) collective-permute-start(f32[2,8,512]{2,1,0:T(8,128)S(1)} %get-tuple-element.29.refs_0_), channel_id=1, source_target_pairs={{0,4},{2,6},{4,0},{6,2},{1,5},{3,7},{5,1},{7,3},{8,12},{10,14},{12... | collective-permute-start | bytes 98312 | tf_op jit(solution)/shard_map/ppermute | solution.py:508
  11.6 4.8 %collective-permute-start.1 = (f32[2,8,512]{2,1,0:T(8,128)S(1)}, f32[2,8,512]{2,1,0:T(8,128)S(1)}, u32[]{:S(2)}, u32[]{:S(2)}) collective-permute-start(f32[2,8,512]{2,1,0:T(8,128)S(1)} %get-tuple-element.29.refs_0_), channel_id=1, source_target_pairs={{0,2},{2,0},{4,6},{6,4},{1,3},{3,1},{5,7},{7,5},{8,10},{10,8},{12,... | collective-permute-start | bytes 98312 | tf_op jit(solution)/shard_map/ppermute | solution.py:508
  23.1 4.7 %collective-permute-start.10 = (f32[8,512]{1,0:T(8,128)S(1)}, f32[8,512]{1,0:T(8,128)S(1)}, u32[]{:S(2)}, u32[]{:S(2)}) collective-permute-start(f32[8,512]{1,0:T(8,128)S(1)} %get-tuple-element.38.refs_0_), channel_id=1, source_target_pairs={{0,24},{8,16},{16,8},{24,0},{1,25},{9,17},{17,9},{25,1},{2,26},{10... | collective-permute-start | bytes 49160 | tf_op jit(solution)/shard_map/ppermute | solution.py:508
  25.7 3.7 %collective-permute-start.9 = (f32[8,512]{1,0:T(8,128)S(1)}, f32[8,512]{1,0:T(8,128)S(1)}, u32[]{:S(2)}, u32[]{:S(2)}) collective-permute-start(f32[8,512]{1,0:T(8,128)S(1)} %get-tuple-element.38.refs_0_), channel_id=1, source_target_pairs={{0,16},{8,24},{16,0},{24,8},{1,17},{9,25},{17,1},{25,9},{2,18},{10... | collective-permute-start | bytes 49160 | tf_op jit(solution)/shard_map/ppermute | solution.py:508
  26.1 3.7 %collective-permute-start.8 = (f32[8,512]{1,0:T(8,128)S(1)}, f32[8,512]{1,0:T(8,128)S(1)}, u32[]{:S(2)}, u32[]{:S(2)}) collective-permute-start(f32[8,512]{1,0:T(8,128)S(1)} %get-tuple-element.38.refs_0_), channel_id=1, source_target_pairs={{0,8},{8,0},{16,24},{24,16},{1,9},{9,1},{17,25},{25,17},{2,10},{10... | collective-permute-start | bytes 49160 | tf_op jit(solution)/shard_map/ppermute | solution.py:508
  29.9 11.3 %collective-permute-start.13 = (f32[8,512]{1,0:T(8,128)S(1)}, f32[8,512]{1,0:T(8,128)S(1)}, u32[]{:S(2)}, u32[]{:S(2)}) collective-permute-start(f32[8,512]{1,0:T(8,128)S(1)} %shard_map.153.refs_0_), channel_id=1, source_target_pairs={{0,6},{2,4},{4,2},{6,0},{1,7},{3,5},{5,3},{7,1},{8,14},{10,12},{12... | collective-permute-start | bytes 49160 | tf_op jit(solution)/shard_map/ppermute | solution.py:508
  31.4 9.8 %collective-permute-start.12 = (f32[8,512]{1,0:T(8,128)S(1)}, f32[8,512]{1,0:T(8,128)S(1)}, u32[]{:S(2)}, u32[]{:S(2)}) collective-permute-start(f32[8,512]{1,0:T(8,128)S(1)} %shard_map.153.refs_0_), channel_id=1, source_target_pairs={{0,4},{2,6},{4,0},{6,2},{1,5},{3,7},{5,1},{7,3},{8,12},{10,14},{12... | collective-permute-start | bytes 49160 | tf_op jit(solution)/shard_map/ppermute | solution.py:508
  32.0 9.2 %collective-permute-start.11 = (f32[8,512]{1,0:T(8,128)S(1)}, f32[8,512]{1,0:T(8,128)S(1)}, u32[]{:S(2)}, u32[]{:S(2)}) collective-permute-start(f32[8,512]{1,0:T(8,128)S(1)} %shard_map.153.refs_0_), channel_id=1, source_target_pairs={{0,2},{2,0},{4,6},{6,4},{1,3},{3,1},{5,7},{7,5},{8,10},{10,8},{12,... | collective-permute-start | bytes 49160 | tf_op jit(solution)/shard_map/ppermute | solution.py:508
  34.3 5.4 %collective-permute-start.7 = (f32[8,128]{1,0:T(8,128)S(1)}, f32[8,128]{1,0:T(8,128)S(1)}, u32[]{:S(2)}, u32[]{:S(2)}) collective-permute-start(f32[8,128]{1,0:T(8,128)S(1)} %get-tuple-element.35), channel_id=1, source_target_pairs={{0,2},{2,4},{4,6},{6,0},{3,1},{5,3},{7,5},{1,7},{8,10},{10,12},{12... | collective-permute-start | bytes 12296 | tf_op jit(solution)/shard_map/ppermute | solution.py:630
  45.5 1.3 %collective-permute-start.14 = (f32[4,16,128]{2,1,0:T(8,128)S(1)}, f32[4,16,128]{2,1,0:T(8,128)S(1)}, u32[]{:S(2)}, u32[]{:S(2)}) collective-permute-start(f32[4,16,128]{2,1,0:T(8,128)S(1)} %shard_map.154.force_ref), channel_id=1, source_target_pairs={{0,1},{1,0},{2,3},{3,2},{4,5},{5,4},{6,7},{7,6},{8,9},{9,8},{10,11... | collective-permute-start | bytes 98312 | tf_op jit(solution)/shard_map/ppermute | solution.py:493
  51.4 4.7 %collective-permute-start.18 = (f32[8,512]{1,0:T(8,128)S(1)}, f32[8,512]{1,0:T(8,128)S(1)}, u32[]{:S(2)}, u32[]{:S(2)}) collective-permute-start(f32[8,512]{1,0:T(8,128)S(1)} %get-tuple-element.43.refs_0_), channel_id=1, source_target_pairs={{0,24},{8,16},{16,8},{24,0},{1,25},{9,17},{17,9},{25,1},{2,26},{10... | collective-permute-start | bytes 49160 | tf_op jit(solution)/shard_map/ppermute | solution.py:508
  52.9 3.7 %collective-permute-start.17 = (f32[8,512]{1,0:T(8,128)S(1)}, f32[8,512]{1,0:T(8,128)S(1)}, u32[]{:S(2)}, u32[]{:S(2)}) collective-permute-start(f32[8,512]{1,0:T(8,128)S(1)} %get-tuple-element.43.refs_0_), channel_id=1, source_target_pairs={{0,16},{8,24},{16,0},{24,8},{1,17},{9,25},{17,1},{25,9},{2,18},{10... | collective-permute-start | bytes 49160 | tf_op jit(solution)/shard_map/ppermute | solution.py:508
  53.4 3.7 %collective-permute-start.16 = (f32[8,512]{1,0:T(8,128)S(1)}, f32[8,512]{1,0:T(8,128)S(1)}, u32[]{:S(2)}, u32[]{:S(2)}) collective-permute-start(f32[8,512]{1,0:T(8,128)S(1)} %get-tuple-element.43.refs_0_), channel_id=1, source_target_pairs={{0,8},{8,0},{16,24},{24,16},{1,9},{9,1},{17,25},{25,17},{2,10},{10... | collective-permute-start | bytes 49160 | tf_op jit(solution)/shard_map/ppermute | solution.py:508
  57.2 11.3 %collective-permute-start.21 = (f32[8,512]{1,0:T(8,128)S(1)}, f32[8,512]{1,0:T(8,128)S(1)}, u32[]{:S(2)}, u32[]{:S(2)}) collective-permute-start(f32[8,512]{1,0:T(8,128)S(1)} %shard_map.157.refs_0_), channel_id=1, source_target_pairs={{0,6},{2,4},{4,2},{6,0},{1,7},{3,5},{5,3},{7,1},{8,14},{10,12},{12... | collective-permute-start | bytes 49160 | tf_op jit(solution)/shard_map/ppermute | solution.py:508
  57.3 11.3 %collective-permute-start.20 = (f32[8,512]{1,0:T(8,128)S(1)}, f32[8,512]{1,0:T(8,128)S(1)}, u32[]{:S(2)}, u32[]{:S(2)}) collective-permute-start(f32[8,512]{1,0:T(8,128)S(1)} %shard_map.157.refs_0_), channel_id=1, source_target_pairs={{0,4},{2,6},{4,0},{6,2},{1,5},{3,7},{5,1},{7,3},{8,12},{10,14},{12... | collective-permute-start | bytes 49160 | tf_op jit(solution)/shard_map/ppermute | solution.py:508
  57.3 11.2 %collective-permute-start.19 = (f32[8,512]{1,0:T(8,128)S(1)}, f32[8,512]{1,0:T(8,128)S(1)}, u32[]{:S(2)}, u32[]{:S(2)}) collective-permute-start(f32[8,512]{1,0:T(8,128)S(1)} %shard_map.157.refs_0_), channel_id=1, source_target_pairs={{0,2},{2,0},{4,6},{6,4},{1,3},{3,1},{5,7},{7,5},{8,10},{10,8},{12,... | collective-permute-start | bytes 49160 | tf_op jit(solution)/shard_map/ppermute | solution.py:508
  61.6 5.4 %collective-permute-start.15 = (f32[8,128]{1,0:T(8,128)S(1)}, f32[8,128]{1,0:T(8,128)S(1)}, u32[]{:S(2)}, u32[]{:S(2)}) collective-permute-start(f32[8,128]{1,0:T(8,128)S(1)} %get-tuple-element.40), channel_id=1, source_target_pairs={{0,2},{2,4},{4,6},{6,0},{3,1},{5,3},{7,5},{1,7},{8,10},{10,12},{12... | collective-permute-start | bytes 12296 | tf_op jit(solution)/shard_map/ppermute | solution.py:630
  72.8 1.3 %collective-permute-start.22 = (f32[4,16,128]{2,1,0:T(8,128)S(1)}, f32[4,16,128]{2,1,0:T(8,128)S(1)}, u32[]{:S(2)}, u32[]{:S(2)}) collective-permute-start(f32[4,16,128]{2,1,0:T(8,128)S(1)} %shard_map.158.mine_ref), channel_id=1, source_target_pairs={{0,1},{1,0},{2,3},{3,2},{4,5},{5,4},{6,7},{7,6},{8,9},{9,8},{10,11... | collective-permute-start | bytes 98312 | tf_op jit(solution)/shard_map/ppermute | solution.py:493

commit v9 on v8

--- a/solution.py
+++ b/solution.py
@@ -12,8 +12,8 @@
 CORES = 2
 DEPTH = 32
 ROWS = 16
-CHUNK = 256
-UNROLL = 4
+CHUNK = 128
+UNROLL = 36
 FAR_SQUARE = 1048576.0
 
 time_step = 0.5
@@ -240,11 +240,12 @@
     return (1 - core) * plan.own + lists_ref[3, 1 + side * plan.listed + k]
 
 
-def for_pairs(lists_ref, body):
+def for_pairs(plan, lists_ref, body):
     def step(n, carry):
         for u in range(UNROLL):
-            place = n * UNROLL + u
-            body(place, lists_ref[0, place], lists_ref[1, place], lists_ref[2, place])
+            entry = n * UNROLL + u
+            place = jnp.minimum(entry, plan.most)
+            body(place, lists_ref[0, entry], lists_ref[1, entry], lists_ref[2, entry])
         return carry
 
     lax.fori_loop(0, lists_ref[3, 0], step, 0)
@@ -271,7 +272,7 @@
             acc[owner, part, :] += g[:, :lanes] + g[:, lanes:]
             kept_ref[place, part, :] = g
 
-    for_pairs(lists_ref, one_pair)
+    for_pairs(plan, lists_ref, one_pair)
     square = (lanes, lanes)
     diagonal = lax.broadcasted_iota(jnp.int32, square, 0) == lax.broadcasted_iota(jnp.int32, square, 1)
     for domain in range(plan.domains):
@@ -431,7 +432,7 @@
         sums[first] += total[:, :lanes]
         sums[second] += total[:, lanes:]
 
-    for_pairs(lists_ref, one_pair)
+    for_pairs(plan, lists_ref, one_pair)
 
     def added(row):
         return sums[0:tiles, row, :] + sums[0:tiles, row + 1, :] + sums[0:tiles, row + 2, :]
@@ -601,13 +602,13 @@
     onward = [(2 * i, (2 * i + 2) % domains) for i in range(heights)]
     onward += [((2 * i + 3) % domains, 2 * i + 1) for i in range(heights)]
     padded = -(-(own + 2 * listed + 1) // 8) * 8
-    most = (tiles * owned + domains) // 2 + UNROLL
+    plan.most = (tiles * owned + domains) // 2
     outs = [
         shape(domains, half),
         shape(rim_rows, lanes),
         shape(8, tiles, lanes),
         shape(tiles + 1, DEPTH, lanes, dtype=bf16),
-        shape(most, half, 2 * lanes),
+        shape(plan.most + 1, half, 2 * lanes),
     ]
     scratch = [(tiles + 1, DEPTH, lanes), (domains, half, lanes)]
     for step in range(STEPS):

time: 74.9 us -> 70.6 us (0.943)
  Pallas kernels: 24.3 us -> 20 us
    pallas_call x12, Pallas kernels: 24.3 us -> 20 us  [call(): pl.pallas_call(kernel, out_shape=tuple(outs) if many else outs, in_specs=...]
  transfers between devices with their start and end apart: 23 -> 23, of which waited for: 12 -> 12; matrix products, arithmetic and copies ran while one was open for 0% -> 0% of each run, Pallas kernels for 6% -> 7%
where the time goes in v9:
time: 70.6 us; the launch traced here: 70.4 us
  starting transfers between devices  25.9 us (37%)
  waiting for transfers between devices  23.7 us (34%)
  Pallas kernels  20 us (28%)
  between operations  0.81 us (1%)
    ppermute x18, starting transfers between devices, exchange(): others.append(lax.ppermute(value, axis, [(i, i ^ n) for i in range(count)]))  25.1 us
    pallas_call x12, Pallas kernels, call(): pl.pallas_call(kernel, out_shape=tuple(outs) if many else outs, in_specs=...  20 us
    ppermute x2, waiting for transfers between devices, program(): far = lax.ppermute(rim, ('z', 'core'), onward)  10.8 us
    ppermute x18, waiting for transfers between devices, exchange(): others.append(lax.ppermute(value, axis, [(i, i ^ n) for i in range(count)]))  9.66 us
    ppermute x3, waiting for transfers between devices, swap_cores(): return lax.ppermute(value, 'core', [(0, 1), (1, 0)])  3.28 us
  transfers between devices with their start and end apart: 23, of which 12 were waited for; matrix products, arithmetic and copies ran while one was open for 0% of the time, Pallas kernels for 7%

profile of v9, /device:TPU:0, one launch (start us, length us, event | category | flops | bytes accessed | tf_op | source)
XLA Modules:
  0.0 70.4 jit_solution(12985530455184907092)
XLA Ops:
  0.6 1.0 %shard_map.148 = (f32[8,1792]{1,0:T(8,128)S(1)}, f32[8,1792]{1,0:T(8,128)S(1)}, s32[16,128]{1,0:T(8,128)S(1)}) custom-call(f32[3,1,1024]{2,1,0:T(1,128)} %bitcast.13, f32[3,1,1024]{2,1,0:T(1,128)} %bitcast.14, f32[1,1024]{1,0:T(1,128)} %bitcast.15, f32[1,1024]{1,0:T(1,128)} %bitcast.16, f32[3,1024]{1,0:T(4,128)} %centre_hbm.1, f32[1,1024]{1,0:T(1,128)} %bitcast.17, ...), custom_call_target="tpu_custom_call" | custom-call | tf_op jit(solution)/shard_map/pallas_call | solution.py:479
  1.6 0.6 collective-permute-start
  2.2 0.9 %collective-permute-done.got_ref = f32[8,1792]{1,0:T(8,128)S(1)} collective-permute-done((f32[8,1792]{1,0:T(8,128)S(1)}, f32[8,1792]{1,0:T(8,128)S(1)}, u32[]{:S(2)}, u32[]{:S(2)}) %collective-permute-start) | collective-permute-done | bytes 57376 | tf_op jit(solution)/shard_map/ppermute | solution.py:494
  3.1 5.0 %collective-permute-start.3 = (f32[2,8,512]{2,1,0:T(8,128)S(1)}, f32[2,8,512]{2,1,0:T(8,128)S(1)}, u32[]{:S(2)}, u32[]{:S(2)}) collective-permute-start(f32[2,8,512]{2,1,0:T(8,128)S(1)} %get-tuple-element.29.refs_0_), channel_id=1, source_target_pairs={{0,6},{2,4},{4,2},{6,0},{1,7},{3,5},{5,3},{7,1},{8,14},{10,12},{12... | collective-permute-start | bytes 98312 | tf_op jit(solution)/shard_map/ppermute | solution.py:509
  8.1 2.4 %collective-permute-start.6 = (f32[2,8,1024]{2,1,0:T(8,128)S(1)}, f32[2,8,1024]{2,1,0:T(8,128)S(1)}, u32[]{:S(2)}, u32[]{:S(2)}) collective-permute-start(f32[2,8,1024]{2,1,0:T(8,128)S(1)} %get-tuple-element.32.refs_0_), channel_id=1, source_target_pairs={{0,24},{8,16},{16,8},{24,0},{1,25},{9,17},{17,9},{25,1},{2,26},{10... | collective-permute-start | bytes 196616 | tf_op jit(solution)/shard_map/ppermute | solution.py:509
  11.0 0.5 collective-permute-start.4
  11.6 0.6 collective-permute-start.1
  12.2 4.2 %collective-permute-done.2.refs_2_ = f32[2,8,512]{2,1,0:T(8,128)S(1)} collective-permute-done((f32[2,8,512]{2,1,0:T(8,128)S(1)}, f32[2,8,512]{2,1,0:T(8,128)S(1)}, u32[]{:S(2)}, u32[]{:S(2)}) %collective-permute-start.2) | collective-permute-done | bytes 32800 | tf_op jit(solution)/shard_map/ppermute | solution.py:509
  16.4 1.9 %shard_map.150 = (f32[8,8,512]{2,1,0:T(8,128)S(1)}, bf16[8,512,32]{2,1,0:T(8,128)(2,1)S(1)}, s32[10,128]{1,0:T(8,128)S(4)}) custom-call(s32[16,128]{1,0:T(8,128)S(1)} %get-tuple-element.25.ints_any.ints_ref, s32[16,128]{1,0:T(8,128)S(1)} %get-tuple-element.28.other_any, f32[2,8,512]{2,1,0:T(8,128)S(1)} %get-tuple-element.29.refs_0_, ...), custom_call_target="tpu_custom_call" | custom-call | tf_op jit(solution)/shard_map/pallas_call | solution.py:479
  18.3 3.7 %shard_map.151 = (f32[8,512]{1,0:T(8,128)S(1)}, f32[8,128]{1,0:T(8,128)S(1)}, f32[8,16,128]{2,1,0:T(8,128)S(1)}, bf16[17,32,128]{2,1,0:T(8,128)(2,1)S(1)}, f32[37,512,256]{2,1,0:T(8,128)S(1)}) custom-call(s32[10,128]{1,0:T(8,128)S(4)} %get-tuple-element.30.lists_ref, s32[16,128]{1,0:T(8,128)S(1)} %get-tuple-element.25.ints_any.ints_ref, ...), custom_call_target="tpu_custom_call" | custom-call | tf_op jit(solution)/shard_map/pallas_call | solution.py:479
  22.0 2.5 %collective-permute-start.10 = (f32[8,512]{1,0:T(8,128)S(1)}, f32[8,512]{1,0:T(8,128)S(1)}, u32[]{:S(2)}, u32[]{:S(2)}) collective-permute-start(f32[8,512]{1,0:T(8,128)S(1)} %get-tuple-element.38.refs_0_), channel_id=1, source_target_pairs={{0,24},{8,16},{16,8},{24,0},{1,25},{9,17},{17,9},{25,1},{2,26},{10... | collective-permute-start | bytes 49160 | tf_op jit(solution)/shard_map/ppermute | solution.py:509
  25.1 0.5 collective-permute-start.8
  25.6 1.1 %collective-permute-done.10.refs_3_ = f32[8,512]{1,0:T(8,128)S(1)} collective-permute-done((f32[8,512]{1,0:T(8,128)S(1)}, f32[8,512]{1,0:T(8,128)S(1)}, u32[]{:S(2)}, u32[]{:S(2)}) %collective-permute-start.10) | collective-permute-done | bytes 16416 | tf_op jit(solution)/shard_map/ppermute | solution.py:509
  26.8 1.6 %collective-permute-done.9.refs_2_ = f32[8,512]{1,0:T(8,128)S(1)} collective-permute-done((f32[8,512]{1,0:T(8,128)S(1)}, f32[8,512]{1,0:T(8,128)S(1)}, u32[]{:S(2)}, u32[]{:S(2)}) %collective-permute-start.9) | collective-permute-done | bytes 16416 | tf_op jit(solution)/shard_map/ppermute | solution.py:509
  28.8 1.5 %collective-permute-start.13 = (f32[8,512]{1,0:T(8,128)S(1)}, f32[8,512]{1,0:T(8,128)S(1)}, u32[]{:S(2)}, u32[]{:S(2)}) collective-permute-start(f32[8,512]{1,0:T(8,128)S(1)} %shard_map.153.refs_0_), channel_id=1, source_target_pairs={{0,6},{2,4},{4,2},{6,0},{1,7},{3,5},{5,3},{7,1},{8,14},{10,12},{12... | collective-permute-start | bytes 49160 | tf_op jit(solution)/shard_map/ppermute | solution.py:509
  30.4 0.6 collective-permute-start.12
  31.0 2.3 %collective-permute-start.11 = (f32[8,512]{1,0:T(8,128)S(1)}, f32[8,512]{1,0:T(8,128)S(1)}, u32[]{:S(2)}, u32[]{:S(2)}) collective-permute-start(f32[8,512]{1,0:T(8,128)S(1)} %shard_map.153.refs_0_), channel_id=1, source_target_pairs={{0,2},{2,0},{4,6},{6,4},{1,3},{3,1},{5,7},{7,5},{8,10},{10,8},{12,... | collective-permute-start | bytes 49160 | tf_op jit(solution)/shard_map/ppermute | solution.py:509
  33.3 5.4 %collective-permute-done.7.far_ref = f32[8,128]{1,0:T(8,128)S(1)} collective-permute-done((f32[8,128]{1,0:T(8,128)S(1)}, f32[8,128]{1,0:T(8,128)S(1)}, u32[]{:S(2)}, u32[]{:S(2)}) %collective-permute-start.7) | collective-permute-done | bytes 4128 | tf_op jit(solution)/shard_map/ppermute | solution.py:631
  38.7 1.4 %shard_map.152.pair_ref = f32[3,8,128]{2,1,0:T(8,128)S(1)} custom-call(s32[10,128]{1,0:T(8,128)S(4)} %get-tuple-element.30.lists_ref, f32[8,16,128]{2,1,0:T(8,128)S(1)} %get-tuple-element.33.state_ref.old_ref, f32[8,128]{1,0:T(8,128)S(1)} %collective-permute-done.7.far_ref, bf16[17,32,128]{2,1,0:T(8,128)(2,1)S(1)} %get-tuple-element.36.points_ref), custom_call_target="tpu_custom_call" | custom-call | tf_op jit(solution)/shard_map/pallas_call | solution.py:479
  40.2 3.0 %shard_map.154.force_ref = f32[4,16,128]{2,1,0:T(8,128)S(1)} custom-call(s32[10,128]{1,0:T(8,128)S(4)} %get-tuple-element.30.lists_ref, f32[8,16,128]{2,1,0:T(8,128)S(1)} %get-tuple-element.33.state_ref.old_ref, f32[8,8,512]{2,1,0:T(8,128)S(1)} %get-tuple-element.34.comp_ref, f32[3,8,128]{2,1,0:T(8,128)S(1)} %shard_map.152.pair_ref, ...), custom_call_target="tpu_custom_call" | custom-call | tf_op jit(solution)/shard_map/pallas_call | solution.py:479
  43.3 1.2 %collective-permute-done.14.swapped_ref = f32[4,16,128]{2,1,0:T(8,128)S(1)} collective-permute-done((f32[4,16,128]{2,1,0:T(8,128)S(1)}, f32[4,16,128]{2,1,0:T(8,128)S(1)}, u32[]{:S(2)}, u32[]{:S(2)}) %collective-permute-start.14) | collective-permute-done | bytes 32800 | tf_op jit(solution)/shard_map/ppermute | solution.py:494
  44.5 3.7 %shard_map.155 = (f32[8,512]{1,0:T(8,128)S(1)}, f32[8,128]{1,0:T(8,128)S(1)}, f32[8,16,128]{2,1,0:T(8,128)S(1)}, bf16[17,32,128]{2,1,0:T(8,128)(2,1)S(1)}, f32[37,512,256]{2,1,0:T(8,128)S(1)}) custom-call(s32[10,128]{1,0:T(8,128)S(4)} %get-tuple-element.30.lists_ref, f32[8,16,128]{2,1,0:T(8,128)S(1)} %get-tuple-element.33.state_ref.old_ref, ...), custom_call_target="tpu_custom_call" | custom-call | tf_op jit(solution)/shard_map/pallas_call | solution.py:479
  48.2 1.6 %collective-permute-start.18 = (f32[8,512]{1,0:T(8,128)S(1)}, f32[8,512]{1,0:T(8,128)S(1)}, u32[]{:S(2)}, u32[]{:S(2)}) collective-permute-start(f32[8,512]{1,0:T(8,128)S(1)} %get-tuple-element.43.refs_0_), channel_id=1, source_target_pairs={{0,24},{8,16},{16,8},{24,0},{1,25},{9,17},{17,9},{25,1},{2,26},{10... | collective-permute-start | bytes 49160 | tf_op jit(solution)/shard_map/ppermute | solution.py:509
  50.3 1.5 %collective-permute-start.16 = (f32[8,512]{1,0:T(8,128)S(1)}, f32[8,512]{1,0:T(8,128)S(1)}, u32[]{:S(2)}, u32[]{:S(2)}) collective-permute-start(f32[8,512]{1,0:T(8,128)S(1)} %get-tuple-element.43.refs_0_), channel_id=1, source_target_pairs={{0,8},{8,0},{16,24},{24,16},{1,9},{9,1},{17,25},{25,17},{2,10},{10... | collective-permute-start | bytes 49160 | tf_op jit(solution)/shard_map/ppermute | solution.py:509
  51.8 1.1 %collective-permute-done.18.refs_3_ = f32[8,512]{1,0:T(8,128)S(1)} collective-permute-done((f32[8,512]{1,0:T(8,128)S(1)}, f32[8,512]{1,0:T(8,128)S(1)}, u32[]{:S(2)}, u32[]{:S(2)}) %collective-permute-start.18) | collective-permute-done | bytes 16416 | tf_op jit(solution)/shard_map/ppermute | solution.py:509
  52.9 0.6 collective-permute-done.17.refs_2_
  54.2 4.3 %collective-permute-start.19 = (f32[8,512]{1,0:T(8,128)S(1)}, f32[8,512]{1,0:T(8,128)S(1)}, u32[]{:S(2)}, u32[]{:S(2)}) collective-permute-start(f32[8,512]{1,0:T(8,128)S(1)} %shard_map.157.refs_0_), channel_id=1, source_target_pairs={{0,2},{2,0},{4,6},{6,4},{1,3},{3,1},{5,7},{7,5},{8,10},{10,8},{12,... | collective-permute-start | bytes 49160 | tf_op jit(solution)/shard_map/ppermute | solution.py:509
  58.5 5.4 %collective-permute-done.15.far_ref = f32[8,128]{1,0:T(8,128)S(1)} collective-permute-done((f32[8,128]{1,0:T(8,128)S(1)}, f32[8,128]{1,0:T(8,128)S(1)}, u32[]{:S(2)}, u32[]{:S(2)}) %collective-permute-start.15) | collective-permute-done | bytes 4128 | tf_op jit(solution)/shard_map/ppermute | solution.py:631
  63.9 1.4 %shard_map.156.pair_ref = f32[3,8,128]{2,1,0:T(8,128)S(1)} custom-call(s32[10,128]{1,0:T(8,128)S(4)} %get-tuple-element.30.lists_ref, f32[8,16,128]{2,1,0:T(8,128)S(1)} %get-tuple-element.39.state_ref.old_ref, f32[8,128]{1,0:T(8,128)S(1)} %collective-permute-done.15.far_ref, bf16[17,32,128]{2,1,0:T(8,128)(2,1)S(1)} %get-tuple-element.41.points_ref), custom_call_target="tpu_custom_call" | custom-call | tf_op jit(solution)/shard_map/pallas_call | solution.py:479
  65.4 3.0 %shard_map.158.mine_ref = f32[4,16,128]{2,1,0:T(8,128)S(1)} custom-call(s32[10,128]{1,0:T(8,128)S(4)} %get-tuple-element.30.lists_ref, f32[8,16,128]{2,1,0:T(8,128)S(1)} %get-tuple-element.39.state_ref.old_ref, f32[8,8,512]{2,1,0:T(8,128)S(1)} %get-tuple-element.34.comp_ref, f32[3,8,128]{2,1,0:T(8,128)S(1)} %shard_map.156.pair_ref, ...), custom_call_target="tpu_custom_call" | custom-call | tf_op jit(solution)/shard_map/pallas_call | solution.py:479
  68.5 1.2 %collective-permute-done.22.theirs_ref = f32[4,16,128]{2,1,0:T(8,128)S(1)} collective-permute-done((f32[4,16,128]{2,1,0:T(8,128)S(1)}, f32[4,16,128]{2,1,0:T(8,128)S(1)}, u32[]{:S(2)}, u32[]{:S(2)}) %collective-permute-start.22) | collective-permute-done | bytes 32800 | tf_op jit(solution)/shard_map/ppermute | solution.py:494
  69.7 0.6 shard_map.159
  (26 shorter events, 2.9 us)
Async XLA Ops:
  1.6 1.4 %collective-permute-start = (f32[8,1792]{1,0:T(8,128)S(1)}, f32[8,1792]{1,0:T(8,128)S(1)}, u32[]{:S(2)}, u32[]{:S(2)}) collective-permute-start(f32[8,1792]{1,0:T(8,128)S(1)} %get-tuple-element.27), channel_id=1, source_target_pairs={{0,1},{1,0},{2,3},{3,2},{4,5},{5,4},{6,7},{7,6},{8,9},{9,8},{10,11... | collective-permute-start | bytes 172040 | tf_op jit(solution)/shard_map/ppermute | solution.py:494
  3.1 8.5 %collective-permute-start.3 = (f32[2,8,512]{2,1,0:T(8,128)S(1)}, f32[2,8,512]{2,1,0:T(8,128)S(1)}, u32[]{:S(2)}, u32[]{:S(2)}) collective-permute-start(f32[2,8,512]{2,1,0:T(8,128)S(1)} %get-tuple-element.29.refs_0_), channel_id=1, source_target_pairs={{0,6},{2,4},{4,2},{6,0},{1,7},{3,5},{5,3},{7,1},{8,14},{10,12},{12... | collective-permute-start | bytes 98312 | tf_op jit(solution)/shard_map/ppermute | solution.py:509
  8.1 10.2 %collective-permute-start.6 = (f32[2,8,1024]{2,1,0:T(8,128)S(1)}, f32[2,8,1024]{2,1,0:T(8,128)S(1)}, u32[]{:S(2)}, u32[]{:S(2)}) collective-permute-start(f32[2,8,1024]{2,1,0:T(8,128)S(1)} %get-tuple-element.32.refs_0_), channel_id=1, source_target_pairs={{0,24},{8,16},{16,8},{24,0},{1,25},{9,17},{17,9},{25,1},{2,26},{10... | collective-permute-start | bytes 196616 | tf_op jit(solution)/shard_map/ppermute | solution.py:509
  10.5 7.8 %collective-permute-start.5 = (f32[2,8,1024]{2,1,0:T(8,128)S(1)}, f32[2,8,1024]{2,1,0:T(8,128)S(1)}, u32[]{:S(2)}, u32[]{:S(2)}) collective-permute-start(f32[2,8,1024]{2,1,0:T(8,128)S(1)} %get-tuple-element.32.refs_0_), channel_id=1, source_target_pairs={{0,16},{8,24},{16,0},{24,8},{1,17},{9,25},{17,1},{25,9},{2,18},{10... | collective-permute-start | bytes 196616 | tf_op jit(solution)/shard_map/ppermute | solution.py:509
  11.0 7.3 %collective-permute-start.4 = (f32[2,8,1024]{2,1,0:T(8,128)S(1)}, f32[2,8,1024]{2,1,0:T(8,128)S(1)}, u32[]{:S(2)}, u32[]{:S(2)}) collective-permute-start(f32[2,8,1024]{2,1,0:T(8,128)S(1)} %get-tuple-element.32.refs_0_), channel_id=1, source_target_pairs={{0,8},{8,0},{16,24},{24,16},{1,9},{9,1},{17,25},{25,17},{2,10},{10... | collective-permute-start | bytes 196616 | tf_op jit(solution)/shard_map/ppermute | solution.py:509
  11.6 4.8 %collective-permute-start.2 = (f32[2,8,512]{2,1,0:T(8,128)S(1)}, f32[2,8,512]{2,1,0:T(8,128)S(1)}, u32[]{:S(2)}, u32[]{:S(2)}) collective-permute-start(f32[2,8,512]{2,1,0:T(8,128)S(1)} %get-tuple-element.29.refs_0_), channel_id=1, source_target_pairs={{0,4},{2,6},{4,0},{6,2},{1,5},{3,7},{5,1},{7,3},{8,12},{10,14},{12... | collective-permute-start | bytes 98312 | tf_op jit(solution)/shard_map/ppermute | solution.py:509
  11.6 4.8 %collective-permute-start.1 = (f32[2,8,512]{2,1,0:T(8,128)S(1)}, f32[2,8,512]{2,1,0:T(8,128)S(1)}, u32[]{:S(2)}, u32[]{:S(2)}) collective-permute-start(f32[2,8,512]{2,1,0:T(8,128)S(1)} %get-tuple-element.29.refs_0_), channel_id=1, source_target_pairs={{0,2},{2,0},{4,6},{6,4},{1,3},{3,1},{5,7},{7,5},{8,10},{10,8},{12,... | collective-permute-start | bytes 98312 | tf_op jit(solution)/shard_map/ppermute | solution.py:509
  22.0 4.7 %collective-permute-start.10 = (f32[8,512]{1,0:T(8,128)S(1)}, f32[8,512]{1,0:T(8,128)S(1)}, u32[]{:S(2)}, u32[]{:S(2)}) collective-permute-start(f32[8,512]{1,0:T(8,128)S(1)} %get-tuple-element.38.refs_0_), channel_id=1, source_target_pairs={{0,24},{8,16},{16,8},{24,0},{1,25},{9,17},{17,9},{25,1},{2,26},{10... | collective-permute-start | bytes 49160 | tf_op jit(solution)/shard_map/ppermute | solution.py:509
  24.6 3.7 %collective-permute-start.9 = (f32[8,512]{1,0:T(8,128)S(1)}, f32[8,512]{1,0:T(8,128)S(1)}, u32[]{:S(2)}, u32[]{:S(2)}) collective-permute-start(f32[8,512]{1,0:T(8,128)S(1)} %get-tuple-element.38.refs_0_), channel_id=1, source_target_pairs={{0,16},{8,24},{16,0},{24,8},{1,17},{9,25},{17,1},{25,9},{2,18},{10... | collective-permute-start | bytes 49160 | tf_op jit(solution)/shard_map/ppermute | solution.py:509
  25.1 3.7 %collective-permute-start.8 = (f32[8,512]{1,0:T(8,128)S(1)}, f32[8,512]{1,0:T(8,128)S(1)}, u32[]{:S(2)}, u32[]{:S(2)}) collective-permute-start(f32[8,512]{1,0:T(8,128)S(1)} %get-tuple-element.38.refs_0_), channel_id=1, source_target_pairs={{0,8},{8,0},{16,24},{24,16},{1,9},{9,1},{17,25},{25,17},{2,10},{10... | collective-permute-start | bytes 49160 | tf_op jit(solution)/shard_map/ppermute | solution.py:509
  28.8 11.3 %collective-permute-start.13 = (f32[8,512]{1,0:T(8,128)S(1)}, f32[8,512]{1,0:T(8,128)S(1)}, u32[]{:S(2)}, u32[]{:S(2)}) collective-permute-start(f32[8,512]{1,0:T(8,128)S(1)} %shard_map.153.refs_0_), channel_id=1, source_target_pairs={{0,6},{2,4},{4,2},{6,0},{1,7},{3,5},{5,3},{7,1},{8,14},{10,12},{12... | collective-permute-start | bytes 49160 | tf_op jit(solution)/shard_map/ppermute | solution.py:509
  30.4 9.8 %collective-permute-start.12 = (f32[8,512]{1,0:T(8,128)S(1)}, f32[8,512]{1,0:T(8,128)S(1)}, u32[]{:S(2)}, u32[]{:S(2)}) collective-permute-start(f32[8,512]{1,0:T(8,128)S(1)} %shard_map.153.refs_0_), channel_id=1, source_target_pairs={{0,4},{2,6},{4,0},{6,2},{1,5},{3,7},{5,1},{7,3},{8,12},{10,14},{12... | collective-permute-start | bytes 49160 | tf_op jit(solution)/shard_map/ppermute | solution.py:509
  31.0 9.2 %collective-permute-start.11 = (f32[8,512]{1,0:T(8,128)S(1)}, f32[8,512]{1,0:T(8,128)S(1)}, u32[]{:S(2)}, u32[]{:S(2)}) collective-permute-start(f32[8,512]{1,0:T(8,128)S(1)} %shard_map.153.refs_0_), channel_id=1, source_target_pairs={{0,2},{2,0},{4,6},{6,4},{1,3},{3,1},{5,7},{7,5},{8,10},{10,8},{12,... | collective-permute-start | bytes 49160 | tf_op jit(solution)/shard_map/ppermute | solution.py:509
  33.3 5.4 %collective-permute-start.7 = (f32[8,128]{1,0:T(8,128)S(1)}, f32[8,128]{1,0:T(8,128)S(1)}, u32[]{:S(2)}, u32[]{:S(2)}) collective-permute-start(f32[8,128]{1,0:T(8,128)S(1)} %get-tuple-element.35), channel_id=1, source_target_pairs={{0,2},{2,4},{4,6},{6,0},{3,1},{5,3},{7,5},{1,7},{8,10},{10,12},{12... | collective-permute-start | bytes 12296 | tf_op jit(solution)/shard_map/ppermute | solution.py:631
  43.2 1.3 %collective-permute-start.14 = (f32[4,16,128]{2,1,0:T(8,128)S(1)}, f32[4,16,128]{2,1,0:T(8,128)S(1)}, u32[]{:S(2)}, u32[]{:S(2)}) collective-permute-start(f32[4,16,128]{2,1,0:T(8,128)S(1)} %shard_map.154.force_ref), channel_id=1, source_target_pairs={{0,1},{1,0},{2,3},{3,2},{4,5},{5,4},{6,7},{7,6},{8,9},{9,8},{10,11... | collective-permute-start | bytes 98312 | tf_op jit(solution)/shard_map/ppermute | solution.py:494
  48.2 4.7 %collective-permute-start.18 = (f32[8,512]{1,0:T(8,128)S(1)}, f32[8,512]{1,0:T(8,128)S(1)}, u32[]{:S(2)}, u32[]{:S(2)}) collective-permute-start(f32[8,512]{1,0:T(8,128)S(1)} %get-tuple-element.43.refs_0_), channel_id=1, source_target_pairs={{0,24},{8,16},{16,8},{24,0},{1,25},{9,17},{17,9},{25,1},{2,26},{10... | collective-permute-start | bytes 49160 | tf_op jit(solution)/shard_map/ppermute | solution.py:509
  49.8 3.7 %collective-permute-start.17 = (f32[8,512]{1,0:T(8,128)S(1)}, f32[8,512]{1,0:T(8,128)S(1)}, u32[]{:S(2)}, u32[]{:S(2)}) collective-permute-start(f32[8,512]{1,0:T(8,128)S(1)} %get-tuple-element.43.refs_0_), channel_id=1, source_target_pairs={{0,16},{8,24},{16,0},{24,8},{1,17},{9,25},{17,1},{25,9},{2,18},{10... | collective-permute-start | bytes 49160 | tf_op jit(solution)/shard_map/ppermute | solution.py:509
  50.3 3.7 %collective-permute-start.16 = (f32[8,512]{1,0:T(8,128)S(1)}, f32[8,512]{1,0:T(8,128)S(1)}, u32[]{:S(2)}, u32[]{:S(2)}) collective-permute-start(f32[8,512]{1,0:T(8,128)S(1)} %get-tuple-element.43.refs_0_), channel_id=1, source_target_pairs={{0,8},{8,0},{16,24},{24,16},{1,9},{9,1},{17,25},{25,17},{2,10},{10... | collective-permute-start | bytes 49160 | tf_op jit(solution)/shard_map/ppermute | solution.py:509
  54.1 11.3 %collective-permute-start.21 = (f32[8,512]{1,0:T(8,128)S(1)}, f32[8,512]{1,0:T(8,128)S(1)}, u32[]{:S(2)}, u32[]{:S(2)}) collective-permute-start(f32[8,512]{1,0:T(8,128)S(1)} %shard_map.157.refs_0_), channel_id=1, source_target_pairs={{0,6},{2,4},{4,2},{6,0},{1,7},{3,5},{5,3},{7,1},{8,14},{10,12},{12... | collective-permute-start | bytes 49160 | tf_op jit(solution)/shard_map/ppermute | solution.py:509
  54.1 11.3 %collective-permute-start.20 = (f32[8,512]{1,0:T(8,128)S(1)}, f32[8,512]{1,0:T(8,128)S(1)}, u32[]{:S(2)}, u32[]{:S(2)}) collective-permute-start(f32[8,512]{1,0:T(8,128)S(1)} %shard_map.157.refs_0_), channel_id=1, source_target_pairs={{0,4},{2,6},{4,0},{6,2},{1,5},{3,7},{5,1},{7,3},{8,12},{10,14},{12... | collective-permute-start | bytes 49160 | tf_op jit(solution)/shard_map/ppermute | solution.py:509
  54.2 11.2 %collective-permute-start.19 = (f32[8,512]{1,0:T(8,128)S(1)}, f32[8,512]{1,0:T(8,128)S(1)}, u32[]{:S(2)}, u32[]{:S(2)}) collective-permute-start(f32[8,512]{1,0:T(8,128)S(1)} %shard_map.157.refs_0_), channel_id=1, source_target_pairs={{0,2},{2,0},{4,6},{6,4},{1,3},{3,1},{5,7},{7,5},{8,10},{10,8},{12,... | collective-permute-start | bytes 49160 | tf_op jit(solution)/shard_map/ppermute | solution.py:509
  58.5 5.4 %collective-permute-start.15 = (f32[8,128]{1,0:T(8,128)S(1)}, f32[8,128]{1,0:T(8,128)S(1)}, u32[]{:S(2)}, u32[]{:S(2)}) collective-permute-start(f32[8,128]{1,0:T(8,128)S(1)} %get-tuple-element.40), channel_id=1, source_target_pairs={{0,2},{2,4},{4,6},{6,0},{3,1},{5,3},{7,5},{1,7},{8,10},{10,12},{12... | collective-permute-start | bytes 12296 | tf_op jit(solution)/shard_map/ppermute | solution.py:631
  68.4 1.3 %collective-permute-start.22 = (f32[4,16,128]{2,1,0:T(8,128)S(1)}, f32[4,16,128]{2,1,0:T(8,128)S(1)}, u32[]{:S(2)}, u32[]{:S(2)}) collective-permute-start(f32[4,16,128]{2,1,0:T(8,128)S(1)} %shard_map.158.mine_ref), channel_id=1, source_target_pairs={{0,1},{1,0},{2,3},{3,2},{4,5},{5,4},{6,7},{7,6},{8,9},{9,8},{10,11... | collective-permute-start | bytes 98312 | tf_op jit(solution)/shard_map/ppermute | solution.py:494
